TPU v7x, 32 devices: a whole 2x2x4 slice. The times are simulated.
32 devices in a mesh: dp: 8 (over y, x, core), tensor: 4 (over z).
Axes of the slice: x: 2, y: 2, z: 4, core: 2. Of those that a mesh axis runs over, the one named last changes fastest.
Arguments:
- tokens: bfloat16 [5120, 2048], P('dp'), may hold values from -6 to 6
- cotangent: bfloat16 [5120, 2048], P('dp'), may hold values from -6 to 6
- token_slots: int32 [5120], replicated, may hold values from 0 to 8191, as said below
- lengths: int32 [8, 3], P('dp'), may hold values from 0 to 1024, as said below
- mixer_gain: bfloat16 [2048], replicated, may hold values from 0.5 to 1.5
- query_weight: bfloat16 [2048, 1024], P(None, 'tensor'), may hold values from -0.125 to 0.125
- key_weight: bfloat16 [2048, 1024], P(None, 'tensor'), may hold values from -0.125 to 0.125
- value_weight: bfloat16 [2048, 2048], P(None, 'tensor'), may hold values from -0.125 to 0.125
- gate_weight: bfloat16 [2048, 2048], P(None, 'tensor'), may hold values from -0.125 to 0.125
- decay_down: bfloat16 [2048, 16], replicated, may hold values from -0.125 to 0.125
- decay_up: bfloat16 [1024, 16], P('tensor'), may hold values from -1.5 to 1.5
- decay_bias: bfloat16 [1024], P('tensor'), may hold values from -3 to 5
- head_gain: bfloat16 [512], replicated, may hold values from 0.5 to 1.5
- out_weight: bfloat16 [2048, 2048], P('tensor'), may hold values from -0.125 to 0.125
- feed_gain: bfloat16 [2048], replicated, may hold values from 0.5 to 1.5
- feed_gate: bfloat16 [2048, 5632], P(None, 'tensor'), may hold values from -0.125 to 0.125
- feed_up: bfloat16 [2048, 5632], P(None, 'tensor'), may hold values from -0.125 to 0.125
- feed_down: bfloat16 [5632, 2048], P('tensor'), may hold values from -0.078125 to 0.078125
Outputs:
- layer_out: bfloat16 [5120, 2048], P('dp')
- token_grad: bfloat16 [5120, 2048], P('dp')
- grad_mixer_gain: float32 [2048], P('dp')
- grad_query: float32 [2048, 1024], P('dp', 'tensor')
- grad_key: float32 [2048, 1024], P('dp', 'tensor')
- grad_value: float32 [2048, 2048], P('dp', 'tensor')
- grad_gate: float32 [2048, 2048], P('dp', 'tensor')
- grad_decay_down: float32 [2048, 16], P('dp')
- grad_decay_up: float32 [4, 256, 16], P('tensor', 'dp')
- grad_decay_bias: float32 [4, 256], P('tensor', 'dp')
- grad_head_gain: float32 [512], P('dp')
- grad_out: float32 [4, 512, 2048], P('tensor', 'dp')
- grad_feed_gain: float32 [2048], P('dp')
- grad_feed_gate: float32 [2048, 5632], P('dp', 'tensor')
- grad_feed_up: float32 [2048, 5632], P('dp', 'tensor')
- grad_feed_down: float32 [4, 1408, 2048], P('tensor', 'dp')
Inputs may be any that keep to these rules, and one draw needn't show every extreme that they name: `token_slots`: the tokens of one sequence fill consecutive positions of one owner, starting at the sum of the lengths before it; every position below the sum of its owner's lengths receives exactly one token and no position above it; the last owner's positions are all filled; of the 640 tokens of one data device's block at most 128 go to one owner, and some owner receives exactly 128 from every block. The lengths of one owner sum to at most 1024, all lengths together to 5120; a length may be 0; some owner holds one sequence of 1024 tokens.
All inputs are finite; a program needn't handle non-finite values.
Results may differ from a plain program's by a relative error of at most 0.019.
Values may be sent and summed in bfloat16 or wider, within the bound.
A program may use at most 256 MiB of HBM per device.

v0:
```python
import jax
import jax.numpy as jnp
from jax import lax
from jax.sharding import PartitionSpec as P

SPAN = 64
OWN_CAP = 1024


epsilon = 1e-06
head_floor = 1.0
highest_precision = lax.Precision.HIGHEST


def segment_ids(lengths_row, row_count):
    boundary = jnp.cumsum(lengths_row)
    position = jnp.arange(row_count, dtype=jnp.int32)
    return jnp.sum((position[:, None] >= boundary[None, :]).astype(jnp.int32), axis=1)


def norm_rows(row_block, gain_row):
    return (
        row_block
        * lax.rsqrt(jnp.mean(row_block * row_block, axis=-1, keepdims=True) + epsilon)
        * gain_row
    )


def gla_head(query_rows, key_rows, value_rows, gate_logits, out_gate, head_gain, segments):
    row_count = query_rows.shape[0]
    key_width = query_rows.shape[1]
    value_width = value_rows.shape[1]
    blocks = row_count // SPAN
    log_decay = (jax.nn.log_sigmoid(gate_logits) / 16.0).reshape(blocks, SPAN, key_width)
    cumulative = jnp.cumsum(log_decay, axis=1)
    span_total = cumulative[:, SPAN - 1, :]
    queries = (query_rows * float(key_width) ** (-0.5)).reshape(blocks, SPAN, key_width)
    key_block = key_rows.reshape(blocks, SPAN, key_width)
    value_vectors = value_rows.reshape(blocks, SPAN, value_width)
    labels = segments.reshape(blocks, SPAN)
    before = jnp.concatenate([jnp.full((1,), -1, jnp.int32), labels[:-1, SPAN - 1]])
    state_carried_in = (labels == before[:, None]).astype(jnp.float32)
    tail_mask = (labels == labels[:, SPAN - 1 :]).astype(jnp.float32)
    position = jnp.arange(SPAN, dtype=jnp.int32)
    allowed = (position[None, :, None] >= position[None, None, :]) & (
        labels[:, :, None] == labels[:, None, :]
    )
    query_decay_scaled = queries * jnp.exp(cumulative)
    key_grown = key_block * jnp.exp(-cumulative)
    key_final = key_block * jnp.exp(span_total[:, None, :] - cumulative) * tail_mask[:, :, None]
    score_matrix = jnp.einsum(
        "nid,njd->nij", query_decay_scaled, key_grown, precision=highest_precision
    )
    score_matrix = jnp.where(allowed, score_matrix, 0.0)
    inside_span_part = jnp.einsum(
        "kgp,kpc->kgc", score_matrix, value_vectors, precision=highest_precision
    )
    updates = jnp.einsum("njd,nje->nde", key_final, value_vectors, precision=highest_precision)

    def advance(carry_state, inputs):
        update, decay_total, keep_flag = inputs
        return (keep_flag * jnp.exp(decay_total)[:, None] * carry_state + update, carry_state)

    _, state_entering_span = lax.scan(
        advance,
        jnp.zeros((key_width, value_width), jnp.float32),
        (updates, span_total, state_carried_in[:, SPAN - 1]),
    )
    cross_span_part = jnp.einsum(
        "rsm,rmh->rsh",
        query_decay_scaled * state_carried_in[:, :, None],
        state_entering_span,
        precision=highest_precision,
    )
    output = (inside_span_part + cross_span_part).reshape(row_count, value_width)
    scaling = lax.rsqrt(jnp.mean(output * output, axis=-1, keepdims=True) + head_floor)
    return output * scaling * head_gain * jax.nn.silu(out_gate)


def contract_rows(left_mat, right_mat):
    return lax.dot_general(
        left_mat, right_mat, (((0,), (0,)), ((), ())), preferred_element_type=jnp.float32
    )


def times_transposed(left_mat, right_mat):
    return lax.dot_general(
        left_mat, right_mat, (((1,), (1,)), ((), ())), preferred_element_type=jnp.float32
    )


def per_device(
    tokens,
    cotangent,
    token_slots,
    lengths,
    mixer_gain,
    query_weight,
    key_weight,
    value_weight,
    gate_weight,
    decay_down,
    decay_up,
    decay_bias,
    head_gain,
    out_weight,
    feed_gain,
    feed_gate,
    feed_up,
    feed_down,
):
    groups = lax.axis_size("dp")
    member = lax.axis_index("dp")
    local_count = tokens.shape[0]
    model_width = tokens.shape[1]
    peer_cap = OWN_CAP // groups
    my_slots = lax.dynamic_slice_in_dim(token_slots, member * local_count, local_count)
    my_owner = my_slots // OWN_CAP
    owner_ids = jnp.arange(groups, dtype=jnp.int32)
    chosen = (my_owner[:, None] == owner_ids[None, :]).astype(jnp.int32)
    rank_in = jnp.sum((jnp.cumsum(chosen, axis=0) - 1) * chosen, axis=1)
    send_pos = my_owner * peer_cap + rank_in

    def pack_rows(row_block):
        buffer_rows = (
            jnp.zeros((groups * peer_cap, model_width), row_block.dtype).at[send_pos].set(row_block)
        )
        return buffer_rows.reshape(groups, peer_cap, model_width)

    arrived = (
        lax.all_to_all(pack_rows(tokens), "dp", split_axis=0, concat_axis=0, tiled=True),
        lax.all_to_all(pack_rows(cotangent), "dp", split_axis=0, concat_axis=0, tiled=True),
    )
    every_owner = (token_slots // OWN_CAP).reshape(groups, local_count)
    is_mine = (every_owner == member).astype(jnp.int32)
    recv_rank = jnp.cumsum(is_mine, axis=1) - 1
    recv_index = jnp.where(
        is_mine > 0, owner_ids[:, None] * peer_cap + recv_rank, groups * peer_cap
    )
    slot_local = (token_slots % OWN_CAP).reshape(groups, local_count)
    slot_map = (
        jnp.full((groups * peer_cap + 1,), OWN_CAP, jnp.int32)
        .at[recv_index.reshape(-1)]
        .set(slot_local.reshape(-1))[: groups * peer_cap]
    )

    def place_rows(row_block):
        flat_block = row_block.reshape(groups * peer_cap, model_width)
        return (
            jnp.zeros((OWN_CAP + 1, model_width), row_block.dtype)
            .at[slot_map]
            .set(flat_block)[:OWN_CAP]
        )

    def unplace_rows(row_block):
        padded = jnp.concatenate([row_block, jnp.zeros((1, model_width), row_block.dtype)], axis=0)
        return padded[slot_map].reshape(groups, peer_cap, model_width)

    def take_back(returned):
        return returned.reshape(groups * peer_cap, model_width)[send_pos]

    owner_rows = place_rows(arrived[0]).astype(jnp.float32)
    upstream = place_rows(arrived[1])
    labels = segment_ids(lengths[0], OWN_CAP)
    mixed_wide, mixer_norm_back = jax.vjp(norm_rows, owner_rows, mixer_gain.astype(jnp.float32))
    normed = mixed_wide.astype(jnp.bfloat16)

    def project(weight):
        return jnp.dot(normed, weight, preferred_element_type=jnp.float32)

    queries = project(query_weight).astype(jnp.bfloat16)
    keys_low = project(key_weight).astype(jnp.bfloat16)
    value_vectors = project(value_weight).astype(jnp.bfloat16)
    gate_pre = project(gate_weight)
    latent = project(decay_down)
    decay_up_wide = decay_up.astype(jnp.float32)
    logits = lax.dot_general(
        latent, decay_up_wide, (((1,), (1,)), ((), ())), precision=highest_precision
    ) + decay_bias.astype(jnp.float32)

    def mixer(query_wide, key_wide, value_wide, logit_wide, gate_wide, gain_wide):
        return gla_head(query_wide, key_wide, value_wide, logit_wide, gate_wide, gain_wide, labels)

    gated_wide, mixer_back = jax.vjp(
        mixer,
        queries.astype(jnp.float32),
        keys_low.astype(jnp.float32),
        value_vectors.astype(jnp.float32),
        logits,
        gate_pre,
        head_gain.astype(jnp.float32),
    )
    gated_low = gated_wide.astype(jnp.bfloat16)
    mixer_partial = jnp.dot(gated_low, out_weight, preferred_element_type=jnp.float32)
    hidden = owner_rows + lax.psum(mixer_partial, "tensor")
    feed_wide, feed_norm_back = jax.vjp(norm_rows, hidden, feed_gain.astype(jnp.float32))
    feed_normed = feed_wide.astype(jnp.bfloat16)
    gate_hidden = jnp.dot(feed_normed, feed_gate, preferred_element_type=jnp.float32)
    up_hidden = jnp.dot(feed_normed, feed_up, preferred_element_type=jnp.float32)
    sigmoid_gate = jax.nn.sigmoid(gate_hidden)
    swish_gate = gate_hidden * sigmoid_gate
    active = (swish_gate * up_hidden).astype(jnp.bfloat16)
    feed_partial = jnp.dot(active, feed_down, preferred_element_type=jnp.float32)
    layer_rows = (
        hidden + lax.psum(feed_partial.astype(jnp.bfloat16), "tensor").astype(jnp.float32)
    ).astype(jnp.bfloat16)
    upstream_wide = upstream.astype(jnp.float32)
    grad_feed_down = contract_rows(active, upstream)
    d_active = times_transposed(upstream, feed_down)
    d_gate_hidden = (
        d_active * up_hidden * sigmoid_gate * (1.0 + gate_hidden * (1.0 - sigmoid_gate))
    ).astype(jnp.bfloat16)
    d_up_hidden = (d_active * swish_gate).astype(jnp.bfloat16)
    grad_feed_gate = contract_rows(feed_normed, d_gate_hidden)
    grad_feed_up = contract_rows(feed_normed, d_up_hidden)
    feed_part = times_transposed(d_gate_hidden, feed_gate) + times_transposed(d_up_hidden, feed_up)
    d_feed = lax.psum(feed_part, "tensor")
    d_hidden_norm, grad_feed_gain = feed_norm_back(d_feed)
    d_hidden = upstream_wide + d_hidden_norm
    d_mixed = d_hidden.astype(jnp.bfloat16)
    gain_term = jnp.zeros((model_width,), jnp.float32)
    grad_out = contract_rows(gated_low, d_mixed)
    d_gated = times_transposed(d_mixed, out_weight)
    d_query, d_key, d_value, d_logits, d_gate, d_head_gain = mixer_back(d_gated)
    d_query_low = d_query.astype(jnp.bfloat16)
    d_key_low = d_key.astype(jnp.bfloat16)
    d_value_low = d_value.astype(jnp.bfloat16)
    d_gate_low = d_gate.astype(jnp.bfloat16)
    grad_decay_bias = jnp.sum(d_logits, axis=0)
    grad_decay_up = lax.dot_general(
        d_logits, latent, (((0,), (0,)), ((), ())), precision=highest_precision
    )
    latent_part = jnp.dot(d_logits, decay_up_wide, precision=highest_precision)
    mixer_part = (
        times_transposed(d_query_low, query_weight)
        + times_transposed(d_key_low, key_weight)
        + times_transposed(d_value_low, value_weight)
        + times_transposed(d_gate_low, gate_weight)
    )
    summed = lax.psum((mixer_part, latent_part, d_head_gain, gain_term), "tensor")
    d_latent = summed[1]
    d_normed = summed[0] + lax.dot_general(
        d_latent,
        decay_down.astype(jnp.float32),
        (((1,), (1,)), ((), ())),
        precision=highest_precision,
    )
    grad_decay_down = lax.dot_general(
        normed.astype(jnp.float32), d_latent, (((0,), (0,)), ((), ())), precision=highest_precision
    )
    grad_query = contract_rows(normed, d_query_low)
    grad_key = contract_rows(normed, d_key_low)
    grad_value = contract_rows(normed, d_value_low)
    grad_gate = contract_rows(normed, d_gate_low)
    d_rows_norm, grad_mixer_gain = mixer_norm_back(d_normed)
    token_rows = (d_hidden + d_rows_norm).astype(jnp.bfloat16)
    shares = (
        lax.psum_scatter(grad_mixer_gain, "dp", scatter_dimension=0, tiled=True),
        lax.psum_scatter(grad_query, "dp", scatter_dimension=0, tiled=True),
        lax.psum_scatter(grad_key, "dp", scatter_dimension=0, tiled=True),
        lax.psum_scatter(grad_value, "dp", scatter_dimension=0, tiled=True),
        lax.psum_scatter(grad_gate, "dp", scatter_dimension=0, tiled=True),
        lax.psum_scatter(grad_decay_down, "dp", scatter_dimension=0, tiled=True),
        lax.psum_scatter(grad_decay_up, "dp", scatter_dimension=0, tiled=True),
        lax.psum_scatter(grad_decay_bias, "dp", scatter_dimension=0, tiled=True),
        lax.psum_scatter(summed[2], "dp", scatter_dimension=0, tiled=True),
        lax.psum_scatter(grad_out, "dp", scatter_dimension=0, tiled=True),
        lax.psum_scatter(grad_feed_gain, "dp", scatter_dimension=0, tiled=True),
        lax.psum_scatter(grad_feed_gate, "dp", scatter_dimension=0, tiled=True),
        lax.psum_scatter(grad_feed_up, "dp", scatter_dimension=0, tiled=True),
        lax.psum_scatter(grad_feed_down, "dp", scatter_dimension=0, tiled=True),
    )
    returned = (
        lax.all_to_all(unplace_rows(layer_rows), "dp", split_axis=0, concat_axis=0, tiled=True),
        lax.all_to_all(unplace_rows(token_rows), "dp", split_axis=0, concat_axis=0, tiled=True),
    )
    layer_out = take_back(returned[0])
    token_grad = take_back(returned[1])
    rank_width = decay_up.shape[1]
    return (
        layer_out,
        token_grad,
        shares[0],
        shares[1],
        shares[2],
        shares[3],
        shares[4],
        shares[5],
        shares[6].reshape(1, -1, rank_width),
        shares[7].reshape(1, -1),
        shares[8],
        shares[9].reshape(1, shares[9].shape[0], model_width),
        shares[10],
        shares[11],
        shares[12],
        shares[13].reshape(1, shares[13].shape[0], model_width),
    )


def solution(mesh):
    placed = (
        P("dp", None),
        P("dp", None),
        P(),
        P("dp", None),
        P(),
        P(None, "tensor"),
        P(None, "tensor"),
        P(None, "tensor"),
        P(None, "tensor"),
        P(),
        P("tensor", None),
        P("tensor"),
        P(),
        P("tensor", None),
        P(),
        P(None, "tensor"),
        P(None, "tensor"),
        P("tensor", None),
    )
    return jax.shard_map(
        per_device,
        mesh=mesh,
        in_specs=placed,
        out_specs=(
            P("dp", None),
            P("dp", None),
            P("dp"),
            P("dp", "tensor"),
            P("dp", "tensor"),
            P("dp", "tensor"),
            P("dp", "tensor"),
            P("dp", None),
            P("tensor", "dp", None),
            P("tensor", "dp"),
            P("dp"),
            P("tensor", "dp", None),
            P("dp"),
            P("dp", "tensor"),
            P("dp", "tensor"),
            P("tensor", "dp", None),
        ),
        check_vma=False,
    )
```

profile of v0, /device:TPU:0, one launch (start us, length us, event | category | flops | bytes accessed | tf_op | source)
XLA Modules:
  0.0 2135.4 jit_solution(18394428422442927344)
XLA Ops:
  11.7 10.5 scatter_custom_fusion.1
  30.1 19.2 scatter_custom_fusion
  50.7 26.0 %all-to-all-done = bf16[8,128,2048]{2,1,0:T(8,128)(2,1)} async-done(((bf16[8,128,2048]{2,1,0:T(8,128)(2,1)}), bf16[8,128,2048]{2,1,0:T(8,128)(2,1)}, u32[]{:S(2)}, u32[]{:S(2)}) %all-to-all-start) | async-done | bytes 4194336 | tf_op jit(solution)/shard_map/all_to_all | solution.py:131
  76.7 10.1 scatter_custom_fusion.2
  109.0 6.9 fusion.66
  120.2 61.8 %while.36 = (s32[]{:T(128)}, f32[256,512]{1,0:T(8,128)S(1)}, f32[16,256,512]{2,1,0:T(8,128)}, f32[16,256]{1,0:T(8,128)S(1)}, f32[16,256,1]{1,2,0:T(1,128)}, /*in...) while((s32[]{:T(128)}, f32[256,512]{1,0:T(8,128)S(1)}, ...), condition=%wide.region_13.14_spmd.clone, body=%wide.region_12.13_spmd.clone.sunk | while | flops 524547 | bytes 2629268 | solution.py:64
  182.6 10.8 multiply_reduce_fusion.4
  193.5 6.9 multiply_convert_fusion.4
  207.1 10.7 scatter_custom_fusion.3
  222.5 49.1 %all-to-all-done.2 = bf16[8,128,2048]{2,1,0:T(8,128)(2,1)} async-done(((bf16[8,128,2048]{2,1,0:T(8,128)(2,1)}), bf16[8,128,2048]{2,1,0:T(8,128)(2,1)}, u32[]{:S(2)}, u32[]{:S(2)}) %all-to-all-start.2) | async-done | bytes 4194336 | tf_op jit(solution)/shard_map/all_to_all | solution.py:132
  271.6 10.1 scatter_custom_fusion.4
  281.6 216.6 %all-reduce.14.cloned.1.call-done = f32[1024,2048]{1,0:T(8,128)} async-done(((f32[1024,2048]{1,0:T(8,128)}), f32[1024,2048]{1,0:T(8,128)}) %all-reduce.14.cloned.1.call-update) | async-done | bytes 8388624 | tf_op jit(solution)/shard_map/psum | solution.py:195
  507.2 11.9 fusion.87
  519.1 10.3 fusion.86
  529.4 15.1 multiply_convert_fusion.1
  544.5 9.9 fusion.88
  554.4 10.9 convolution_add_fusion.1
  565.4 10.9 convolution_convert_fusion
  576.4 278.9 %all-reduce.18.cloned.1.call-done = f32[1024,2048]{1,0:T(8,128)} async-done(((f32[1024,2048]{1,0:T(8,128)}), f32[1024,2048]{1,0:T(8,128)}) %all-reduce.18.cloned.1.call-update) | async-done | bytes 8388624 | tf_op jit(solution)/shard_map/psum | solution.py:217
  855.3 7.6 multiply_reduce_fusion
  862.9 148.8 %all-reduce.16.cloned.1.call-done = bf16[1024,2048]{1,0:T(8,128)(2,1)} async-done(((bf16[1024,2048]{1,0:T(8,128)(2,1)}), bf16[1024,2048]{1,0:T(8,128)(2,1)}) %all-reduce.16.cloned.1.call-update) | async-done | bytes 4194320 | tf_op jit(solution)/shard_map/psum | solution.py:205
  1011.7 12.5 fusion.6
  1024.2 6.9 multiply_reduce_fusion.3
  1037.7 10.0 fusion.57
  1049.5 9.4 fusion.34
  1068.9 78.4 %while.37 = (s32[]{:T(128)}, f32[256,512]{1,0:T(8,128)S(1)}, f32[16,256,512]{2,1,0:T(8,128)}, f32[16,256]{1,0:T(8,128)S(1)}, f32[16,256,512]{2,1,0:T(8,128)}, /*...) while((s32[]{:T(128)}, f32[256,512]{1,0:T(8,128)S(1)}, ...), condition=%wide.region_25.26_spmd.clone, body=%wide.region_23.25_spmd.clone.sunk | while | flops 786692 | bytes 3157176 | solution.py:64
  1147.4 8.5 fusion.62
  1177.6 9.1 add_add_fusion.2
  1201.2 7.8 fusion.24
  1224.8 254.7 %all-reduce.20.cloned.1.call-done = (f32[1024,2048]{1,0:T(8,128)}, f32[1024,16]{0,1:T(8,128)}) async-done(((f32[1024,2048]{1,0:T(8,128)}, f32[1024,16]{0,1:T(8,128)}), (f32[1024,2048]{1,0:T(8,128)}, f32[1024,16]{0,1:T(8,128)})) %all-reduce.20.cloned.1.call-update) | async-done | bytes 8454160 | tf_op jit(solution)/shard_map/psum | solution.py:240
  1484.2 11.4 fusion.12
  1495.8 11.9 fusion.99
  1507.8 11.9 fusion.98
  1524.5 11.8 gather_fusion
  1541.2 8.8 fusion.5
  1558.6 11.6 gather_fusion.2
  1570.2 26.2 %all-to-all-done.1 = bf16[8,128,2048]{2,1,0:T(8,128)(2,1)} async-done(((bf16[8,128,2048]{2,1,0:T(8,128)(2,1)}), bf16[8,128,2048]{2,1,0:T(8,128)(2,1)}, u32[]{:S(2)}, u32[]{:S(2)}) %all-to-all-start.1) | async-done | bytes 4194336 | tf_op jit(solution)/shard_map/all_to_all | solution.py:274
  1605.1 9.7 gather_fusion.1
  1614.9 60.6 %all-reduce.7 = (f32[2048]{0:T(1024)S(1)}, f32[256]{0:T(256)S(1)}, f32[512]{0:T(512)S(1)}, f32[2048]{0:T(1024)S(1)}) all-reduce(f32[2048]{0:T(1024)S(1)} %get-tuple-element.304, f32[256]{0:T(256)S(1)} %neg.53, f32[512]{0:T(512)S(1)} %copy-done.70, f32[2048]{0:T(1024)S(1)} %copy-done.62), channel_id=2, replica_groups=mesh['dp'=8,'tensor'=4] {'dp'}, use_global_device_ids=true, to_apply=%region_32.33.clone | all-reduce | flops 4864 | bytes 38912
  1676.7 12.3 psum.48
  1689.6 9.9 gather_fusion.3
  1699.5 8.6 reduce-scatter.23.cloned.1.call-done
  1708.1 55.7 %reduce-scatter.19.cloned.1.call-done = f32[256,512]{1,0:T(8,128)} async-done(((f32[2048,512]{1,0:T(8,128)}), f32[256,512]{1,0:T(8,128)}) %reduce-scatter.19.cloned.1.call-update) | async-done | bytes 524304 | tf_op jit(solution)/shard_map/reduce_scatter | solution.py:262
  1763.8 55.1 %reduce-scatter.17.cloned.1.call-done = f32[256,512]{1,0:T(8,128)} async-done(((f32[2048,512]{1,0:T(8,128)}), f32[256,512]{1,0:T(8,128)}) %reduce-scatter.17.cloned.1.call-update) | async-done | bytes 524304 | tf_op jit(solution)/shard_map/reduce_scatter | solution.py:261
  1818.9 37.3 %reduce-scatter.21.cloned.1.call-done = f32[256,16]{0,1:T(8,128)} async-done(((f32[2048,16]{0,1:T(8,128)}), f32[256,16]{0,1:T(8,128)}) %reduce-scatter.21.cloned.1.call-update) | async-done | bytes 16400 | tf_op jit(solution)/shard_map/reduce_scatter | solution.py:263
  1856.1 90.8 %reduce-scatter.29.cloned.1.call-done = f32[176,2048]{1,0:T(8,128)} async-done(((f32[1408,2048]{1,0:T(8,128)}), f32[176,2048]{1,0:T(8,128)}) %reduce-scatter.29.cloned.1.call-update) | async-done | bytes 1441808 | tf_op jit(solution)/shard_map/reduce_scatter | solution.py:271
  1946.9 90.9 %reduce-scatter.27.cloned.1.call-done = f32[256,1408]{1,0:T(8,128)} async-done(((f32[2048,1408]{1,0:T(8,128)}), f32[256,1408]{1,0:T(8,128)}) %reduce-scatter.27.cloned.1.call-update) | async-done | bytes 1441808 | tf_op jit(solution)/shard_map/reduce_scatter | solution.py:270
  2037.8 90.8 %reduce-scatter.25.cloned.1.call-done = f32[256,1408]{1,0:T(8,128)} async-done(((f32[2048,1408]{1,0:T(8,128)}), f32[256,1408]{1,0:T(8,128)}) %reduce-scatter.25.cloned.1.call-update) | async-done | bytes 1441808 | tf_op jit(solution)/shard_map/reduce_scatter | solution.py:269
  (516 shorter events, 301.8 us)
Async XLA Ops:
  7.2 186.3 %copy-start = (bf16[2048,512]{1,0:T(8,128)(2,1)S(1)}, bf16[2048,512]{1,0:T(8,128)(2,1)}, u32[]{:S(2)}) copy-start(bf16[2048,512]{1,0:T(8,128)(2,1)} %param.30) | copy-start | bytes 6291460
  11.7 195.4 %copy-start.64 = (s32[640]{0:T(1024)}, s32[640]{0:T(1024)S(1)}, u32[]{:S(2)}) copy-start(s32[640]{0:T(1024)S(1)} %compare_select_fusion.4) | copy-start | bytes 7684
  22.2 54.5 %all-to-all-start = ((bf16[8,128,2048]{2,1,0:T(8,128)(2,1)}), bf16[8,128,2048]{2,1,0:T(8,128)(2,1)}, u32[]{:S(2)}, u32[]{:S(2)}) async-start(bf16[8,128,2048]{2,1,0:T(8,128)(2,1)} %bitcast.199), calls=%async_computation | async-start | bytes 8388608 | tf_op jit(solution)/shard_map/all_to_all | solution.py:131
  27.5 470.7 %all-reduce.14.cloned.1.call-start = ((), (), s32[]{:S(2)}) async-start(), calls=%async_computation.14 | async-start | bytes 16777216 | tf_op jit(solution)/shard_map/psum | solution.py:195
  28.0 76.0 %copy-start.41 = (s32[16,64]{1,0:T(8,128)}, s32[16,64]{1,0:T(8,128)S(1)}, u32[]{:S(2)}) copy-start(s32[16,64]{1,0:T(8,128)S(1)} %eq.92) | copy-start | bytes 12292
  28.0 62.0 %copy-start.51 = (f32[2048]{0:T(1024)}, f32[2048]{0:T(1024)S(1)}, u32[]{:S(2)}) copy-start(f32[2048]{0:T(1024)S(1)} %convert_element_type.127) | copy-start | bytes 24580
  49.7 54.3 %copy-start.55 = (pred[64,64]{1,0:T(8,128)(4,1)}, pred[64,64]{1,0:T(8,128)(4,1)S(1)}, u32[]{:S(2)}) copy-start(pred[64,64]{1,0:T(8,128)(4,1)S(1)} %iota_compare_fusion) | copy-start | bytes 12292
  49.9 59.1 %copy-start.53 = (f32[16,64]{1,0:T(8,128)}, f32[16,64]{1,0:T(8,128)S(1)}, u32[]{:S(2)}) copy-start(f32[16,64]{1,0:T(8,128)S(1)} %get-tuple-element.369) | copy-start | bytes 12292
  96.7 12.3 copy-start.12
  99.1 9.9 copy-start.15
  182.6 10.8 copy-start.43
  182.6 10.8 copy-start.72
  217.7 53.8 %all-to-all-start.2 = ((bf16[8,128,2048]{2,1,0:T(8,128)(2,1)}), bf16[8,128,2048]{2,1,0:T(8,128)(2,1)}, u32[]{:S(2)}, u32[]{:S(2)}) async-start(bf16[8,128,2048]{2,1,0:T(8,128)(2,1)} %bitcast.200), calls=%async_computation.2 | async-start | bytes 8388608 | tf_op jit(solution)/shard_map/all_to_all | solution.py:132
  222.4 632.9 %all-reduce.18.cloned.1.call-start = ((), (), s32[]{:S(2)}) async-start(), calls=%async_computation.16 | async-start | bytes 16777216 | tf_op jit(solution)/shard_map/psum | solution.py:217
  507.2 11.9 copy-start.23
  507.2 22.2 %slice-start.6 = ((s8[4227072]{0:T(1024)(128)(4,1)}), s8[4194304]{0:T(1024)(128)(4,1)S(1)}, s32[]{:S(2)}) async-start(s8[4227072]{0:T(1024)(128)(4,1)} %bitcast.191), calls=%async_computation.34 | async-start | bytes 8388608
  519.1 10.3 slice-start.7
  544.5 9.9 copy-start.80
  565.3 446.4 %all-reduce.16.cloned.1.call-start = ((), (), s32[]{:S(2)}) async-start(), calls=%async_computation.15 | async-start | bytes 8388608 | tf_op jit(solution)/shard_map/psum | solution.py:205
  576.3 903.2 %all-reduce.20.cloned.1.call-start = ((), (), s32[]{:S(2)}) async-start(), calls=%async_computation.27 | async-start | bytes 16908288 | tf_op jit(solution)/shard_map/psum | solution.py:240
  1011.7 12.5 copy-start.18
  1011.7 12.5 copy-start.30
  1033.1 25.7 %copy-start.34 = (bf16[1024,512]{1,0:T(8,128)(2,1)}, bf16[1024,512]{1,0:T(8,128)(2,1)S(1)}, u32[]{:S(2)}) copy-start(bf16[1024,512]{1,0:T(8,128)(2,1)S(1)} %get-tuple-element.363) | copy-start | bytes 3145732
  1033.2 16.3 slice-start.2
  1034.4 13.4 copy-start.21
  1037.7 10.1 copy-start.6
  1037.7 10.1 copy-start.13
  1037.7 11.8 slice-start.3
  1068.9 78.5 %copy-start.14 = (bf16[1024,256]{1,0:T(8,128)(2,1)S(1)}, bf16[1024,256]{1,0:T(8,128)(2,1)}, u32[]{:S(2)}) copy-start(bf16[1024,256]{1,0:T(8,128)(2,1)} %copy-done.12) | copy-start | bytes 1572868
  1068.9 78.5 %copy-start.44 = (f32[16,256]{1,0:T(8,128)S(1)}, f32[16,256]{1,0:T(8,128)}, u32[]{:S(2)}) copy-start(f32[16,256]{1,0:T(8,128)} %copy-done.43) | copy-start | bytes 49156
  1068.9 78.5 %copy-start.54 = (f32[16,64]{1,0:T(8,128)S(1)}, f32[16,64]{1,0:T(8,128)}, u32[]{:S(2)}) copy-start(f32[16,64]{1,0:T(8,128)} %copy-done.53) | copy-start | bytes 12292
  1165.1 10.2 copy-start.27
  1186.7 417.0 %reduce-scatter.31.cloned.1.call-start = ((), (), s32[]{:S(2)}) async-start(), calls=%async_computation.26 | async-start | bytes 147456
  1190.0 509.5 %reduce-scatter.15.cloned.1.call-start = ((), (), s32[]{:S(2)}) async-start(), calls=%async_computation.18 | async-start | bytes 2359296 | tf_op jit(solution)/shard_map/reduce_scatter | solution.py:260
  1195.8 503.7 %reduce-scatter.13.cloned.1.call-start = ((), (), s32[]{:S(2)}) async-start(), calls=%async_computation.17 | async-start | bytes 2359296 | tf_op jit(solution)/shard_map/reduce_scatter | solution.py:259
  1200.8 507.3 %reduce-scatter.23.cloned.1.call-start = ((), (), s32[]{:S(2)}) async-start(), calls=%async_computation.22 | async-start | bytes 4718592 | tf_op jit(solution)/shard_map/reduce_scatter | solution.py:267
  1209.1 554.7 %reduce-scatter.19.cloned.1.call-start = ((), (), s32[]{:S(2)}) async-start(), calls=%async_computation.20 | async-start | bytes 4718592 | tf_op jit(solution)/shard_map/reduce_scatter | solution.py:262
  1217.0 601.9 %reduce-scatter.17.cloned.1.call-start = ((), (), s32[]{:S(2)}) async-start(), calls=%async_computation.19 | async-start | bytes 4718592 | tf_op jit(solution)/shard_map/reduce_scatter | solution.py:261
  1224.8 631.4 %reduce-scatter.21.cloned.1.call-start = ((), (), s32[]{:S(2)}) async-start(), calls=%async_computation.21 | async-start | bytes 147456 | tf_op jit(solution)/shard_map/reduce_scatter | solution.py:263
  1484.1 462.8 %reduce-scatter.29.cloned.1.call-start = ((), (), s32[]{:S(2)}) async-start(), calls=%async_computation.25 | async-start | bytes 12976128 | tf_op jit(solution)/shard_map/reduce_scatter | solution.py:271
  1495.6 542.2 %reduce-scatter.27.cloned.1.call-start = ((), (), s32[]{:S(2)}) async-start(), calls=%async_computation.24 | async-start | bytes 12976128 | tf_op jit(solution)/shard_map/reduce_scatter | solution.py:270
  1507.7 620.8 %reduce-scatter.25.cloned.1.call-start = ((), (), s32[]{:S(2)}) async-start(), calls=%async_computation.23 | async-start | bytes 12976128 | tf_op jit(solution)/shard_map/reduce_scatter | solution.py:269
  1536.2 13.8 slice-start
  1536.2 60.1 %all-to-all-start.1 = ((bf16[8,128,2048]{2,1,0:T(8,128)(2,1)}), bf16[8,128,2048]{2,1,0:T(8,128)(2,1)}, u32[]{:S(2)}, u32[]{:S(2)}) async-start(bf16[8,128,2048]{2,1,0:T(8,128)(2,1)} %bitcast.198), calls=%async_computation.1 | async-start | bytes 8388608 | tf_op jit(solution)/shard_map/all_to_all | solution.py:274
  1596.4 93.2 %all-to-all-start.3 = ((bf16[8,128,2048]{2,1,0:T(8,128)(2,1)}), bf16[8,128,2048]{2,1,0:T(8,128)(2,1)}, u32[]{:S(2)}, u32[]{:S(2)}) async-start(bf16[8,128,2048]{2,1,0:T(8,128)(2,1)} %bitcast.197), calls=%async_computation.3 | async-start | bytes 8388608 | tf_op jit(solution)/shard_map/all_to_all | solution.py:275
  1605.1 9.7 copy-start.62
  1605.1 9.7 copy-start.70
  1689.6 439.0 %copy-start.1 = (bf16[2048,512]{1,0:T(8,128)(2,1)S(1)}, bf16[2048,512]{1,0:T(8,128)(2,1)}, u32[]{:S(2)}) copy-start(bf16[2048,512]{1,0:T(8,128)(2,1)} %param.30) | copy-start | bytes 6291460
  (61 other events, 285.5 us)
Sparse Core Ops, SparseCore 0:
  207.2 290.9 all-reduce.13
  565.4 289.8 all-reduce.17
  857.7 153.9 all-reduce.15
  1186.8 292.6 all-reduce.19
  1482.6 32.3 reduce-scatter.30
  1518.7 60.8 reduce-scatter.14
  1583.8 69.8 reduce-scatter.12
  1657.6 50.4 reduce-scatter.22
  1712.4 51.3 reduce-scatter.18
  1767.6 51.2 reduce-scatter.16
  1822.7 33.3 reduce-scatter.20
  1860.1 86.8 reduce-scatter.28
  1951.0 86.7 reduce-scatter.26
  2041.7 86.7 reduce-scatter.24
where the time goes:
time: 2150 us; the launch traced here: 2140 us
  waiting for transfers between devices  1430 us (67%)
  matrix products  267 us (12%)
  local copies, waits for them, and re-layouts  168 us (8%)
  other arithmetic  159 us (7%)
  blocking collectives  72.8 us (3%)
    psum x1, waiting for transfers between devices, per_device(): d_feed = lax.psum(feed_part, 'tensor')  279 us
    psum x1, waiting for transfers between devices, per_device(): lax.psum((mixer_part, latent_part, d_head_gain, gain_term), 'tensor')  255 us
    psum x1, waiting for transfers between devices, per_device(): hidden = owner_rows + lax.psum(mixer_partial, 'tensor')  217 us
    psum x1, waiting for transfers between devices, per_device(): lax.psum(feed_partial.astype(jnp.bfloat16), 'tensor').astype(jnp.float32)  149 us
    reduce_scatter x1, waiting for transfers between devices, per_device(): lax.psum_scatter(grad_feed_up, 'dp', scatter_dimension=0, tiled=True)  90.9 us
    reduce_scatter x1, waiting for transfers between devices, per_device(): lax.psum_scatter(grad_feed_down, 'dp', scatter_dimension=0, tiled=True)  90.8 us
    reduce_scatter x1, waiting for transfers between devices, per_device(): lax.psum_scatter(grad_feed_gate, 'dp', scatter_dimension=0, tiled=True)  90.8 us
    dot_general x8, matrix products, contract_rows(): lax.dot_general(left_mat, right_mat, (((0,), (0,)), ((), ())), preferred_...  66.8 us
  transfers between devices with their start and end apart: 18, of which 14 were waited for; matrix products, arithmetic and copies ran while one was open for 10% of the time, Pallas kernels for 0%

commit v1 on v0

v1 whole, which is shorter than its diff:
```python
import functools

import jax
import jax.numpy as jnp
from jax import lax
from jax.experimental import pallas as pl
from jax.experimental.pallas import tpu as pltpu
from jax.sharding import PartitionSpec as P

OWN_CAP = 1024
SPAN = 128
LANES = 128
epsilon = 1e-06
head_floor = 1.0

f32 = jnp.float32
bf16 = jnp.bfloat16
MESH = pl.DeviceIdType.MESH


def rows_dot(left, right):
    return lax.dot_general(left, right, (((0,), (0,)), ((), ())), preferred_element_type=f32)


def dot_t(left, right):
    return lax.dot_general(left, right, (((1,), (1,)), ((), ())), preferred_element_type=f32)


def dot(left, right):
    return jnp.dot(left, right, preferred_element_type=f32)


def span_terms(first, ends, logits):
    rows = logits.shape[0]

    def label(position):
        count = jnp.zeros_like(position)
        for end in ends:
            count = count + (position >= end).astype(jnp.int32)
        return count

    log_decay = jax.nn.log_sigmoid(logits) * (1.0 / 16.0)
    row = lax.broadcasted_iota(jnp.int32, (rows, rows), 0)
    column = lax.broadcasted_iota(jnp.int32, (rows, rows), 1)
    lower = (row >= column).astype(f32)
    cumulative = jnp.dot(
        lower, log_decay, precision=lax.Precision.HIGHEST, preferred_element_type=f32
    )
    total = cumulative[rows - 1 :, :]
    middle = cumulative[rows // 2 - 1 : rows // 2, :]
    label_column = label(first + lax.broadcasted_iota(jnp.int32, (rows, 1), 0))
    label_row = label(first + lax.broadcasted_iota(jnp.int32, (1, rows), 1))
    before = jnp.where(first > 0, label(first - 1), -1)
    last = label(first + rows - 1)
    carried = (label_column == before).astype(f32)
    tail = (label_column == last).astype(f32)
    keep = (before == last).astype(f32)
    allowed = (row >= column) & (label_column == label_row)
    return log_decay, cumulative, total, middle, carried, tail, keep, allowed


def recur_forward_kernel(
    dk, dv, slot_row_ref, slot_column_ref, lengths_ref, up_ref, bias_ref, arrived_ref,
    out_ref, held_ref, states_ref, state, result,
):
    step = pl.program_id(0)
    first = step * SPAN
    end0 = lengths_ref[0, 0]
    end1 = end0 + lengths_ref[0, 1]
    end2 = end1 + lengths_ref[0, 2]
    slots = slot_row_ref.shape[1]

    @pl.when(step == 0)
    def _():
        state[...] = jnp.zeros_like(state)

    position = first + lax.broadcasted_iota(jnp.int32, (SPAN, slots), 0)
    place = (slot_row_ref[...] == position).astype(f32).astype(bf16)
    held = dot(place, arrived_ref[...]).astype(bf16)
    held_ref[...] = held
    queries = held[:, :dk].astype(f32) * (float(dk) ** -0.5)
    keys = held[:, dk : 2 * dk].astype(f32)
    values = held[:, 2 * dk : 2 * dk + dv]
    logits = dot(held[:, 2 * dk + dv :], up_ref[...]) + bias_ref[...]
    _, cumulative, total, middle, carried, tail, keep, allowed = span_terms(
        first, (end0, end1, end2), logits
    )
    query_mid = (queries * jnp.exp(cumulative - middle)).astype(bf16)
    key_mid = (keys * jnp.exp(middle - cumulative)).astype(bf16)
    query_start = (queries * jnp.exp(cumulative) * carried).astype(bf16)
    key_end = (keys * jnp.exp(total - cumulative) * tail).astype(bf16)
    scores = jnp.where(allowed, dot_t(query_mid, key_mid), 0.0).astype(bf16)
    entering = state[...]
    entering_low = entering.astype(bf16)
    states_ref[0] = entering_low
    attended = dot(scores, values) + dot(query_start, entering_low)
    result[pl.ds(pl.multiple_of(first, SPAN), SPAN), :] = attended.astype(bf16)
    decay_column = jnp.transpose(jnp.broadcast_to(keep * jnp.exp(total), (8, dk)))[:, :1]
    state[...] = decay_column * entering + rows_dot(key_end, values)

    @pl.when(step == pl.num_programs(0) - 1)
    def _():
        return_rows(slot_column_ref, result, out_ref)


def return_rows(slot_column_ref, source, out_ref):
    positions = source.shape[0]
    block = 256

    def body(i, carry):
        at = pl.ds(pl.multiple_of(i * block, block), block)
        column = lax.broadcasted_iota(jnp.int32, (block, positions), 1)
        pick = (slot_column_ref[at, :] == column).astype(f32).astype(bf16)
        out_ref[at, :] = dot(pick, source[...]).astype(out_ref.dtype)
        return carry

    lax.fori_loop(0, out_ref.shape[0] // block, body, 0)


def recur_backward_kernel(
    dk, dv, slot_row_ref, slot_column_ref, lengths_ref, up_ref, bias_ref, down_ref, arrived_ref,
    held_ref, states_ref, out_ref, grad_up_ref, grad_bias_ref, d_state, result,
):
    step = pl.num_programs(0) - 1 - pl.program_id(0)
    first = step * SPAN
    end0 = lengths_ref[0, 0]
    end1 = end0 + lengths_ref[0, 1]
    end2 = end1 + lengths_ref[0, 2]
    slots = slot_row_ref.shape[1]

    @pl.when(pl.program_id(0) == 0)
    def _():
        d_state[...] = jnp.zeros_like(d_state)
        grad_up_ref[...] = jnp.zeros_like(grad_up_ref)
        grad_bias_ref[...] = jnp.zeros_like(grad_bias_ref)

    position = first + lax.broadcasted_iota(jnp.int32, (SPAN, slots), 0)
    place = (slot_row_ref[...] == position).astype(f32).astype(bf16)
    d_out = dot(place, arrived_ref[...]).astype(bf16)
    scale = float(dk) ** -0.5
    queries = held_ref[:, :dk].astype(f32) * scale
    keys = held_ref[:, dk : 2 * dk].astype(f32)
    values = held_ref[:, 2 * dk : 2 * dk + dv]
    latent = held_ref[:, 2 * dk + dv :]
    logits = dot(latent, up_ref[...]) + bias_ref[...]
    _, cumulative, total, middle, carried, tail, keep, allowed = span_terms(
        first, (end0, end1, end2), logits
    )
    grow_query = jnp.exp(cumulative - middle)
    grow_key = jnp.exp(middle - cumulative)
    start_decay = jnp.exp(cumulative) * carried
    end_decay = jnp.exp(total - cumulative) * tail
    query_mid = (queries * grow_query).astype(bf16)
    key_mid = (keys * grow_key).astype(bf16)
    query_start = (queries * start_decay).astype(bf16)
    key_end = (keys * end_decay).astype(bf16)
    scores = jnp.where(allowed, dot_t(query_mid, key_mid), 0.0).astype(bf16)
    d_scores = jnp.where(allowed, dot_t(d_out, values), 0.0).astype(bf16)
    leaving = d_state[...]
    leaving_low = leaving.astype(bf16)
    entering = states_ref[0]
    d_values = rows_dot(scores, d_out) + dot(key_end, leaving_low)
    d_queries = dot(d_scores, key_mid) * grow_query + dot_t(d_out, entering) * start_decay
    d_key_end = dot_t(values, leaving_low) * end_decay
    d_keys = rows_dot(d_scores, query_mid) * grow_key + d_key_end
    kept = keep * jnp.exp(total)
    state_pair = jnp.sum(entering.astype(f32) * leaving, axis=1, keepdims=True)
    state_row = jnp.transpose(jnp.broadcast_to(state_pair, (dk, LANES)))[:1, :]
    d_total = jnp.sum(keys * d_key_end, axis=0, keepdims=True) + kept * state_row
    d_cumulative = queries * d_queries - keys * d_keys
    row = lax.broadcasted_iota(jnp.int32, (SPAN, SPAN), 0)
    column = lax.broadcasted_iota(jnp.int32, (SPAN, SPAN), 1)
    upper = (row <= column).astype(f32)
    d_log_decay = (
        jnp.dot(upper, d_cumulative, precision=lax.Precision.HIGHEST, preferred_element_type=f32)
        + d_total
    )
    d_logits = d_log_decay * (1.0 / 16.0) * jax.nn.sigmoid(-logits)
    grad_bias_ref[...] += jnp.broadcast_to(jnp.sum(d_logits, axis=0, keepdims=True), (8, dk))
    d_logits_high = d_logits.astype(bf16)
    d_logits_low = (d_logits - d_logits_high.astype(f32)).astype(bf16)
    grad_up_ref[...] += rows_dot(d_logits_high, latent) + rows_dot(d_logits_low, latent)
    d_latent = dot(d_logits_high, down_ref[...]) + dot(d_logits_low, down_ref[...])
    high = d_latent.astype(bf16).astype(f32)
    lane = lax.broadcasted_iota(jnp.int32, d_latent.shape, 1)
    d_latent_packed = jnp.where(lane < LANES // 4, high, d_latent - high)
    at = pl.ds(pl.multiple_of(first, SPAN), SPAN)
    result[at, :dk] = (d_queries * scale).astype(bf16)
    result[at, dk : 2 * dk] = d_keys.astype(bf16)
    result[at, 2 * dk : 2 * dk + dv] = d_values.astype(bf16)
    result[at, 2 * dk + dv :] = d_latent_packed.astype(bf16)
    kept_column = jnp.transpose(jnp.broadcast_to(kept, (8, dk)))[:, :1]
    d_state[...] = kept_column * leaving + rows_dot(query_start, d_out)

    @pl.when(step == 0)
    def _():
        return_rows(slot_column_ref, result, out_ref)


def whole(shape):
    return pl.BlockSpec(shape, lambda i: (0,) * len(shape))


def recur_forward(slot_map, lengths, up_wide, bias, arrived, dk, dv):
    slots, width = arrived.shape
    steps = OWN_CAP // SPAN
    return pl.pallas_call(
        functools.partial(recur_forward_kernel, dk, dv),
        grid=(steps,),
        in_specs=[
            whole((1, slots)),
            whole((slots, 1)),
            pl.BlockSpec(memory_space=pltpu.SMEM),
            whole((LANES, dk)),
            whole((1, dk)),
            whole((slots, width)),
        ],
        out_specs=[
            whole((slots, dv)),
            pl.BlockSpec((SPAN, width), lambda i: (i, 0)),
            pl.BlockSpec((1, dk, dv), lambda i: (i, 0, 0)),
        ],
        out_shape=[
            jax.ShapeDtypeStruct((slots, dv), bf16),
            jax.ShapeDtypeStruct((OWN_CAP, width), bf16),
            jax.ShapeDtypeStruct((steps, dk, dv), bf16),
        ],
        scratch_shapes=[pltpu.VMEM((dk, dv), f32), pltpu.VMEM((OWN_CAP, dv), bf16)],
        compiler_params=pltpu.CompilerParams(vmem_limit_bytes=40 << 20),
        cost_estimate=pl.CostEstimate(
            flops=6_000_000_000, bytes_accessed=10_000_000, transcendentals=2_000_000
        ),
        name="recur_forward",
    )(slot_map.reshape(1, -1), slot_map.reshape(-1, 1), lengths, up_wide, bias, arrived)


def recur_backward(slot_map, lengths, up_wide, bias, down_wide, arrived, held, states, dk, dv):
    slots = arrived.shape[0]
    width = held.shape[1]
    steps = OWN_CAP // SPAN
    return pl.pallas_call(
        functools.partial(recur_backward_kernel, dk, dv),
        grid=(steps,),
        in_specs=[
            whole((1, slots)),
            whole((slots, 1)),
            pl.BlockSpec(memory_space=pltpu.SMEM),
            whole((LANES, dk)),
            whole((1, dk)),
            whole((dk, LANES)),
            whole((slots, dv)),
            pl.BlockSpec((SPAN, width), lambda i: (steps - 1 - i, 0)),
            pl.BlockSpec((1, dk, dv), lambda i: (steps - 1 - i, 0, 0)),
        ],
        out_specs=[whole((slots, width)), whole((dk, LANES)), whole((8, dk))],
        out_shape=[
            jax.ShapeDtypeStruct((slots, width), bf16),
            jax.ShapeDtypeStruct((dk, LANES), f32),
            jax.ShapeDtypeStruct((8, dk), f32),
        ],
        scratch_shapes=[pltpu.VMEM((dk, dv), f32), pltpu.VMEM((OWN_CAP, width), bf16)],
        compiler_params=pltpu.CompilerParams(vmem_limit_bytes=40 << 20),
        cost_estimate=pl.CostEstimate(
            flops=12_000_000_000, bytes_accessed=12_000_000, transcendentals=4_000_000
        ),
        name="recur_backward",
    )(
        slot_map.reshape(1, -1), slot_map.reshape(-1, 1), lengths, up_wide, bias, down_wide,
        arrived, held, states,
    )


CHUNK = 32


def line_kernel(mode, n, *refs):
    share_ref, x_ref, base_ref, gain_ref = refs[:4]
    if mode == "norm":
        out_ref, kept_ref = refs[4:6]
        scratch = refs[6:]
    elif mode == "back":
        out_ref, kept_ref, gain_grad_ref = refs[4:7]
        scratch = refs[7:]
    else:
        out_ref = refs[4]
        kept_ref = None
        scratch = refs[5:]
    up_in, up_out, down_in, down_out, sems = scratch
    me = lax.axis_index("tensor")
    half = up_in.shape[0]
    count = half // CHUNK

    barrier = pltpu.get_barrier_semaphore()

    @pl.when(me > 0)
    def _():
        pl.semaphore_signal(barrier, inc=1, device_id={"tensor": me - 1}, device_id_type=MESH)

    @pl.when(me < n - 1)
    def _():
        pl.semaphore_signal(barrier, inc=1, device_id={"tensor": me + 1}, device_id_type=MESH)

    inside = (me > 0) & (me < n - 1)

    @pl.when(inside)
    def _():
        pl.semaphore_wait(barrier, 2)

    @pl.when(jnp.logical_not(inside))
    def _():
        pl.semaphore_wait(barrier, 1)

    def at(g):
        return pl.ds(pl.multiple_of(g * CHUNK, CHUNK), CHUNK)

    def low(g):
        return pl.ds(pl.multiple_of(half + g * CHUNK, CHUNK), CHUNK)

    def right(source, target, lane, g):
        return pltpu.make_async_remote_copy(
            source, target, sems.at[2 * lane, g], sems.at[2 * lane + 1, g],
            device_id={"tensor": jnp.minimum(me + 1, n - 1)}, device_id_type=MESH,
        )

    def left(source, target, lane, g):
        return pltpu.make_async_remote_copy(
            source, target, sems.at[2 * lane, g], sems.at[2 * lane + 1, g],
            device_id={"tensor": jnp.maximum(me - 1, 0)}, device_id_type=MESH,
        )

    def up_copy(g):
        return right(up_out.at[at(g), :], up_in.at[at(g), :], 0, g)

    def down_copy(g):
        return left(down_out.at[at(g), :], down_in.at[at(g), :], 1, g)

    def first_up_copy(g):
        return right(share_ref.at[at(g), :], up_in.at[at(g), :], 0, g)

    def first_down_copy(g):
        return left(share_ref.at[low(g), :], down_in.at[at(g), :], 1, g)

    def up_back_copy(g):
        return left(out_ref.at[at(g), :], out_ref.at[at(g), :], 2, g)

    def down_back_copy(g):
        return right(out_ref.at[low(g), :], out_ref.at[low(g), :], 3, g)

    if mode == "back":
        gain_grad_ref[...] = jnp.zeros_like(gain_grad_ref)

    def finish(total, g, place):
        base = base_ref[at(g), :].astype(f32)
        if mode == "sum":
            out_ref[place, :] = (base + total).astype(out_ref.dtype)
            return
        if mode == "norm":
            hidden = base + total
            kept_ref[at(g), :] = hidden
            scaling = lax.rsqrt(jnp.mean(hidden * hidden, axis=1, keepdims=True) + epsilon)
            out_ref[place, :] = (hidden * scaling * gain_ref[...]).astype(out_ref.dtype)
            return
        rows = x_ref[at(g), :].astype(f32)
        scaling = lax.rsqrt(jnp.mean(rows * rows, axis=1, keepdims=True) + epsilon)
        unit = rows * scaling
        gained = gain_ref[...] * total
        grad = base + scaling * (gained - unit * jnp.mean(gained * unit, axis=1, keepdims=True))
        kept_ref[at(g), :] = grad
        out_ref[place, :] = grad.astype(out_ref.dtype)
        term = total * unit
        part = term[0:8, :]
        for i in range(1, CHUNK // 8):
            part = part + term[8 * i : 8 * i + 8, :]
        gain_grad_ref[...] += part

    @pl.when(me == 0)
    def _():
        @pl.loop(0, count)
        def _(g):
            first_up_copy(g).start()

    @pl.when(me == n - 1)
    def _():
        @pl.loop(0, count)
        def _(g):
            first_down_copy(g).start()

    @pl.loop(0, count + n - 2)
    def _(step):
        g_up = step - (me - 1)

        @pl.when((me > 0) & (g_up >= 0) & (g_up < count))
        def _():
            up_copy(g_up).wait_recv()
            total = up_in[at(g_up), :].astype(f32) + share_ref[at(g_up), :].astype(f32)

            @pl.when(me < n - 1)
            def _():
                up_out[at(g_up), :] = total.astype(bf16)
                up_copy(g_up).start()

            @pl.when(me == n - 1)
            def _():
                finish(total, g_up, at(g_up))
                up_back_copy(g_up).start()

        g_down = step - (n - 2 - me)

        @pl.when((me < n - 1) & (g_down >= 0) & (g_down < count))
        def _():
            down_copy(g_down).wait_recv()
            total = down_in[at(g_down), :].astype(f32) + share_ref[low(g_down), :].astype(f32)

            @pl.when(me > 0)
            def _():
                down_out[at(g_down), :] = total.astype(bf16)
                down_copy(g_down).start()

            @pl.when(me == 0)
            def _():
                finish(total, g_down, low(g_down))
                down_back_copy(g_down).start()

    @pl.loop(0, count + n - 2)
    def _(step):
        g_up = step - (n - 2 - me)

        @pl.when((me < n - 1) & (g_up >= 0) & (g_up < count))
        def _():
            up_back_copy(g_up).wait_recv()

            @pl.when(me > 0)
            def _():
                up_back_copy(g_up).start()

        g_down = step - (me - 1)

        @pl.when((me > 0) & (g_down >= 0) & (g_down < count))
        def _():
            down_back_copy(g_down).wait_recv()

            @pl.when(me < n - 1)
            def _():
                down_back_copy(g_down).start()

    @pl.loop(0, count)
    def _(g):
        @pl.when(me < n - 1)
        def _():
            up_copy(g).wait_send()
            down_back_copy(g).wait_send()

        @pl.when(me > 0)
        def _():
            down_copy(g).wait_send()
            up_back_copy(g).wait_send()


def line_sum(mode, call, n, share, x_own, base_own, gain):
    rows, width = share.shape
    half = rows // 2
    vmem = pl.BlockSpec(memory_space=pltpu.VMEM)
    outs = [jax.ShapeDtypeStruct((rows, width), bf16)]
    if mode != "sum":
        outs.append(jax.ShapeDtypeStruct((half, width), f32))
    if mode == "back":
        outs.append(jax.ShapeDtypeStruct((8, width), f32))
    return pl.pallas_call(
        functools.partial(line_kernel, mode, n),
        in_specs=[vmem] * 4,
        out_specs=[vmem] * len(outs),
        out_shape=outs,
        scratch_shapes=[
            pltpu.VMEM((half, width), bf16),
            pltpu.VMEM((half, width), bf16),
            pltpu.VMEM((half, width), bf16),
            pltpu.VMEM((half, width), bf16),
            pltpu.SemaphoreType.DMA((8, half // CHUNK)),
        ],
        compiler_params=pltpu.CompilerParams(
            collective_id=call, has_side_effects=True, vmem_limit_bytes=40 << 20
        ),
        cost_estimate=pl.CostEstimate(
            flops=10_000_000, bytes_accessed=200_000_000, transcendentals=0
        ),
        name="line_" + mode,
    )(share, x_own, base_own, gain)


def per_device(
    tokens,
    cotangent,
    token_slots,
    lengths,
    mixer_gain,
    query_weight,
    key_weight,
    value_weight,
    gate_weight,
    decay_down,
    decay_up,
    decay_bias,
    head_gain,
    out_weight,
    feed_gain,
    feed_gate,
    feed_up,
    feed_down,
):
    groups = lax.axis_size("dp")
    lines = lax.axis_size("tensor")
    member = lax.axis_index("dp")
    place = lax.axis_index("tensor")
    count, width = tokens.shape
    cap = OWN_CAP // groups
    slots = groups * cap
    dk = query_weight.shape[1]
    dv = value_weight.shape[1]
    rank = decay_up.shape[1]
    parity = lax.rem(member, 2)
    pairs = [(i, i ^ 1) for i in range(groups)]
    same_parity = [[i for i in range(groups) if i % 2 == b] for b in range(2)]

    owners = (token_slots // OWN_CAP).reshape(groups, count)
    mine = (owners == member).astype(bf16)
    my_slots = lax.dynamic_slice_in_dim(token_slots, member * count, count)
    my_owner = my_slots // OWN_CAP
    chosen = (my_owner[None, :] == jnp.arange(groups, dtype=jnp.int32)[:, None]).astype(bf16)
    index = jnp.arange(count, dtype=jnp.int32)
    before = (index[:, None] < index[None, :]).astype(bf16)
    ranks = dot(jnp.concatenate([mine, chosen], axis=0), before).astype(jnp.int32)
    recv_rank, send_rank = ranks[:groups], ranks[groups:]
    hit = (recv_rank[:, None, :] == jnp.arange(cap, dtype=jnp.int32)[None, :, None]) & (
        owners == member
    )[:, None, :]
    local = (token_slots % OWN_CAP).reshape(groups, count)
    slot_map = (
        jnp.sum(jnp.where(hit, local[:, None, :] - OWN_CAP, 0), axis=2) + OWN_CAP
    ).reshape(slots)
    send_pos = my_owner * cap + jnp.sum(
        jnp.where(chosen > 0, send_rank, 0), axis=0, dtype=jnp.int32
    )
    slot_ids = jnp.arange(slots, dtype=jnp.int32)
    pack = (slot_ids[:, None] == send_pos[None, :]).astype(bf16)
    unpack = (send_pos[:, None] == slot_ids[None, :]).astype(bf16)

    def exchange(row_block):
        blocks = row_block.reshape(groups, cap, row_block.shape[1])
        moved = lax.all_to_all(blocks, "dp", split_axis=0, concat_axis=0, tiled=True)
        return moved.reshape(slots, row_block.shape[1])

    half = count // 2
    own_at = jnp.where(place == 0, half, 0)
    tokens_own = lax.dynamic_slice_in_dim(tokens, own_at, half)
    cotangent_own = lax.dynamic_slice_in_dim(cotangent, own_at, half)

    tokens_wide = tokens.astype(f32)
    mixer_gain_wide = mixer_gain.astype(f32)
    feed_gain_wide = feed_gain.astype(f32)
    normed = (
        tokens_wide
        * lax.rsqrt(jnp.mean(tokens_wide * tokens_wide, axis=-1, keepdims=True) + epsilon)
        * mixer_gain_wide
    ).astype(bf16)
    queries = dot(normed, query_weight).astype(bf16)
    keys_low = dot(normed, key_weight).astype(bf16)
    value_rows = dot(normed, value_weight).astype(bf16)
    gate_pre = dot(normed, gate_weight)
    third = LANES // 4
    down_pad = jnp.pad(decay_down, ((0, 0), (0, third - rank)))
    latent = dot(
        normed,
        jnp.concatenate([down_pad, down_pad, down_pad, jnp.zeros_like(down_pad)], axis=1),
    )
    latent_high = latent.astype(bf16)
    latent_rest = latent - latent_high.astype(f32)
    latent_mid = latent_rest.astype(bf16)
    latent_low = (latent_rest - latent_mid.astype(f32)).astype(bf16)
    lane = jnp.arange(LANES, dtype=jnp.int32)[None, :]
    latent_packed = jnp.where(
        lane < third, latent_high, jnp.where(lane < 2 * third, latent_mid, latent_low)
    )
    rows_out = jnp.concatenate([queries, keys_low, value_rows, latent_packed], axis=1)
    arrived = exchange(dot(pack, rows_out).astype(bf16))
    up_pad = jnp.pad(decay_up, ((0, 0), (0, third - rank)))
    up_wide = jnp.concatenate([up_pad, up_pad, up_pad, jnp.zeros_like(up_pad)], axis=1).T
    down_wide = jnp.concatenate(
        [up_pad, up_pad, jnp.zeros_like(up_pad), jnp.zeros_like(up_pad)], axis=1
    )
    bias = decay_bias.astype(f32).reshape(1, dk)
    attended_slots, held, states = recur_forward(
        slot_map, lengths, up_wide, bias, arrived, dk, dv
    )
    attended = dot(unpack, exchange(attended_slots))

    head_gain_wide = head_gain.astype(f32)

    def head_output(rows, gate_rows, gain_row):
        scaling = lax.rsqrt(jnp.mean(rows * rows, axis=-1, keepdims=True) + head_floor)
        return rows * scaling * gain_row * jax.nn.silu(gate_rows)

    gated_wide, head_back = jax.vjp(head_output, attended, gate_pre, head_gain_wide)
    gated = gated_wide.astype(bf16)
    mixer_share = dot(gated, out_weight).astype(bf16)
    feed_normed, hidden_own = line_sum(
        "norm", 1, lines, mixer_share, tokens_own, tokens_own, feed_gain_wide.reshape(1, -1)
    )

    gate_hidden = dot(feed_normed, feed_gate)
    up_hidden = dot(feed_normed, feed_up)
    d_active = dot_t(cotangent, feed_down)
    sigmoid_gate = jax.nn.sigmoid(gate_hidden)
    swish_gate = gate_hidden * sigmoid_gate
    active = (swish_gate * up_hidden).astype(bf16)
    d_gate_hidden = (
        d_active * up_hidden * sigmoid_gate * (1.0 + gate_hidden * (1.0 - sigmoid_gate))
    ).astype(bf16)
    d_up_hidden = (d_active * swish_gate).astype(bf16)
    feed_share = (dot_t(d_gate_hidden, feed_gate) + dot_t(d_up_hidden, feed_up)).astype(bf16)
    d_mixed, d_hidden_own, feed_gain_part = line_sum(
        "back", 2, lines, feed_share, hidden_own, cotangent_own, feed_gain_wide.reshape(1, -1)
    )

    d_gated = dot_t(d_mixed, out_weight)
    d_attended, d_gate_pre, head_gain_part = head_back(d_gated)
    d_gate_low = d_gate_pre.astype(bf16)
    d_arrived = exchange(dot(pack, d_attended.astype(bf16)).astype(bf16))
    d_slots, up_part, bias_part = recur_backward(
        slot_map, lengths, up_wide, bias, down_wide, d_arrived, held, states, dk, dv
    )
    d_rows = dot(unpack, exchange(d_slots)).astype(bf16)
    d_query_low = d_rows[:, :dk]
    d_key_low = d_rows[:, dk : 2 * dk]
    d_value_low = d_rows[:, 2 * dk : 2 * dk + dv]
    d_latent_low = d_rows[:, 2 * dk + dv :]
    down_both = jnp.concatenate(
        [down_pad, down_pad, jnp.zeros_like(down_pad), jnp.zeros_like(down_pad)], axis=1
    )
    normed_share = (
        dot_t(d_query_low, query_weight)
        + dot_t(d_key_low, key_weight)
        + dot_t(d_value_low, value_weight)
        + dot_t(d_gate_low, gate_weight)
        + dot_t(d_latent_low, down_both)
    ).astype(bf16)
    token_grad, _, mixer_gain_part = line_sum(
        "back", 3, lines, normed_share, tokens_own, d_hidden_own, mixer_gain_wide.reshape(1, -1)
    )
    layer_share = dot(active, feed_down).astype(bf16)
    (layer_out,) = line_sum(
        "sum", 4, lines, layer_share, tokens_own, hidden_own, feed_gain_wide.reshape(1, -1)
    )

    def halves(row_block, dims):
        split = row_block.reshape(row_block.shape[0], groups // 2, 2, dims // groups)
        keep = lax.dynamic_index_in_dim(split, parity, 2, keepdims=False)
        send = lax.dynamic_index_in_dim(split, 1 - parity, 2, keepdims=False)
        got = lax.ppermute(send, "dp", pairs)
        shape = (row_block.shape[0], dims // 2)
        return keep.reshape(shape), got.reshape(shape)

    def partner(row_block):
        return row_block, lax.ppermute(row_block, "dp", pairs)

    def summed_share(left, right):
        share = (rows_dot(left[0], right[0]) + rows_dot(left[1], right[1])).astype(bf16)
        rows = share.shape[0] // (groups // 2)
        blocks = share.reshape(groups // 2, rows, share.shape[1])
        moved = lax.all_to_all(
            blocks, "dp", split_axis=0, concat_axis=0, tiled=True, axis_index_groups=same_parity
        )
        return jnp.sum(moved.astype(f32), axis=0)

    feed_halves = halves(feed_normed, width)
    normed_halves = halves(normed, width)
    grad_feed_down = summed_share(halves(active, active.shape[1]), partner(cotangent))
    grad_feed_gate = summed_share(feed_halves, partner(d_gate_hidden))
    grad_feed_up = summed_share(feed_halves, partner(d_up_hidden))
    grad_out = summed_share(halves(gated, dv), partner(d_mixed))
    grad_query = summed_share(normed_halves, partner(d_query_low))
    grad_key = summed_share(normed_halves, partner(d_key_low))
    grad_value = summed_share(normed_halves, partner(d_value_low))
    grad_gate = summed_share(normed_halves, partner(d_gate_low))

    down_part = rows_dot(normed, d_latent_low)
    down_part = down_part[:, :rank] + down_part[:, third : third + rank]
    up_part = up_part[:, :rank] + up_part[:, third : third + rank] + (
        up_part[:, 2 * third : 2 * third + rank]
    )

    def by_owner(vector):
        return vector.reshape(groups, -1)

    over_all = jnp.concatenate(
        [
            by_owner(jnp.sum(mixer_gain_part, axis=0)),
            by_owner(jnp.sum(feed_gain_part, axis=0)),
            by_owner(head_gain_part),
            by_owner(down_part),
        ],
        axis=1,
    )
    over_owners = jnp.concatenate([by_owner(up_part), by_owner(bias_part[0])], axis=1)
    wide = over_all.shape[1]
    small = lax.psum_scatter(
        jnp.concatenate([over_all, over_owners], axis=1), "dp", scatter_dimension=0, tiled=True
    )[0]
    summed = lax.psum(small[:wide], "tensor")
    per = width // groups
    head_per = dv // groups
    return (
        layer_out,
        token_grad,
        summed[:per],
        grad_query,
        grad_key,
        grad_value,
        grad_gate,
        summed[2 * per + head_per :].reshape(per, rank),
        small[wide : wide + dk // groups * rank].reshape(1, dk // groups, rank),
        small[wide + dk // groups * rank :].reshape(1, dk // groups),
        summed[2 * per : 2 * per + head_per],
        grad_out[None],
        summed[per : 2 * per],
        grad_feed_gate,
        grad_feed_up,
        grad_feed_down[None],
    )


def solution(mesh):
    placed = (
        P("dp", None),
        P("dp", None),
        P(),
        P("dp", None),
        P(),
        P(None, "tensor"),
        P(None, "tensor"),
        P(None, "tensor"),
        P(None, "tensor"),
        P(),
        P("tensor", None),
        P("tensor"),
        P(),
        P("tensor", None),
        P(),
        P(None, "tensor"),
        P(None, "tensor"),
        P("tensor", None),
    )
    return jax.shard_map(
        per_device,
        mesh=mesh,
        in_specs=placed,
        out_specs=(
            P("dp", None),
            P("dp", None),
            P("dp"),
            P("dp", "tensor"),
            P("dp", "tensor"),
            P("dp", "tensor"),
            P("dp", "tensor"),
            P("dp", None),
            P("tensor", "dp", None),
            P("tensor", "dp"),
            P("dp"),
            P("tensor", "dp", None),
            P("dp"),
            P("dp", "tensor"),
            P("dp", "tensor"),
            P("tensor", "dp", None),
        ),
        check_vma=False,
    )
```

time: 2150 us -> 821 us (0.38)
  waiting for transfers between devices: 1430 us -> 97.6 us
  Pallas kernels: 0 us -> 342 us
  other arithmetic: 159 us -> 29.2 us
  matrix products: 267 us -> 165 us
  local copies, waits for them, and re-layouts: 168 us -> 88.3 us
  blocking collectives: 72.8 us -> 18.9 us
  starting transfers between devices: 20.8 us -> 56.2 us
    psum x4 -> x0, waiting for transfers between devices: 899 us -> none  [the longest x1 279 us: per_device(): d_feed = lax.psum(feed_part, 'tensor')]
    reduce_scatter x9 -> x0, waiting for transfers between devices: 429 us -> none  [the longest x1 90.9 us: per_device(): lax.psum_scatter(grad_feed_up, 'dp', scatter_dimension=0, tiled=True)]
    pallas_call x0 -> x6, Pallas kernels: none -> 342 us  [the longest x4 305 us: line_sum(): pl.pallas_call(functools.partial(line_kernel, mode, n), in_specs=[vmem] *...]
    dot_general x41 -> x40, matrix products: 265 us -> 165 us  [the longest x17 63.5 us: rows_dot(): lax.dot_general(left, right, (((0,), (0,)), ((), ())), preferred_element_...]
    scatter x5 -> x0, local copies, waits for them, and re-layouts: 60.6 us -> none  [the longest x2 21.2 us: pack_rows(): jnp.zeros((groups * peer_cap, model_width), row_block.dtype).at[send_pos]]
    unnamed x1 -> x0, blocking collectives: 60.6 us -> none
    all_to_all x4 -> x12, waiting for transfers between devices: 101 us -> 45.8 us  [the longest x4 26.4 us: exchange(): lax.all_to_all(blocks, 'dp', split_axis=0, concat_axis=0, tiled=True)]
    unnamed x15 -> x2, waiting for transfers between devices: 0.25 us -> 51.8 us
  transfers between devices with their start and end apart: 18 -> 25, of which waited for: 14 -> 6; matrix products, arithmetic and copies ran while one was open for 10% -> 29% of each run, Pallas kernels for 0% -> 42%
where the time goes in v1:
time: 821 us; the launch traced here: 813 us
  Pallas kernels  342 us (42%)
  matrix products  165 us (20%)
  waiting for transfers between devices  97.6 us (12%)
  local copies, waits for them, and re-layouts  88.3 us (11%)
  starting transfers between devices  56.2 us (7%)
  other arithmetic  29.2 us (4%)
  blocking collectives  18.9 us (2%)
  between operations  15.2 us (2%)
    pallas_call x4, Pallas kernels, line_sum(): pl.pallas_call(functools.partial(line_kernel, mode, n), in_specs=[vmem] *...  305 us
    dot_general x17, matrix products, rows_dot(): lax.dot_general(left, right, (((0,), (0,)), ((), ())), preferred_element_...  63.5 us
    dot_general x9, matrix products, dot_t(): lax.dot_general(left, right, (((1,), (1,)), ((), ())), preferred_element_...  54.7 us
    unnamed x2, waiting for transfers between devices  51.8 us
    dot_general x14, matrix products, dot(): return jnp.dot(left, right, preferred_element_type=f32)  47 us
    unnamed x157, local copies, waits for them, and re-layouts  42.6 us
    all_to_all x8, starting transfers between devices, summed_share(): lax.all_to_all(blocks, 'dp', split_axis=0, concat_axis=0, tiled=True, axi...  35.4 us
    all_to_all x4, waiting for transfers between devices, exchange(): lax.all_to_all(blocks, 'dp', split_axis=0, concat_axis=0, tiled=True)  26.4 us
  transfers between devices with their start and end apart: 25, of which 6 were waited for; matrix products, arithmetic and copies ran while one was open for 29% of the time, Pallas kernels for 42%

profile of v1, /device:TPU:0, one launch (start us, length us, event | category | flops | bytes accessed | tf_op | source)
XLA Modules:
  0.0 812.9 jit_solution(1927765561092359418)
XLA Ops:
  10.6 4.4 copy.98
  24.1 3.6 convolution_convert_fusion
  27.7 5.4 all-to-all-start
  44.4 18.2 %all-to-all-done = bf16[8,128,1152]{2,1,0:T(8,128)(2,1)} async-done(((bf16[8,128,1152]{2,1,0:T(8,128)(2,1)}), bf16[8,128,1152]{2,1,0:T(8,128)(2,1)}, u32[]{:S(2)}, u32[]{:S(2)}) %all-to-all-start) | async-done | bytes 2359328 | tf_op jit(solution)/shard_map/all_to_all | solution.py:549
  63.7 16.9 %recur_forward.1 = (bf16[1024,512]{1,0:T(8,128)(2,1)}, bf16[1024,1152]{1,0:T(8,128)(2,1)S(1)}, bf16[8,256,512]{2,1,0:T(8,128)(2,1)S(1)}) custom-call(s32[1,1024]{1,0:T(1,128)S(1)} %bitcast.114, s32[1024,1]{1,0:T(8,128)S(1)} %copy-done.15, s32[1,3]{1,0:T(1,128)S(1)} %copy-done.25, bf16[128,256]{1,0:T(8,128)(2,1)S(1)} %copy.100.up_ref, ...), custom_call_target="tpu_custom_call" | custom-call | flops 6000000000 | bytes 10000000 | tf_op jit(solution)/shard_map/recur_forward/pallas_call | solution.py:207
  83.4 4.4 all-to-all-start.1
  95.1 8.1 all-to-all-done.1
  105.8 4.8 multiply_convert_fusion.3
  112.2 78.4 %line_norm.1 = (bf16[640,2048]{1,0:T(8,128)(2,1)S(1)}, f32[320,2048]{1,0:T(8,128)S(1)}) custom-call(bf16[640,2048]{1,0:T(8,128)(2,1)S(1)} %convolution_convert_fusion.2.refs_0_, bf16[320,2048]{1,0:T(8,128)(2,1)S(1)} %constant_dynamic-slice_fusion.6.refs_1_.refs_2_, bf16[320,2048]{1,0:T(8,128)(2,1)S(1)} %constant_dynamic-slice_fusion.6.refs_1_.refs_2_, ...), custom_call_target="tpu_custom_call" | custom-call | flops 10000000 | bytes 200000000 | tf_op jit(solution)/shard_map/line_norm/pallas_call | solution.py:468
  190.7 6.0 fusion.86
  196.7 8.8 %fusion.87 = f32[640,1408]{1,0:T(8,128)} fusion(bf16[640,2048]{1,0:T(8,128)(2,1)S(1)} %get-tuple-element.30, bf16[2048,1408]{1,0:T(8,128)(2,1)} %param.34), kind=kOutput, calls=%fused_computation.166 | convolution fusion | flops 3690987520 | bytes 11993088 | tf_op jit(solution)/shard_map/dot_general | solution.py:30
  205.5 10.8 %multiply_convert_fusion = (bf16[640,1408]{1,0:T(8,128)(2,1)}, bf16[640,1408]{1,0:T(8,128)(2,1)}, bf16[640,1408]{1,0:T(8,128)(2,1)}) fusion(f32[640,1408]{1,0:T(8,128)} %fusion.86, f32[640,1408]{1,0:T(8,128)} %fusion.87, bf16[640,2048]{1,0:T(8,128)(2,1)S(1)} %copy-done.54, bf16[1408,2048]{1,0:T(8,128)(2,1)} %param.35), kind=kOutput, calls=%fused_computation.14 | convolution fusion | flops 3704504320 | bytes 21004288 | tf_op jit(solution)/shard_map/dot_general | solution.py:26
  216.3 7.5 fusion.88
  224.4 8.9 %add_convert_fusion.4.refs_0_ = bf16[640,2048]{1,0:T(8,128)(2,1)S(1)} fusion(f32[640,2048]{1,0:T(8,128)} %fusion.88, bf16[640,1408]{1,0:T(8,128)(2,1)} %get-tuple-element.108, bf16[2048,1408]{1,0:T(8,128)(2,1)} %param.34), kind=kOutput, calls=%fused_computation.12 | convolution fusion | flops 3693608960 | bytes 15433728 | tf_op jit(solution)/shard_map/dot_general | solution.py:26
  233.4 77.0 %line_back.2 = (bf16[640,2048]{1,0:T(8,128)(2,1)}, f32[320,2048]{1,0:T(8,128)S(1)}, f32[8,2048]{1,0:T(8,128)S(1)}) custom-call(bf16[640,2048]{1,0:T(8,128)(2,1)S(1)} %add_convert_fusion.4.refs_0_, f32[320,2048]{1,0:T(8,128)S(1)} %get-tuple-element.31.refs_2_.refs_1_, bf16[320,2048]{1,0:T(8,128)(2,1)S(1)} %copy-done.5, f32[1,2048]{1,0:T(1,128)S(1)} %bitcast.110), custom_call_target="tpu_custom_call" | custom-call | flops 10000000 | bytes 200000000 | tf_op jit(solution)/shard_map/line_back/pallas_call | solution.py:468
  310.4 5.9 multiply_reduce_fusion
  322.3 8.9 %convolution_convert_fusion.1.refs_0_ = bf16[640,2048]{1,0:T(8,128)(2,1)} fusion(bf16[640,1408]{1,0:T(8,128)(2,1)} %get-tuple-element.110, bf16[1408,2048]{1,0:T(8,128)(2,1)} %param.35), kind=kOutput, calls=%fused_computation.19 | convolution fusion | flops 3692298240 | bytes 10190848 | tf_op jit(solution)/shard_map/dot_general | solution.py:30
  331.2 5.5 reshape.283
  341.3 4.3 all-to-all-start.7
  353.5 20.5 %recur_backward.1 = (bf16[1024,1152]{1,0:T(8,128)(2,1)S(1)}, f32[256,128]{1,0:T(8,128)S(1)}, f32[8,256]{1,0:T(8,128)S(1)}) custom-call(s32[1,1024]{1,0:T(1,128)S(1)} %bitcast.115, s32[1024,1]{1,0:T(8,128)S(1)} %copy-done.16, s32[1,3]{1,0:T(1,128)S(1)} %copy-done.25, bf16[128,256]{1,0:T(8,128)(2,1)S(1)} %copy-done.23, f32[1,256]{1,0:T(1,128)S(1)} %bitcast.117, ...), custom_call_target="tpu_custom_call" | custom-call | flops 12000000000 | bytes 12000000 | tf_op jit(solution)/shard_map/recur_backward/pallas_call | solution.py:241
  375.9 4.6 all-to-all-start.3
  380.5 10.2 %constant_dynamic-slice_fusion = (bf16[640,4,1,256]{3,2,1,0:T(2,128)(2,1)}, bf16[640,4,1,256]{3,2,1,0:T(2,128)(2,1)}) fusion(bf16[640,4,2,256]{3,2,1,0:T(2,128)(2,1)} %reshape.283, s32[]{:T(128)S(6)} %select_n.66, s32[]{:T(128)S(6)} %select_n.65), kind=kLoop, calls=%fused_computation.134 | loop fusion | bytes 5242888 | tf_op jit(solution)/shard_map/jit(dynamic_index_in_dim)/dynamic_slice | solution.py:657
  401.4 4.9 fusion.89
  406.7 5.8 add_convert_fusion
  412.5 5.0 all-to-all-start.11
  417.5 4.0 fusion.91
  421.6 6.1 copy.117
  432.0 73.9 %line_sum.1 = bf16[640,2048]{1,0:T(8,128)(2,1)S(1)} custom-call(bf16[640,2048]{1,0:T(8,128)(2,1)S(1)} %copy-done.11, bf16[320,2048]{1,0:T(8,128)(2,1)S(1)} %constant_dynamic-slice_fusion.6.refs_1_.refs_2_, f32[320,2048]{1,0:T(8,128)S(1)} %copy-done.3, f32[1,2048]{1,0:T(1,128)S(1)} %bitcast.111), custom_call_target="tpu_custom_call" | custom-call | flops 10000000 | bytes 200000000 | tf_op jit(solution)/shard_map/line_sum/pallas_call | solution.py:468
  505.9 6.7 fusion.93
  512.6 5.8 fusion.92
  522.1 4.3 fusion.7
  526.4 3.6 convolution_convert_fusion.3
  530.1 5.5 all-to-all-start.8
  542.0 3.7 all-to-all-done.8
  555.8 4.1 all-to-all-start.4
  559.9 7.7 add_convert_fusion.1
  567.6 4.8 all-to-all-start.10
  572.5 7.9 add_convert_fusion.2
  585.7 3.9 fusion.81
  589.7 13.4 %all-to-all-done.10 = bf16[4,256,1408]{2,1,0:T(8,128)(2,1)} async-done(((bf16[4,256,1408]{2,1,0:T(8,128)(2,1)}), bf16[4,256,1408]{2,1,0:T(8,128)(2,1)}, u32[]{:S(2)}, u32[]{:S(2)}) %all-to-all-start.10) | async-done | bytes 2883616 | tf_op jit(solution)/shard_map/all_to_all | solution.py:669
  603.1 4.6 all-to-all-start.9
  610.1 7.0 add_convert_fusion.3.refs_0_
  619.5 75.7 %line_back.3 = (bf16[640,2048]{1,0:T(8,128)(2,1)S(1)}, f32[320,2048]{1,0:T(8,128)}, f32[8,2048]{1,0:T(8,128)S(1)}) custom-call(bf16[640,2048]{1,0:T(8,128)(2,1)S(1)} %add_convert_fusion.3.refs_0_, bf16[320,2048]{1,0:T(8,128)(2,1)S(1)} %constant_dynamic-slice_fusion.6.refs_1_.refs_2_, f32[320,2048]{1,0:T(8,128)S(1)} %copy-done.7, f32[1,2048]{1,0:T(1,128)S(1)} %bitcast.112), custom_call_target="tpu_custom_call" | custom-call | flops 10000000 | bytes 200000000 | tf_op jit(solution)/shard_map/line_back/pallas_call | solution.py:468
  702.1 51.8 %all-reduce.5.cloned.1.call-done = f32[8,5216]{1,0:T(8,128)} async-done(((f32[8,5216]{1,0:T(8,128)}), f32[8,5216]{1,0:T(8,128)}) %all-reduce.5.cloned.1.call-update) | async-done | bytes 166928
  755.5 18.9 %psum.7 = f32[4672]{0:T(1024)S(1)} all-reduce(f32[4672]{0:T(1024)S(1)} %dynamic-slice_reduce_fusion), channel_id=1, replica_groups=mesh['dp'=8,'tensor'=4] {'tensor'}, use_global_device_ids=true, to_apply=%region_9.10 | all-reduce | flops 4672 | bytes 37376 | tf_op jit(solution)/shard_map/psum | solution.py:708
  780.5 3.8 add_convert_fusion.6
  784.3 3.7 all-to-all-start.6
  800.7 3.7 copy.124
  (281 shorter events, 134.2 us)
Async XLA Ops:
  7.2 103.5 %copy-start = (bf16[512,2048]{1,0:T(8,128)(2,1)S(1)}, bf16[512,2048]{1,0:T(8,128)(2,1)}, u32[]{:S(2)}) copy-start(bf16[512,2048]{1,0:T(8,128)(2,1)} %param.31) | copy-start | bytes 6291460
  10.6 13.5 %copy-start.64 = (s32[640]{0:T(1024)}, s32[640]{0:T(1024)S(1)}, u32[]{:S(2)}) copy-start(s32[640]{0:T(1024)S(1)} %multiply_add_fusion.1) | copy-start | bytes 7684
  27.7 34.9 %all-to-all-start = ((bf16[8,128,1152]{2,1,0:T(8,128)(2,1)}), bf16[8,128,1152]{2,1,0:T(8,128)(2,1)}, u32[]{:S(2)}, u32[]{:S(2)}) async-start(bf16[8,128,1152]{2,1,0:T(8,128)(2,1)} %bitcast.132), calls=%async_computation | async-start | bytes 4718592 | tf_op jit(solution)/shard_map/all_to_all | solution.py:549
  36.2 26.5 %copy-start.25 = (s32[1,3]{1,0:T(1,128)S(1)}, s32[1,3]{1,0:T(1,128)}, u32[]{:S(2)}) copy-start(s32[1,3]{1,0:T(1,128)} %lengths_ref.3) | copy-start | bytes 40
  37.6 55.0 %collective-permute-start = (bf16[640,4,256]{2,0,1:T(8,128)(2,1)}, bf16[640,4,256]{2,0,1:T(8,128)(2,1)}, u32[]{:S(2)}, u32[]{:S(2)}) collective-permute-start(bf16[640,4,256]{2,0,1:T(8,128)(2,1)} %bitcast.137), channel_id=1, source_target_pairs={{0,4},{4,0},{8,12},{12,8},{16,20},{20,16},{24,28},{28,24},{1,5},{5... | collective-permute-start | bytes 3932168 | tf_op jit(solution)/shard_map/ppermute | solution.py:658
  41.4 21.3 %copy-start.66 = (bf16[128]{0:T(256)(128)(2,1)}, bf16[128]{0:T(256)(128)(2,1)S(1)}, u32[]{:S(2)}) copy-start(bf16[128]{0:T(256)(128)(2,1)S(1)} %pad.15.clone) | copy-start | bytes 772
  43.7 36.9 %copy-start.22 = (bf16[128,256]{1,0:T(8,128)(2,1)}, bf16[128,256]{1,0:T(8,128)(2,1)S(1)}, u32[]{:S(2)}) copy-start(bf16[128,256]{1,0:T(8,128)(2,1)S(1)} %copy.100.up_ref) | copy-start | bytes 196612
  44.4 36.2 %copy-start.26 = (f32[256]{0:T(256)}, f32[256]{0:T(256)S(1)}, u32[]{:S(2)}) copy-start(f32[256]{0:T(256)S(1)} %reshape.292) | copy-start | bytes 3076
  83.4 19.8 %all-to-all-start.1 = ((bf16[8,128,512]{2,1,0:T(8,128)(2,1)}), bf16[8,128,512]{2,1,0:T(8,128)(2,1)}, u32[]{:S(2)}, u32[]{:S(2)}) async-start(bf16[8,128,512]{2,1,0:T(8,128)(2,1)} %bitcast.6), calls=%async_computation.1 | async-start | bytes 2097152 | tf_op jit(solution)/shard_map/all_to_all | solution.py:549
  87.8 318.5 %collective-permute-start.11 = (bf16[640,2048]{1,0:T(8,128)(2,1)}, bf16[640,2048]{1,0:T(8,128)(2,1)}, u32[]{:S(2)}, u32[]{:S(2)}) collective-permute-start(bf16[640,2048]{1,0:T(8,128)(2,1)} %param.19), channel_id=1, source_target_pairs={{0,4},{4,0},{8,12},{12,8},{16,20},{20,16},{24,28},{28,24},{1,5},{5... | collective-permute-start | bytes 7864328 | tf_op jit(solution)/shard_map/ppermute | solution.py:663
  91.4 11.8 %copy-start.65 = (s32[640]{0:T(1024)S(1)}, s32[640]{0:T(1024)}, u32[]{:S(2)}) copy-start(s32[640]{0:T(1024)} %copy-done.64) | copy-start | bytes 7684
  103.2 87.4 %slice-start = ((s8[5767168]{0:T(1024)(128)(4,1)}), s8[4194304]{0:T(1024)(128)(4,1)S(1)}, s32[]{:S(2)}) async-start(s8[5767168]{0:T(1024)(128)(4,1)} %bitcast.144), calls=%async_computation.13 | async-start | bytes 8388608
  105.8 84.8 %slice-start.1 = ((s8[5767168]{0:T(1024)(128)(4,1)}), s8[1572864]{0:T(1024)(128)(4,1)S(1)}, s32[]{:S(2)}) async-start(s8[5767168]{0:T(1024)(128)(4,1)} %bitcast.144), calls=%async_computation.14 | async-start | bytes 3145728
  190.6 6.1 copy-start.10
  190.6 42.7 %copy-start.2 = (f32[320,2048]{1,0:T(8,128)}, f32[320,2048]{1,0:T(8,128)S(1)}, u32[]{:S(2)}) copy-start(f32[320,2048]{1,0:T(8,128)S(1)} %get-tuple-element.31.refs_2_.refs_1_) | copy-start | bytes 7864324
  196.7 8.8 %copy-start.54 = (bf16[640,2048]{1,0:T(8,128)(2,1)S(1)}, bf16[640,2048]{1,0:T(8,128)(2,1)}, u32[]{:S(2)}) copy-start(bf16[640,2048]{1,0:T(8,128)(2,1)} %param.19) | copy-start | bytes 7864324
  216.3 356.1 %collective-permute-start.8 = (bf16[640,1408]{1,0:T(8,128)(2,1)}, bf16[640,1408]{1,0:T(8,128)(2,1)}, u32[]{:S(2)}, u32[]{:S(2)}) collective-permute-start(bf16[640,1408]{1,0:T(8,128)(2,1)} %get-tuple-element.109), channel_id=1, source_target_pairs={{0,4},{4,0},{8,12},{12,8},{16,20},{20,16},{24,28},{28,24},{1,5},{5... | collective-permute-start | bytes 5406728 | tf_op jit(solution)/shard_map/ppermute | solution.py:663
  223.9 9.5 %copy-start.5 = (bf16[320,2048]{1,0:T(8,128)(2,1)S(1)}, bf16[320,2048]{1,0:T(8,128)(2,1)}, u32[]{:S(2)}) copy-start(bf16[320,2048]{1,0:T(8,128)(2,1)} %constant_dynamic-slice_fusion.5.refs_2_) | copy-start | bytes 3932164
  223.9 336.1 %collective-permute-start.9 = (bf16[640,1408]{1,0:T(8,128)(2,1)}, bf16[640,1408]{1,0:T(8,128)(2,1)}, u32[]{:S(2)}, u32[]{:S(2)}) collective-permute-start(bf16[640,1408]{1,0:T(8,128)(2,1)} %get-tuple-element.108), channel_id=1, source_target_pairs={{0,4},{4,0},{8,12},{12,8},{16,20},{20,16},{24,28},{28,24},{1,5},{5... | collective-permute-start | bytes 5406728 | tf_op jit(solution)/shard_map/ppermute | solution.py:663
  233.4 77.1 %copy-start.71 = (f32[640,512]{0,1:T(8,128)S(1)}, f32[640,512]{0,1:T(8,128)}, u32[]{:S(2)}) copy-start(f32[640,512]{0,1:T(8,128)} %get-tuple-element.131) | copy-start | bytes 3932164
  310.3 6.0 copy-start.6
  310.4 211.7 %collective-permute-start.6 = (bf16[640,2048]{1,0:T(8,128)(2,1)}, bf16[640,2048]{1,0:T(8,128)(2,1)}, u32[]{:S(2)}, u32[]{:S(2)}) collective-permute-start(bf16[640,2048]{1,0:T(8,128)(2,1)} %get-tuple-element.32), channel_id=1, source_target_pairs={{0,4},{4,0},{8,12},{12,8},{16,20},{20,16},{24,28},{28,24},{1,5},{5... | collective-permute-start | bytes 7864328 | tf_op jit(solution)/shard_map/ppermute | solution.py:663
  316.4 22.9 %collective-permute-start.4 = (bf16[640,512]{0,1:T(8,128)(2,1)}, bf16[640,512]{0,1:T(8,128)(2,1)S(1)}, u32[]{:S(2)}, u32[]{:S(2)}) collective-permute-start(bf16[640,512]{0,1:T(8,128)(2,1)} %get-tuple-element.111), channel_id=1, source_target_pairs={{0,4},{4,0},{8,12},{12,8},{16,20},{20,16},{24,28},{28,24},{1,5},{5... | collective-permute-start | bytes 1966088 | tf_op jit(solution)/shard_map/ppermute | solution.py:663
  318.7 22.6 %all-to-all-start.2 = ((bf16[8,128,512]{2,1,0:T(8,128)(2,1)}), bf16[8,128,512]{2,1,0:T(8,128)(2,1)S(1)}, u32[]{:S(2)}, u32[]{:S(2)}) async-start(bf16[8,128,512]{2,1,0:T(8,128)(2,1)} %bitcast.9), calls=%async_computation.2 | async-start | bytes 2097152 | tf_op jit(solution)/shard_map/all_to_all | solution.py:549
  341.3 34.6 %all-to-all-start.7 = ((bf16[4,256,512]{2,1,0:T(8,128)(2,1)}), bf16[4,256,512]{2,1,0:T(8,128)(2,1)}, u32[]{:S(2)}, u32[]{:S(2)}) async-start(bf16[4,256,512]{2,1,0:T(8,128)(2,1)} %bitcast.21), calls=%async_computation.7 | async-start | bytes 2097152 | tf_op jit(solution)/shard_map/all_to_all | solution.py:669
  375.9 36.6 %all-to-all-start.3 = ((bf16[8,128,1152]{2,1,0:T(8,128)(2,1)}), bf16[8,128,1152]{2,1,0:T(8,128)(2,1)}, u32[]{:S(2)}, u32[]{:S(2)}) async-start(bf16[8,128,1152]{2,1,0:T(8,128)(2,1)} %bitcast.107), calls=%async_computation.3 | async-start | bytes 4718592 | tf_op jit(solution)/shard_map/all_to_all | solution.py:549
  397.2 9.6 %collective-permute-start.10 = (bf16[640,4,176]{0,2,1:T(8,128)(2,1)S(1)}, bf16[640,4,176]{0,2,1:T(8,128)(2,1)S(1)}, u32[]{:S(2)}, u32[]{:S(2)}) collective-permute-start(bf16[640,4,176]{0,2,1:T(8,128)(2,1)S(1)} %get-tuple-element.116), channel_id=1, source_target_pairs={{0,4},{4,0},{8,12},{12,8},{16,20},{20,16},{24,28},{28,24},{1,5},{5... | collective-permute-start | bytes 2703368 | tf_op jit(solution)/shard_map/ppermute | solution.py:658
  406.3 114.4 %collective-permute-start.7 = (bf16[640,4,256]{2,0,1:T(8,128)(2,1)}, bf16[640,4,256]{2,0,1:T(8,128)(2,1)S(1)}, u32[]{:S(2)}, u32[]{:S(2)}) collective-permute-start(bf16[640,4,256]{2,0,1:T(8,128)(2,1)} %bitcast.106), channel_id=1, source_target_pairs={{0,4},{4,0},{8,12},{12,8},{16,20},{20,16},{24,28},{28,24},{1,5},{5... | collective-permute-start | bytes 3932168 | tf_op jit(solution)/shard_map/ppermute | solution.py:658
  412.5 117.6 %all-to-all-start.11 = ((bf16[4,176,2048]{2,1,0:T(8,128)(2,1)}), bf16[4,176,2048]{2,1,0:T(8,128)(2,1)}, u32[]{:S(2)}, u32[]{:S(2)}) async-start(bf16[4,176,2048]{2,1,0:T(8,128)(2,1)} %bitcast.130), calls=%async_computation.11 | async-start | bytes 5767168 | tf_op jit(solution)/shard_map/all_to_all | solution.py:669
  421.6 6.9 copy-start.21
  427.7 94.4 %collective-permute-start.5 = (bf16[640,4,64]{0,2,1:T(8,128)(2,1)}, bf16[640,4,64]{0,2,1:T(8,128)(2,1)S(1)}, u32[]{:S(2)}, u32[]{:S(2)}) collective-permute-start(bf16[640,4,64]{0,2,1:T(8,128)(2,1)} %get-tuple-element.120), channel_id=1, source_target_pairs={{0,4},{4,0},{8,12},{12,8},{16,20},{20,16},{24,28},{28,24},{1,5},{5... | collective-permute-start | bytes 983048 | tf_op jit(solution)/shard_map/ppermute | solution.py:658
  432.0 73.9 %copy-start.49 = (bf16[640,4,1,256]{0,3,1,2:T(8,128)(2,1)S(1)}, bf16[640,4,1,256]{0,3,1,2:T(8,128)(2,1)}, u32[]{:S(2)}) copy-start(bf16[640,4,1,256]{0,3,1,2:T(8,128)(2,1)} %copy.117) | copy-start | bytes 3932164
  505.9 6.7 copy-start.4
  530.1 6.2 copy-start.40
  530.1 15.7 %all-to-all-start.8 = ((bf16[4,64,2048]{2,1,0:T(8,128)(2,1)}), bf16[4,64,2048]{2,1,0:T(8,128)(2,1)}, u32[]{:S(2)}, u32[]{:S(2)}) async-start(bf16[4,64,2048]{2,1,0:T(8,128)(2,1)} %bitcast.128), calls=%async_computation.8 | async-start | bytes 2097152 | tf_op jit(solution)/shard_map/all_to_all | solution.py:669
  536.3 4.3 collective-permute-start.2
  538.6 12.5 %collective-permute-start.1 = (bf16[640,256]{1,0:T(8,128)(2,1)}, bf16[640,256]{1,0:T(8,128)(2,1)}, u32[]{:S(2)}, u32[]{:S(2)}) collective-permute-start(bf16[640,256]{1,0:T(8,128)(2,1)} %get-tuple-element.119), channel_id=1, source_target_pairs={{0,4},{4,0},{8,12},{12,8},{16,20},{20,16},{24,28},{28,24},{1,5},{5... | collective-permute-start | bytes 983048 | tf_op jit(solution)/shard_map/ppermute | solution.py:663
  545.8 10.0 %all-to-all-start.5 = ((bf16[4,256,256]{2,1,0:T(8,128)(2,1)}), bf16[4,256,256]{2,1,0:T(8,128)(2,1)S(1)}, u32[]{:S(2)}, u32[]{:S(2)}) async-start(bf16[4,256,256]{2,1,0:T(8,128)(2,1)} %bitcast.19), calls=%async_computation.5 | async-start | bytes 1048576 | tf_op jit(solution)/shard_map/all_to_all | solution.py:669
  555.8 11.9 %copy-start.43 = (bf16[4,256,256]{2,1,0:T(8,128)(2,1)}, bf16[4,256,256]{2,1,0:T(8,128)(2,1)S(1)}, u32[]{:S(2)}) copy-start(bf16[4,256,256]{2,1,0:T(8,128)(2,1)S(1)} %all-to-all-done.5) | copy-start | bytes 1572868
  555.8 11.9 %all-to-all-start.4 = ((bf16[4,256,256]{2,1,0:T(8,128)(2,1)}), bf16[4,256,256]{2,1,0:T(8,128)(2,1)}, u32[]{:S(2)}, u32[]{:S(2)}) async-start(bf16[4,256,256]{2,1,0:T(8,128)(2,1)} %bitcast.18), calls=%async_computation.4 | async-start | bytes 1048576 | tf_op jit(solution)/shard_map/all_to_all | solution.py:669
  567.6 35.4 %all-to-all-start.10 = ((bf16[4,256,1408]{2,1,0:T(8,128)(2,1)}), bf16[4,256,1408]{2,1,0:T(8,128)(2,1)}, u32[]{:S(2)}, u32[]{:S(2)}) async-start(bf16[4,256,1408]{2,1,0:T(8,128)(2,1)} %bitcast.131), calls=%async_computation.10 | async-start | bytes 5767168 | tf_op jit(solution)/shard_map/all_to_all | solution.py:669
  572.4 7.9 copy-start.41
  572.4 8.8 %copy-start.38 = (bf16[640,2048]{0,1:T(8,128)(2,1)S(1)}, bf16[640,2048]{0,1:T(8,128)(2,1)}, u32[]{:S(2)}) copy-start(bf16[640,2048]{0,1:T(8,128)(2,1)} %copy-done.36) | copy-start | bytes 7864324
  581.2 199.3 %collective-permute-start.3 = (bf16[640,512]{1,0:T(8,128)(2,1)}, bf16[640,512]{1,0:T(8,128)(2,1)}, u32[]{:S(2)}, u32[]{:S(2)}) collective-permute-start(bf16[640,512]{1,0:T(8,128)(2,1)} %slice.94), channel_id=1, source_target_pairs={{0,4},{4,0},{8,12},{12,8},{16,20},{20,16},{24,28},{28,24},{1,5},{5... | collective-permute-start | bytes 1966088 | tf_op jit(solution)/shard_map/ppermute | solution.py:663
  603.1 181.2 %all-to-all-start.9 = ((bf16[4,256,1408]{2,1,0:T(8,128)(2,1)}), bf16[4,256,1408]{2,1,0:T(8,128)(2,1)}, u32[]{:S(2)}, u32[]{:S(2)}) async-start(bf16[4,256,1408]{2,1,0:T(8,128)(2,1)} %bitcast.129), calls=%async_computation.9 | async-start | bytes 5767168 | tf_op jit(solution)/shard_map/all_to_all | solution.py:669
  607.7 146.2 %all-reduce.5.cloned.1.call-start = ((), (), s32[]{:S(2)}) async-start(), calls=%async_computation.12 | async-start | bytes 335872
  610.1 7.0 copy-start.35
  784.3 15.4 %all-to-all-start.6 = ((bf16[4,256,512]{2,1,0:T(8,128)(2,1)}), bf16[4,256,512]{2,1,0:T(8,128)(2,1)S(1)}, u32[]{:S(2)}, u32[]{:S(2)}) async-start(bf16[4,256,512]{2,1,0:T(8,128)(2,1)} %bitcast.20), calls=%async_computation.6 | async-start | bytes 2097152 | tf_op jit(solution)/shard_map/all_to_all | solution.py:669
  (51 other events, 119.3 us)
Sparse Core Ops, SparseCore 0:
  698.6 55.2 all-reduce.4

commit v2 on v1

--- a/solution.py
+++ b/solution.py
@@ -270,7 +270,7 @@
     )
 
 
-CHUNK = 32
+CHUNK = 16
 
 
 def line_kernel(mode, n, *refs):
@@ -485,6 +485,109 @@
         ),
         name="line_" + mode,
     )(share, x_own, base_own, gain)
+
+
+def small_sum_kernel(groups, n, rows_all, part_ref, out_ref, held, line, line_in, sems, line_sems):
+    me = lax.axis_index("dp")
+    place = lax.axis_index("tensor")
+    barrier = pltpu.get_barrier_semaphore()
+
+    def peer(k):
+        return lax.rem(me + k, groups)
+
+    def mate(k):
+        return lax.rem(place + k, n)
+
+    @pl.loop(1, groups)
+    def _(k):
+        pl.semaphore_signal(barrier, inc=1, device_id={"dp": peer(k)}, device_id_type=MESH)
+
+    @pl.loop(1, n)
+    def _(k):
+        pl.semaphore_signal(barrier, inc=1, device_id={"tensor": mate(k)}, device_id_type=MESH)
+
+    pl.semaphore_wait(barrier, groups + n - 2)
+
+    def copy(k, source):
+        return pltpu.make_async_remote_copy(
+            part_ref.at[peer(k)], held.at[source], sems.at[0, k], sems.at[1, source],
+            device_id={"dp": peer(k)}, device_id_type=MESH,
+        )
+
+    def line_copy(k, source):
+        return pltpu.make_async_remote_copy(
+            line, line_in.at[source], line_sems.at[0, k], line_sems.at[1, source],
+            device_id={"tensor": mate(k)}, device_id_type=MESH,
+        )
+
+    @pl.loop(1, groups)
+    def _(k):
+        copy(k, me).start()
+
+    held[pl.ds(me, 1)] = part_ref[pl.ds(me, 1)]
+
+    @pl.loop(1, groups)
+    def _(k):
+        copy(k, peer(k)).wait_recv()
+
+    total = held[0]
+    for i in range(1, groups):
+        total = total + held[i]
+    line[...] = total[:rows_all]
+    out_ref[...] = total
+
+    @pl.loop(1, n)
+    def _(k):
+        line_copy(k, place).start()
+
+    line_in[pl.ds(place, 1)] = total[None, :rows_all]
+
+    @pl.loop(1, n)
+    def _(k):
+        line_copy(k, mate(k)).wait_recv()
+
+    total = line_in[0]
+    for i in range(1, n):
+        total = total + line_in[i]
+    out_ref[:rows_all] = total
+
+    @pl.loop(1, groups)
+    def _(k):
+        copy(k, me).wait_send()
+
+    @pl.loop(1, n)
+    def _(k):
+        line_copy(k, place).wait_send()
+
+
+def small_sum(over_all, over_owners, groups, n, call):
+    def tiles(blocks):
+        short = -blocks.shape[1] % (8 * LANES)
+        return jnp.pad(blocks, ((0, 0), (0, short))).reshape(groups, -1, LANES)
+
+    first, second = tiles(over_all), tiles(over_owners)
+    rows_all = first.shape[1]
+    part = jnp.concatenate([first, second], axis=1)
+    vmem = pl.BlockSpec(memory_space=pltpu.VMEM)
+    total = pl.pallas_call(
+        functools.partial(small_sum_kernel, groups, n, rows_all),
+        in_specs=[vmem],
+        out_specs=vmem,
+        out_shape=jax.ShapeDtypeStruct(part.shape[1:], f32),
+        scratch_shapes=[
+            pltpu.VMEM(part.shape, f32),
+            pltpu.VMEM((rows_all, LANES), f32),
+            pltpu.VMEM((n, rows_all, LANES), f32),
+            pltpu.SemaphoreType.DMA((2, groups)),
+            pltpu.SemaphoreType.DMA((2, n)),
+        ],
+        compiler_params=pltpu.CompilerParams(collective_id=call, has_side_effects=True),
+        name="small_sum",
+    )(part)
+    return (
+        total[:rows_all].reshape(-1)[: over_all.shape[1]],
+        total[rows_all:].reshape(-1)[: over_owners.shape[1]],
+    )
 
 
 def per_device(
@@ -646,10 +749,11 @@
     token_grad, _, mixer_gain_part = line_sum(
         "back", 3, lines, normed_share, tokens_own, d_hidden_own, mixer_gain_wide.reshape(1, -1)
     )
-    layer_share = dot(active, feed_down).astype(bf16)
-    (layer_out,) = line_sum(
-        "sum", 4, lines, layer_share, tokens_own, hidden_own, feed_gain_wide.reshape(1, -1)
-    )
+    hidden_placed = jnp.concatenate(
+        [jnp.where(place == lines - 1, hidden_own, 0.0), jnp.where(place == 0, hidden_own, 0.0)],
+        axis=0,
+    )
+    layer_out = lax.psum((dot(active, feed_down) + hidden_placed).astype(bf16), "tensor")
 
     def halves(row_block, dims):
         split = row_block.reshape(row_block.shape[0], groups // 2, 2, dims // groups)
@@ -701,11 +805,7 @@
         axis=1,
     )
     over_owners = jnp.concatenate([by_owner(up_part), by_owner(bias_part[0])], axis=1)
-    wide = over_all.shape[1]
-    small = lax.psum_scatter(
-        jnp.concatenate([over_all, over_owners], axis=1), "dp", scatter_dimension=0, tiled=True
-    )[0]
-    summed = lax.psum(small[:wide], "tensor")
+    summed, small = small_sum(over_all, over_owners, groups, lines, 5)
     per = width // groups
     head_per = dv // groups
     return (
@@ -717,8 +817,8 @@
         grad_value,
         grad_gate,
         summed[2 * per + head_per :].reshape(per, rank),
-        small[wide : wide + dk // groups * rank].reshape(1, dk // groups, rank),
-        small[wide + dk // groups * rank :].reshape(1, dk // groups),
+        small[: dk // groups * rank].reshape(1, dk // groups, rank),
+        small[dk // groups * rank :].reshape(1, dk // groups),
         summed[2 * per : 2 * per + head_per],
         grad_out[None],
         summed[per : 2 * per],

time: 821 us -> 810 us (0.987)
  waiting for transfers between devices: 97.6 us -> 67.4 us
  Pallas kernels: 342 us -> 366 us
  blocking collectives: 18.9 us -> 0 us
    unnamed x2 -> x1, waiting for transfers between devices: 51.8 us -> 0.02 us
    psum x1 -> x0, blocking collectives: 18.9 us -> none  [per_device(): summed = lax.psum(small[:wide], 'tensor')]
    all_to_all x4, waiting for transfers between devices: 26.4 us -> 39.5 us  [exchange(): lax.all_to_all(blocks, 'dp', split_axis=0, concat_axis=0, tiled=True)]
    pallas_call x0 -> x1, Pallas kernels: none -> 12.7 us  [small_sum(): pl.pallas_call(functools.partial(small_sum_kernel, groups, n, rows_all),...]
    dot_general x17, matrix products: 63.5 us -> 74.8 us  [rows_dot(): lax.dot_general(left, right, (((0,), (0,)), ((), ())), preferred_element_...]
    pallas_call x4 -> x3, Pallas kernels: 305 us -> 315 us  [line_sum(): pl.pallas_call(functools.partial(line_kernel, mode, n), in_specs=[vmem] *...]
    dot_general x9, matrix products: 54.7 us -> 45.8 us  [dot_t(): lax.dot_general(left, right, (((1,), (1,)), ((), ())), preferred_element_...]
    all_to_all x8, waiting for transfers between devices: 19.4 us -> 27.8 us  [summed_share(): lax.all_to_all(blocks, 'dp', split_axis=0, concat_axis=0, tiled=True, axi...]
  transfers between devices with their start and end apart: 25 -> 25, of which waited for: 6 -> 9; matrix products, arithmetic and copies ran while one was open for 29% -> 31% of each run, Pallas kernels for 42% -> 46%
where the time goes in v2:
time: 810 us; the launch traced here: 800 us
  Pallas kernels  366 us (45%)
  matrix products  173 us (21%)
  local copies, waits for them, and re-layouts  89.8 us (11%)
  waiting for transfers between devices  67.4 us (8%)
  starting transfers between devices  55 us (7%)
  other arithmetic  34.4 us (4%)
  between operations  15.2 us (2%)
    pallas_call x3, Pallas kernels, line_sum(): pl.pallas_call(functools.partial(line_kernel, mode, n), in_specs=[vmem] *...  315 us
    dot_general x17, matrix products, rows_dot(): lax.dot_general(left, right, (((0,), (0,)), ((), ())), preferred_element_...  74.8 us
    dot_general x14, matrix products, dot(): return jnp.dot(left, right, preferred_element_type=f32)  52 us
    dot_general x9, matrix products, dot_t(): lax.dot_general(left, right, (((1,), (1,)), ((), ())), preferred_element_...  45.8 us
    unnamed x169, local copies, waits for them, and re-layouts  44.8 us
    all_to_all x4, waiting for transfers between devices, exchange(): lax.all_to_all(blocks, 'dp', split_axis=0, concat_axis=0, tiled=True)  39.5 us
    all_to_all x8, starting transfers between devices, summed_share(): lax.all_to_all(blocks, 'dp', split_axis=0, concat_axis=0, tiled=True, axi...  34.2 us
    all_to_all x8, waiting for transfers between devices, summed_share(): lax.all_to_all(blocks, 'dp', split_axis=0, concat_axis=0, tiled=True, axi...  27.8 us
  transfers between devices with their start and end apart: 25, of which 9 were waited for; matrix products, arithmetic and copies ran while one was open for 31% of the time, Pallas kernels for 46%

profile of v2, /device:TPU:0, one launch (start us, length us, event | category | flops | bytes accessed | tf_op | source)
XLA Modules:
  0.0 799.9 jit_solution(10125747511951111316)
XLA Ops:
  10.6 4.4 copy.81
  27.8 5.4 all-to-all-start
  44.4 18.3 %all-to-all-done = bf16[8,128,1152]{2,1,0:T(8,128)(2,1)} async-done(((bf16[8,128,1152]{2,1,0:T(8,128)(2,1)}), bf16[8,128,1152]{2,1,0:T(8,128)(2,1)}, u32[]{:S(2)}, u32[]{:S(2)}) %all-to-all-start) | async-done | bytes 2359328 | tf_op jit(solution)/shard_map/all_to_all | solution.py:652
  63.8 17.0 %recur_forward.1 = (bf16[1024,512]{1,0:T(8,128)(2,1)}, bf16[1024,1152]{1,0:T(8,128)(2,1)S(1)}, bf16[8,256,512]{2,1,0:T(8,128)(2,1)S(1)}) custom-call(s32[1,1024]{1,0:T(1,128)S(1)} %bitcast.132, s32[1024,1]{1,0:T(8,128)S(1)} %copy-done.16, s32[1,3]{1,0:T(1,128)S(1)} %copy-done.25, bf16[128,256]{1,0:T(8,128)(2,1)S(1)} %copy.83.up_ref, f32[1,256]{1,0:T(1,128)S(1)} %bitcast.134, ...), custom_call_target="tpu_custom_call" | custom-call | flops 6000000000 | bytes 10000000 | tf_op jit(solution)/shard_map/recur_forward/pallas_call | solution.py:207
  83.5 4.4 all-to-all-start.1
  95.1 8.2 %all-to-all-done.1 = bf16[8,128,512]{2,1,0:T(8,128)(2,1)} async-done(((bf16[8,128,512]{2,1,0:T(8,128)(2,1)}), bf16[8,128,512]{2,1,0:T(8,128)(2,1)}, u32[]{:S(2)}, u32[]{:S(2)}) %all-to-all-start.1) | async-done | bytes 1048608 | tf_op jit(solution)/shard_map/all_to_all | solution.py:652
  105.9 5.2 multiply_convert_fusion.3
  112.7 105.3 %line_norm.1 = (bf16[640,2048]{1,0:T(8,128)(2,1)S(1)}, f32[320,2048]{1,0:T(8,128)S(1)}) custom-call(bf16[640,2048]{1,0:T(8,128)(2,1)S(1)} %convolution_convert_fusion.1.refs_0_, bf16[320,2048]{1,0:T(8,128)(2,1)S(1)} %constant_dynamic-slice_fusion.6.refs_1_.refs_2_, bf16[320,2048]{1,0:T(8,128)(2,1)S(1)} %constant_dynamic-slice_fusion.6.refs_1_.refs_2_, ...), custom_call_target="tpu_custom_call" | custom-call | flops 10000000 | bytes 200000000 | tf_op jit(solution)/shard_map/line_norm/pallas_call | solution.py:468
  220.9 5.5 reshape.289
  226.4 7.9 fusion.87
  234.4 8.8 %fusion.88 = f32[640,1408]{1,0:T(8,128)} fusion(bf16[640,2048]{1,0:T(8,128)(2,1)S(1)} %copy-done.12, bf16[2048,1408]{1,0:T(8,128)(2,1)} %param.34), kind=kOutput, calls=%fused_computation.178 | convolution fusion | flops 3690987520 | bytes 11993088 | tf_op jit(solution)/shard_map/dot_general | solution.py:30
  243.2 10.4 %multiply_convert_fusion = (bf16[640,1408]{1,0:T(8,128)(2,1)}, bf16[640,1408]{1,0:T(8,128)(2,1)}, bf16[640,1408]{1,0:T(8,128)(2,1)}) fusion(f32[640,1408]{1,0:T(8,128)S(1)} %fusion.87, f32[640,1408]{1,0:T(8,128)} %fusion.88, bf16[640,2048]{1,0:T(8,128)(2,1)S(1)} %copy-done.58, bf16[1408,2048]{1,0:T(8,128)(2,1)} %param.35), kind=kOutput, calls=%fused_computation.16 | convolution fusion | flops 3704504320 | bytes 21004288 | tf_op jit(solution)/shard_map/dot_general | solution.py:26
  253.6 7.8 fusion.89
  261.5 7.7 constant_dynamic-slice_fusion
  269.2 6.1 copy.100
  275.8 7.1 fusion.93
  282.9 8.1 %add_convert_fusion.4.refs_0_ = bf16[640,2048]{1,0:T(8,128)(2,1)S(1)} fusion(f32[640,2048]{1,0:T(8,128)} %fusion.89, bf16[640,1408]{1,0:T(8,128)(2,1)S(1)} %copy-done.69, bf16[2048,1408]{1,0:T(8,128)(2,1)} %param.34), kind=kOutput, calls=%fused_computation.14 | convolution fusion | flops 3693608960 | bytes 15433728 | tf_op jit(solution)/shard_map/dot_general | solution.py:26
  291.0 104.1 %line_back.2 = (bf16[640,2048]{1,0:T(8,128)(2,1)}, f32[320,2048]{1,0:T(8,128)S(1)}, f32[8,2048]{1,0:T(8,128)S(1)}) custom-call(bf16[640,2048]{1,0:T(8,128)(2,1)S(1)} %add_convert_fusion.4.refs_0_, f32[320,2048]{1,0:T(8,128)S(1)} %copy-done.3, bf16[320,2048]{1,0:T(8,128)(2,1)S(1)} %copy-done.6, f32[1,2048]{1,0:T(1,128)S(1)} %bitcast.130), custom_call_target="tpu_custom_call" | custom-call | flops 10000000 | bytes 200000000 | tf_op jit(solution)/shard_map/line_back/pallas_call | solution.py:468
  395.3 6.3 multiply_reduce_fusion
  408.1 4.5 fusion.10
  416.5 3.7 all-to-all-start.2
  422.2 6.7 fusion.95
  435.5 4.2 all-to-all-start.7
  447.7 20.6 %recur_backward.1 = (bf16[1024,1152]{1,0:T(8,128)(2,1)S(1)}, f32[256,128]{1,0:T(8,128)S(1)}, f32[8,256]{1,0:T(8,128)S(1)}) custom-call(s32[1,1024]{1,0:T(1,128)S(1)} %bitcast.133, s32[1024,1]{1,0:T(8,128)S(1)} %copy-done.17, s32[1,3]{1,0:T(1,128)S(1)} %copy-done.25, bf16[128,256]{1,0:T(8,128)(2,1)S(1)} %copy-done.24, f32[1,256]{1,0:T(1,128)S(1)} %bitcast.135, ...), custom_call_target="tpu_custom_call" | custom-call | flops 12000000000 | bytes 12000000 | tf_op jit(solution)/shard_map/recur_backward/pallas_call | solution.py:241
  469.7 4.8 all-to-all-start.3
  474.5 5.8 fusion.90
  480.3 4.2 fusion.92
  488.0 6.1 add_convert_fusion
  494.0 9.9 %all-to-all-done.3 = bf16[8,128,1152]{2,1,0:T(8,128)(2,1)} async-done(((bf16[8,128,1152]{2,1,0:T(8,128)(2,1)}), bf16[8,128,1152]{2,1,0:T(8,128)(2,1)}, u32[]{:S(2)}, u32[]{:S(2)}) %all-to-all-start.3) | async-done | bytes 2359328 | tf_op jit(solution)/shard_map/all_to_all | solution.py:652
  503.9 4.8 all-to-all-start.11
  508.8 9.4 %fusion.3 = bf16[640,2048]{1,0:T(8,128)(2,1)} fusion(f32[320,2048]{1,0:T(8,128)} %get-tuple-element.117, f32[320,2048]{1,0:T(8,128)} %get-tuple-element.116, bf16[640,1408]{1,0:T(8,128)(2,1)S(1)} %copy-done.50, bf16[1408,2048]{1,0:T(8,128)(2,1)} %param.35), kind=kOutput, calls=%fused_computation.12 | convolution fusion | flops 3694919680 | bytes 15433728 | tf_op jit(solution)/shard_map/dot_general | solution.py:30
  518.2 6.9 fusion.94
  530.3 4.5 fusion.8
  534.7 3.6 convolution_convert_fusion.2
  541.3 4.4 all-to-all-start.8
  545.8 7.8 add_convert_fusion.1
  566.3 4.1 all-to-all-done.5
  570.5 4.1 all-to-all-start.4
  574.6 7.8 add_convert_fusion.2
  582.4 4.6 all-to-all-start.10
  587.1 3.9 fusion.52
  596.7 4.1 add_convert_fusion.3.refs_0_
  600.7 19.4 %all-to-all-done.10 = bf16[4,256,1408]{2,1,0:T(8,128)(2,1)} async-done(((bf16[4,256,1408]{2,1,0:T(8,128)(2,1)}), bf16[4,256,1408]{2,1,0:T(8,128)(2,1)}, u32[]{:S(2)}, u32[]{:S(2)}) %all-to-all-start.10) | async-done | bytes 2883616 | tf_op jit(solution)/shard_map/all_to_all | solution.py:773
  620.1 4.7 all-to-all-start.9
  630.0 105.9 %line_back.3 = (bf16[640,2048]{1,0:T(8,128)(2,1)S(1)}, f32[320,2048]{1,0:T(8,128)}, f32[8,2048]{1,0:T(8,128)S(1)}) custom-call(bf16[640,2048]{1,0:T(8,128)(2,1)S(1)} %copy-done.5, bf16[320,2048]{1,0:T(8,128)(2,1)S(1)} %constant_dynamic-slice_fusion.6.refs_1_.refs_2_, f32[320,2048]{1,0:T(8,128)S(1)} %copy-done.8, f32[1,2048]{1,0:T(1,128)S(1)} %bitcast.128), custom_call_target="tpu_custom_call" | custom-call | flops 10000000 | bytes 200000000 | tf_op jit(solution)/shard_map/line_back/pallas_call | solution.py:468
  742.4 12.7 %small_sum.1 = f32[48,128]{1,0:T(8,128)} custom-call(f32[8,48,128]{2,1,0:T(8,128)} %pad_maximum_fusion.part_ref), custom_call_target="tpu_custom_call" | custom-call | tf_op jit(solution)/shard_map/small_sum/pallas_call | solution.py:572
  769.8 3.8 all-to-all-start.6
  787.6 3.7 copy.112
  (298 shorter events, 145.9 us)
Async XLA Ops:
  7.2 103.9 %copy-start = (bf16[512,2048]{1,0:T(8,128)(2,1)S(1)}, bf16[512,2048]{1,0:T(8,128)(2,1)}, u32[]{:S(2)}) copy-start(bf16[512,2048]{1,0:T(8,128)(2,1)} %param.31) | copy-start | bytes 6291460
  10.6 13.6 %copy-start.63 = (s32[640]{0:T(1024)}, s32[640]{0:T(1024)S(1)}, u32[]{:S(2)}) copy-start(s32[640]{0:T(1024)S(1)} %multiply_add_fusion.1) | copy-start | bytes 7684
  27.8 35.0 %all-to-all-start = ((bf16[8,128,1152]{2,1,0:T(8,128)(2,1)}), bf16[8,128,1152]{2,1,0:T(8,128)(2,1)}, u32[]{:S(2)}, u32[]{:S(2)}) async-start(bf16[8,128,1152]{2,1,0:T(8,128)(2,1)} %bitcast.152), calls=%async_computation | async-start | bytes 4718592 | tf_op jit(solution)/shard_map/all_to_all | solution.py:652
  36.2 26.5 %copy-start.25 = (s32[1,3]{1,0:T(1,128)S(1)}, s32[1,3]{1,0:T(1,128)}, u32[]{:S(2)}) copy-start(s32[1,3]{1,0:T(1,128)} %lengths_ref.3) | copy-start | bytes 40
  37.7 55.0 %collective-permute-start = (bf16[640,4,256]{2,0,1:T(8,128)(2,1)}, bf16[640,4,256]{2,0,1:T(8,128)(2,1)}, u32[]{:S(2)}, u32[]{:S(2)}) collective-permute-start(bf16[640,4,256]{2,0,1:T(8,128)(2,1)} %bitcast.157), channel_id=1, source_target_pairs={{0,4},{4,0},{8,12},{12,8},{16,20},{20,16},{24,28},{28,24},{1,5},{5... | collective-permute-start | bytes 3932168 | tf_op jit(solution)/shard_map/ppermute | solution.py:762
  41.4 21.3 %copy-start.65 = (bf16[128]{0:T(256)(128)(2,1)}, bf16[128]{0:T(256)(128)(2,1)S(1)}, u32[]{:S(2)}) copy-start(bf16[128]{0:T(256)(128)(2,1)S(1)} %pad.29.clone) | copy-start | bytes 772
  43.7 37.0 %copy-start.23 = (bf16[128,256]{1,0:T(8,128)(2,1)}, bf16[128,256]{1,0:T(8,128)(2,1)S(1)}, u32[]{:S(2)}) copy-start(bf16[128,256]{1,0:T(8,128)(2,1)S(1)} %copy.83.up_ref) | copy-start | bytes 196612
  44.4 36.3 %copy-start.26 = (f32[256]{0:T(256)}, f32[256]{0:T(256)S(1)}, u32[]{:S(2)}) copy-start(f32[256]{0:T(256)S(1)} %reshape.298) | copy-start | bytes 3076
  83.5 19.8 %all-to-all-start.1 = ((bf16[8,128,512]{2,1,0:T(8,128)(2,1)}), bf16[8,128,512]{2,1,0:T(8,128)(2,1)}, u32[]{:S(2)}, u32[]{:S(2)}) async-start(bf16[8,128,512]{2,1,0:T(8,128)(2,1)} %bitcast.6), calls=%async_computation.1 | async-start | bytes 2097152 | tf_op jit(solution)/shard_map/all_to_all | solution.py:652
  87.9 399.6 %collective-permute-start.11 = (bf16[640,2048]{1,0:T(8,128)(2,1)}, bf16[640,2048]{1,0:T(8,128)(2,1)}, u32[]{:S(2)}, u32[]{:S(2)}) collective-permute-start(bf16[640,2048]{1,0:T(8,128)(2,1)} %param.19), channel_id=1, source_target_pairs={{0,4},{4,0},{8,12},{12,8},{16,20},{20,16},{24,28},{28,24},{1,5},{5... | collective-permute-start | bytes 7864328 | tf_op jit(solution)/shard_map/ppermute | solution.py:767
  91.4 11.9 %copy-start.64 = (s32[640]{0:T(1024)S(1)}, s32[640]{0:T(1024)}, u32[]{:S(2)}) copy-start(s32[640]{0:T(1024)} %copy-done.63) | copy-start | bytes 7684
  226.4 7.9 copy-start.12
  234.3 8.9 %copy-start.58 = (bf16[640,2048]{1,0:T(8,128)(2,1)S(1)}, bf16[640,2048]{1,0:T(8,128)(2,1)}, u32[]{:S(2)}) copy-start(bf16[640,2048]{1,0:T(8,128)(2,1)} %param.19) | copy-start | bytes 7864324
  234.4 19.2 %slice-start.2 = ((s8[5767168]{0:T(1024)(128)(4,1)}), s8[4194304]{0:T(1024)(128)(4,1)S(1)}, s32[]{:S(2)}) async-start(s8[5767168]{0:T(1024)(128)(4,1)} %bitcast.165), calls=%async_computation.15 | async-start | bytes 8388608
  243.2 10.4 %slice-start.3 = ((s8[5767168]{0:T(1024)(128)(4,1)}), s8[1572864]{0:T(1024)(128)(4,1)S(1)}, s32[]{:S(2)}) async-start(s8[5767168]{0:T(1024)(128)(4,1)} %bitcast.165), calls=%async_computation.16 | async-start | bytes 3145728
  253.6 321.0 %collective-permute-start.8 = (bf16[640,1408]{1,0:T(8,128)(2,1)}, bf16[640,1408]{1,0:T(8,128)(2,1)}, u32[]{:S(2)}, u32[]{:S(2)}) collective-permute-start(bf16[640,1408]{1,0:T(8,128)(2,1)} %get-tuple-element.109), channel_id=1, source_target_pairs={{0,4},{4,0},{8,12},{12,8},{16,20},{20,16},{24,28},{28,24},{1,5},{5... | collective-permute-start | bytes 5406728 | tf_op jit(solution)/shard_map/ppermute | solution.py:767
  253.6 7.9 copy-start.39
  275.3 270.5 %collective-permute-start.9 = (bf16[640,1408]{1,0:T(8,128)(2,1)}, bf16[640,1408]{1,0:T(8,128)(2,1)}, u32[]{:S(2)}, u32[]{:S(2)}) collective-permute-start(bf16[640,1408]{1,0:T(8,128)(2,1)} %get-tuple-element.108), channel_id=1, source_target_pairs={{0,4},{4,0},{8,12},{12,8},{16,20},{20,16},{24,28},{28,24},{1,5},{5... | collective-permute-start | bytes 5406728 | tf_op jit(solution)/shard_map/ppermute | solution.py:767
  282.9 8.1 %copy-start.3 = (f32[320,2048]{1,0:T(8,128)S(1)}, f32[320,2048]{1,0:T(8,128)}, u32[]{:S(2)}) copy-start(f32[320,2048]{1,0:T(8,128)} %copy-done.2) | copy-start | bytes 7864324
  282.9 8.1 %copy-start.6 = (bf16[320,2048]{1,0:T(8,128)(2,1)S(1)}, bf16[320,2048]{1,0:T(8,128)(2,1)}, u32[]{:S(2)}) copy-start(bf16[320,2048]{1,0:T(8,128)(2,1)} %constant_dynamic-slice_fusion.5.refs_2_) | copy-start | bytes 3932164
  291.0 104.2 %copy-start.71 = (f32[640,512]{0,1:T(8,128)S(1)}, f32[640,512]{0,1:T(8,128)}, u32[]{:S(2)}) copy-start(f32[640,512]{0,1:T(8,128)} %copy-done.70) | copy-start | bytes 3932164
  291.0 104.2 %copy-start.72 = (f32[640,512]{0,1:T(8,128)S(1)}, f32[640,512]{0,1:T(8,128)}, u32[]{:S(2)}) copy-start(f32[640,512]{0,1:T(8,128)} %get-tuple-element.135) | copy-start | bytes 3932164
  395.2 135.1 %collective-permute-start.6 = (bf16[640,2048]{1,0:T(8,128)(2,1)}, bf16[640,2048]{1,0:T(8,128)(2,1)}, u32[]{:S(2)}, u32[]{:S(2)}) collective-permute-start(bf16[640,2048]{1,0:T(8,128)(2,1)} %get-tuple-element.32), channel_id=1, source_target_pairs={{0,4},{4,0},{8,12},{12,8},{16,20},{20,16},{24,28},{28,24},{1,5},{5... | collective-permute-start | bytes 7864328 | tf_op jit(solution)/shard_map/ppermute | solution.py:767
  401.6 27.3 %collective-permute-start.4 = (bf16[640,512]{0,1:T(8,128)(2,1)}, bf16[640,512]{0,1:T(8,128)(2,1)}, u32[]{:S(2)}, u32[]{:S(2)}) collective-permute-start(bf16[640,512]{0,1:T(8,128)(2,1)} %get-tuple-element.111), channel_id=1, source_target_pairs={{0,4},{4,0},{8,12},{12,8},{16,20},{20,16},{24,28},{28,24},{1,5},{5... | collective-permute-start | bytes 1966088 | tf_op jit(solution)/shard_map/ppermute | solution.py:767
  416.5 19.0 %all-to-all-start.2 = ((bf16[8,128,512]{2,1,0:T(8,128)(2,1)}), bf16[8,128,512]{2,1,0:T(8,128)(2,1)S(1)}, u32[]{:S(2)}, u32[]{:S(2)}) async-start(bf16[8,128,512]{2,1,0:T(8,128)(2,1)} %bitcast.9), calls=%async_computation.2 | async-start | bytes 2097152 | tf_op jit(solution)/shard_map/all_to_all | solution.py:652
  422.2 7.2 copy-start.44
  428.9 59.0 %collective-permute-start.10 = (bf16[640,4,176]{0,2,1:T(8,128)(2,1)}, bf16[640,4,176]{0,2,1:T(8,128)(2,1)}, u32[]{:S(2)}, u32[]{:S(2)}) collective-permute-start(bf16[640,4,176]{0,2,1:T(8,128)(2,1)} %get-tuple-element.118), channel_id=1, source_target_pairs={{0,4},{4,0},{8,12},{12,8},{16,20},{20,16},{24,28},{28,24},{1,5},{5... | collective-permute-start | bytes 2703368 | tf_op jit(solution)/shard_map/ppermute | solution.py:762
  435.5 34.1 %all-to-all-start.7 = ((bf16[4,256,512]{2,1,0:T(8,128)(2,1)}), bf16[4,256,512]{2,1,0:T(8,128)(2,1)}, u32[]{:S(2)}, u32[]{:S(2)}) async-start(bf16[4,256,512]{2,1,0:T(8,128)(2,1)} %bitcast.22), calls=%async_computation.7 | async-start | bytes 2097152 | tf_op jit(solution)/shard_map/all_to_all | solution.py:773
  469.7 34.3 %all-to-all-start.3 = ((bf16[8,128,1152]{2,1,0:T(8,128)(2,1)}), bf16[8,128,1152]{2,1,0:T(8,128)(2,1)}, u32[]{:S(2)}, u32[]{:S(2)}) async-start(bf16[8,128,1152]{2,1,0:T(8,128)(2,1)} %bitcast.126), calls=%async_computation.3 | async-start | bytes 4718592 | tf_op jit(solution)/shard_map/all_to_all | solution.py:652
  474.5 13.5 %slice-start.4 = ((s8[5767168]{0:T(1024)(128)(4,1)}), s8[4194304]{0:T(1024)(128)(4,1)S(1)}, s32[]{:S(2)}) async-start(s8[5767168]{0:T(1024)(128)(4,1)} %bitcast.167), calls=%async_computation.17 | async-start | bytes 8388608
  480.3 7.7 slice-start.5
  487.5 38.2 %collective-permute-start.7 = (bf16[640,4,256]{2,0,1:T(8,128)(2,1)}, bf16[640,4,256]{2,0,1:T(8,128)(2,1)}, u32[]{:S(2)}, u32[]{:S(2)}) collective-permute-start(bf16[640,4,256]{2,0,1:T(8,128)(2,1)} %bitcast.123), channel_id=1, source_target_pairs={{0,4},{4,0},{8,12},{12,8},{16,20},{20,16},{24,28},{28,24},{1,5},{5... | collective-permute-start | bytes 3932168 | tf_op jit(solution)/shard_map/ppermute | solution.py:762
  487.9 42.4 %collective-permute-start.5 = (bf16[640,4,64]{0,2,1:T(8,128)(2,1)}, bf16[640,4,64]{0,2,1:T(8,128)(2,1)}, u32[]{:S(2)}, u32[]{:S(2)}) collective-permute-start(bf16[640,4,64]{0,2,1:T(8,128)(2,1)} %get-tuple-element.122), channel_id=1, source_target_pairs={{0,4},{4,0},{8,12},{12,8},{16,20},{20,16},{24,28},{28,24},{1,5},{5... | collective-permute-start | bytes 983048 | tf_op jit(solution)/shard_map/ppermute | solution.py:762
  503.9 37.4 %all-to-all-start.11 = ((bf16[4,176,2048]{2,1,0:T(8,128)(2,1)}), bf16[4,176,2048]{2,1,0:T(8,128)(2,1)}, u32[]{:S(2)}, u32[]{:S(2)}) async-start(bf16[4,176,2048]{2,1,0:T(8,128)(2,1)} %bitcast.150), calls=%async_computation.11 | async-start | bytes 5767168 | tf_op jit(solution)/shard_map/all_to_all | solution.py:773
  508.7 278.9 %all-reduce.6.cloned.1.call-start = ((), (), s32[]{:S(2)}) async-start(), calls=%async_computation.12 | async-start | bytes 5242880 | tf_op jit(solution)/shard_map/psum | solution.py:756
  538.4 7.4 copy-start.41
  539.2 16.1 %collective-permute-start.2 = (bf16[640,256]{1,0:T(8,128)(2,1)S(1)}, bf16[640,256]{1,0:T(8,128)(2,1)}, u32[]{:S(2)}, u32[]{:S(2)}) collective-permute-start(bf16[640,256]{1,0:T(8,128)(2,1)S(1)} %get-tuple-element.120), channel_id=1, source_target_pairs={{0,4},{4,0},{8,12},{12,8},{16,20},{20,16},{24,28},{28,24},{1,5},{5... | collective-permute-start | bytes 983048 | tf_op jit(solution)/shard_map/ppermute | solution.py:767
  541.3 17.2 %all-to-all-start.8 = ((bf16[4,64,2048]{2,1,0:T(8,128)(2,1)}), bf16[4,64,2048]{2,1,0:T(8,128)(2,1)}, u32[]{:S(2)}, u32[]{:S(2)}) async-start(bf16[4,64,2048]{2,1,0:T(8,128)(2,1)} %bitcast.148), calls=%async_computation.8 | async-start | bytes 2097152 | tf_op jit(solution)/shard_map/all_to_all | solution.py:773
  545.8 7.9 copy-start.35
  553.7 10.3 %collective-permute-start.1 = (bf16[640,256]{1,0:T(8,128)(2,1)}, bf16[640,256]{1,0:T(8,128)(2,1)}, u32[]{:S(2)}, u32[]{:S(2)}) collective-permute-start(bf16[640,256]{1,0:T(8,128)(2,1)} %get-tuple-element.121), channel_id=1, source_target_pairs={{0,4},{4,0},{8,12},{12,8},{16,20},{20,16},{24,28},{28,24},{1,5},{5... | collective-permute-start | bytes 983048 | tf_op jit(solution)/shard_map/ppermute | solution.py:767
  558.5 11.9 %all-to-all-start.5 = ((bf16[4,256,256]{2,1,0:T(8,128)(2,1)}), bf16[4,256,256]{2,1,0:T(8,128)(2,1)S(1)}, u32[]{:S(2)}, u32[]{:S(2)}) async-start(bf16[4,256,256]{2,1,0:T(8,128)(2,1)} %bitcast.20), calls=%async_computation.5 | async-start | bytes 1048576 | tf_op jit(solution)/shard_map/all_to_all | solution.py:773
  570.5 12.0 %copy-start.45 = (bf16[4,256,256]{2,1,0:T(8,128)(2,1)}, bf16[4,256,256]{2,1,0:T(8,128)(2,1)S(1)}, u32[]{:S(2)}) copy-start(bf16[4,256,256]{2,1,0:T(8,128)(2,1)S(1)} %all-to-all-done.5) | copy-start | bytes 1572868
  570.5 12.0 %all-to-all-start.4 = ((bf16[4,256,256]{2,1,0:T(8,128)(2,1)}), bf16[4,256,256]{2,1,0:T(8,128)(2,1)}, u32[]{:S(2)}, u32[]{:S(2)}) async-start(bf16[4,256,256]{2,1,0:T(8,128)(2,1)} %bitcast.19), calls=%async_computation.4 | async-start | bytes 1048576 | tf_op jit(solution)/shard_map/all_to_all | solution.py:773
  582.4 37.7 %all-to-all-start.10 = ((bf16[4,256,1408]{2,1,0:T(8,128)(2,1)}), bf16[4,256,1408]{2,1,0:T(8,128)(2,1)}, u32[]{:S(2)}, u32[]{:S(2)}) async-start(bf16[4,256,1408]{2,1,0:T(8,128)(2,1)} %bitcast.151), calls=%async_computation.10 | async-start | bytes 5767168 | tf_op jit(solution)/shard_map/all_to_all | solution.py:773
  591.9 174.9 %collective-permute-start.3 = (bf16[640,512]{1,0:T(8,128)(2,1)}, bf16[640,512]{1,0:T(8,128)(2,1)}, u32[]{:S(2)}, u32[]{:S(2)}) collective-permute-start(bf16[640,512]{1,0:T(8,128)(2,1)} %slice.112), channel_id=1, source_target_pairs={{0,4},{4,0},{8,12},{12,8},{16,20},{20,16},{24,28},{28,24},{1,5},{5... | collective-permute-start | bytes 1966088 | tf_op jit(solution)/shard_map/ppermute | solution.py:767
  620.1 149.7 %all-to-all-start.9 = ((bf16[4,256,1408]{2,1,0:T(8,128)(2,1)}), bf16[4,256,1408]{2,1,0:T(8,128)(2,1)}, u32[]{:S(2)}, u32[]{:S(2)}) async-start(bf16[4,256,1408]{2,1,0:T(8,128)(2,1)} %bitcast.149), calls=%async_computation.9 | async-start | bytes 5767168 | tf_op jit(solution)/shard_map/all_to_all | solution.py:773
  737.4 23.8 %copy-start.36 = (bf16[640,4,1,256]{0,3,2,1:T(8,128)(2,1)S(1)}, bf16[640,4,1,256]{0,3,2,1:T(8,128)(2,1)}, u32[]{:S(2)}) copy-start(bf16[640,4,1,256]{0,3,2,1:T(8,128)(2,1)} %get-tuple-element.115) | copy-start | bytes 3932164
  769.8 16.9 %all-to-all-start.6 = ((bf16[4,256,512]{2,1,0:T(8,128)(2,1)}), bf16[4,256,512]{2,1,0:T(8,128)(2,1)S(1)}, u32[]{:S(2)}, u32[]{:S(2)}) async-start(bf16[4,256,512]{2,1,0:T(8,128)(2,1)} %bitcast.21), calls=%async_computation.6 | async-start | bytes 2097152 | tf_op jit(solution)/shard_map/all_to_all | solution.py:773
  (56 other events, 178.3 us)
Sparse Core Ops, SparseCore 0:
  525.4 106.1 all-reduce.5

commit v3 on v2

--- a/solution.py
+++ b/solution.py
@@ -270,7 +270,7 @@
     )
 
 
-CHUNK = 16
+CHUNK = 32
 
 
 def line_kernel(mode, n, *refs):
@@ -485,6 +485,483 @@
         ),
         name="line_" + mode,
     )(share, x_own, base_own, gain)
+
+
+FINE = 16
+SKEW = 2
+
+
+def partner_of(index):
+    return index + 1 - 2 * lax.rem(index, 2)
+
+
+class GradPlan:
+    def __init__(self, groups, count, width, row_widths, row_tiles, col_rows):
+        self.groups, self.count, self.width = groups, count, width
+        self.team = groups // 2
+        self.block = width // groups
+        self.half = width // 2
+        self.row_widths, self.row_tiles, self.col_rows = row_widths, row_tiles, col_rows
+        self.offsets = []
+        total = 0
+        for wide in row_widths:
+            self.offsets.append(total)
+            total += wide
+        self.total = total
+        self.col_tile = 256
+        self.col_steps = self.half // self.col_tile
+
+
+def sum_grads_kernel(n, plan, *refs):
+    refs = list(refs)
+
+    def take(k):
+        out = refs[:k]
+        del refs[:k]
+        return out
+
+    rows, cols = len(plan.row_widths), len(plan.col_rows)
+    share_ref, x_ref, base_ref, gain_ref, left_ref = take(5)
+    right_refs = take(rows)
+    col_lefts = take(cols)
+    col_rights = take(cols)
+    out_ref, kept_ref, gain_grad_ref = take(3)
+    row_outs = take(rows)
+    col_outs = take(cols)
+    up_in, down_in, left_in = take(3)
+    right_in = take(rows)
+    col_left_in = take(cols)
+    col_right_in = take(cols)
+    row_send, row_recv = take(2)
+    col_send = take(cols)
+    col_recv = take(cols)
+    sems, left_sems, right_sems, row_sems = take(4)
+    if cols:
+        pair_sems, col_sems = take(2)
+
+    me = lax.axis_index("tensor")
+    member = lax.axis_index("dp")
+    parity = lax.rem(member, 2)
+    mine = member // 2
+    partner = partner_of(member)
+    groups, team, block = plan.groups, plan.team, plan.block
+    half = up_in.shape[0]
+    count = half // FINE
+    inside = (me > 0) & (me < n - 1)
+
+    barrier = pltpu.get_barrier_semaphore()
+
+    @pl.when(me > 0)
+    def _():
+        pl.semaphore_signal(barrier, inc=1, device_id={"tensor": me - 1}, device_id_type=MESH)
+
+    @pl.when(me < n - 1)
+    def _():
+        pl.semaphore_signal(barrier, inc=1, device_id={"tensor": me + 1}, device_id_type=MESH)
+
+    if cols:
+        greeted = groups - 1
+
+        @pl.loop(1, groups)
+        def _(k):
+            pl.semaphore_signal(
+                barrier, inc=1, device_id={"dp": lax.rem(member + k, groups)}, device_id_type=MESH
+            )
+    else:
+        greeted = team
+        pl.semaphore_signal(barrier, inc=1, device_id={"dp": partner}, device_id_type=MESH)
+
+        @pl.loop(1, team)
+        def _(k):
+            pl.semaphore_signal(
+                barrier, inc=1, device_id={"dp": 2 * lax.rem(mine + k, team) + parity},
+                device_id_type=MESH,
+            )
+
+    @pl.when(inside)
+    def _():
+        pl.semaphore_wait(barrier, greeted + 2)
+
+    @pl.when(jnp.logical_not(inside))
+    def _():
+        pl.semaphore_wait(barrier, greeted + 1)
+
+    def at(g):
+        return pl.ds(pl.multiple_of(g * FINE, FINE), FINE)
+
+    def low(g):
+        return pl.ds(pl.multiple_of(half + g * FINE, FINE), FINE)
+
+    def right(source, target, lane, g):
+        return pltpu.make_async_remote_copy(
+            source, target, sems.at[2 * lane, g], sems.at[2 * lane + 1, g],
+            device_id={"tensor": jnp.minimum(me + 1, n - 1)}, device_id_type=MESH,
+        )
+
+    def left(source, target, lane, g):
+        return pltpu.make_async_remote_copy(
+            source, target, sems.at[2 * lane, g], sems.at[2 * lane + 1, g],
+            device_id={"tensor": jnp.maximum(me - 1, 0)}, device_id_type=MESH,
+        )
+
+    def up_copy(g):
+        return right(up_in.at[at(g), :], up_in.at[at(g), :], 0, g)
+
+    def down_copy(g):
+        return left(down_in.at[at(g), :], down_in.at[at(g), :], 1, g)
+
+    def first_up_copy(g):
+        return right(share_ref.at[at(g), :], up_in.at[at(g), :], 0, g)
+
+    def first_down_copy(g):
+        return left(share_ref.at[low(g), :], down_in.at[at(g), :], 1, g)
+
+    def up_back_copy(g):
+        return left(out_ref.at[at(g), :], out_ref.at[at(g), :], 2, g)
+
+    def down_back_copy(g):
+        return right(out_ref.at[low(g), :], out_ref.at[low(g), :], 3, g)
+
+    def to_partner(source, target, send, recv):
+        return pltpu.make_async_remote_copy(
+            source, target, send, recv, device_id={"dp": partner}, device_id_type=MESH
+        )
+
+    def columns(j):
+        return pl.ds(pl.multiple_of(j * block, block), block)
+
+    def left_copy(q):
+        return to_partner(
+            left_ref.at[:, columns(2 * q + 1 - parity)], left_in.at[:, columns(q)],
+            left_sems.at[0, q], left_sems.at[1, q],
+        )
+
+    def right_copy(i):
+        return to_partner(
+            right_refs[i].at[:, : plan.row_widths[i]], right_in[i],
+            right_sems.at[0, i], right_sems.at[1, i],
+        )
+
+    half_of = pl.ds(pl.multiple_of(parity * plan.half, plan.half), plan.half)
+    other_half = pl.ds(pl.multiple_of((1 - parity) * plan.half, plan.half), plan.half)
+
+    def pair_copies(i):
+        return (
+            to_partner(
+                col_lefts[i], col_left_in[i], pair_sems.at[0, 2 * i], pair_sems.at[1, 2 * i]
+            ),
+            to_partner(
+                col_rights[i].at[:, other_half], col_right_in[i],
+                pair_sems.at[0, 2 * i + 1], pair_sems.at[1, 2 * i + 1],
+            ),
+        )
+
+    def tile_columns(t):
+        i, start, wide = plan.row_tiles[t]
+        return pl.ds(plan.offsets[i] + start, wide)
+
+    def row_copy(t, to, source):
+        return pltpu.make_async_remote_copy(
+            row_send.at[to, :, tile_columns(t)], row_recv.at[source, :, tile_columns(t)],
+            row_sems.at[0, t, to], row_sems.at[1, t, source],
+            device_id={"dp": 2 * to + parity}, device_id_type=MESH,
+        )
+
+    def col_copy(i, to, source):
+        size = plan.col_rows[i] // groups
+        return pltpu.make_async_remote_copy(
+            col_send[i].at[pl.ds(pl.multiple_of(to * size, 16), size), :],
+            col_recv[i].at[source],
+            col_sems.at[0, i, to], col_sems.at[1, i, source],
+            device_id={"dp": to}, device_id_type=MESH,
+        )
+
+    gain_grad_ref[...] = jnp.zeros_like(gain_grad_ref)
+
+    def finish(total, g, place):
+        rows_x = x_ref[at(g), :].astype(f32)
+        scaling = lax.rsqrt(jnp.mean(rows_x * rows_x, axis=1, keepdims=True) + epsilon)
+        unit = rows_x * scaling
+        gained = gain_ref[...] * total
+        grad = base_ref[at(g), :].astype(f32) + scaling * (
+            gained - unit * jnp.mean(gained * unit, axis=1, keepdims=True)
+        )
+        kept_ref[at(g), :] = grad.astype(kept_ref.dtype)
+        out_ref[place, :] = grad.astype(out_ref.dtype)
+        term = total * unit
+        part = term[0:8, :]
+        for i in range(1, FINE // 8):
+            part = part + term[8 * i : 8 * i + 8, :]
+        gain_grad_ref[...] += part
+
+    @pl.when(me == 0)
+    def _():
+        @pl.loop(0, count)
+        def _(g):
+            first_up_copy(g).start()
+
+    @pl.when(me == n - 1)
+    def _():
+        @pl.loop(0, count)
+        def _(g):
+            first_down_copy(g).start()
+
+    for i in range(cols):
+        for c in pair_copies(i):
+            c.start()
+    for i in range(rows):
+        right_copy(i).start()
+
+    @pl.loop(0, team)
+    def _(q):
+        left_copy(q).start()
+
+    tiles = len(plan.row_tiles)
+    col_items = cols * plan.col_steps
+    items = col_items + team * tiles
+
+    def work(w):
+        for i in range(cols):
+            base = i * plan.col_steps
+
+            @pl.when(w == base)
+            def _():
+                for c in pair_copies(i):
+                    c.wait_recv()
+
+            @pl.when((w >= base) & (w < base + plan.col_steps))
+            def _():
+                offset = pl.multiple_of((w - base) * plan.col_tile, plan.col_tile)
+                own = pl.ds(
+                    pl.multiple_of(parity * plan.half + offset, plan.col_tile), plan.col_tile
+                )
+                there = pl.ds(offset, plan.col_tile)
+                product = rows_dot(col_lefts[i][...], col_rights[i][:, own]) + rows_dot(
+                    col_left_in[i][...], col_right_in[i][:, there]
+                )
+                col_send[i][:, there] = product.astype(bf16)
+
+            @pl.when(w == base + plan.col_steps - 1)
+            def _():
+                @pl.loop(1, groups)
+                def _(k):
+                    col_copy(i, lax.rem(member + k, groups), member).start()
+
+        r = w - col_items
+
+        @pl.when(r == 0)
+        def _():
+            for i in range(rows):
+                right_copy(i).wait_recv()
+
+            @pl.loop(0, team)
+            def _(q):
+                left_copy(q).wait_recv()
+
+        k = r // tiles
+        to = lax.rem(mine + 1 + k, team)
+        for t in range(tiles):
+            i, start, wide = plan.row_tiles[t]
+
+            @pl.when((r >= 0) & (r < team * tiles) & (lax.rem(r, tiles) == t))
+            def _():
+                span = pl.ds(start, wide)
+                product = rows_dot(
+                    left_ref[:, columns(2 * to + parity)], right_refs[i][:, span]
+                ) + rows_dot(left_in[:, columns(to)], right_in[i][:, span])
+                low_product = product.astype(bf16)
+
+                @pl.when(k < team - 1)
+                def _():
+                    row_send[to, :, tile_columns(t)] = low_product
+                    row_copy(t, to, mine).start()
+
+                @pl.when(k == team - 1)
+                def _():
+                    row_recv[mine, :, tile_columns(t)] = low_product
+
+    delay = SKEW * (n - 2)
+    second = count + 2
+    start_work = 8
+
+    @pl.loop(0, second + count + delay)
+    def _(step):
+        g_up = step - SKEW * (me - 1)
+
+        @pl.when((me > 0) & (g_up >= 0) & (g_up < count))
+        def _():
+            up_copy(g_up).wait_recv()
+            total = up_in[at(g_up), :].astype(f32) + share_ref[at(g_up), :].astype(f32)
+
+            @pl.when(me < n - 1)
+            def _():
+                up_in[at(g_up), :] = total.astype(bf16)
+                up_copy(g_up).start()
+
+            @pl.when(me == n - 1)
+            def _():
+                finish(total, g_up, at(g_up))
+                up_back_copy(g_up).start()
+
+        g_down = step - SKEW * (n - 2 - me)
+
+        @pl.when((me < n - 1) & (g_down >= 0) & (g_down < count))
+        def _():
+            down_copy(g_down).wait_recv()
+            total = down_in[at(g_down), :].astype(f32) + share_ref[low(g_down), :].astype(f32)
+
+            @pl.when(me > 0)
+            def _():
+                down_in[at(g_down), :] = total.astype(bf16)
+                down_copy(g_down).start()
+
+            @pl.when(me == 0)
+            def _():
+                finish(total, g_down, low(g_down))
+                down_back_copy(g_down).start()
+
+        work(step - start_work)
+
+        g_up_back = step - second - SKEW * (n - 2 - me)
+
+        @pl.when((me < n - 1) & (g_up_back >= 0) & (g_up_back < count))
+        def _():
+            up_back_copy(g_up_back).wait_recv()
+
+            @pl.when(me > 0)
+            def _():
+                up_back_copy(g_up_back).start()
+
+        g_down_back = step - second - SKEW * (me - 1)
+
+        @pl.when((me > 0) & (g_down_back >= 0) & (g_down_back < count))
+        def _():
+            down_back_copy(g_down_back).wait_recv()
+
+            @pl.when(me < n - 1)
+            def _():
+                down_back_copy(g_down_back).start()
+
+    for i in range(cols):
+        size = plan.col_rows[i] // groups
+        own_rows = pl.ds(pl.multiple_of(member * size, 16), size)
+        col_recv[i][pl.ds(member, 1)] = col_send[i][own_rows, :][None]
+
+        @pl.loop(1, groups)
+        def _(k):
+            col_copy(i, 0, lax.rem(member + k, groups)).wait_recv()
+
+        for b in range(2):
+            total = col_recv[i][b].astype(f32)
+            for q in range(1, team):
+                total = total + col_recv[i][2 * q + b].astype(f32)
+            col_outs[i][:, b * plan.half : (b + 1) * plan.half] = total
+    for t in range(tiles):
+        @pl.loop(1, team)
+        def _(k):
+            row_copy(t, 0, lax.rem(mine + k, team)).wait_recv()
+    for i in range(rows):
+        span = pl.ds(plan.offsets[i], plan.row_widths[i])
+        total = row_recv[0, :, span].astype(f32)
+        for q in range(1, team):
+            total = total + row_recv[q, :, span].astype(f32)
+        row_outs[i][...] = total
+
+    @pl.loop(0, count)
+    def _(g):
+        @pl.when(me < n - 1)
+        def _():
+            up_copy(g).wait_send()
+            down_back_copy(g).wait_send()
+
+        @pl.when(me > 0)
+        def _():
+            down_copy(g).wait_send()
+            up_back_copy(g).wait_send()
+
+    for i in range(cols):
+        for c in pair_copies(i):
+            c.wait_send()
+
+        @pl.loop(1, groups)
+        def _(k):
+            col_copy(i, lax.rem(member + k, groups), member).wait_send()
+    for i in range(rows):
+        right_copy(i).wait_send()
+
+    @pl.loop(0, team)
+    def _(q):
+        left_copy(q).wait_send()
+
+    for t in range(tiles):
+        @pl.loop(1, team)
+        def _(k):
+            row_copy(t, lax.rem(mine + k, team), mine).wait_send()
+
+
+def tiles_of(widths, most):
+    return [
+        (i, start, min(most, wide - start))
+        for i, wide in enumerate(widths)
+        for start in range(0, wide, most)
+    ]
+
+
+def sum_grads(
+    name, call, n, groups, share, x_own, base_own, gain, kept_type, row_left, row_rights, row_widths,
+    row_tiles, col_pairs,
+):
+    count, width = share.shape
+    half = count // 2
+    col_rows = [pair[0].shape[1] for pair in col_pairs]
+    plan = GradPlan(groups, count, width, row_widths, row_tiles, col_rows)
+    team = plan.team
+    vmem = pl.BlockSpec(memory_space=pltpu.VMEM)
+    outs = [
+        jax.ShapeDtypeStruct((count, width), bf16),
+        jax.ShapeDtypeStruct((half, width), kept_type),
+        jax.ShapeDtypeStruct((8, width), f32),
+    ]
+    outs += [jax.ShapeDtypeStruct((plan.block, wide), f32) for wide in row_widths]
+    outs += [jax.ShapeDtypeStruct((r // groups, width), f32) for r in col_rows]
+    scratch = [
+        pltpu.VMEM((half, width), bf16),
+        pltpu.VMEM((half, width), bf16),
+        pltpu.VMEM((count, plan.half), bf16),
+    ]
+    scratch += [pltpu.VMEM((count, wide), bf16) for wide in row_widths]
+    scratch += [pltpu.VMEM((count, r), bf16) for r in col_rows]
+    scratch += [pltpu.VMEM((count, plan.half), bf16) for _ in col_rows]
+    scratch += [pltpu.VMEM((team, plan.block, plan.total), bf16)] * 2
+    scratch += [pltpu.VMEM((r, plan.half), bf16) for r in col_rows]
+    scratch += [pltpu.VMEM((groups, r // groups, plan.half), bf16) for r in col_rows]
+    scratch += [
+        pltpu.SemaphoreType.DMA((8, half // FINE)),
+        pltpu.SemaphoreType.DMA((2, team)),
+        pltpu.SemaphoreType.DMA((2, len(row_widths))),
+        pltpu.SemaphoreType.DMA((2, len(row_tiles), team)),
+    ]
+    if col_rows:
+        scratch += [
+            pltpu.SemaphoreType.DMA((2, 2 * len(col_rows))),
+            pltpu.SemaphoreType.DMA((2, len(col_rows), groups)),
+        ]
+    operands = [share, x_own, base_own, gain, row_left, *row_rights]
+    operands += [pair[0] for pair in col_pairs] + [pair[1] for pair in col_pairs]
+    return pl.pallas_call(
+        functools.partial(sum_grads_kernel, n, plan),
+        in_specs=[vmem] * len(operands),
+        out_specs=[vmem] * len(outs),
+        out_shape=outs,
+        scratch_shapes=scratch,
+        compiler_params=pltpu.CompilerParams(
+            collective_id=call, has_side_effects=True, vmem_limit_bytes=60 << 20
+        ),
+        cost_estimate=pl.CostEstimate(
+            flops=12_000_000_000, bytes_accessed=200_000_000, transcendentals=0
+        ),
+        name=name,
+    )(*operands)
 
 
 def small_sum_kernel(groups, n, rows_all, part_ref, out_ref, held, line, line_in, sems, line_sems):
@@ -720,9 +1197,17 @@
     ).astype(bf16)
     d_up_hidden = (d_active * swish_gate).astype(bf16)
     feed_share = (dot_t(d_gate_hidden, feed_gate) + dot_t(d_up_hidden, feed_up)).astype(bf16)
-    d_mixed, d_hidden_own, feed_gain_part = line_sum(
-        "back", 2, lines, feed_share, hidden_own, cotangent_own, feed_gain_wide.reshape(1, -1)
-    )
+    fused = (width // groups) % LANES == 0
+    if fused:
+        d_mixed, d_hidden_own, feed_gain_part, grad_feed_gate, grad_feed_up = sum_grads(
+            "back_feed", 2, lines, groups, feed_share, hidden_own, cotangent_own,
+            feed_gain_wide.reshape(1, -1), f32, feed_normed, [d_gate_hidden, d_up_hidden],
+            [d_gate_hidden.shape[1]] * 2, tiles_of([d_gate_hidden.shape[1]] * 2, 768), [],
+        )
+    else:
+        d_mixed, d_hidden_own, feed_gain_part = line_sum(
+            "back", 2, lines, feed_share, hidden_own, cotangent_own, feed_gain_wide.reshape(1, -1)
+        )
 
     d_gated = dot_t(d_mixed, out_weight)
     d_attended, d_gate_pre, head_gain_part = head_back(d_gated)
@@ -746,9 +1231,23 @@
         + dot_t(d_gate_low, gate_weight)
         + dot_t(d_latent_low, down_both)
     ).astype(bf16)
-    token_grad, _, mixer_gain_part = line_sum(
-        "back", 3, lines, normed_share, tokens_own, d_hidden_own, mixer_gain_wide.reshape(1, -1)
-    )
+    if fused:
+        (
+            token_grad, _, mixer_gain_part, grad_rows, grad_gate, grad_out, grad_feed_down,
+        ) = sum_grads(
+            "back_mixer", 3, lines, groups, normed_share, tokens_own, d_hidden_own,
+            mixer_gain_wide.reshape(1, -1), bf16, normed, [d_rows, d_gate_low],
+            [2 * dk + dv, dv], tiles_of([2 * dk + dv, dv], 512),
+            [(gated, d_mixed), (active, cotangent)],
+        )
+        grad_query = grad_rows[:, :dk]
+        grad_key = grad_rows[:, dk : 2 * dk]
+        grad_value = grad_rows[:, 2 * dk :]
+    else:
+        token_grad, _, mixer_gain_part = line_sum(
+            "back", 3, lines, normed_share, tokens_own, d_hidden_own,
+            mixer_gain_wide.reshape(1, -1),
+        )
     hidden_placed = jnp.concatenate(
         [jnp.where(place == lines - 1, hidden_own, 0.0), jnp.where(place == 0, hidden_own, 0.0)],
         axis=0,
@@ -775,16 +1274,17 @@
         )
         return jnp.sum(moved.astype(f32), axis=0)
 
-    feed_halves = halves(feed_normed, width)
-    normed_halves = halves(normed, width)
-    grad_feed_down = summed_share(halves(active, active.shape[1]), partner(cotangent))
-    grad_feed_gate = summed_share(feed_halves, partner(d_gate_hidden))
-    grad_feed_up = summed_share(feed_halves, partner(d_up_hidden))
-    grad_out = summed_share(halves(gated, dv), partner(d_mixed))
-    grad_query = summed_share(normed_halves, partner(d_query_low))
-    grad_key = summed_share(normed_halves, partner(d_key_low))
-    grad_value = summed_share(normed_halves, partner(d_value_low))
-    grad_gate = summed_share(normed_halves, partner(d_gate_low))
+    if not fused:
+        feed_halves = halves(feed_normed, width)
+        normed_halves = halves(normed, width)
+        grad_feed_down = summed_share(halves(active, active.shape[1]), partner(cotangent))
+        grad_feed_gate = summed_share(feed_halves, partner(d_gate_hidden))
+        grad_feed_up = summed_share(feed_halves, partner(d_up_hidden))
+        grad_out = summed_share(halves(gated, dv), partner(d_mixed))
+        grad_query = summed_share(normed_halves, partner(d_query_low))
+        grad_key = summed_share(normed_halves, partner(d_key_low))
+        grad_value = summed_share(normed_halves, partner(d_value_low))
+        grad_gate = summed_share(normed_halves, partner(d_gate_low))
 
     down_part = rows_dot(normed, d_latent_low)
     down_part = down_part[:, :rank] + down_part[:, third : third + rank]

time: 810 us -> 609 us (0.75)
  matrix products: 173 us -> 92.9 us
  local copies, waits for them, and re-layouts: 89.8 us -> 41.1 us
  starting transfers between devices: 55 us -> 23.2 us
  other arithmetic: 34.4 us -> 11.1 us
  Pallas kernels: 366 us -> 350 us
    pallas_call x3 -> x1, Pallas kernels: 315 us -> 77.9 us  [line_sum(): pl.pallas_call(functools.partial(line_kernel, mode, n), in_specs=[vmem] *...]
    pallas_call x0 -> x2, Pallas kernels: none -> 223 us  [sum_grads(): pl.pallas_call(functools.partial(sum_grads_kernel, n, plan), in_specs=[vm...]
    dot_general x17 -> x1, matrix products: 74.8 us -> 0.63 us  [rows_dot(): lax.dot_general(left, right, (((0,), (0,)), ((), ())), preferred_element_...]
    all_to_all x8 -> x0, starting transfers between devices: 34.2 us -> none  [summed_share(): lax.all_to_all(blocks, 'dp', split_axis=0, concat_axis=0, tiled=True, axi...]
    all_to_all x8 -> x0, waiting for transfers between devices: 27.8 us -> none  [summed_share(): lax.all_to_all(blocks, 'dp', split_axis=0, concat_axis=0, tiled=True, axi...]
    all_to_all x4, waiting for transfers between devices: 39.5 us -> 66.5 us  [exchange(): lax.all_to_all(blocks, 'dp', split_axis=0, concat_axis=0, tiled=True)]
    reduce_sum x8 -> x0, other arithmetic: 18.5 us -> none  [summed_share(): return jnp.sum(moved.astype(f32), axis=0)]
    unnamed x169 -> x143, local copies, waits for them, and re-layouts: 44.8 us -> 26.9 us
  transfers between devices with their start and end apart: 25 -> 5, of which waited for: 9 -> 4; matrix products, arithmetic and copies ran while one was open for 31% -> 7% of each run, Pallas kernels for 46% -> 24%
where the time goes in v3:
time: 609 us; the launch traced here: 600 us
  Pallas kernels  350 us (57%)
  matrix products  92.9 us (15%)
  waiting for transfers between devices  66.5 us (11%)
  local copies, waits for them, and re-layouts  41.1 us (7%)
  starting transfers between devices  23.2 us (4%)
  between operations  15.4 us (3%)
  other arithmetic  11.1 us (2%)
    pallas_call x2, Pallas kernels, sum_grads(): pl.pallas_call(functools.partial(sum_grads_kernel, n, plan), in_specs=[vm...  223 us
    pallas_call x1, Pallas kernels, line_sum(): pl.pallas_call(functools.partial(line_kernel, mode, n), in_specs=[vmem] *...  77.9 us
    all_to_all x4, waiting for transfers between devices, exchange(): lax.all_to_all(blocks, 'dp', split_axis=0, concat_axis=0, tiled=True)  66.5 us
    dot_general x14, matrix products, dot(): return jnp.dot(left, right, preferred_element_type=f32)  51.2 us
    dot_general x9, matrix products, dot_t(): lax.dot_general(left, right, (((1,), (1,)), ((), ())), preferred_element_...  41 us
    unnamed x143, local copies, waits for them, and re-layouts  26.9 us
    all_to_all x4, starting transfers between devices, exchange(): lax.all_to_all(blocks, 'dp', split_axis=0, concat_axis=0, tiled=True)  22.9 us
    pallas_call x1, Pallas kernels, recur_backward(): pl.pallas_call(functools.partial(recur_backward_kernel, dk, dv), grid=(st...  20.5 us
  transfers between devices with their start and end apart: 5, of which 4 were waited for; matrix products, arithmetic and copies ran while one was open for 7% of the time, Pallas kernels for 24%

profile of v3, /device:TPU:0, one launch (start us, length us, event | category | flops | bytes accessed | tf_op | source)
XLA Modules:
  0.0 600.1 jit_solution(16286733170913293106)
XLA Ops:
  8.9 2.3 fusion
  11.7 2.5 fusion.2.refs_4_
  17.8 1.8 convolution_convert_fusion.3
  21.3 3.6 convolution_convert_fusion
  24.9 5.3 all-to-all-start
  31.6 28.2 %all-to-all-done = bf16[8,128,1152]{2,1,0:T(8,128)(2,1)} async-done(((bf16[8,128,1152]{2,1,0:T(8,128)(2,1)}), bf16[8,128,1152]{2,1,0:T(8,128)(2,1)}, u32[]{:S(2)}, u32[]{:S(2)}) %all-to-all-start) | async-done | bytes 2359328 | tf_op jit(solution)/shard_map/all_to_all | solution.py:1129
  59.8 17.0 %recur_forward.1 = (bf16[1024,512]{1,0:T(8,128)(2,1)}, bf16[1024,1152]{1,0:T(8,128)(2,1)S(1)}, bf16[8,256,512]{2,1,0:T(8,128)(2,1)S(1)}) custom-call(s32[1,1024]{1,0:T(1,128)S(1)} %bitcast.75, s32[1024,1]{1,0:T(8,128)S(1)} %copy.60.slot_column_ref, s32[1,3]{1,0:T(1,128)S(1)} %copy-done.10, bf16[128,256]{1,0:T(8,128)(2,1)S(1)} %copy.61.up_ref, ...), custom_call_target="tpu_custom_call" | custom-call | flops 6000000000 | bytes 10000000 | tf_op jit(solution)/shard_map/recur_forward/pallas_call | solution.py:207
  76.8 1.4 copy-done.13
  78.2 1.3 copy-done.15
  79.5 4.6 all-to-all-start.1
  84.7 1.6 constant_dynamic-slice_fusion.1.refs_1_.refs_2_
  86.8 1.3 constant_dynamic-slice_fusion.refs_2_
  88.2 11.3 %all-to-all-done.1 = bf16[8,128,512]{2,1,0:T(8,128)(2,1)} async-done(((bf16[8,128,512]{2,1,0:T(8,128)(2,1)}), bf16[8,128,512]{2,1,0:T(8,128)(2,1)}, u32[]{:S(2)}, u32[]{:S(2)}) %all-to-all-start.1) | async-done | bytes 1048608 | tf_op jit(solution)/shard_map/all_to_all | solution.py:1129
  99.5 4.1 multiply_reduce_fusion.2
  103.6 2.8 copy.62
  107.1 5.4 multiply_convert_fusion.3
  112.5 1.5 convolution_convert_fusion.1.refs_0_
  114.1 77.9 %line_norm.1 = (bf16[640,2048]{1,0:T(8,128)(2,1)S(1)}, f32[320,2048]{1,0:T(8,128)S(1)}) custom-call(bf16[640,2048]{1,0:T(8,128)(2,1)S(1)} %convolution_convert_fusion.1.refs_0_, bf16[320,2048]{1,0:T(8,128)(2,1)S(1)} %constant_dynamic-slice_fusion.1.refs_1_.refs_2_, bf16[320,2048]{1,0:T(8,128)(2,1)S(1)} %constant_dynamic-slice_fusion.1.refs_1_.refs_2_, ...), custom_call_target="tpu_custom_call" | custom-call | flops 10000000 | bytes 200000000 | tf_op jit(solution)/shard_map/line_norm/pallas_call | solution.py:468
  192.0 10.6 %fusion.79 = f32[640,1408]{1,0:T(8,128)} fusion(bf16[640,2048]{1,0:T(8,128)(2,1)S(1)} %get-tuple-element.36.refs_4_, bf16[2048,1408]{1,0:T(8,128)(2,1)} %param.34), kind=kOutput, calls=%fused_computation.144 | convolution fusion | flops 3690987520 | bytes 11993088 | tf_op jit(solution)/shard_map/dot_general | solution.py:30
  202.7 6.1 %fusion.78 = f32[640,1408]{1,0:T(8,128)} fusion(bf16[640,2048]{1,0:T(8,128)(2,1)S(1)} %get-tuple-element.36.refs_4_, bf16[2048,1408]{1,0:T(8,128)(2,1)S(1)} %bitcast.89), kind=kOutput, calls=%fused_computation.143 | convolution fusion | flops 3690987520 | bytes 11993088 | tf_op jit(solution)/shard_map/dot_general | solution.py:30
  208.8 10.3 %multiply_convert_fusion = (bf16[640,1408]{1,0:T(8,128)(2,1)S(1)}, bf16[640,1408]{1,0:T(8,128)(2,1)S(1)}, bf16[640,1408]{1,0:T(8,128)(2,1)}) fusion(f32[640,1408]{1,0:T(8,128)} %fusion.78, f32[640,1408]{1,0:T(8,128)} %fusion.79, bf16[640,2048]{1,0:T(8,128)(2,1)S(1)} %copy-done.34, bf16[1408,2048]{1,0:T(8,128)(2,1)} %param.35), kind=kOutput, calls=%fused_computation.10 | convolution fusion | flops 3704504320 | bytes 21004288 | tf_op jit(solution)/shard_map/dot_general | solution.py:26
  219.1 4.3 fusion.80
  223.4 8.4 %add_convert_fusion.1.refs_0_ = bf16[640,2048]{1,0:T(8,128)(2,1)} fusion(f32[640,2048]{1,0:T(8,128)S(1)} %fusion.80, bf16[640,1408]{1,0:T(8,128)(2,1)S(1)} %get-tuple-element.104.refs_6_, bf16[2048,1408]{1,0:T(8,128)(2,1)} %param.34), kind=kOutput, calls=%fused_computation.8 | convolution fusion | flops 3693608960 | bytes 15433728 | tf_op jit(solution)/shard_map/dot_general | solution.py:26
  231.7 93.1 %back_feed.1 = (bf16[640,2048]{1,0:T(8,128)(2,1)}, f32[320,2048]{1,0:T(8,128)}, f32[8,2048]{1,0:T(8,128)}, f32[256,1408]{1,0:T(8,128)}, f32[256,1408]{1,0:T(8,128)}) custom-call(bf16[640,2048]{1,0:T(8,128)(2,1)} %add_convert_fusion.1.refs_0_, f32[320,2048]{1,0:T(8,128)} %copy-done.3, bf16[320,2048]{1,0:T(8,128)(2,1)} %constant_dynamic-slice_fusion.refs_2_, ...), custom_call_target="tpu_custom_call" | custom-call | flops 12000000000 | bytes 200000000 | tf_op jit(solution)/shard_map/back_feed/pallas_call | solution.py:951
  324.9 5.9 multiply_reduce_fusion
  330.8 2.2 fusion.9
  333.1 8.5 %all-to-all-start.2 = ((bf16[8,128,512]{2,1,0:T(8,128)(2,1)}), bf16[8,128,512]{2,1,0:T(8,128)(2,1)S(1)}, u32[]{:S(2)}, u32[]{:S(2)}) async-start(bf16[8,128,512]{2,1,0:T(8,128)(2,1)} %bitcast.83), calls=%async_computation.2 | async-start | bytes 2097152 | tf_op jit(solution)/shard_map/all_to_all | solution.py:1129
  341.9 15.1 %all-to-all-done.2 = bf16[8,128,512]{2,1,0:T(8,128)(2,1)S(1)} async-done(((bf16[8,128,512]{2,1,0:T(8,128)(2,1)}), bf16[8,128,512]{2,1,0:T(8,128)(2,1)S(1)}, u32[]{:S(2)}, u32[]{:S(2)}) %all-to-all-start.2) | async-done | bytes 1048608 | tf_op jit(solution)/shard_map/all_to_all | solution.py:1129
  357.0 1.7 copy-done.14
  358.7 1.6 copy-done.16
  360.3 20.5 %recur_backward.1 = (bf16[1024,1152]{1,0:T(8,128)(2,1)S(1)}, f32[256,128]{1,0:T(8,128)S(1)}, f32[8,256]{1,0:T(8,128)S(1)}) custom-call(s32[1,1024]{1,0:T(1,128)S(1)} %bitcast.76, s32[1024,1]{1,0:T(8,128)S(1)} %copy-done.7, s32[1,3]{1,0:T(1,128)S(1)} %copy-done.10, bf16[128,256]{1,0:T(8,128)(2,1)S(1)} %copy.61.up_ref, f32[1,256]{1,0:T(1,128)S(1)} %bitcast.78, ...), custom_call_target="tpu_custom_call" | custom-call | flops 12000000000 | bytes 12000000 | tf_op jit(solution)/shard_map/recur_backward/pallas_call | solution.py:241
  380.8 1.5 copy-done.5
  382.2 4.5 all-to-all-start.3
  388.5 8.7 %fusion.3 = bf16[640,2048]{1,0:T(8,128)(2,1)} fusion(f32[320,2048]{1,0:T(8,128)S(1)} %get-tuple-element.109, f32[320,2048]{1,0:T(8,128)S(1)} %get-tuple-element.108, bf16[640,1408]{1,0:T(8,128)(2,1)S(1)} %copy-done.58, bf16[1408,2048]{1,0:T(8,128)(2,1)} %param.35), kind=kOutput, calls=%fused_computation.6 | convolution fusion | flops 3694919680 | bytes 15433728 | tf_op jit(solution)/shard_map/dot_general | solution.py:30
  398.9 5.0 fusion.81
  404.3 11.9 %all-to-all-done.3 = bf16[8,128,1152]{2,1,0:T(8,128)(2,1)} async-done(((bf16[8,128,1152]{2,1,0:T(8,128)(2,1)}), bf16[8,128,1152]{2,1,0:T(8,128)(2,1)}, u32[]{:S(2)}, u32[]{:S(2)}) %all-to-all-start.3) | async-done | bytes 2359328 | tf_op jit(solution)/shard_map/all_to_all | solution.py:1129
  416.2 3.8 convolution_convert_fusion.2.refs_5_
  420.7 1.5 copy-done.23
  422.2 1.6 fusion.28
  426.8 3.9 add_convert_fusion.refs_0_
  431.7 130.0 %back_mixer.1 = (bf16[640,2048]{1,0:T(8,128)(2,1)}, bf16[320,2048]{1,0:T(8,128)(2,1)}, f32[8,2048]{1,0:T(8,128)}, f32[256,1024]{1,0:T(8,128)}, f32[256,512]{1,0:...) custom-call(bf16[640,2048]{1,0:T(8,128)(2,1)} %add_convert_fusion.refs_0_, bf16[320,2048]{1,0:T(8,128)(2,1)} %copy-done.2, ...), custom_call_target="tpu_custom_call" | custom-call | flops 12000000000 | bytes 200000000 | tf_op jit(solution)/shard_map/back_mixer/pallas_call | solution.py:951
  563.6 11.5 %small_sum.1 = f32[48,128]{1,0:T(8,128)} custom-call(f32[8,48,128]{2,1,0:T(8,128)} %pad_maximum_fusion.part_ref), custom_call_target="tpu_custom_call" | custom-call | tf_op jit(solution)/shard_map/small_sum/pallas_call | solution.py:1049
  580.6 1.3 slice_bitcast_fusion.1
  582.7 3.7 copy.85
  586.5 1.5 copy.86
  589.5 1.1 copy.89
  590.7 1.1 copy.90
  591.8 1.1 copy.91
  (199 shorter events, 28.9 us)
Async XLA Ops:
  7.2 105.3 %copy-start = (bf16[512,2048]{1,0:T(8,128)(2,1)S(1)}, bf16[512,2048]{1,0:T(8,128)(2,1)}, u32[]{:S(2)}) copy-start(bf16[512,2048]{1,0:T(8,128)(2,1)} %param.31) | copy-start | bytes 6291460
  7.2 4.4 copy-start.39
  7.2 4.1 copy-start.45
  11.3 2.9 copy-start.42
  11.7 9.6 %copy-start.47 = (s32[640]{0:T(1024)}, s32[640]{0:T(1024)S(1)}, u32[]{:S(2)}) copy-start(s32[640]{0:T(1024)S(1)} %multiply_add_fusion.1) | copy-start | bytes 7684
  11.7 2.5 copy-start.28
  14.2 5.6 copy-start.17
  24.9 5.4 copy-start.55
  24.9 5.4 copy-start.44
  24.9 34.9 %copy-start.10 = (s32[1,3]{1,0:T(1,128)S(1)}, s32[1,3]{1,0:T(1,128)}, u32[]{:S(2)}) copy-start(s32[1,3]{1,0:T(1,128)} %lengths_ref.3) | copy-start | bytes 40
  24.9 34.9 %all-to-all-start = ((bf16[8,128,1152]{2,1,0:T(8,128)(2,1)}), bf16[8,128,1152]{2,1,0:T(8,128)(2,1)}, u32[]{:S(2)}, u32[]{:S(2)}) async-start(bf16[8,128,1152]{2,1,0:T(8,128)(2,1)} %bitcast.81), calls=%async_computation | async-start | bytes 4718592 | tf_op jit(solution)/shard_map/all_to_all | solution.py:1129
  30.3 46.5 %copy-start.11 = (f32[256]{0:T(256)}, f32[256]{0:T(256)S(1)}, u32[]{:S(2)}) copy-start(f32[256]{0:T(256)S(1)} %reshape.214) | copy-start | bytes 3076
  31.6 45.2 %copy-start.6 = (s32[1024,1]{1,0:T(8,128)}, s32[1024,1]{1,0:T(8,128)S(1)}, u32[]{:S(2)}) copy-start(s32[1024,1]{1,0:T(8,128)S(1)} %copy.60.slot_column_ref) | copy-start | bytes 12292
  59.8 24.3 %copy-start.54 = (bf16[512]{0:T(512)(128)(2,1)S(1)}, bf16[512]{0:T(512)(128)(2,1)}, u32[]{:S(2)}) copy-start(bf16[512]{0:T(512)(128)(2,1)} %param.30) | copy-start | bytes 3076
  59.8 24.9 %copy-start.46 = (bf16[2048]{0:T(1024)(128)(2,1)S(1)}, bf16[2048]{0:T(1024)(128)(2,1)}, u32[]{:S(2)}) copy-start(bf16[2048]{0:T(1024)(128)(2,1)} %param.32) | copy-start | bytes 12292
  79.5 20.0 %all-to-all-start.1 = ((bf16[8,128,512]{2,1,0:T(8,128)(2,1)}), bf16[8,128,512]{2,1,0:T(8,128)(2,1)}, u32[]{:S(2)}, u32[]{:S(2)}) async-start(bf16[8,128,512]{2,1,0:T(8,128)(2,1)} %bitcast.6), calls=%async_computation.1 | async-start | bytes 2097152 | tf_op jit(solution)/shard_map/all_to_all | solution.py:1129
  84.7 29.4 %copy-start.8 = (f32[2048]{0:T(1024)}, f32[2048]{0:T(1024)S(1)}, u32[]{:S(2)}) copy-start(f32[2048]{0:T(1024)S(1)} %reshape.216) | copy-start | bytes 24580
  86.8 27.2 %copy-start.2 = (bf16[320,2048]{1,0:T(8,128)(2,1)}, bf16[320,2048]{1,0:T(8,128)(2,1)S(1)}, u32[]{:S(2)}) copy-start(bf16[320,2048]{1,0:T(8,128)(2,1)S(1)} %constant_dynamic-slice_fusion.1.refs_1_.refs_2_) | copy-start | bytes 3932164
  114.1 88.6 %slice-start.2 = ((s8[5767168]{0:T(1024)(128)(4,1)}), s8[4194304]{0:T(1024)(128)(4,1)S(1)}, s32[]{:S(2)}) async-start(s8[5767168]{0:T(1024)(128)(4,1)} %bitcast.88), calls=%async_computation.7 | async-start | bytes 8388608
  192.0 10.6 %copy-start.3 = (f32[320,2048]{1,0:T(8,128)}, f32[320,2048]{1,0:T(8,128)S(1)}, u32[]{:S(2)}) copy-start(f32[320,2048]{1,0:T(8,128)S(1)} %get-tuple-element.37.refs_1_) | copy-start | bytes 7864324
  192.0 10.6 %copy-start.9 = (bf16[640,2048]{1,0:T(8,128)(2,1)}, bf16[640,2048]{1,0:T(8,128)(2,1)S(1)}, u32[]{:S(2)}) copy-start(bf16[640,2048]{1,0:T(8,128)(2,1)S(1)} %get-tuple-element.36.refs_4_) | copy-start | bytes 7864324
  192.0 10.6 %slice-start.3 = ((s8[5767168]{0:T(1024)(128)(4,1)}), s8[1572864]{0:T(1024)(128)(4,1)S(1)}, s32[]{:S(2)}) async-start(s8[5767168]{0:T(1024)(128)(4,1)} %bitcast.88), calls=%async_computation.8 | async-start | bytes 3145728
  202.7 6.2 %copy-start.34 = (bf16[640,2048]{1,0:T(8,128)(2,1)S(1)}, bf16[640,2048]{1,0:T(8,128)(2,1)}, u32[]{:S(2)}) copy-start(bf16[640,2048]{1,0:T(8,128)(2,1)} %refs_10_.1) | copy-start | bytes 7864324
  219.1 4.3 copy-start.59
  219.1 4.3 copy-start.60
  231.7 93.1 %copy-start.27 = (f32[640,512]{1,0:T(8,128)S(1)}, f32[640,512]{1,0:T(8,128)}, u32[]{:S(2)}) copy-start(f32[640,512]{1,0:T(8,128)} %copy.62) | copy-start | bytes 3932164
  231.7 93.1 %copy-start.53 = (f32[512]{0:T(512)S(1)}, f32[512]{0:T(512)}, u32[]{:S(2)}) copy-start(f32[512]{0:T(512)} %convert_element_type.112) | copy-start | bytes 6148
  324.9 5.9 copy-start.43
  324.9 5.9 copy-start.48
  324.9 5.9 copy-start.57
  330.8 10.8 %copy-start.36 = (bf16[2048,32]{0,1:T(8,128)(2,1)S(1)}, bf16[2048,32]{0,1:T(8,128)(2,1)}, u32[]{:S(2)}) copy-start(bf16[2048,32]{0,1:T(8,128)(2,1)} %copy-done.35) | copy-start | bytes 393220
  333.1 23.9 %copy-start.7 = (s32[1024,1]{1,0:T(8,128)S(1)}, s32[1024,1]{1,0:T(8,128)}, u32[]{:S(2)}) copy-start(s32[1024,1]{1,0:T(8,128)} %copy-done.6) | copy-start | bytes 12292
  333.1 23.9 %copy-start.12 = (f32[256]{0:T(256)S(1)}, f32[256]{0:T(256)}, u32[]{:S(2)}) copy-start(f32[256]{0:T(256)} %copy-done.11) | copy-start | bytes 3076
  333.1 23.9 %all-to-all-start.2 = ((bf16[8,128,512]{2,1,0:T(8,128)(2,1)}), bf16[8,128,512]{2,1,0:T(8,128)(2,1)S(1)}, u32[]{:S(2)}, u32[]{:S(2)}) async-start(bf16[8,128,512]{2,1,0:T(8,128)(2,1)} %bitcast.83), calls=%async_computation.2 | async-start | bytes 2097152 | tf_op jit(solution)/shard_map/all_to_all | solution.py:1129
  380.8 6.2 %copy-start.4 = (f32[320,2048]{1,0:T(8,128)S(1)}, f32[320,2048]{1,0:T(8,128)}, u32[]{:S(2)}) copy-start(f32[320,2048]{1,0:T(8,128)} %copy-done.3) | copy-start | bytes 7864324
  382.2 34.0 %all-to-all-start.3 = ((bf16[8,128,1152]{2,1,0:T(8,128)(2,1)}), bf16[8,128,1152]{2,1,0:T(8,128)(2,1)}, u32[]{:S(2)}, u32[]{:S(2)}) async-start(bf16[8,128,1152]{2,1,0:T(8,128)(2,1)} %bitcast.70), calls=%async_computation.3 | async-start | bytes 4718592 | tf_op jit(solution)/shard_map/all_to_all | solution.py:1129
  386.8 196.0 %all-reduce.6.cloned.1.call-start = ((), (), s32[]{:S(2)}) async-start(), calls=%async_computation.4 | async-start | bytes 5242880 | tf_op jit(solution)/shard_map/psum | solution.py:1255
  398.9 17.3 %copy-start.49 = (s32[640]{0:T(1024)S(1)}, s32[640]{0:T(1024)}, u32[]{:S(2)}) copy-start(s32[640]{0:T(1024)} %copy-done.47) | copy-start | bytes 7684
  416.2 3.8 copy-start.18
  420.1 4.6 copy-start.19
  423.8 2.5 slice-start
  561.7 16.8 %copy-start.32 = (f32[256,1024]{1,0:T(8,128)S(1)}, f32[256,1024]{1,0:T(8,128)}, u32[]{:S(2)}) copy-start(f32[256,1024]{1,0:T(8,128)} %get-tuple-element.48) | copy-start | bytes 3145732
  582.7 3.7 copy-start.20
  586.4 2.3 copy-start.37
  586.4 3.1 copy-start.25
  588.0 2.7 copy-start.24
  589.5 2.2 copy-start.26
  589.5 3.3 copy-start.1
  (22 other events, 33.1 us)
Sparse Core Ops, SparseCore 0:
  397.4 145.0 all-reduce.5

commit v4 on v3

--- a/solution.py
+++ b/solution.py
@@ -117,35 +117,19 @@
     lax.fori_loop(0, out_ref.shape[0] // block, body, 0)
 
 
-def recur_backward_kernel(
-    dk, dv, slot_row_ref, slot_column_ref, lengths_ref, up_ref, bias_ref, down_ref, arrived_ref,
-    held_ref, states_ref, out_ref, grad_up_ref, grad_bias_ref, d_state, result,
+def span_backward(
+    dk, dv, step, ends, d_out, held_ref, entering, up_ref, bias_ref, down_ref, d_state, result,
+    grad_up_ref, grad_bias_ref,
 ):
-    step = pl.num_programs(0) - 1 - pl.program_id(0)
     first = step * SPAN
-    end0 = lengths_ref[0, 0]
-    end1 = end0 + lengths_ref[0, 1]
-    end2 = end1 + lengths_ref[0, 2]
-    slots = slot_row_ref.shape[1]
-
-    @pl.when(pl.program_id(0) == 0)
-    def _():
-        d_state[...] = jnp.zeros_like(d_state)
-        grad_up_ref[...] = jnp.zeros_like(grad_up_ref)
-        grad_bias_ref[...] = jnp.zeros_like(grad_bias_ref)
-
-    position = first + lax.broadcasted_iota(jnp.int32, (SPAN, slots), 0)
-    place = (slot_row_ref[...] == position).astype(f32).astype(bf16)
-    d_out = dot(place, arrived_ref[...]).astype(bf16)
+    at = pl.ds(pl.multiple_of(first, SPAN), SPAN)
     scale = float(dk) ** -0.5
-    queries = held_ref[:, :dk].astype(f32) * scale
-    keys = held_ref[:, dk : 2 * dk].astype(f32)
-    values = held_ref[:, 2 * dk : 2 * dk + dv]
-    latent = held_ref[:, 2 * dk + dv :]
+    queries = held_ref[at, :dk].astype(f32) * scale
+    keys = held_ref[at, dk : 2 * dk].astype(f32)
+    values = held_ref[at, 2 * dk : 2 * dk + dv]
+    latent = held_ref[at, 2 * dk + dv :]
     logits = dot(latent, up_ref[...]) + bias_ref[...]
-    _, cumulative, total, middle, carried, tail, keep, allowed = span_terms(
-        first, (end0, end1, end2), logits
-    )
+    _, cumulative, total, middle, carried, tail, keep, allowed = span_terms(first, ends, logits)
     grow_query = jnp.exp(cumulative - middle)
     grow_key = jnp.exp(middle - cumulative)
     start_decay = jnp.exp(cumulative) * carried
@@ -158,7 +142,6 @@
     d_scores = jnp.where(allowed, dot_t(d_out, values), 0.0).astype(bf16)
     leaving = d_state[...]
     leaving_low = leaving.astype(bf16)
-    entering = states_ref[0]
     d_values = rows_dot(scores, d_out) + dot(key_end, leaving_low)
     d_queries = dot(d_scores, key_mid) * grow_query + dot_t(d_out, entering) * start_decay
     d_key_end = dot_t(values, leaving_low) * end_decay
@@ -184,17 +167,12 @@
     high = d_latent.astype(bf16).astype(f32)
     lane = lax.broadcasted_iota(jnp.int32, d_latent.shape, 1)
     d_latent_packed = jnp.where(lane < LANES // 4, high, d_latent - high)
-    at = pl.ds(pl.multiple_of(first, SPAN), SPAN)
     result[at, :dk] = (d_queries * scale).astype(bf16)
     result[at, dk : 2 * dk] = d_keys.astype(bf16)
     result[at, 2 * dk : 2 * dk + dv] = d_values.astype(bf16)
     result[at, 2 * dk + dv :] = d_latent_packed.astype(bf16)
     kept_column = jnp.transpose(jnp.broadcast_to(kept, (8, dk)))[:, :1]
     d_state[...] = kept_column * leaving + rows_dot(query_start, d_out)
-
-    @pl.when(step == 0)
-    def _():
-        return_rows(slot_column_ref, result, out_ref)
 
 
 def whole(shape):
@@ -234,235 +212,227 @@
     )(slot_map.reshape(1, -1), slot_map.reshape(-1, 1), lengths, up_wide, bias, arrived)
 
 
-def recur_backward(slot_map, lengths, up_wide, bias, down_wide, arrived, held, states, dk, dv):
-    slots = arrived.shape[0]
-    width = held.shape[1]
-    steps = OWN_CAP // SPAN
-    return pl.pallas_call(
-        functools.partial(recur_backward_kernel, dk, dv),
-        grid=(steps,),
-        in_specs=[
-            whole((1, slots)),
-            whole((slots, 1)),
-            pl.BlockSpec(memory_space=pltpu.SMEM),
-            whole((LANES, dk)),
-            whole((1, dk)),
-            whole((dk, LANES)),
-            whole((slots, dv)),
-            pl.BlockSpec((SPAN, width), lambda i: (steps - 1 - i, 0)),
-            pl.BlockSpec((1, dk, dv), lambda i: (steps - 1 - i, 0, 0)),
-        ],
-        out_specs=[whole((slots, width)), whole((dk, LANES)), whole((8, dk))],
-        out_shape=[
-            jax.ShapeDtypeStruct((slots, width), bf16),
-            jax.ShapeDtypeStruct((dk, LANES), f32),
-            jax.ShapeDtypeStruct((8, dk), f32),
-        ],
-        scratch_shapes=[pltpu.VMEM((dk, dv), f32), pltpu.VMEM((OWN_CAP, width), bf16)],
-        compiler_params=pltpu.CompilerParams(vmem_limit_bytes=40 << 20),
-        cost_estimate=pl.CostEstimate(
-            flops=12_000_000_000, bytes_accessed=12_000_000, transcendentals=4_000_000
-        ),
-        name="recur_backward",
-    )(
-        slot_map.reshape(1, -1), slot_map.reshape(-1, 1), lengths, up_wide, bias, down_wide,
-        arrived, held, states,
-    )
-
-
-CHUNK = 32
-
-
-def line_kernel(mode, n, *refs):
-    share_ref, x_ref, base_ref, gain_ref = refs[:4]
-    if mode == "norm":
-        out_ref, kept_ref = refs[4:6]
-        scratch = refs[6:]
-    elif mode == "back":
-        out_ref, kept_ref, gain_grad_ref = refs[4:7]
-        scratch = refs[7:]
-    else:
-        out_ref = refs[4]
-        kept_ref = None
-        scratch = refs[5:]
-    up_in, up_out, down_in, down_out, sems = scratch
-    me = lax.axis_index("tensor")
-    half = up_in.shape[0]
-    count = half // CHUNK
-
-    barrier = pltpu.get_barrier_semaphore()
-
-    @pl.when(me > 0)
-    def _():
-        pl.semaphore_signal(barrier, inc=1, device_id={"tensor": me - 1}, device_id_type=MESH)
-
-    @pl.when(me < n - 1)
-    def _():
-        pl.semaphore_signal(barrier, inc=1, device_id={"tensor": me + 1}, device_id_type=MESH)
-
-    inside = (me > 0) & (me < n - 1)
-
-    @pl.when(inside)
-    def _():
-        pl.semaphore_wait(barrier, 2)
-
-    @pl.when(jnp.logical_not(inside))
-    def _():
-        pl.semaphore_wait(barrier, 1)
-
-    def at(g):
-        return pl.ds(pl.multiple_of(g * CHUNK, CHUNK), CHUNK)
-
-    def low(g):
-        return pl.ds(pl.multiple_of(half + g * CHUNK, CHUNK), CHUNK)
-
-    def right(source, target, lane, g):
+FINE = 16
+SKEW = 2
+
+
+class Line:
+    def __init__(self, n, share_ref, up_in, down_in, out_ref, sems, finish):
+        self.n, self.me = n, lax.axis_index("tensor")
+        self.share, self.up_in, self.down_in, self.out = share_ref, up_in, down_in, out_ref
+        self.sems, self.finish = sems, finish
+        self.half = up_in.shape[0]
+        self.count = self.half // FINE
+        self.second = self.count + 2
+        self.steps = self.second + self.count + SKEW * (n - 2)
+
+    @staticmethod
+    def scratch(half, width):
+        return [pltpu.VMEM((half, width), bf16), pltpu.VMEM((half, width), bf16)]
+
+    @staticmethod
+    def semaphores(half):
+        return pltpu.SemaphoreType.DMA((8, half // FINE))
+
+    def greet(self, barrier, others):
+        n, me = self.n, self.me
+
+        @pl.when(me > 0)
+        def _():
+            pl.semaphore_signal(barrier, inc=1, device_id={"tensor": me - 1}, device_id_type=MESH)
+
+        @pl.when(me < n - 1)
+        def _():
+            pl.semaphore_signal(barrier, inc=1, device_id={"tensor": me + 1}, device_id_type=MESH)
+
+        inside = (me > 0) & (me < n - 1)
+
+        @pl.when(inside)
+        def _():
+            pl.semaphore_wait(barrier, others + 2)
+
+        @pl.when(jnp.logical_not(inside))
+        def _():
+            pl.semaphore_wait(barrier, others + 1)
+
+    def at(self, g):
+        return pl.ds(pl.multiple_of(g * FINE, FINE), FINE)
+
+    def low(self, g):
+        return pl.ds(pl.multiple_of(self.half + g * FINE, FINE), FINE)
+
+    def right(self, source, target, lane, g):
         return pltpu.make_async_remote_copy(
-            source, target, sems.at[2 * lane, g], sems.at[2 * lane + 1, g],
-            device_id={"tensor": jnp.minimum(me + 1, n - 1)}, device_id_type=MESH,
-        )
-
-    def left(source, target, lane, g):
+            source, target, self.sems.at[2 * lane, g], self.sems.at[2 * lane + 1, g],
+            device_id={"tensor": jnp.minimum(self.me + 1, self.n - 1)}, device_id_type=MESH,
+        )
+
+    def left(self, source, target, lane, g):
         return pltpu.make_async_remote_copy(
-            source, target, sems.at[2 * lane, g], sems.at[2 * lane + 1, g],
-            device_id={"tensor": jnp.maximum(me - 1, 0)}, device_id_type=MESH,
-        )
-
-    def up_copy(g):
-        return right(up_out.at[at(g), :], up_in.at[at(g), :], 0, g)
-
-    def down_copy(g):
-        return left(down_out.at[at(g), :], down_in.at[at(g), :], 1, g)
-
-    def first_up_copy(g):
-        return right(share_ref.at[at(g), :], up_in.at[at(g), :], 0, g)
-
-    def first_down_copy(g):
-        return left(share_ref.at[low(g), :], down_in.at[at(g), :], 1, g)
-
-    def up_back_copy(g):
-        return left(out_ref.at[at(g), :], out_ref.at[at(g), :], 2, g)
-
-    def down_back_copy(g):
-        return right(out_ref.at[low(g), :], out_ref.at[low(g), :], 3, g)
-
-    if mode == "back":
-        gain_grad_ref[...] = jnp.zeros_like(gain_grad_ref)
-
-    def finish(total, g, place):
-        base = base_ref[at(g), :].astype(f32)
-        if mode == "sum":
-            out_ref[place, :] = (base + total).astype(out_ref.dtype)
-            return
-        if mode == "norm":
-            hidden = base + total
-            kept_ref[at(g), :] = hidden
-            scaling = lax.rsqrt(jnp.mean(hidden * hidden, axis=1, keepdims=True) + epsilon)
-            out_ref[place, :] = (hidden * scaling * gain_ref[...]).astype(out_ref.dtype)
-            return
-        rows = x_ref[at(g), :].astype(f32)
+            source, target, self.sems.at[2 * lane, g], self.sems.at[2 * lane + 1, g],
+            device_id={"tensor": jnp.maximum(self.me - 1, 0)}, device_id_type=MESH,
+        )
+
+    def up_copy(self, g):
+        rows = self.up_in.at[self.at(g), :]
+        return self.right(rows, rows, 0, g)
+
+    def down_copy(self, g):
+        rows = self.down_in.at[self.at(g), :]
+        return self.left(rows, rows, 1, g)
+
+    def up_back_copy(self, g):
+        rows = self.out.at[self.at(g), :]
+        return self.left(rows, rows, 2, g)
+
+    def down_back_copy(self, g):
+        rows = self.out.at[self.low(g), :]
+        return self.right(rows, rows, 3, g)
+
+    def prime(self):
+        @pl.when(self.me == 0)
+        def _():
+            @pl.loop(0, self.count)
+            def _(g):
+                self.right(
+                    self.share.at[self.at(g), :], self.up_in.at[self.at(g), :], 0, g
+                ).start()
+
+        @pl.when(self.me == self.n - 1)
+        def _():
+            @pl.loop(0, self.count)
+            def _(g):
+                self.left(
+                    self.share.at[self.low(g), :], self.down_in.at[self.at(g), :], 1, g
+                ).start()
+
+    def step(self, step):
+        n, me, count = self.n, self.me, self.count
+        at, low = self.at, self.low
+        g_up = step - SKEW * (me - 1)
+
+        @pl.when((me > 0) & (g_up >= 0) & (g_up < count))
+        def _():
+            self.up_copy(g_up).wait_recv()
+            total = self.up_in[at(g_up), :].astype(f32) + self.share[at(g_up), :].astype(f32)
+
+            @pl.when(me < n - 1)
+            def _():
+                self.up_in[at(g_up), :] = total.astype(bf16)
+                self.up_copy(g_up).start()
+
+            @pl.when(me == n - 1)
+            def _():
+                self.finish(total, at(g_up), at(g_up))
+                self.up_back_copy(g_up).start()
+
+        g_down = step - SKEW * (n - 2 - me)
+
+        @pl.when((me < n - 1) & (g_down >= 0) & (g_down < count))
+        def _():
+            self.down_copy(g_down).wait_recv()
+            total = self.down_in[at(g_down), :].astype(f32) + (
+                self.share[low(g_down), :].astype(f32)
+            )
+
+            @pl.when(me > 0)
+            def _():
+                self.down_in[at(g_down), :] = total.astype(bf16)
+                self.down_copy(g_down).start()
+
+            @pl.when(me == 0)
+            def _():
+                self.finish(total, at(g_down), low(g_down))
+                self.down_back_copy(g_down).start()
+
+        g_up_back = step - self.second - SKEW * (n - 2 - me)
+
+        @pl.when((me < n - 1) & (g_up_back >= 0) & (g_up_back < count))
+        def _():
+            self.up_back_copy(g_up_back).wait_recv()
+
+            @pl.when(me > 0)
+            def _():
+                self.up_back_copy(g_up_back).start()
+
+        g_down_back = step - self.second - SKEW * (me - 1)
+
+        @pl.when((me > 0) & (g_down_back >= 0) & (g_down_back < count))
+        def _():
+            self.down_back_copy(g_down_back).wait_recv()
+
+            @pl.when(me < n - 1)
+            def _():
+                self.down_back_copy(g_down_back).start()
+
+    def run(self, first, last):
+        @pl.loop(first, last)
+        def _(step):
+            self.step(step)
+
+    def drain(self):
+        n, me = self.n, self.me
+
+        @pl.loop(0, self.count)
+        def _(g):
+            @pl.when(me < n - 1)
+            def _():
+                self.up_copy(g).wait_send()
+                self.down_back_copy(g).wait_send()
+
+            @pl.when(me > 0)
+            def _():
+                self.down_copy(g).wait_send()
+                self.up_back_copy(g).wait_send()
+
+
+def norm_back(x_ref, base_ref, gain_ref, out_ref, kept_ref, gain_grad_ref):
+    gain_grad_ref[...] = jnp.zeros_like(gain_grad_ref)
+
+    def finish(total, own, place):
+        rows = x_ref[own, :].astype(f32)
         scaling = lax.rsqrt(jnp.mean(rows * rows, axis=1, keepdims=True) + epsilon)
         unit = rows * scaling
         gained = gain_ref[...] * total
-        grad = base + scaling * (gained - unit * jnp.mean(gained * unit, axis=1, keepdims=True))
-        kept_ref[at(g), :] = grad
+        grad = base_ref[own, :].astype(f32) + scaling * (
+            gained - unit * jnp.mean(gained * unit, axis=1, keepdims=True)
+        )
+        kept_ref[own, :] = grad.astype(kept_ref.dtype)
         out_ref[place, :] = grad.astype(out_ref.dtype)
         term = total * unit
         part = term[0:8, :]
-        for i in range(1, CHUNK // 8):
+        for i in range(1, FINE // 8):
             part = part + term[8 * i : 8 * i + 8, :]
         gain_grad_ref[...] += part
 
-    @pl.when(me == 0)
-    def _():
-        @pl.loop(0, count)
-        def _(g):
-            first_up_copy(g).start()
-
-    @pl.when(me == n - 1)
-    def _():
-        @pl.loop(0, count)
-        def _(g):
-            first_down_copy(g).start()
-
-    @pl.loop(0, count + n - 2)
-    def _(step):
-        g_up = step - (me - 1)
-
-        @pl.when((me > 0) & (g_up >= 0) & (g_up < count))
-        def _():
-            up_copy(g_up).wait_recv()
-            total = up_in[at(g_up), :].astype(f32) + share_ref[at(g_up), :].astype(f32)
-
-            @pl.when(me < n - 1)
-            def _():
-                up_out[at(g_up), :] = total.astype(bf16)
-                up_copy(g_up).start()
-
-            @pl.when(me == n - 1)
-            def _():
-                finish(total, g_up, at(g_up))
-                up_back_copy(g_up).start()
-
-        g_down = step - (n - 2 - me)
-
-        @pl.when((me < n - 1) & (g_down >= 0) & (g_down < count))
-        def _():
-            down_copy(g_down).wait_recv()
-            total = down_in[at(g_down), :].astype(f32) + share_ref[low(g_down), :].astype(f32)
-
-            @pl.when(me > 0)
-            def _():
-                down_out[at(g_down), :] = total.astype(bf16)
-                down_copy(g_down).start()
-
-            @pl.when(me == 0)
-            def _():
-                finish(total, g_down, low(g_down))
-                down_back_copy(g_down).start()
-
-    @pl.loop(0, count + n - 2)
-    def _(step):
-        g_up = step - (n - 2 - me)
-
-        @pl.when((me < n - 1) & (g_up >= 0) & (g_up < count))
-        def _():
-            up_back_copy(g_up).wait_recv()
-
-            @pl.when(me > 0)
-            def _():
-                up_back_copy(g_up).start()
-
-        g_down = step - (me - 1)
-
-        @pl.when((me > 0) & (g_down >= 0) & (g_down < count))
-        def _():
-            down_back_copy(g_down).wait_recv()
-
-            @pl.when(me < n - 1)
-            def _():
-                down_back_copy(g_down).start()
-
-    @pl.loop(0, count)
-    def _(g):
-        @pl.when(me < n - 1)
-        def _():
-            up_copy(g).wait_send()
-            down_back_copy(g).wait_send()
-
-        @pl.when(me > 0)
-        def _():
-            down_copy(g).wait_send()
-            up_back_copy(g).wait_send()
+    return finish
+
+
+def line_kernel(mode, n, *refs):
+    share_ref, x_ref, base_ref, gain_ref, out_ref, kept_ref = refs[:6]
+    if mode == "norm":
+        up_in, down_in, sems = refs[6:]
+
+        def finish(total, own, place):
+            hidden = base_ref[own, :].astype(f32) + total
+            kept_ref[own, :] = hidden
+            scaling = lax.rsqrt(jnp.mean(hidden * hidden, axis=1, keepdims=True) + epsilon)
+            out_ref[place, :] = (hidden * scaling * gain_ref[...]).astype(out_ref.dtype)
+    else:
+        gain_grad_ref, up_in, down_in, sems = refs[6:]
+        finish = norm_back(x_ref, base_ref, gain_ref, out_ref, kept_ref, gain_grad_ref)
+    line = Line(n, share_ref, up_in, down_in, out_ref, sems, finish)
+    line.greet(pltpu.get_barrier_semaphore(), 0)
+    line.prime()
+    line.run(0, line.steps)
+    line.drain()
 
 
 def line_sum(mode, call, n, share, x_own, base_own, gain):
     rows, width = share.shape
     half = rows // 2
     vmem = pl.BlockSpec(memory_space=pltpu.VMEM)
-    outs = [jax.ShapeDtypeStruct((rows, width), bf16)]
-    if mode != "sum":
-        outs.append(jax.ShapeDtypeStruct((half, width), f32))
+    outs = [jax.ShapeDtypeStruct((rows, width), bf16), jax.ShapeDtypeStruct((half, width), f32)]
     if mode == "back":
         outs.append(jax.ShapeDtypeStruct((8, width), f32))
     return pl.pallas_call(
@@ -470,13 +440,7 @@
         in_specs=[vmem] * 4,
         out_specs=[vmem] * len(outs),
         out_shape=outs,
-        scratch_shapes=[
-            pltpu.VMEM((half, width), bf16),
-            pltpu.VMEM((half, width), bf16),
-            pltpu.VMEM((half, width), bf16),
-            pltpu.VMEM((half, width), bf16),
-            pltpu.SemaphoreType.DMA((8, half // CHUNK)),
-        ],
+        scratch_shapes=Line.scratch(half, width) + [Line.semaphores(half)],
         compiler_params=pltpu.CompilerParams(
             collective_id=call, has_side_effects=True, vmem_limit_bytes=40 << 20
         ),
@@ -485,10 +449,6 @@
         ),
         name="line_" + mode,
     )(share, x_own, base_own, gain)
-
-
-FINE = 16
-SKEW = 2
 
 
 def partner_of(index):
@@ -539,26 +499,15 @@
     if cols:
         pair_sems, col_sems = take(2)
 
-    me = lax.axis_index("tensor")
     member = lax.axis_index("dp")
     parity = lax.rem(member, 2)
     mine = member // 2
     partner = partner_of(member)
     groups, team, block = plan.groups, plan.team, plan.block
-    half = up_in.shape[0]
-    count = half // FINE
-    inside = (me > 0) & (me < n - 1)
+    finish = norm_back(x_ref, base_ref, gain_ref, out_ref, kept_ref, gain_grad_ref)
+    line = Line(n, share_ref, up_in, down_in, out_ref, sems, finish)
 
     barrier = pltpu.get_barrier_semaphore()
-
-    @pl.when(me > 0)
-    def _():
-        pl.semaphore_signal(barrier, inc=1, device_id={"tensor": me - 1}, device_id_type=MESH)
-
-    @pl.when(me < n - 1)
-    def _():
-        pl.semaphore_signal(barrier, inc=1, device_id={"tensor": me + 1}, device_id_type=MESH)
-
     if cols:
         greeted = groups - 1
 
@@ -577,50 +526,7 @@
                 barrier, inc=1, device_id={"dp": 2 * lax.rem(mine + k, team) + parity},
                 device_id_type=MESH,
             )
-
-    @pl.when(inside)
-    def _():
-        pl.semaphore_wait(barrier, greeted + 2)
-
-    @pl.when(jnp.logical_not(inside))
-    def _():
-        pl.semaphore_wait(barrier, greeted + 1)
-
-    def at(g):
-        return pl.ds(pl.multiple_of(g * FINE, FINE), FINE)
-
-    def low(g):
-        return pl.ds(pl.multiple_of(half + g * FINE, FINE), FINE)
-
-    def right(source, target, lane, g):
-        return pltpu.make_async_remote_copy(
-            source, target, sems.at[2 * lane, g], sems.at[2 * lane + 1, g],
-            device_id={"tensor": jnp.minimum(me + 1, n - 1)}, device_id_type=MESH,
-        )
-
-    def left(source, target, lane, g):
-        return pltpu.make_async_remote_copy(
-            source, target, sems.at[2 * lane, g], sems.at[2 * lane + 1, g],
-            device_id={"tensor": jnp.maximum(me - 1, 0)}, device_id_type=MESH,
-        )
-
-    def up_copy(g):
-        return right(up_in.at[at(g), :], up_in.at[at(g), :], 0, g)
-
-    def down_copy(g):
-        return left(down_in.at[at(g), :], down_in.at[at(g), :], 1, g)
-
-    def first_up_copy(g):
-        return right(share_ref.at[at(g), :], up_in.at[at(g), :], 0, g)
-
-    def first_down_copy(g):
-        return left(share_ref.at[low(g), :], down_in.at[at(g), :], 1, g)
-
-    def up_back_copy(g):
-        return left(out_ref.at[at(g), :], out_ref.at[at(g), :], 2, g)
-
-    def down_back_copy(g):
-        return right(out_ref.at[low(g), :], out_ref.at[low(g), :], 3, g)
+    line.greet(barrier, greeted)
 
     def to_partner(source, target, send, recv):
         return pltpu.make_async_remote_copy(
@@ -676,36 +582,7 @@
             device_id={"dp": to}, device_id_type=MESH,
         )
 
-    gain_grad_ref[...] = jnp.zeros_like(gain_grad_ref)
-
-    def finish(total, g, place):
-        rows_x = x_ref[at(g), :].astype(f32)
-        scaling = lax.rsqrt(jnp.mean(rows_x * rows_x, axis=1, keepdims=True) + epsilon)
-        unit = rows_x * scaling
-        gained = gain_ref[...] * total
-        grad = base_ref[at(g), :].astype(f32) + scaling * (
-            gained - unit * jnp.mean(gained * unit, axis=1, keepdims=True)
-        )
-        kept_ref[at(g), :] = grad.astype(kept_ref.dtype)
-        out_ref[place, :] = grad.astype(out_ref.dtype)
-        term = total * unit
-        part = term[0:8, :]
-        for i in range(1, FINE // 8):
-            part = part + term[8 * i : 8 * i + 8, :]
-        gain_grad_ref[...] += part
-
-    @pl.when(me == 0)
-    def _():
-        @pl.loop(0, count)
-        def _(g):
-            first_up_copy(g).start()
-
-    @pl.when(me == n - 1)
-    def _():
-        @pl.loop(0, count)
-        def _(g):
-            first_down_copy(g).start()
-
+    line.prime()
     for i in range(cols):
         for c in pair_copies(i):
             c.start()
@@ -780,67 +657,12 @@
                 def _():
                     row_recv[mine, :, tile_columns(t)] = low_product
 
-    delay = SKEW * (n - 2)
-    second = count + 2
     start_work = 8
 
-    @pl.loop(0, second + count + delay)
+    @pl.loop(0, line.steps)
     def _(step):
-        g_up = step - SKEW * (me - 1)
-
-        @pl.when((me > 0) & (g_up >= 0) & (g_up < count))
-        def _():
-            up_copy(g_up).wait_recv()
-            total = up_in[at(g_up), :].astype(f32) + share_ref[at(g_up), :].astype(f32)
-
-            @pl.when(me < n - 1)
-            def _():
-                up_in[at(g_up), :] = total.astype(bf16)
-                up_copy(g_up).start()
-
-            @pl.when(me == n - 1)
-            def _():
-                finish(total, g_up, at(g_up))
-                up_back_copy(g_up).start()
-
-        g_down = step - SKEW * (n - 2 - me)
-
-        @pl.when((me < n - 1) & (g_down >= 0) & (g_down < count))
-        def _():
-            down_copy(g_down).wait_recv()
-            total = down_in[at(g_down), :].astype(f32) + share_ref[low(g_down), :].astype(f32)
-
-            @pl.when(me > 0)
-            def _():
-                down_in[at(g_down), :] = total.astype(bf16)
-                down_copy(g_down).start()
-
-            @pl.when(me == 0)
-            def _():
-                finish(total, g_down, low(g_down))
-                down_back_copy(g_down).start()
-
+        line.step(step)
         work(step - start_work)
-
-        g_up_back = step - second - SKEW * (n - 2 - me)
-
-        @pl.when((me < n - 1) & (g_up_back >= 0) & (g_up_back < count))
-        def _():
-            up_back_copy(g_up_back).wait_recv()
-
-            @pl.when(me > 0)
-            def _():
-                up_back_copy(g_up_back).start()
-
-        g_down_back = step - second - SKEW * (me - 1)
-
-        @pl.when((me > 0) & (g_down_back >= 0) & (g_down_back < count))
-        def _():
-            down_back_copy(g_down_back).wait_recv()
-
-            @pl.when(me < n - 1)
-            def _():
-                down_back_copy(g_down_back).start()
 
     for i in range(cols):
         size = plan.col_rows[i] // groups
@@ -867,18 +689,7 @@
             total = total + row_recv[q, :, span].astype(f32)
         row_outs[i][...] = total
 
-    @pl.loop(0, count)
-    def _(g):
-        @pl.when(me < n - 1)
-        def _():
-            up_copy(g).wait_send()
-            down_back_copy(g).wait_send()
-
-        @pl.when(me > 0)
-        def _():
-            down_copy(g).wait_send()
-            up_back_copy(g).wait_send()
-
+    line.drain()
     for i in range(cols):
         for c in pair_copies(i):
             c.wait_send()
@@ -924,11 +735,7 @@
     ]
     outs += [jax.ShapeDtypeStruct((plan.block, wide), f32) for wide in row_widths]
     outs += [jax.ShapeDtypeStruct((r // groups, width), f32) for r in col_rows]
-    scratch = [
-        pltpu.VMEM((half, width), bf16),
-        pltpu.VMEM((half, width), bf16),
-        pltpu.VMEM((count, plan.half), bf16),
-    ]
+    scratch = Line.scratch(half, width) + [pltpu.VMEM((count, plan.half), bf16)]
     scratch += [pltpu.VMEM((count, wide), bf16) for wide in row_widths]
     scratch += [pltpu.VMEM((count, r), bf16) for r in col_rows]
     scratch += [pltpu.VMEM((count, plan.half), bf16) for _ in col_rows]
@@ -936,7 +743,7 @@
     scratch += [pltpu.VMEM((r, plan.half), bf16) for r in col_rows]
     scratch += [pltpu.VMEM((groups, r // groups, plan.half), bf16) for r in col_rows]
     scratch += [
-        pltpu.SemaphoreType.DMA((8, half // FINE)),
+        Line.semaphores(half),
         pltpu.SemaphoreType.DMA((2, team)),
         pltpu.SemaphoreType.DMA((2, len(row_widths))),
         pltpu.SemaphoreType.DMA((2, len(row_tiles), team)),
@@ -961,6 +768,209 @@
             flops=12_000_000_000, bytes_accessed=200_000_000, transcendentals=0
         ),
         name=name,
+    )(*operands)
+
+
+def one_hot(index, base, shape, dim):
+    return (index == base + lax.broadcasted_iota(jnp.int32, shape, dim)).astype(f32).astype(bf16)
+
+
+def recur_back_kernel(n, groups, dk, dv, *refs):
+    (
+        lengths_ref, send_row_ref, send_column_ref, slot_row_ref, slot_column_ref,
+        d_mixed_ref, out_weight_ref, attended_ref, gate_ref, gain_ref, up_ref, bias_ref, down_ref,
+        held_ref, states_ref, share_ref, hidden_ref,
+        d_rows_ref, d_gate_ref, head_gain_ref, grad_up_ref, grad_bias_ref, layer_ref,
+        up_in, down_in, d_attended, sent, came, d_state, result, back_sent, back_came,
+        sems, go_sems, back_sems,
+    ) = refs
+    member = lax.axis_index("dp")
+    count = d_mixed_ref.shape[0]
+    slots = slot_row_ref.shape[1]
+    cap = slots // groups
+    end0 = lengths_ref[0, 0]
+    end1 = end0 + lengths_ref[0, 1]
+    ends = (end0, end1, end1 + lengths_ref[0, 2])
+
+    def finish(total, own, place):
+        layer_ref[place, :] = (hidden_ref[own, :] + total).astype(layer_ref.dtype)
+
+    line = Line(n, share_ref, up_in, down_in, layer_ref, sems, finish)
+    barrier = pltpu.get_barrier_semaphore()
+
+    @pl.loop(1, groups)
+    def _(k):
+        pl.semaphore_signal(
+            barrier, inc=1, device_id={"dp": lax.rem(member + k, groups)}, device_id_type=MESH
+        )
+
+    line.greet(barrier, groups - 1)
+    line.prime()
+
+    def part(j):
+        return pl.ds(pl.multiple_of(j * cap, cap), cap)
+
+    def go_copy(to, source):
+        return pltpu.make_async_remote_copy(
+            sent.at[part(to), :], came.at[part(source), :], go_sems.at[0, to],
+            go_sems.at[1, source], device_id={"dp": to}, device_id_type=MESH,
+        )
+
+    def back_copy(to, source):
+        return pltpu.make_async_remote_copy(
+            back_sent.at[part(to), :], back_came.at[part(source), :], back_sems.at[0, to],
+            back_sems.at[1, source], device_id={"dp": to}, device_id_type=MESH,
+        )
+
+    head_gain_ref[...] = jnp.zeros_like(head_gain_ref)
+    tile = count // 5
+
+    @pl.loop(0, 5)
+    def _(i):
+        rows = pl.ds(pl.multiple_of(i * tile, tile), tile)
+        d_gated = dot_t(d_mixed_ref[rows, :], out_weight_ref[...])
+        attended = attended_ref[rows, :].astype(f32)
+        gate = gate_ref[rows, :]
+        scaling = lax.rsqrt(jnp.mean(attended * attended, axis=1, keepdims=True) + head_floor)
+        unit = attended * scaling
+        sigmoid = jax.nn.sigmoid(gate)
+        swish = gate * sigmoid
+        gained = d_gated * gain_ref[...]
+        d_gate_ref[rows, :] = (
+            gained * unit * sigmoid * (1.0 + gate * (1.0 - sigmoid))
+        ).astype(bf16)
+        d_unit = gained * swish
+        d_attended[rows, :] = (
+            scaling * (d_unit - unit * jnp.mean(d_unit * unit, axis=1, keepdims=True))
+        ).astype(bf16)
+        term = d_gated * unit * swish
+        piece = term[0:8, :]
+        for r in range(1, tile // 8):
+            piece = piece + term[8 * r : 8 * r + 8, :]
+        head_gain_ref[...] += piece
+        line.step(i)
+
+    @pl.loop(1, groups + 1)
+    def _(k):
+        to = lax.rem(member + k, groups)
+        pick = one_hot(send_row_ref[...], to * cap, (cap, count), 0)
+        block = dot(pick, d_attended[...]).astype(bf16)
+
+        @pl.when(k < groups)
+        def _():
+            sent[part(to), :] = block
+            go_copy(to, member).start()
+
+        @pl.when(k == groups)
+        def _():
+            came[part(member), :] = block
+
+    d_state[...] = jnp.zeros_like(d_state)
+    grad_up_ref[...] = jnp.zeros_like(grad_up_ref)
+    grad_bias_ref[...] = jnp.zeros_like(grad_bias_ref)
+    line.run(5, 13)
+
+    @pl.loop(1, groups)
+    def _(k):
+        go_copy(0, lax.rem(member + k, groups)).wait_recv()
+
+    spans = held_ref.shape[0] // SPAN
+
+    @pl.loop(0, spans)
+    def _(i):
+        step = spans - 1 - i
+        place = one_hot(slot_row_ref[...], step * SPAN, (SPAN, slots), 0)
+        d_out = dot(place, came[...]).astype(bf16)
+        span_backward(
+            dk, dv, step, ends, d_out, held_ref, states_ref[step], up_ref, bias_ref, down_ref,
+            d_state, result, grad_up_ref, grad_bias_ref,
+        )
+        line.step(13 + 2 * i)
+        line.step(14 + 2 * i)
+
+    positions = result.shape[0]
+
+    @pl.loop(1, groups + 1)
+    def _(k):
+        to = lax.rem(member + k, groups)
+        pick = one_hot(slot_column_ref[part(to), :], 0, (cap, positions), 1)
+        block = dot(pick, result[...]).astype(bf16)
+
+        @pl.when(k < groups)
+        def _():
+            back_sent[part(to), :] = block
+            back_copy(to, member).start()
+
+        @pl.when(k == groups)
+        def _():
+            back_came[part(member), :] = block
+
+    line.run(13 + 2 * spans, line.steps)
+
+    @pl.loop(1, groups)
+    def _(k):
+        back_copy(0, lax.rem(member + k, groups)).wait_recv()
+
+    @pl.loop(0, 5)
+    def _(i):
+        rows = pl.ds(pl.multiple_of(i * tile, tile), tile)
+        pick = one_hot(send_column_ref[rows, :], 0, (tile, slots), 1)
+        d_rows_ref[rows, :] = dot(pick, back_came[...]).astype(bf16)
+
+    line.drain()
+
+    @pl.loop(1, groups)
+    def _(k):
+        to = lax.rem(member + k, groups)
+        go_copy(to, member).wait_send()
+        back_copy(to, member).wait_send()
+
+
+def recur_back(
+    call, n, groups, dk, dv, lengths, send_pos, slot_map, d_mixed, out_weight, attended, gate_pre,
+    head_gain, up_wide, bias, down_wide, held, states, share, hidden_own,
+):
+    count, width = d_mixed.shape
+    slots, wide = held.shape
+    half = count // 2
+    vmem = pl.BlockSpec(memory_space=pltpu.VMEM)
+    operands = [
+        lengths, send_pos.reshape(1, -1), send_pos.reshape(-1, 1), slot_map.reshape(1, -1),
+        slot_map.reshape(-1, 1), d_mixed, out_weight, attended, gate_pre, head_gain, up_wide, bias,
+        down_wide, held, states, share, hidden_own,
+    ]
+    return pl.pallas_call(
+        functools.partial(recur_back_kernel, n, groups, dk, dv),
+        in_specs=[pl.BlockSpec(memory_space=pltpu.SMEM)] + [vmem] * (len(operands) - 1),
+        out_specs=[vmem] * 6,
+        out_shape=[
+            jax.ShapeDtypeStruct((count, wide), bf16),
+            jax.ShapeDtypeStruct((count, dv), bf16),
+            jax.ShapeDtypeStruct((8, dv), f32),
+            jax.ShapeDtypeStruct((dk, LANES), f32),
+            jax.ShapeDtypeStruct((8, dk), f32),
+            jax.ShapeDtypeStruct((count, width), bf16),
+        ],
+        scratch_shapes=Line.scratch(half, width)
+        + [
+            pltpu.VMEM((count, dv), bf16),
+            pltpu.VMEM((slots, dv), bf16),
+            pltpu.VMEM((slots, dv), bf16),
+            pltpu.VMEM((dk, dv), f32),
+            pltpu.VMEM((slots, wide), bf16),
+            pltpu.VMEM((slots, wide), bf16),
+            pltpu.VMEM((slots, wide), bf16),
+            Line.semaphores(half),
+            pltpu.SemaphoreType.DMA((2, groups)),
+            pltpu.SemaphoreType.DMA((2, groups)),
+        ],
+        compiler_params=pltpu.CompilerParams(
+            collective_id=call, has_side_effects=True, vmem_limit_bytes=60 << 20
+        ),
+        cost_estimate=pl.CostEstimate(
+            flops=12_000_000_000, bytes_accessed=200_000_000, transcendentals=4_000_000
+        ),
+        name="recur_back",
     )(*operands)
 
 
@@ -1171,16 +1181,15 @@
     attended_slots, held, states = recur_forward(
         slot_map, lengths, up_wide, bias, arrived, dk, dv
     )
-    attended = dot(unpack, exchange(attended_slots))
-
+    attended = dot(unpack, exchange(attended_slots)).astype(bf16)
     head_gain_wide = head_gain.astype(f32)
-
-    def head_output(rows, gate_rows, gain_row):
-        scaling = lax.rsqrt(jnp.mean(rows * rows, axis=-1, keepdims=True) + head_floor)
-        return rows * scaling * gain_row * jax.nn.silu(gate_rows)
-
-    gated_wide, head_back = jax.vjp(head_output, attended, gate_pre, head_gain_wide)
-    gated = gated_wide.astype(bf16)
+    attended_wide = attended.astype(f32)
+    gated = (
+        attended_wide
+        * lax.rsqrt(jnp.mean(attended_wide * attended_wide, axis=-1, keepdims=True) + head_floor)
+        * head_gain_wide
+        * jax.nn.silu(gate_pre)
+    ).astype(bf16)
     mixer_share = dot(gated, out_weight).astype(bf16)
     feed_normed, hidden_own = line_sum(
         "norm", 1, lines, mixer_share, tokens_own, tokens_own, feed_gain_wide.reshape(1, -1)
@@ -1209,14 +1218,12 @@
             "back", 2, lines, feed_share, hidden_own, cotangent_own, feed_gain_wide.reshape(1, -1)
         )
 
-    d_gated = dot_t(d_mixed, out_weight)
-    d_attended, d_gate_pre, head_gain_part = head_back(d_gated)
-    d_gate_low = d_gate_pre.astype(bf16)
-    d_arrived = exchange(dot(pack, d_attended.astype(bf16)).astype(bf16))
-    d_slots, up_part, bias_part = recur_backward(
-        slot_map, lengths, up_wide, bias, down_wide, d_arrived, held, states, dk, dv
-    )
-    d_rows = dot(unpack, exchange(d_slots)).astype(bf16)
+    layer_share = dot(active, feed_down).astype(bf16)
+    d_rows, d_gate_low, head_gain_part, up_part, bias_part, layer_out = recur_back(
+        4, lines, groups, dk, dv, lengths, send_pos, slot_map, d_mixed, out_weight, attended,
+        gate_pre, head_gain_wide.reshape(1, -1), up_wide, bias, down_wide, held, states,
+        layer_share, hidden_own,
+    )
     d_query_low = d_rows[:, :dk]
     d_key_low = d_rows[:, dk : 2 * dk]
     d_value_low = d_rows[:, 2 * dk : 2 * dk + dv]
@@ -1248,12 +1255,6 @@
             "back", 3, lines, normed_share, tokens_own, d_hidden_own,
             mixer_gain_wide.reshape(1, -1),
         )
-    hidden_placed = jnp.concatenate(
-        [jnp.where(place == lines - 1, hidden_own, 0.0), jnp.where(place == 0, hidden_own, 0.0)],
-        axis=0,
-    )
-    layer_out = lax.psum((dot(active, feed_down) + hidden_placed).astype(bf16), "tensor")
-
     def halves(row_block, dims):
         split = row_block.reshape(row_block.shape[0], groups // 2, 2, dims // groups)
         keep = lax.dynamic_index_in_dim(split, parity, 2, keepdims=False)
@@ -1299,7 +1300,7 @@
         [
             by_owner(jnp.sum(mixer_gain_part, axis=0)),
             by_owner(jnp.sum(feed_gain_part, axis=0)),
-            by_owner(head_gain_part),
+            by_owner(jnp.sum(head_gain_part, axis=0)),
             by_owner(down_part),
         ],
         axis=1,

time: 609 us -> 574 us (0.943)
  Pallas kernels: 350 us -> 401 us
  waiting for transfers between devices: 66.5 us -> 27.2 us
  matrix products: 92.9 us -> 78.6 us
  between operations: 15.4 us -> 1.69 us
  starting transfers between devices: 23.2 us -> 9.87 us
    pallas_call x1, Pallas kernels: 20.5 us -> 98.4 us  [recur_back(): pl.pallas_call(functools.partial(recur_back_kernel, n, groups, dk, dv), i...]
    all_to_all x4 -> x2, waiting for transfers between devices: 66.5 us -> 27.2 us  [exchange(): lax.all_to_all(blocks, 'dp', split_axis=0, concat_axis=0, tiled=True)]
    pallas_call x2, Pallas kernels: 223 us -> 201 us  [sum_grads(): pl.pallas_call(functools.partial(sum_grads_kernel, n, plan), in_specs=[vm...]
    dot_general x14 -> x12, matrix products: 51.2 us -> 35.3 us  [dot(): return jnp.dot(left, right, preferred_element_type=f32)]
    all_to_all x4 -> x2, starting transfers between devices: 22.9 us -> 9.87 us  [exchange(): lax.all_to_all(blocks, 'dp', split_axis=0, concat_axis=0, tiled=True)]
    unnamed x143 -> x123, local copies, waits for them, and re-layouts: 26.9 us -> 18.5 us
    dot_general x9 -> x8, matrix products: 41 us -> 40.9 us  [dot_t(): lax.dot_general(left, right, (((1,), (1,)), ((), ())), preferred_element_...]
  transfers between devices with their start and end apart: 5 -> 2, of which waited for: 4 -> 2; matrix products, arithmetic and copies ran while one was open for 7% -> 3% of each run, Pallas kernels for 24% -> 0%
where the time goes in v4:
time: 574 us; the launch traced here: 565 us
  Pallas kernels  401 us (70%)
  matrix products  78.6 us (14%)
  local copies, waits for them, and re-layouts  37 us (6%)
  waiting for transfers between devices  27.2 us (5%)
  starting transfers between devices  9.87 us (2%)
  other arithmetic  9.84 us (2%)
    pallas_call x2, Pallas kernels, sum_grads(): pl.pallas_call(functools.partial(sum_grads_kernel, n, plan), in_specs=[vm...  201 us
    pallas_call x1, Pallas kernels, recur_back(): pl.pallas_call(functools.partial(recur_back_kernel, n, groups, dk, dv), i...  98.4 us
    pallas_call x1, Pallas kernels, line_sum(): pl.pallas_call(functools.partial(line_kernel, mode, n), in_specs=[vmem] *...  73.5 us
    dot_general x8, matrix products, dot_t(): lax.dot_general(left, right, (((1,), (1,)), ((), ())), preferred_element_...  40.9 us
    dot_general x12, matrix products, dot(): return jnp.dot(left, right, preferred_element_type=f32)  35.3 us
    all_to_all x2, waiting for transfers between devices, exchange(): lax.all_to_all(blocks, 'dp', split_axis=0, concat_axis=0, tiled=True)  27.2 us
    unnamed x123, local copies, waits for them, and re-layouts  18.5 us
    pallas_call x1, Pallas kernels, recur_forward(): pl.pallas_call(functools.partial(recur_forward_kernel, dk, dv), grid=(ste...  16 us
  transfers between devices with their start and end apart: 2, of which 2 were waited for; matrix products, arithmetic and copies ran while one was open for 3% of the time, Pallas kernels for 0%

profile of v4, /device:TPU:0, one launch (start us, length us, event | category | flops | bytes accessed | tf_op | source)
XLA Modules:
  0.0 564.7 jit_solution(16161272191534357794)
XLA Ops:
  2.4 2.3 fusion
  5.1 2.5 fusion.2.refs_4_
  7.7 1.0 convolution_convert_fusion.4
  8.7 1.0 copy-done.26
  9.7 1.0 convolution_convert_fusion.5
  11.3 1.8 convolution_convert_fusion.3
  14.2 3.6 convolution_convert_fusion
  17.8 5.3 all-to-all-start
  24.6 1.0 copy.63
  27.4 1.0 copy.61.slot_column_ref.refs_4_
  28.5 3.0 constant_dynamic-slice_fusion
  31.5 21.2 %all-to-all-done = bf16[8,128,1152]{2,1,0:T(8,128)(2,1)} async-done(((bf16[8,128,1152]{2,1,0:T(8,128)(2,1)}), bf16[8,128,1152]{2,1,0:T(8,128)(2,1)}, u32[]{:S(2)}, u32[]{:S(2)}) %all-to-all-start) | async-done | bytes 2359328 | tf_op jit(solution)/shard_map/all_to_all | solution.py:1139
  52.7 1.0 copy-done.3
  53.8 16.0 %recur_forward.1 = (bf16[1024,512]{1,0:T(8,128)(2,1)S(1)}, bf16[1024,1152]{1,0:T(8,128)(2,1)S(1)}, bf16[8,256,512]{2,1,0:T(8,128)(2,1)S(1)}) custom-call(s32[1,1024]{1,0:T(1,128)S(1)} %bitcast.68, s32[1024,1]{1,0:T(8,128)S(1)} %copy-done.3, s32[1,3]{1,0:T(1,128)S(1)} %copy-done.9, bf16[128,256]{1,0:T(8,128)(2,1)S(1)} %copy.58.up_ref.refs_10_, ...), custom_call_target="tpu_custom_call" | custom-call | flops 6000000000 | bytes 10000000 | tf_op jit(solution)/shard_map/recur_forward/pallas_call | solution.py:185
  69.7 1.0 copy-done.2
  70.7 1.5 copy-done.11
  72.1 1.3 copy-done.12
  73.5 4.6 all-to-all-start.1
  78.0 9.4 %fusion.67 = f32[640,1408]{1,0:T(8,128)} fusion(bf16[640,2048]{1,0:T(8,128)(2,1)} %refs_10_.1, bf16[1408,2048]{1,0:T(8,128)(2,1)} %param.35), kind=kOutput, calls=%fused_computation.125 | convolution fusion | flops 3690987520 | bytes 11993088 | tf_op jit(solution)/shard_map/dot_general | solution.py:26
  87.5 6.0 %all-to-all-done.1 = bf16[8,128,512]{2,1,0:T(8,128)(2,1)} async-done(((bf16[8,128,512]{2,1,0:T(8,128)(2,1)}), bf16[8,128,512]{2,1,0:T(8,128)(2,1)}, u32[]{:S(2)}, u32[]{:S(2)}) %all-to-all-start.1) | async-done | bytes 1048608 | tf_op jit(solution)/shard_map/all_to_all | solution.py:1139
  93.4 2.3 fusion.15
  95.9 2.7 fusion.18
  98.6 1.5 convolution_convert_fusion.2.refs_0_
  100.2 73.5 %line_norm.1 = (bf16[640,2048]{1,0:T(8,128)(2,1)S(1)}, f32[320,2048]{1,0:T(8,128)S(1)}) custom-call(bf16[640,2048]{1,0:T(8,128)(2,1)S(1)} %convolution_convert_fusion.2.refs_0_, bf16[320,2048]{1,0:T(8,128)(2,1)S(1)} %get-tuple-element.128.refs_1_.refs_2_, bf16[320,2048]{1,0:T(8,128)(2,1)S(1)} %get-tuple-element.128.refs_1_.refs_2_, f32[1,2048]{1,0:T(1,128)S(1)} %bitcast.65), custom_call_target="tpu_custom_call" | custom-call | flops 10000000 | bytes 200000000 | tf_op jit(solution)/shard_map/line_norm/pallas_call | solution.py:438
  173.8 6.0 %fusion.68 = f32[640,1408]{1,0:T(8,128)} fusion(bf16[640,2048]{1,0:T(8,128)(2,1)S(1)} %get-tuple-element.39.refs_4_, bf16[2048,1408]{1,0:T(8,128)(2,1)S(1)} %bitcast.84), kind=kOutput, calls=%fused_computation.126 | convolution fusion | flops 3690987520 | bytes 11993088 | tf_op jit(solution)/shard_map/dot_general | solution.py:30
  179.8 8.4 %multiply_convert_fusion = (bf16[640,1408]{1,0:T(8,128)(2,1)S(1)}, bf16[640,1408]{1,0:T(8,128)(2,1)S(1)}, bf16[640,1408]{1,0:T(8,128)(2,1)}) fusion(f32[640,1408]{1,0:T(8,128)} %fusion.68, f32[640,1408]{1,0:T(8,128)} %fusion.67, bf16[640,2048]{1,0:T(8,128)(2,1)S(1)} %get-tuple-element.39.refs_4_, bf16[2048,1408]{1,0:T(8,128)(2,1)S(1)} %bitcast.86), kind=kOutput, calls=%fused_computation.8 | convolution fusion | flops 3704504320 | bytes 21004288 | tf_op jit(solution)/shard_map/dot_general | solution.py:30
  188.3 5.6 convolution_convert_fusion.1.refs_15_
  193.8 4.2 fusion.69
  198.1 7.1 %add_convert_fusion.1.refs_0_ = bf16[640,2048]{1,0:T(8,128)(2,1)} fusion(f32[640,2048]{1,0:T(8,128)S(1)} %fusion.69, bf16[640,1408]{1,0:T(8,128)(2,1)} %get-tuple-element.110.refs_6_, bf16[2048,1408]{1,0:T(8,128)(2,1)S(1)} %bitcast.86), kind=kOutput, calls=%fused_computation.6 | convolution fusion | flops 3693608960 | bytes 15433728 | tf_op jit(solution)/shard_map/dot_general | solution.py:26
  205.2 89.5 %back_feed.1 = (bf16[640,2048]{1,0:T(8,128)(2,1)}, f32[320,2048]{1,0:T(8,128)}, f32[8,2048]{1,0:T(8,128)}, f32[256,1408]{1,0:T(8,128)}, f32[256,1408]{1,0:T(8,128)}) custom-call(bf16[640,2048]{1,0:T(8,128)(2,1)} %add_convert_fusion.1.refs_0_, f32[320,2048]{1,0:T(8,128)} %copy-done.7, bf16[320,2048]{1,0:T(8,128)(2,1)} %get-tuple-element.127.refs_2_, ...), custom_call_target="tpu_custom_call" | custom-call | flops 12000000000 | bytes 200000000 | tf_op jit(solution)/shard_map/back_feed/pallas_call | solution.py:758
  294.7 98.4 %recur_back.1 = (bf16[640,1152]{1,0:T(8,128)(2,1)}, bf16[640,512]{1,0:T(8,128)(2,1)}, f32[8,512]{1,0:T(8,128)}, f32[256,128]{1,0:T(8,128)}, f32[8,256]{1,0:T(8,128)}, /*index=5*/bf16[640,2048]{1,0:T(8,128)(2,1)}) custom-call(s32[1,3]{1,0:T(1,128)} %refs_0_.1, s32[1,640]{1,0:T(1,128)} %reshape.175.refs_1_, s32[640,1]{1,0:T(8,128)} %reshape.199.refs_2_, ...), custom_call_target="tpu_custom_call" | custom-call | flops 12000000000 | bytes 200000000 | tf_op jit(solution)/shard_map/recur_back/pallas_call | solution.py:942
  393.1 2.5 fusion.45
  396.0 3.9 fusion.22
  399.9 3.2 fusion.35
  403.0 3.3 fusion.37
  407.6 1.3 copy.65
  408.9 1.9 reshape.188
  410.8 2.8 fusion.70
  413.7 7.0 %add_convert_fusion.refs_0_ = bf16[640,2048]{1,0:T(8,128)(2,1)} fusion(f32[640,2048]{1,0:T(8,128)S(1)} %fusion.70, f32[640,2048]{1,0:T(8,128)} %fusion.22, f32[640,2048]{1,0:T(8,128)} %fusion.37, f32[640,2048]{1,0:T(8,128)S(1)} %bitcast.73, bf16[2048,32]{1,0:T(8,128)(2,1)S(1)} %copy-done.19, bf16[128]{0:T(256)(128)(2,1)S(1)} %pad.29.clone, ...), kind=kOutput, calls=%fused_computation.5 | convolution fusion | flops 343670784 | bytes 23888128 | tf_op jit(solution)/shard_map/dot_general | solution.py:26
  420.7 111.8 %back_mixer.1 = (bf16[640,2048]{1,0:T(8,128)(2,1)}, bf16[320,2048]{1,0:T(8,128)(2,1)}, f32[8,2048]{1,0:T(8,128)}, f32[256,1024]{1,0:T(8,128)}, f32[256,512]{1,0:...) custom-call(bf16[640,2048]{1,0:T(8,128)(2,1)} %add_convert_fusion.refs_0_, bf16[320,2048]{1,0:T(8,128)(2,1)} %copy-done.1, ...), custom_call_target="tpu_custom_call" | custom-call | flops 12000000000 | bytes 200000000 | tf_op jit(solution)/shard_map/back_mixer/pallas_call | solution.py:758
  534.4 11.3 %small_sum.1 = f32[48,128]{1,0:T(8,128)} custom-call(f32[8,48,128]{2,1,0:T(8,128)} %pad_maximum_fusion.part_ref), custom_call_target="tpu_custom_call" | custom-call | tf_op jit(solution)/shard_map/small_sum/pallas_call | solution.py:1059
  546.4 1.3 slice_bitcast_fusion.1
  549.1 1.9 slice.109
  554.4 3.7 copy.82
  558.1 1.5 copy.83
  561.2 1.1 copy.86
  562.3 1.1 copy.87
  563.4 1.1 copy.88
  (170 shorter events, 17.4 us)
Async XLA Ops:
  0.6 95.2 %copy-start = (bf16[2048,512]{1,0:T(8,128)(2,1)S(1)}, bf16[2048,512]{1,0:T(8,128)(2,1)}, u32[]{:S(2)}) copy-start(bf16[2048,512]{1,0:T(8,128)(2,1)} %param.26) | copy-start | bytes 6291460
  0.7 4.4 copy-start.31
  0.7 4.1 copy-start.37
  4.8 2.9 copy-start.34
  5.1 2.5 copy-start.24
  7.7 5.6 copy-start.13
  17.8 7.9 %copy-start.42 = (bf16[256]{0:T(256)(128)(2,1)S(1)}, bf16[256]{0:T(256)(128)(2,1)}, u32[]{:S(2)}) copy-start(bf16[256]{0:T(256)(128)(2,1)} %param.29) | copy-start | bytes 1540
  17.8 7.9 %copy-start.40 = (bf16[512]{0:T(512)(128)(2,1)S(1)}, bf16[512]{0:T(512)(128)(2,1)}, u32[]{:S(2)}) copy-start(bf16[512]{0:T(512)(128)(2,1)} %param.30) | copy-start | bytes 3076
  17.8 7.9 %copy-start.38 = (bf16[2048]{0:T(1024)(128)(2,1)S(1)}, bf16[2048]{0:T(1024)(128)(2,1)}, u32[]{:S(2)}) copy-start(bf16[2048]{0:T(1024)(128)(2,1)} %param.32) | copy-start | bytes 12292
  17.8 8.0 %copy-start.36 = (bf16[256,16]{0,1:T(8,128)(2,1)S(1)}, bf16[256,16]{0,1:T(8,128)(2,1)}, u32[]{:S(2)}) copy-start(bf16[256,16]{0,1:T(8,128)(2,1)} %param.28) | copy-start | bytes 24580
  17.8 34.9 %all-to-all-start = ((bf16[8,128,1152]{2,1,0:T(8,128)(2,1)}), bf16[8,128,1152]{2,1,0:T(8,128)(2,1)}, u32[]{:S(2)}, u32[]{:S(2)}) async-start(bf16[8,128,1152]{2,1,0:T(8,128)(2,1)} %bitcast.74), calls=%async_computation | async-start | bytes 4718592 | tf_op jit(solution)/shard_map/all_to_all | solution.py:1139
  25.7 27.0 %copy-start.10 = (f32[256]{0:T(256)}, f32[256]{0:T(256)S(1)}, u32[]{:S(2)}) copy-start(f32[256]{0:T(256)S(1)} %reshape.195) | copy-start | bytes 3076
  25.7 70.1 %copy-start.39 = (f32[512]{0:T(512)}, f32[512]{0:T(512)S(1)}, u32[]{:S(2)}) copy-start(f32[512]{0:T(512)S(1)} %convert_element_type.108) | copy-start | bytes 6148
  25.7 74.4 %copy-start.5 = (f32[2048]{0:T(1024)}, f32[2048]{0:T(1024)S(1)}, u32[]{:S(2)}) copy-start(f32[2048]{0:T(1024)S(1)} %reshape.197) | copy-start | bytes 24580
  26.8 25.9 %copy-start.4 = (bf16[128,256]{1,0:T(8,128)(2,1)}, bf16[128,256]{1,0:T(8,128)(2,1)S(1)}, u32[]{:S(2)}) copy-start(bf16[128,256]{1,0:T(8,128)(2,1)S(1)} %copy.58.up_ref.refs_10_) | copy-start | bytes 196612
  27.4 25.3 %copy-start.6 = (s32[8,128]{1,0:T(8,128)}, s32[8,128]{1,0:T(8,128)S(1)}, u32[]{:S(2)}) copy-start(s32[8,128]{1,0:T(8,128)S(1)} %broadcast_add_fusion) | copy-start | bytes 12292
  28.4 24.2 %copy-start.9 = (s32[1,3]{1,0:T(1,128)S(1)}, s32[1,3]{1,0:T(1,128)}, u32[]{:S(2)}) copy-start(s32[1,3]{1,0:T(1,128)} %refs_0_.1) | copy-start | bytes 40
  31.5 68.7 %copy-start.1 = (bf16[320,2048]{1,0:T(8,128)(2,1)}, bf16[320,2048]{1,0:T(8,128)(2,1)S(1)}, u32[]{:S(2)}) copy-start(bf16[320,2048]{1,0:T(8,128)(2,1)S(1)} %get-tuple-element.128.refs_1_.refs_2_) | copy-start | bytes 3932164
  73.5 20.0 %all-to-all-start.1 = ((bf16[8,128,512]{2,1,0:T(8,128)(2,1)}), bf16[8,128,512]{2,1,0:T(8,128)(2,1)}, u32[]{:S(2)}, u32[]{:S(2)}) async-start(bf16[8,128,512]{2,1,0:T(8,128)(2,1)} %bitcast.64), calls=%async_computation.1 | async-start | bytes 2097152 | tf_op jit(solution)/shard_map/all_to_all | solution.py:1139
  93.4 2.4 copy-start.14
  93.4 80.3 %slice-start.4 = ((s8[5767168]{0:T(1024)(128)(4,1)}), s8[4194304]{0:T(1024)(128)(4,1)S(1)}, s32[]{:S(2)}) async-start(s8[5767168]{0:T(1024)(128)(4,1)} %bitcast.83), calls=%async_computation.6 | async-start | bytes 8388608
  95.8 2.8 copy-start.43
  95.8 2.8 copy-start.41
  95.8 77.9 %slice-start.5 = ((s8[5767168]{0:T(1024)(128)(4,1)}), s8[1572864]{0:T(1024)(128)(4,1)S(1)}, s32[]{:S(2)}) async-start(s8[5767168]{0:T(1024)(128)(4,1)} %bitcast.83), calls=%async_computation.7 | async-start | bytes 3145728
  100.2 79.6 %slice-start.6 = ((s8[5767168]{0:T(1024)(128)(4,1)}), s8[4194304]{0:T(1024)(128)(4,1)S(1)}, s32[]{:S(2)}) async-start(s8[5767168]{0:T(1024)(128)(4,1)} %bitcast.85), calls=%async_computation.8 | async-start | bytes 8388608
  173.7 6.1 %copy-start.7 = (f32[320,2048]{1,0:T(8,128)}, f32[320,2048]{1,0:T(8,128)S(1)}, u32[]{:S(2)}) copy-start(f32[320,2048]{1,0:T(8,128)S(1)} %get-tuple-element.40.refs_1_.refs_16_) | copy-start | bytes 7864324
  173.7 6.1 %copy-start.8 = (bf16[640,2048]{1,0:T(8,128)(2,1)}, bf16[640,2048]{1,0:T(8,128)(2,1)S(1)}, u32[]{:S(2)}) copy-start(bf16[640,2048]{1,0:T(8,128)(2,1)S(1)} %get-tuple-element.39.refs_4_) | copy-start | bytes 7864324
  173.8 6.0 %slice-start.7 = ((s8[5767168]{0:T(1024)(128)(4,1)}), s8[1572864]{0:T(1024)(128)(4,1)S(1)}, s32[]{:S(2)}) async-start(s8[5767168]{0:T(1024)(128)(4,1)} %bitcast.85), calls=%async_computation.9 | async-start | bytes 3145728
  173.8 14.5 %slice-start.2 = ((s8[5767168]{0:T(1024)(128)(4,1)}), s8[4194304]{0:T(1024)(128)(4,1)S(1)}, s32[]{:S(2)}) async-start(s8[5767168]{0:T(1024)(128)(4,1)} %bitcast.81), calls=%async_computation.4 | async-start | bytes 8388608
  179.8 8.5 %slice-start.3 = ((s8[5767168]{0:T(1024)(128)(4,1)}), s8[1572864]{0:T(1024)(128)(4,1)S(1)}, s32[]{:S(2)}) async-start(s8[5767168]{0:T(1024)(128)(4,1)} %bitcast.81), calls=%async_computation.5 | async-start | bytes 3145728
  188.3 5.6 copy-start.46
  188.3 5.6 copy-start.45
  393.1 2.5 copy-start.15
  393.1 2.9 copy-start.18
  396.0 3.9 copy-start.25
  399.9 3.2 copy-start.27
  403.0 4.0 copy-start.35
  403.0 4.2 copy-start.33
  403.0 4.2 copy-start.23
  408.9 4.7 slice-start
  410.8 2.8 slice-start.1
  410.8 2.8 copy-start.19
  532.5 18.5 %copy-start.28 = (f32[256,1024]{1,0:T(8,128)S(1)}, f32[256,1024]{1,0:T(8,128)}, u32[]{:S(2)}) copy-start(f32[256,1024]{1,0:T(8,128)} %get-tuple-element.54) | copy-start | bytes 3145732
  554.4 3.7 copy-start.16
  558.1 2.3 copy-start.29
  558.1 3.1 copy-start.21
  559.6 2.7 copy-start.20
  561.2 2.2 copy-start.22
  (9 other events, 13.3 us)

commit v5 on v4

--- a/solution.py
+++ b/solution.py
@@ -255,6 +255,19 @@
         def _():
             pl.semaphore_wait(barrier, others + 1)
 
+    def greet_all(self, barrier, others):
+        n, me = self.n, self.me
+
+        @pl.when(me > 0)
+        def _():
+            pl.semaphore_signal(barrier, inc=1, device_id={"tensor": me - 1}, device_id_type=MESH)
+
+        @pl.when(me < n - 1)
+        def _():
+            pl.semaphore_signal(barrier, inc=1, device_id={"tensor": me + 1}, device_id_type=MESH)
+
+        pl.semaphore_wait(barrier, others + n - 1)
+
     def at(self, g):
         return pl.ds(pl.multiple_of(g * FINE, FINE), FINE)
 
@@ -455,24 +468,261 @@
     return index + 1 - 2 * lax.rem(index, 2)
 
 
-class GradPlan:
-    def __init__(self, groups, count, width, row_widths, row_tiles, col_rows):
-        self.groups, self.count, self.width = groups, count, width
+def to_dp(source, target, send, recv, device):
+    return pltpu.make_async_remote_copy(
+        source, target, send, recv, device_id={"dp": device}, device_id_type=MESH
+    )
+
+
+def greet_dp(barrier, groups):
+    member = lax.axis_index("dp")
+
+    @pl.loop(1, groups)
+    def _(k):
+        pl.semaphore_signal(
+            barrier, inc=1, device_id={"dp": lax.rem(member + k, groups)}, device_id_type=MESH
+        )
+
+
+class ColGrad:
+    TILE = 256
+
+    def __init__(self, groups, left, right, out, refs):
+        (
+            self.left, self.right, self.left_in, self.right_in, self.send, self.recv,
+            self.load_sems, self.pair_sems, self.sems,
+        ) = refs
+        self.left_far, self.right_far, self.out, self.groups = left, right, out, groups
+        self.member = lax.axis_index("dp")
+        self.parity = lax.rem(self.member, 2)
+        self.half = self.right_in.shape[1]
+        self.size = self.send.shape[0] // groups
+        self.items = self.half // self.TILE
+
+    @staticmethod
+    def scratch(groups, count, rows, width):
+        half = width // 2
+        return [
+            pltpu.VMEM((count, rows), bf16),
+            pltpu.VMEM((count, half), bf16),
+            pltpu.VMEM((count, rows), bf16),
+            pltpu.VMEM((count, half), bf16),
+            pltpu.VMEM((rows, half), bf16),
+            pltpu.VMEM((groups, rows // groups, half), bf16),
+            pltpu.SemaphoreType.DMA((2,)),
+            pltpu.SemaphoreType.DMA((2, 2)),
+            pltpu.SemaphoreType.DMA((2, groups)),
+        ]
+
+    def halves(self, parity):
+        return self.right_far.at[:, pl.ds(pl.multiple_of(parity * self.half, self.half), self.half)]
+
+    def loads(self):
+        return (
+            pltpu.make_async_copy(self.left_far, self.left, self.load_sems.at[0]),
+            pltpu.make_async_copy(self.halves(self.parity), self.right, self.load_sems.at[1]),
+        )
+
+    def pair_copies(self):
+        partner = partner_of(self.member)
+        sems = self.pair_sems
+        return (
+            to_dp(self.left_far, self.left_in, sems.at[0, 0], sems.at[1, 0], partner),
+            to_dp(
+                self.halves(1 - self.parity), self.right_in, sems.at[0, 1], sems.at[1, 1], partner
+            ),
+        )
+
+    def start(self):
+        for c in self.pair_copies() + self.loads():
+            c.start()
+
+    def ready(self):
+        for c in self.loads():
+            c.wait()
+        for c in self.pair_copies():
+            c.wait_recv()
+
+    def item(self, t):
+        span = pl.ds(pl.multiple_of(t * self.TILE, self.TILE), self.TILE)
+        product = rows_dot(self.left[...], self.right[:, span]) + rows_dot(
+            self.left_in[...], self.right_in[:, span]
+        )
+        self.send[:, span] = product.astype(bf16)
+
+    def copy(self, to, source):
+        rows = pl.ds(pl.multiple_of(to * self.size, 16), self.size)
+        return to_dp(
+            self.send.at[rows, :], self.recv.at[source], self.sems.at[0, to],
+            self.sems.at[1, source], to,
+        )
+
+    def send_all(self):
+        @pl.loop(1, self.groups)
+        def _(k):
+            self.copy(lax.rem(self.member + k, self.groups), self.member).start()
+
+        own = pl.ds(pl.multiple_of(self.member * self.size, 16), self.size)
+        self.recv[pl.ds(self.member, 1)] = self.send[own, :][None]
+
+    def receive(self):
+        @pl.loop(1, self.groups)
+        def _(k):
+            self.copy(0, lax.rem(self.member + k, self.groups)).wait_recv()
+
+        for b in range(2):
+            total = self.recv[b].astype(f32)
+            for q in range(1, self.groups // 2):
+                total = total + self.recv[2 * q + b].astype(f32)
+            self.out[:, b * self.half : (b + 1) * self.half] = total
+
+    def drain(self):
+        for c in self.pair_copies():
+            c.wait_send()
+
+        @pl.loop(1, self.groups)
+        def _(k):
+            self.copy(lax.rem(self.member + k, self.groups), self.member).wait_send()
+
+
+class RowGrads:
+    def __init__(self, groups, left, parts, tiles, outs, outputs, refs):
+        (
+            self.left, self.all, self.left_in, self.all_in, self.send, self.recv,
+            self.load_sems, self.left_sems, self.part_sems, self.sems,
+        ) = refs
+        self.left_far, self.parts, self.tiles = left, parts, tiles
+        self.outs, self.outputs = outs, outputs
+        self.member = lax.axis_index("dp")
+        self.parity = lax.rem(self.member, 2)
+        self.mine = self.member // 2
         self.team = groups // 2
-        self.block = width // groups
-        self.half = width // 2
-        self.row_widths, self.row_tiles, self.col_rows = row_widths, row_tiles, col_rows
-        self.offsets = []
-        total = 0
-        for wide in row_widths:
-            self.offsets.append(total)
-            total += wide
-        self.total = total
-        self.col_tile = 256
-        self.col_steps = self.half // self.col_tile
-
-
-def sum_grads_kernel(n, plan, *refs):
+        self.block = left.shape[1] // groups
+        self.offsets = [0]
+        for part in parts:
+            self.offsets.append(self.offsets[-1] + part.shape[1])
+        self.items = self.team * len(tiles)
+
+    @staticmethod
+    def scratch(groups, count, width, total, parts, tiles):
+        team = groups // 2
+        return [
+            pltpu.VMEM((count, width), bf16),
+            pltpu.VMEM((count, total), bf16),
+            pltpu.VMEM((count, width // 2), bf16),
+            pltpu.VMEM((count, total), bf16),
+            pltpu.VMEM((team, width // groups, total), bf16),
+            pltpu.VMEM((team, width // groups, total), bf16),
+            pltpu.SemaphoreType.DMA((1 + parts,)),
+            pltpu.SemaphoreType.DMA((2, team)),
+            pltpu.SemaphoreType.DMA((2, parts)),
+            pltpu.SemaphoreType.DMA((2, tiles, team)),
+        ]
+
+    def columns(self, j):
+        return pl.ds(pl.multiple_of(j * self.block, self.block), self.block)
+
+    def left_load(self):
+        return pltpu.make_async_copy(self.left_far, self.left, self.load_sems.at[0])
+
+    def part_columns(self, i):
+        return pl.ds(self.offsets[i], self.offsets[i + 1] - self.offsets[i])
+
+    def part_load(self, i):
+        return pltpu.make_async_copy(
+            self.parts[i], self.all.at[:, self.part_columns(i)], self.load_sems.at[1 + i]
+        )
+
+    def left_copy(self, q):
+        return to_dp(
+            self.left_far.at[:, self.columns(2 * q + 1 - self.parity)],
+            self.left_in.at[:, self.columns(q)],
+            self.left_sems.at[0, q], self.left_sems.at[1, q], partner_of(self.member),
+        )
+
+    def part_copy(self, i):
+        return to_dp(
+            self.parts[i], self.all_in.at[:, self.part_columns(i)],
+            self.part_sems.at[0, i], self.part_sems.at[1, i], partner_of(self.member),
+        )
+
+    def start_left(self):
+        @pl.loop(0, self.team)
+        def _(q):
+            self.left_copy(q).start()
+
+        self.left_load().start()
+
+    def start_part(self, i):
+        self.part_copy(i).start()
+        self.part_load(i).start()
+
+    def ready_left(self):
+        self.left_load().wait()
+
+        @pl.loop(0, self.team)
+        def _(q):
+            self.left_copy(q).wait_recv()
+
+    def copy(self, t, to, source):
+        start, wide = self.tiles[t]
+        span = pl.ds(start, wide)
+        return to_dp(
+            self.send.at[to, :, span], self.recv.at[source, :, span],
+            self.sems.at[0, t, to], self.sems.at[1, t, source], 2 * to + self.parity,
+        )
+
+    def item(self, w):
+        count = len(self.tiles)
+        k = w // count
+        to = lax.rem(self.mine + 1 + k, self.team)
+        for t in range(count):
+            start, wide = self.tiles[t]
+
+            @pl.when((w >= 0) & (w < self.items) & (lax.rem(w, count) == t))
+            def _():
+                span = pl.ds(start, wide)
+                product = rows_dot(
+                    self.left[:, self.columns(2 * to + self.parity)], self.all[:, span]
+                ) + rows_dot(self.left_in[:, self.columns(to)], self.all_in[:, span])
+                low_product = product.astype(bf16)
+
+                @pl.when(k < self.team - 1)
+                def _():
+                    self.send[to, :, span] = low_product
+                    self.copy(t, to, self.mine).start()
+
+                @pl.when(k == self.team - 1)
+                def _():
+                    self.recv[self.mine, :, span] = low_product
+
+    def receive(self):
+        for t in range(len(self.tiles)):
+            @pl.loop(1, self.team)
+            def _(k):
+                self.copy(t, 0, lax.rem(self.mine + k, self.team)).wait_recv()
+
+        for (start, wide), output in zip(self.outs, self.outputs):
+            span = pl.ds(start, wide)
+            total = self.recv[0, :, span].astype(f32)
+            for q in range(1, self.team):
+                total = total + self.recv[q, :, span].astype(f32)
+            output[...] = total
+
+    def drain(self):
+        @pl.loop(0, self.team)
+        def _(q):
+            self.left_copy(q).wait_send()
+
+        for i in range(len(self.parts)):
+            self.part_copy(i).wait_send()
+        for t in range(len(self.tiles)):
+            @pl.loop(1, self.team)
+            def _(k):
+                self.copy(t, lax.rem(self.mine + k, self.team), self.mine).wait_send()
+
+
+def splitter(refs):
     refs = list(refs)
 
     def take(k):
@@ -480,310 +730,384 @@
         del refs[:k]
         return out
 
-    rows, cols = len(plan.row_widths), len(plan.col_rows)
-    share_ref, x_ref, base_ref, gain_ref, left_ref = take(5)
-    right_refs = take(rows)
-    col_lefts = take(cols)
-    col_rights = take(cols)
+    return take
+
+
+def back_feed_kernel(n, groups, tiles, outs, *refs):
+    take = splitter(refs)
+    share_ref, gain_ref, x_far, base_far, left_far = take(5)
+    parts = take(2)
     out_ref, kept_ref, gain_grad_ref = take(3)
-    row_outs = take(rows)
-    col_outs = take(cols)
-    up_in, down_in, left_in = take(3)
-    right_in = take(rows)
-    col_left_in = take(cols)
-    col_right_in = take(cols)
-    row_send, row_recv = take(2)
-    col_send = take(cols)
-    col_recv = take(cols)
-    sems, left_sems, right_sems, row_sems = take(4)
-    if cols:
-        pair_sems, col_sems = take(2)
-
-    member = lax.axis_index("dp")
-    parity = lax.rem(member, 2)
-    mine = member // 2
-    partner = partner_of(member)
-    groups, team, block = plan.groups, plan.team, plan.block
+    outputs = take(2)
+    up_in, down_in, x_ref, base_ref, load_sems, sems = take(6)
+    rows = RowGrads(groups, left_far, parts, tiles, outs, outputs, take(10))
     finish = norm_back(x_ref, base_ref, gain_ref, out_ref, kept_ref, gain_grad_ref)
     line = Line(n, share_ref, up_in, down_in, out_ref, sems, finish)
-
+    loads = (
+        pltpu.make_async_copy(x_far, x_ref, load_sems.at[0]),
+        pltpu.make_async_copy(base_far, base_ref, load_sems.at[1]),
+    )
     barrier = pltpu.get_barrier_semaphore()
-    if cols:
-        greeted = groups - 1
-
-        @pl.loop(1, groups)
-        def _(k):
-            pl.semaphore_signal(
-                barrier, inc=1, device_id={"dp": lax.rem(member + k, groups)}, device_id_type=MESH
-            )
-    else:
-        greeted = team
-        pl.semaphore_signal(barrier, inc=1, device_id={"dp": partner}, device_id_type=MESH)
-
-        @pl.loop(1, team)
-        def _(k):
-            pl.semaphore_signal(
-                barrier, inc=1, device_id={"dp": 2 * lax.rem(mine + k, team) + parity},
-                device_id_type=MESH,
-            )
-    line.greet(barrier, greeted)
-
-    def to_partner(source, target, send, recv):
-        return pltpu.make_async_remote_copy(
-            source, target, send, recv, device_id={"dp": partner}, device_id_type=MESH
-        )
-
-    def columns(j):
-        return pl.ds(pl.multiple_of(j * block, block), block)
-
-    def left_copy(q):
-        return to_partner(
-            left_ref.at[:, columns(2 * q + 1 - parity)], left_in.at[:, columns(q)],
-            left_sems.at[0, q], left_sems.at[1, q],
-        )
-
-    def right_copy(i):
-        return to_partner(
-            right_refs[i].at[:, : plan.row_widths[i]], right_in[i],
-            right_sems.at[0, i], right_sems.at[1, i],
-        )
-
-    half_of = pl.ds(pl.multiple_of(parity * plan.half, plan.half), plan.half)
-    other_half = pl.ds(pl.multiple_of((1 - parity) * plan.half, plan.half), plan.half)
-
-    def pair_copies(i):
-        return (
-            to_partner(
-                col_lefts[i], col_left_in[i], pair_sems.at[0, 2 * i], pair_sems.at[1, 2 * i]
-            ),
-            to_partner(
-                col_rights[i].at[:, other_half], col_right_in[i],
-                pair_sems.at[0, 2 * i + 1], pair_sems.at[1, 2 * i + 1],
-            ),
-        )
-
-    def tile_columns(t):
-        i, start, wide = plan.row_tiles[t]
-        return pl.ds(plan.offsets[i] + start, wide)
-
-    def row_copy(t, to, source):
-        return pltpu.make_async_remote_copy(
-            row_send.at[to, :, tile_columns(t)], row_recv.at[source, :, tile_columns(t)],
-            row_sems.at[0, t, to], row_sems.at[1, t, source],
-            device_id={"dp": 2 * to + parity}, device_id_type=MESH,
-        )
-
-    def col_copy(i, to, source):
-        size = plan.col_rows[i] // groups
-        return pltpu.make_async_remote_copy(
-            col_send[i].at[pl.ds(pl.multiple_of(to * size, 16), size), :],
-            col_recv[i].at[source],
-            col_sems.at[0, i, to], col_sems.at[1, i, source],
-            device_id={"dp": to}, device_id_type=MESH,
-        )
-
+    greet_dp(barrier, groups)
+    line.greet(barrier, groups - 1)
     line.prime()
-    for i in range(cols):
-        for c in pair_copies(i):
-            c.start()
-    for i in range(rows):
-        right_copy(i).start()
-
-    @pl.loop(0, team)
-    def _(q):
-        left_copy(q).start()
-
-    tiles = len(plan.row_tiles)
-    col_items = cols * plan.col_steps
-    items = col_items + team * tiles
-
-    def work(w):
-        for i in range(cols):
-            base = i * plan.col_steps
-
-            @pl.when(w == base)
-            def _():
-                for c in pair_copies(i):
-                    c.wait_recv()
-
-            @pl.when((w >= base) & (w < base + plan.col_steps))
-            def _():
-                offset = pl.multiple_of((w - base) * plan.col_tile, plan.col_tile)
-                own = pl.ds(
-                    pl.multiple_of(parity * plan.half + offset, plan.col_tile), plan.col_tile
-                )
-                there = pl.ds(offset, plan.col_tile)
-                product = rows_dot(col_lefts[i][...], col_rights[i][:, own]) + rows_dot(
-                    col_left_in[i][...], col_right_in[i][:, there]
-                )
-                col_send[i][:, there] = product.astype(bf16)
-
-            @pl.when(w == base + plan.col_steps - 1)
-            def _():
-                @pl.loop(1, groups)
-                def _(k):
-                    col_copy(i, lax.rem(member + k, groups), member).start()
-
-        r = w - col_items
-
-        @pl.when(r == 0)
-        def _():
-            for i in range(rows):
-                right_copy(i).wait_recv()
-
-            @pl.loop(0, team)
-            def _(q):
-                left_copy(q).wait_recv()
-
-        k = r // tiles
-        to = lax.rem(mine + 1 + k, team)
-        for t in range(tiles):
-            i, start, wide = plan.row_tiles[t]
-
-            @pl.when((r >= 0) & (r < team * tiles) & (lax.rem(r, tiles) == t))
-            def _():
-                span = pl.ds(start, wide)
-                product = rows_dot(
-                    left_ref[:, columns(2 * to + parity)], right_refs[i][:, span]
-                ) + rows_dot(left_in[:, columns(to)], right_in[i][:, span])
-                low_product = product.astype(bf16)
-
-                @pl.when(k < team - 1)
-                def _():
-                    row_send[to, :, tile_columns(t)] = low_product
-                    row_copy(t, to, mine).start()
-
-                @pl.when(k == team - 1)
-                def _():
-                    row_recv[mine, :, tile_columns(t)] = low_product
-
-    start_work = 8
+    rows.start_left()
+    for i in range(2):
+        rows.start_part(i)
+    for c in loads:
+        c.start()
+    for c in loads:
+        c.wait()
+    first_work = 3
 
     @pl.loop(0, line.steps)
     def _(step):
         line.step(step)
-        work(step - start_work)
-
-    for i in range(cols):
-        size = plan.col_rows[i] // groups
-        own_rows = pl.ds(pl.multiple_of(member * size, 16), size)
-        col_recv[i][pl.ds(member, 1)] = col_send[i][own_rows, :][None]
-
-        @pl.loop(1, groups)
-        def _(k):
-            col_copy(i, 0, lax.rem(member + k, groups)).wait_recv()
-
-        for b in range(2):
-            total = col_recv[i][b].astype(f32)
-            for q in range(1, team):
-                total = total + col_recv[i][2 * q + b].astype(f32)
-            col_outs[i][:, b * plan.half : (b + 1) * plan.half] = total
-    for t in range(tiles):
-        @pl.loop(1, team)
-        def _(k):
-            row_copy(t, 0, lax.rem(mine + k, team)).wait_recv()
-    for i in range(rows):
-        span = pl.ds(plan.offsets[i], plan.row_widths[i])
-        total = row_recv[0, :, span].astype(f32)
-        for q in range(1, team):
-            total = total + row_recv[q, :, span].astype(f32)
-        row_outs[i][...] = total
-
+        w = step - first_work
+
+        @pl.when(w == 0)
+        def _():
+            rows.ready_left()
+            rows.part_load(0).wait()
+            rows.part_copy(0).wait_recv()
+
+        @pl.when(w == len(tiles) // 2)
+        def _():
+            rows.part_load(1).wait()
+            rows.part_copy(1).wait_recv()
+
+        rows.item(w)
+
+    rows.receive()
     line.drain()
-    for i in range(cols):
-        for c in pair_copies(i):
-            c.wait_send()
-
-        @pl.loop(1, groups)
-        def _(k):
-            col_copy(i, lax.rem(member + k, groups), member).wait_send()
-    for i in range(rows):
-        right_copy(i).wait_send()
-
-    @pl.loop(0, team)
-    def _(q):
-        left_copy(q).wait_send()
-
-    for t in range(tiles):
-        @pl.loop(1, team)
-        def _(k):
-            row_copy(t, lax.rem(mine + k, team), mine).wait_send()
-
-
-def tiles_of(widths, most):
-    return [
-        (i, start, min(most, wide - start))
-        for i, wide in enumerate(widths)
-        for start in range(0, wide, most)
-    ]
-
-
-def sum_grads(
-    name, call, n, groups, share, x_own, base_own, gain, kept_type, row_left, row_rights, row_widths,
-    row_tiles, col_pairs,
-):
+    rows.drain()
+
+
+def back_feed(call, n, groups, share, gain, x_own, base_own, left, parts):
     count, width = share.shape
     half = count // 2
-    col_rows = [pair[0].shape[1] for pair in col_pairs]
-    plan = GradPlan(groups, count, width, row_widths, row_tiles, col_rows)
-    team = plan.team
+    wide = parts[0].shape[1]
+    cut = (wide // 2 + LANES - 1) // LANES * LANES
+    tiles = [(0, cut), (cut, wide - cut), (wide, cut), (wide + cut, wide - cut)]
+    outs = [(0, wide), (wide, wide)]
     vmem = pl.BlockSpec(memory_space=pltpu.VMEM)
-    outs = [
-        jax.ShapeDtypeStruct((count, width), bf16),
-        jax.ShapeDtypeStruct((half, width), kept_type),
-        jax.ShapeDtypeStruct((8, width), f32),
-    ]
-    outs += [jax.ShapeDtypeStruct((plan.block, wide), f32) for wide in row_widths]
-    outs += [jax.ShapeDtypeStruct((r // groups, width), f32) for r in col_rows]
-    scratch = Line.scratch(half, width) + [pltpu.VMEM((count, plan.half), bf16)]
-    scratch += [pltpu.VMEM((count, wide), bf16) for wide in row_widths]
-    scratch += [pltpu.VMEM((count, r), bf16) for r in col_rows]
-    scratch += [pltpu.VMEM((count, plan.half), bf16) for _ in col_rows]
-    scratch += [pltpu.VMEM((team, plan.block, plan.total), bf16)] * 2
-    scratch += [pltpu.VMEM((r, plan.half), bf16) for r in col_rows]
-    scratch += [pltpu.VMEM((groups, r // groups, plan.half), bf16) for r in col_rows]
-    scratch += [
-        Line.semaphores(half),
-        pltpu.SemaphoreType.DMA((2, team)),
-        pltpu.SemaphoreType.DMA((2, len(row_widths))),
-        pltpu.SemaphoreType.DMA((2, len(row_tiles), team)),
-    ]
-    if col_rows:
-        scratch += [
-            pltpu.SemaphoreType.DMA((2, 2 * len(col_rows))),
-            pltpu.SemaphoreType.DMA((2, len(col_rows), groups)),
+    far = pl.BlockSpec(memory_space=pl.ANY)
+    return pl.pallas_call(
+        functools.partial(back_feed_kernel, n, groups, tiles, outs),
+        in_specs=[vmem] * 2 + [far] * 5,
+        out_specs=[vmem] * 5,
+        out_shape=[
+            jax.ShapeDtypeStruct((count, width), bf16),
+            jax.ShapeDtypeStruct((half, width), f32),
+            jax.ShapeDtypeStruct((8, width), f32),
+            jax.ShapeDtypeStruct((width // groups, wide), f32),
+            jax.ShapeDtypeStruct((width // groups, wide), f32),
+        ],
+        scratch_shapes=Line.scratch(half, width)
+        + [
+            pltpu.VMEM((half, width), x_own.dtype),
+            pltpu.VMEM((half, width), base_own.dtype),
+            pltpu.SemaphoreType.DMA((2,)),
+            Line.semaphores(half),
         ]
-    operands = [share, x_own, base_own, gain, row_left, *row_rights]
-    operands += [pair[0] for pair in col_pairs] + [pair[1] for pair in col_pairs]
-    return pl.pallas_call(
-        functools.partial(sum_grads_kernel, n, plan),
-        in_specs=[vmem] * len(operands),
-        out_specs=[vmem] * len(outs),
-        out_shape=outs,
-        scratch_shapes=scratch,
+        + RowGrads.scratch(groups, count, width, 2 * wide, 2, len(tiles)),
         compiler_params=pltpu.CompilerParams(
             collective_id=call, has_side_effects=True, vmem_limit_bytes=60 << 20
         ),
         cost_estimate=pl.CostEstimate(
             flops=12_000_000_000, bytes_accessed=200_000_000, transcendentals=0
         ),
-        name=name,
-    )(*operands)
+        name="back_feed",
+    )(share, gain, x_own, base_own, left, *parts)
+
+
+class SmallSum:
+    def __init__(self, n, groups, wide, near, near_all, wide_out, near_out, refs):
+        (
+            self.wide_in, self.near_in, self.wide_line, self.near_line, self.sems, self.line_sems,
+        ) = refs
+        self.n, self.groups, self.near_all = n, groups, near_all
+        self.wide, self.near, self.wide_out, self.near_out = wide, near, wide_out, near_out
+        self.member, self.place = lax.axis_index("dp"), lax.axis_index("tensor")
+        self.block = wide.shape[1] // groups
+
+    @staticmethod
+    def scratch(n, groups, wide, near):
+        block = wide[1] // groups
+        return [
+            pltpu.VMEM((groups, wide[0], block), f32),
+            pltpu.VMEM(near, f32),
+            pltpu.VMEM((n, wide[0], block), f32),
+            pltpu.VMEM((n,) + near[1:], f32),
+            pltpu.SemaphoreType.DMA((2, 2, groups)),
+            pltpu.SemaphoreType.DMA((2, 2, n)),
+        ]
+
+    def greet(self, barrier):
+        n, place = self.n, self.place
+        for k in range(2, n):
+            @pl.when(place + k < n)
+            def _():
+                pl.semaphore_signal(
+                    barrier, inc=1, device_id={"tensor": place + k}, device_id_type=MESH
+                )
+
+            @pl.when(place - k >= 0)
+            def _():
+                pl.semaphore_signal(
+                    barrier, inc=1, device_id={"tensor": place - k}, device_id_type=MESH
+                )
+
+    def cut(self, j):
+        return pl.ds(pl.multiple_of(j * self.block, self.block), self.block)
+
+    def copies(self, to, source):
+        return (
+            to_dp(
+                self.wide.at[:, self.cut(to)], self.wide_in.at[source],
+                self.sems.at[0, 0, to], self.sems.at[1, 0, source], to,
+            ),
+            to_dp(
+                self.near.at[to], self.near_in.at[source],
+                self.sems.at[0, 1, to], self.sems.at[1, 1, source], to,
+            ),
+        )
+
+    def line_copies(self, to, source):
+        return tuple(
+            pltpu.make_async_remote_copy(
+                line.at[self.place], line.at[source], self.line_sems.at[0, i, to],
+                self.line_sems.at[1, i, source], device_id={"tensor": to}, device_id_type=MESH,
+            )
+            for i, line in enumerate((self.wide_line, self.near_line))
+        )
+
+    def send(self):
+        @pl.loop(1, self.groups)
+        def _(k):
+            for c in self.copies(lax.rem(self.member + k, self.groups), self.member):
+                c.start()
+
+        self.wide_in[pl.ds(self.member, 1)] = self.wide[:, self.cut(self.member)][None]
+        self.near_in[pl.ds(self.member, 1)] = self.near[pl.ds(self.member, 1)]
+
+    def forward(self):
+        @pl.loop(1, self.groups)
+        def _(k):
+            for c in self.copies(0, lax.rem(self.member + k, self.groups)):
+                c.wait_recv()
+
+        for came, line in ((self.wide_in, self.wide_line), (self.near_in, self.near_line)):
+            total = came[0]
+            for j in range(1, self.groups):
+                total = total + came[j]
+            line[pl.ds(self.place, 1)] = total[None]
+
+        @pl.loop(1, self.n)
+        def _(k):
+            for c in self.line_copies(lax.rem(self.place + k, self.n), self.place):
+                c.start()
+
+    def receive(self):
+        @pl.loop(1, self.n)
+        def _(k):
+            for c in self.line_copies(0, lax.rem(self.place + k, self.n)):
+                c.wait_recv()
+
+        total = self.wide_line[0]
+        for j in range(1, self.n):
+            total = total + self.wide_line[j]
+        self.wide_out[...] = total
+        own = self.near_line[pl.ds(self.place, 1)][0]
+        total = self.near_line[0]
+        for j in range(1, self.n):
+            total = total + self.near_line[j]
+        row = lax.broadcasted_iota(jnp.int32, own.shape, 0)
+        self.near_out[...] = jnp.where(row < self.near_all, total, own)
+
+    def drain(self):
+        @pl.loop(1, self.groups)
+        def _(k):
+            for c in self.copies(lax.rem(self.member + k, self.groups), self.member):
+                c.wait_send()
+
+        @pl.loop(1, self.n)
+        def _(k):
+            for c in self.line_copies(lax.rem(self.place + k, self.n), self.place):
+                c.wait_send()
+
+
+def back_mixer_kernel(n, groups, widths, near_all, tiles, outs, *refs):
+    take = splitter(refs)
+    gain_ref, near_ref, x_far, base_far, left_far = take(5)
+    parts = take(2)
+    col_left, col_right = take(2)
+    weights = take(len(widths))
+    out_ref, wide_out, near_out = take(3)
+    outputs = take(len(outs))
+    (col_out,) = take(1)
+    up_in, down_in, x_ref, base_ref, kept_ref, share_ref, wide_ref, gain_grad_ref = take(8)
+    weight_ref, load_sems, sems = take(3)
+    rows = RowGrads(groups, left_far, parts, tiles, outs, outputs, take(10))
+    cols = ColGrad(groups, col_left, col_right, col_out, take(9))
+    small = SmallSum(n, groups, wide_ref, near_ref, near_all, wide_out, near_out, take(6))
+    finish = norm_back(x_ref, base_ref, gain_ref, out_ref, kept_ref, gain_grad_ref)
+    line = Line(n, share_ref, up_in, down_in, out_ref, sems, finish)
+    loads = [
+        pltpu.make_async_copy(x_far, x_ref, load_sems.at[0]),
+        pltpu.make_async_copy(base_far, base_ref, load_sems.at[1]),
+    ]
+    weight_loads = []
+    offset = 0
+    for i, wide in enumerate(widths):
+        weight_loads.append(
+            pltpu.make_async_copy(
+                weights[i], weight_ref.at[:, pl.ds(offset, wide)], load_sems.at[2 + i]
+            )
+        )
+        offset += wide
+    for i in range(2):
+        rows.part_load(i).start()
+    for c in weight_loads:
+        c.start()
+    barrier = pltpu.get_barrier_semaphore()
+    greet_dp(barrier, groups)
+    small.greet(barrier)
+    line.greet_all(barrier, groups - 1)
+    rows.start_left()
+    for i in range(2):
+        rows.part_copy(i).start()
+    cols.start()
+    for c in loads:
+        c.start()
+    for i in range(2):
+        rows.part_load(i).wait()
+    for c in weight_loads:
+        c.wait()
+
+    count, width = share_ref.shape
+    tile_rows, tile_columns = count // 2, 512
+    across = width // tile_columns
+
+    @pl.loop(0, 2 * across)
+    def _(i):
+        at = pl.ds(pl.multiple_of((i // across) * tile_rows, tile_rows), tile_rows)
+        to = pl.ds(pl.multiple_of(lax.rem(i, across) * tile_columns, tile_columns), tile_columns)
+        share_ref[at, to] = dot_t(rows.all[at, :], weight_ref[to, :]).astype(bf16)
+
+    line.prime()
+    for c in loads:
+        c.wait()
+    third = LANES // 4
+    latent_at = offset - widths[-1] - LANES
+    first_cols = rows.items
+    last_item = first_cols + cols.items
+
+    @pl.loop(0, line.steps)
+    def _(step):
+        line.step(step)
+
+        @pl.when(step == 0)
+        def _():
+            rows.ready_left()
+            for i in range(2):
+                rows.part_copy(i).wait_recv()
+
+        rows.item(step)
+
+        @pl.when(step == first_cols)
+        def _():
+            cols.ready()
+
+        @pl.when((step >= first_cols) & (step < last_item))
+        def _():
+            cols.item(step - first_cols)
+
+        @pl.when(step == last_item)
+        def _():
+            cols.send_all()
+            product = rows_dot(rows.all[:, pl.ds(latent_at, LANES)], rows.left[...])
+            wide_ref[:16, :] = product[:16, :] + product[third : third + 16, :]
+
+        @pl.when(step == line.second + 4)
+        def _():
+            wide_ref[16:, :] = gain_grad_ref[...]
+            small.send()
+
+        @pl.when(step == line.second + 14)
+        def _():
+            small.forward()
+
+    rows.receive()
+    cols.receive()
+    small.receive()
+    line.drain()
+    rows.drain()
+    cols.drain()
+    small.drain()
+
+
+def back_mixer(call, n, groups, gain, near, near_all, x_own, base_own, left, parts, outs, pair, weights):
+    count, width = left.shape
+    half = count // 2
+    widths = [w.shape[1] for w in weights]
+    total = sum(part.shape[1] for part in parts)
+    start = parts[0].shape[1]
+    tiles = [(0, 512), (512, 512), (start, parts[1].shape[1])]
+    col_rows = pair[0].shape[1]
+    vmem = pl.BlockSpec(memory_space=pltpu.VMEM)
+    far = pl.BlockSpec(memory_space=pl.ANY)
+    wide_shape = (24, width)
+    return pl.pallas_call(
+        functools.partial(back_mixer_kernel, n, groups, widths, near_all, tiles, outs),
+        in_specs=[vmem] * 2 + [far] * (7 + len(weights)),
+        out_specs=[vmem] * (4 + len(outs)),
+        out_shape=[
+            jax.ShapeDtypeStruct((count, width), bf16),
+            jax.ShapeDtypeStruct((24, width // groups), f32),
+            jax.ShapeDtypeStruct(near.shape[1:], f32),
+        ]
+        + [jax.ShapeDtypeStruct((width // groups, wide), f32) for _, wide in outs]
+        + [jax.ShapeDtypeStruct((col_rows // groups, width), f32)],
+        scratch_shapes=Line.scratch(half, width)
+        + [
+            pltpu.VMEM((half, width), x_own.dtype),
+            pltpu.VMEM((half, width), base_own.dtype),
+            pltpu.VMEM((half, width), bf16),
+            pltpu.VMEM((count, width), bf16),
+            pltpu.VMEM(wide_shape, f32),
+            pltpu.VMEM((8, width), f32),
+            pltpu.VMEM((width, total), bf16),
+            pltpu.SemaphoreType.DMA((2 + len(weights),)),
+            Line.semaphores(half),
+        ]
+        + RowGrads.scratch(groups, count, width, total, 2, len(tiles))
+        + ColGrad.scratch(groups, count, col_rows, width)
+        + SmallSum.scratch(n, groups, wide_shape, near.shape),
+        compiler_params=pltpu.CompilerParams(
+            collective_id=call, has_side_effects=True, vmem_limit_bytes=61 << 20
+        ),
+        cost_estimate=pl.CostEstimate(
+            flops=12_000_000_000, bytes_accessed=200_000_000, transcendentals=0
+        ),
+        name="back_mixer",
+    )(gain, near, x_own, base_own, left, *parts, *pair, *weights)
 
 
 def one_hot(index, base, shape, dim):
     return (index == base + lax.broadcasted_iota(jnp.int32, shape, dim)).astype(f32).astype(bf16)
 
 
-def recur_back_kernel(n, groups, dk, dv, *refs):
+def recur_back_kernel(n, groups, dk, dv, beside, *refs):
     (
         lengths_ref, send_row_ref, send_column_ref, slot_row_ref, slot_column_ref,
         d_mixed_ref, out_weight_ref, attended_ref, gate_ref, gain_ref, up_ref, bias_ref, down_ref,
-        held_ref, states_ref, share_ref, hidden_ref,
-        d_rows_ref, d_gate_ref, head_gain_ref, grad_up_ref, grad_bias_ref, layer_ref,
+        share_ref, held_far, states_far, hidden_far, active_far, cotangent_far,
+        d_rows_ref, d_gate_ref, head_gain_ref, grad_up_ref, grad_bias_ref, layer_ref, grad_down_ref,
         up_in, down_in, d_attended, sent, came, d_state, result, back_sent, back_came,
-        sems, go_sems, back_sems,
-    ) = refs
+        held_ref, states_ref, hidden_ref, load_sems, sems, go_sems, back_sems,
+    ) = refs[:42]
+    cols = ColGrad(groups, active_far, cotangent_far, grad_down_ref, refs[42:]) if beside else None
     member = lax.axis_index("dp")
     count = d_mixed_ref.shape[0]
     slots = slot_row_ref.shape[1]
@@ -796,16 +1120,20 @@
         layer_ref[place, :] = (hidden_ref[own, :] + total).astype(layer_ref.dtype)
 
     line = Line(n, share_ref, up_in, down_in, layer_ref, sems, finish)
+    loads = (
+        pltpu.make_async_copy(hidden_far, hidden_ref, load_sems.at[0]),
+        pltpu.make_async_copy(held_far, held_ref, load_sems.at[1]),
+        pltpu.make_async_copy(states_far, states_ref, load_sems.at[2]),
+    )
     barrier = pltpu.get_barrier_semaphore()
-
-    @pl.loop(1, groups)
-    def _(k):
-        pl.semaphore_signal(
-            barrier, inc=1, device_id={"dp": lax.rem(member + k, groups)}, device_id_type=MESH
-        )
-
+    greet_dp(barrier, groups)
     line.greet(barrier, groups - 1)
     line.prime()
+    for c in loads:
+        c.start()
+    if beside:
+        cols.start()
+    loads[0].wait()
 
     def part(j):
         return pl.ds(pl.multiple_of(j * cap, cap), cap)
@@ -868,7 +1196,22 @@
     d_state[...] = jnp.zeros_like(d_state)
     grad_up_ref[...] = jnp.zeros_like(grad_up_ref)
     grad_bias_ref[...] = jnp.zeros_like(grad_bias_ref)
-    line.run(5, 13)
+    done = 13
+    if beside:
+        cols.ready()
+
+        @pl.loop(0, cols.items)
+        def _(i):
+            cols.item(i)
+            line.step(5 + 2 * i)
+            line.step(6 + 2 * i)
+
+        done = 5 + 2 * cols.items
+        cols.send_all()
+    else:
+        line.run(5, done)
+    for c in loads[1:]:
+        c.wait()
 
     @pl.loop(1, groups)
     def _(k):
@@ -885,8 +1228,8 @@
             dk, dv, step, ends, d_out, held_ref, states_ref[step], up_ref, bias_ref, down_ref,
             d_state, result, grad_up_ref, grad_bias_ref,
         )
-        line.step(13 + 2 * i)
-        line.step(14 + 2 * i)
+        line.step(done + 2 * i)
+        line.step(done + 1 + 2 * i)
 
     positions = result.shape[0]
 
@@ -905,7 +1248,9 @@
         def _():
             back_came[part(member), :] = block
 
-    line.run(13 + 2 * spans, line.steps)
+    line.run(done + 2 * spans, line.steps)
+    if beside:
+        cols.receive()
 
     @pl.loop(1, groups)
     def _(k):
@@ -918,6 +1263,8 @@
         d_rows_ref[rows, :] = dot(pick, back_came[...]).astype(bf16)
 
     line.drain()
+    if beside:
+        cols.drain()
 
     @pl.loop(1, groups)
     def _(k):
@@ -927,8 +1274,8 @@
 
 
 def recur_back(
-    call, n, groups, dk, dv, lengths, send_pos, slot_map, d_mixed, out_weight, attended, gate_pre,
-    head_gain, up_wide, bias, down_wide, held, states, share, hidden_own,
+    call, n, groups, dk, dv, beside, lengths, send_pos, slot_map, d_mixed, out_weight, attended, gate_pre,
+    head_gain, up_wide, bias, down_wide, share, held, states, hidden_own, active, cotangent,
 ):
     count, width = d_mixed.shape
     slots, wide = held.shape
@@ -937,12 +1284,13 @@
     operands = [
         lengths, send_pos.reshape(1, -1), send_pos.reshape(-1, 1), slot_map.reshape(1, -1),
         slot_map.reshape(-1, 1), d_mixed, out_weight, attended, gate_pre, head_gain, up_wide, bias,
-        down_wide, held, states, share, hidden_own,
+        down_wide, share, held, states, hidden_own, active, cotangent,
     ]
+    far = pl.BlockSpec(memory_space=pl.ANY)
     return pl.pallas_call(
-        functools.partial(recur_back_kernel, n, groups, dk, dv),
-        in_specs=[pl.BlockSpec(memory_space=pltpu.SMEM)] + [vmem] * (len(operands) - 1),
-        out_specs=[vmem] * 6,
+        functools.partial(recur_back_kernel, n, groups, dk, dv, beside),
+        in_specs=[pl.BlockSpec(memory_space=pltpu.SMEM)] + [vmem] * (len(operands) - 6) + [far] * 5,
+        out_specs=[vmem] * 7,
         out_shape=[
             jax.ShapeDtypeStruct((count, wide), bf16),
             jax.ShapeDtypeStruct((count, dv), bf16),
@@ -950,6 +1298,7 @@
             jax.ShapeDtypeStruct((dk, LANES), f32),
             jax.ShapeDtypeStruct((8, dk), f32),
             jax.ShapeDtypeStruct((count, width), bf16),
+            jax.ShapeDtypeStruct((active.shape[1] // groups if beside else 8, width), f32),
         ],
         scratch_shapes=Line.scratch(half, width)
         + [
@@ -960,10 +1309,15 @@
             pltpu.VMEM((slots, wide), bf16),
             pltpu.VMEM((slots, wide), bf16),
             pltpu.VMEM((slots, wide), bf16),
+            pltpu.VMEM(held.shape, bf16),
+            pltpu.VMEM(states.shape, bf16),
+            pltpu.VMEM((half, width), f32),
+            pltpu.SemaphoreType.DMA((3,)),
             Line.semaphores(half),
             pltpu.SemaphoreType.DMA((2, groups)),
             pltpu.SemaphoreType.DMA((2, groups)),
-        ],
+        ]
+        + (ColGrad.scratch(groups, count, active.shape[1], width) if beside else []),
         compiler_params=pltpu.CompilerParams(
             collective_id=call, has_side_effects=True, vmem_limit_bytes=60 << 20
         ),
@@ -1208,10 +1562,9 @@
     feed_share = (dot_t(d_gate_hidden, feed_gate) + dot_t(d_up_hidden, feed_up)).astype(bf16)
     fused = (width // groups) % LANES == 0
     if fused:
-        d_mixed, d_hidden_own, feed_gain_part, grad_feed_gate, grad_feed_up = sum_grads(
-            "back_feed", 2, lines, groups, feed_share, hidden_own, cotangent_own,
-            feed_gain_wide.reshape(1, -1), f32, feed_normed, [d_gate_hidden, d_up_hidden],
-            [d_gate_hidden.shape[1]] * 2, tiles_of([d_gate_hidden.shape[1]] * 2, 768), [],
+        d_mixed, d_hidden_own, feed_gain_part, grad_feed_gate, grad_feed_up = back_feed(
+            2, lines, groups, feed_share, feed_gain_wide.reshape(1, -1), hidden_own, cotangent_own,
+            feed_normed, [d_gate_hidden, d_up_hidden],
         )
     else:
         d_mixed, d_hidden_own, feed_gain_part = line_sum(
@@ -1219,42 +1572,85 @@
         )
 
     layer_share = dot(active, feed_down).astype(bf16)
-    d_rows, d_gate_low, head_gain_part, up_part, bias_part, layer_out = recur_back(
-        4, lines, groups, dk, dv, lengths, send_pos, slot_map, d_mixed, out_weight, attended,
-        gate_pre, head_gain_wide.reshape(1, -1), up_wide, bias, down_wide, held, states,
-        layer_share, hidden_own,
-    )
-    d_query_low = d_rows[:, :dk]
-    d_key_low = d_rows[:, dk : 2 * dk]
-    d_value_low = d_rows[:, 2 * dk : 2 * dk + dv]
-    d_latent_low = d_rows[:, 2 * dk + dv :]
+    d_rows, d_gate_low, head_gain_part, up_part, bias_part, layer_out, grad_feed_down = recur_back(
+        4, lines, groups, dk, dv, fused, lengths, send_pos, slot_map, d_mixed, out_weight, attended,
+        gate_pre, head_gain_wide.reshape(1, -1), up_wide, bias, down_wide, layer_share, held, states,
+        hidden_own, active, cotangent,
+    )
     down_both = jnp.concatenate(
         [down_pad, down_pad, jnp.zeros_like(down_pad), jnp.zeros_like(down_pad)], axis=1
     )
-    normed_share = (
-        dot_t(d_query_low, query_weight)
-        + dot_t(d_key_low, key_weight)
-        + dot_t(d_value_low, value_weight)
-        + dot_t(d_gate_low, gate_weight)
-        + dot_t(d_latent_low, down_both)
-    ).astype(bf16)
+    up_part = up_part[:, :rank] + up_part[:, third : third + rank] + (
+        up_part[:, 2 * third : 2 * third + rank]
+    )
+
+    def by_owner(vector):
+        return vector.reshape(groups, -1)
+
+    per = width // groups
+    head_per = dv // groups
+    up_per = dk // groups * rank
     if fused:
+        near = [
+            by_owner(jnp.sum(feed_gain_part, axis=0)),
+            jnp.pad(by_owner(jnp.sum(head_gain_part, axis=0)), ((0, 0), (0, -head_per % LANES))),
+            by_owner(up_part),
+            jnp.pad(by_owner(bias_part[0]), ((0, 0), (0, -(dk // groups) % LANES))),
+        ]
+        near_all = (per + head_per + LANES - 1) // LANES
+        near = jnp.concatenate(near, axis=1)
+        near = jnp.pad(near, ((0, 0), (0, -near.shape[1] % (8 * LANES))))
         (
-            token_grad, _, mixer_gain_part, grad_rows, grad_gate, grad_out, grad_feed_down,
-        ) = sum_grads(
-            "back_mixer", 3, lines, groups, normed_share, tokens_own, d_hidden_own,
-            mixer_gain_wide.reshape(1, -1), bf16, normed, [d_rows, d_gate_low],
-            [2 * dk + dv, dv], tiles_of([2 * dk + dv, dv], 512),
-            [(gated, d_mixed), (active, cotangent)],
-        )
-        grad_query = grad_rows[:, :dk]
-        grad_key = grad_rows[:, dk : 2 * dk]
-        grad_value = grad_rows[:, 2 * dk :]
+            token_grad, wide_sum, near_sum, grad_query, grad_key, grad_value, grad_gate, grad_out,
+        ) = back_mixer(
+            3, lines, groups, mixer_gain_wide.reshape(1, -1), near.reshape(groups, -1, LANES),
+            near_all, tokens_own, d_hidden_own, normed, [d_rows, d_gate_low],
+            [(0, dk), (dk, dk), (2 * dk, dv), (2 * dk + dv + LANES, dv)], (gated, d_mixed),
+            [query_weight, key_weight, value_weight, down_both, gate_weight],
+        )
+        near_sum = near_sum.reshape(-1)
+        mixer_sum = jnp.sum(wide_sum[16:], axis=0)
+        feed_sum = near_sum[:per]
+        head_sum = near_sum[per : per + head_per]
+        down_sum = wide_sum[:16].T
+        up_sum = near_sum[near_all * LANES : near_all * LANES + up_per]
+        bias_sum = near_sum[near_all * LANES + up_per :][: dk // groups]
     else:
+        d_query_low = d_rows[:, :dk]
+        d_key_low = d_rows[:, dk : 2 * dk]
+        d_value_low = d_rows[:, 2 * dk : 2 * dk + dv]
+        d_latent_low = d_rows[:, 2 * dk + dv :]
+        normed_share = (
+            dot_t(d_query_low, query_weight)
+            + dot_t(d_key_low, key_weight)
+            + dot_t(d_value_low, value_weight)
+            + dot_t(d_gate_low, gate_weight)
+            + dot_t(d_latent_low, down_both)
+        ).astype(bf16)
         token_grad, _, mixer_gain_part = line_sum(
             "back", 3, lines, normed_share, tokens_own, d_hidden_own,
             mixer_gain_wide.reshape(1, -1),
         )
+        down_part = rows_dot(normed, d_latent_low)
+        down_part = down_part[:, :rank] + down_part[:, third : third + rank]
+        over_all = jnp.concatenate(
+            [
+                by_owner(jnp.sum(mixer_gain_part, axis=0)),
+                by_owner(jnp.sum(feed_gain_part, axis=0)),
+                by_owner(jnp.sum(head_gain_part, axis=0)),
+                by_owner(down_part),
+            ],
+            axis=1,
+        )
+        over_owners = jnp.concatenate([by_owner(up_part), by_owner(bias_part[0])], axis=1)
+        summed, small = small_sum(over_all, over_owners, groups, lines, 5)
+        mixer_sum = summed[:per]
+        feed_sum = summed[per : 2 * per]
+        head_sum = summed[2 * per : 2 * per + head_per]
+        down_sum = summed[2 * per + head_per :].reshape(per, rank)
+        up_sum = small[:up_per]
+        bias_sum = small[up_per:]
+
     def halves(row_block, dims):
         split = row_block.reshape(row_block.shape[0], groups // 2, 2, dims // groups)
         keep = lax.dynamic_index_in_dim(split, parity, 2, keepdims=False)
@@ -1276,9 +1672,9 @@
         return jnp.sum(moved.astype(f32), axis=0)
 
     if not fused:
+        grad_feed_down = summed_share(halves(active, active.shape[1]), partner(cotangent))
         feed_halves = halves(feed_normed, width)
         normed_halves = halves(normed, width)
-        grad_feed_down = summed_share(halves(active, active.shape[1]), partner(cotangent))
         grad_feed_gate = summed_share(feed_halves, partner(d_gate_hidden))
         grad_feed_up = summed_share(feed_halves, partner(d_up_hidden))
         grad_out = summed_share(halves(gated, dv), partner(d_mixed))
@@ -1287,42 +1683,20 @@
         grad_value = summed_share(normed_halves, partner(d_value_low))
         grad_gate = summed_share(normed_halves, partner(d_gate_low))
 
-    down_part = rows_dot(normed, d_latent_low)
-    down_part = down_part[:, :rank] + down_part[:, third : third + rank]
-    up_part = up_part[:, :rank] + up_part[:, third : third + rank] + (
-        up_part[:, 2 * third : 2 * third + rank]
-    )
-
-    def by_owner(vector):
-        return vector.reshape(groups, -1)
-
-    over_all = jnp.concatenate(
-        [
-            by_owner(jnp.sum(mixer_gain_part, axis=0)),
-            by_owner(jnp.sum(feed_gain_part, axis=0)),
-            by_owner(jnp.sum(head_gain_part, axis=0)),
-            by_owner(down_part),
-        ],
-        axis=1,
-    )
-    over_owners = jnp.concatenate([by_owner(up_part), by_owner(bias_part[0])], axis=1)
-    summed, small = small_sum(over_all, over_owners, groups, lines, 5)
-    per = width // groups
-    head_per = dv // groups
     return (
         layer_out,
         token_grad,
-        summed[:per],
+        mixer_sum,
         grad_query,
         grad_key,
         grad_value,
         grad_gate,
-        summed[2 * per + head_per :].reshape(per, rank),
-        small[: dk // groups * rank].reshape(1, dk // groups, rank),
-        small[dk // groups * rank :].reshape(1, dk // groups),
-        summed[2 * per : 2 * per + head_per],
+        down_sum,
+        up_sum.reshape(1, dk // groups, rank),
+        bias_sum.reshape(1, dk // groups),
+        head_sum,
         grad_out[None],
-        summed[per : 2 * per],
+        feed_sum,
         grad_feed_gate,
         grad_feed_up,
         grad_feed_down[None],

time: 574 us -> 507 us (0.88)
  Pallas kernels: 401 us -> 363 us
  matrix products: 78.6 us -> 55.3 us
  local copies, waits for them, and re-layouts: 37 us -> 29.7 us
    pallas_call x4 -> x3, Pallas kernels: 311 us -> 272 us  [the longest x1 99 us: recur_back(): pl.pallas_call(functools.partial(recur_back_kernel, n, groups, dk, dv, be...]
    dot_general x8 -> x3, matrix products: 40.9 us -> 19.2 us  [dot_t(): lax.dot_general(left, right, (((1,), (1,)), ((), ())), preferred_element_...]
    unnamed x123 -> x112, local copies, waits for them, and re-layouts: 18.5 us -> 17.8 us
where the time goes in v5:
time: 507 us; the launch traced here: 498 us
  Pallas kernels  363 us (72%)
  matrix products  55.3 us (11%)
  local copies, waits for them, and re-layouts  29.7 us (6%)
  waiting for transfers between devices  27.5 us (5%)
  other arithmetic  12 us (2%)
  starting transfers between devices  9.1 us (2%)
    pallas_call x1, Pallas kernels, recur_back(): pl.pallas_call(functools.partial(recur_back_kernel, n, groups, dk, dv, be...  99 us
    pallas_call x1, Pallas kernels, back_mixer(): pl.pallas_call(functools.partial(back_mixer_kernel, n, groups, widths, ne...  91 us
    pallas_call x1, Pallas kernels, back_feed(): pl.pallas_call(functools.partial(back_feed_kernel, n, groups, tiles, outs...  82.4 us
    pallas_call x1, Pallas kernels, line_sum(): pl.pallas_call(functools.partial(line_kernel, mode, n), in_specs=[vmem] *...  74 us
    dot_general x12, matrix products, dot(): return jnp.dot(left, right, preferred_element_type=f32)  36.1 us
    all_to_all x2, waiting for transfers between devices, exchange(): lax.all_to_all(blocks, 'dp', split_axis=0, concat_axis=0, tiled=True)  27.5 us
    dot_general x3, matrix products, dot_t(): lax.dot_general(left, right, (((1,), (1,)), ((), ())), preferred_element_...  19.2 us
    unnamed x112, local copies, waits for them, and re-layouts  17.8 us
  transfers between devices with their start and end apart: 2, of which 2 were waited for; matrix products, arithmetic and copies ran while one was open for 3% of the time, Pallas kernels for 0%

profile of v5, /device:TPU:0, one launch (start us, length us, event | category | flops | bytes accessed | tf_op | source)
XLA Modules:
  0.0 498.5 jit_solution(168288770923973167)
XLA Ops:
  0.7 0.9 fusion.36
  1.6 0.8 add_select_fusion.2
  2.7 0.8 multiply_add_fusion
  4.1 2.3 fusion
  7.5 0.9 copy-done.33
  8.4 1.8 convolution_convert_fusion.3
  10.4 1.0 convolution_convert_fusion.4
  11.6 1.0 convolution_convert_fusion.5
  12.8 1.2 fusion.29
  14.0 3.6 convolution_convert_fusion
  17.7 5.5 %all-to-all-start = ((bf16[8,128,1152]{2,1,0:T(8,128)(2,1)}), bf16[8,128,1152]{2,1,0:T(8,128)(2,1)}, u32[]{:S(2)}, u32[]{:S(2)}) async-start(bf16[8,128,1152]{2,1,0:T(8,128)(2,1)} %bitcast.4), calls=%async_computation | async-start | bytes 4718592 | tf_op jit(solution)/shard_map/all_to_all | solution.py:1493
  23.2 0.9 reshape.181.refs_2_
  26.8 3.1 constant_dynamic-slice_fusion
  29.9 1.2 fusion.26.refs_12_
  31.1 21.6 %all-to-all-done = bf16[8,128,1152]{2,1,0:T(8,128)(2,1)} async-done(((bf16[8,128,1152]{2,1,0:T(8,128)(2,1)}), bf16[8,128,1152]{2,1,0:T(8,128)(2,1)}, u32[]{:S(2)}, u32[]{:S(2)}) %all-to-all-start) | async-done | bytes 2359328 | tf_op jit(solution)/shard_map/all_to_all | solution.py:1493
  52.7 17.0 %recur_forward.1 = (bf16[1024,512]{1,0:T(8,128)(2,1)}, bf16[1024,1152]{1,0:T(8,128)(2,1)S(1)}, bf16[8,256,512]{2,1,0:T(8,128)(2,1)S(1)}) custom-call(s32[1,1024]{1,0:T(1,128)S(1)} %bitcast.51, s32[1024,1]{1,0:T(8,128)S(1)} %copy.57.slot_column_ref.refs_4_, s32[1,3]{1,0:T(1,128)S(1)} %copy-done.7, bf16[128,256]{1,0:T(8,128)(2,1)S(1)} %copy.54.up_ref.refs_10_, ...), custom_call_target="tpu_custom_call" | custom-call | flops 6000000000 | bytes 10000000 | tf_op jit(solution)/shard_map/recur_forward/pallas_call | solution.py:185
  69.7 1.4 copy-done.9
  71.1 1.3 copy-done.10
  72.4 3.6 all-to-all-start.1
  76.0 9.5 %fusion.51 = f32[640,1408]{1,0:T(8,128)} fusion(bf16[640,2048]{1,0:T(8,128)(2,1)} %refs_18_.1, bf16[1408,2048]{1,0:T(8,128)(2,1)} %param.35), kind=kOutput, calls=%fused_computation.106 | convolution fusion | flops 3690987520 | bytes 11993088 | tf_op jit(solution)/shard_map/dot_general | solution.py:26
  85.5 5.9 %all-to-all-done.1 = bf16[8,128,512]{2,1,0:T(8,128)(2,1)S(1)} async-done(((bf16[8,128,512]{2,1,0:T(8,128)(2,1)}), bf16[8,128,512]{2,1,0:T(8,128)(2,1)S(1)}, u32[]{:S(2)}, u32[]{:S(2)}) %all-to-all-start.1) | async-done | bytes 1048608 | tf_op jit(solution)/shard_map/all_to_all | solution.py:1493
  91.3 1.0 fusion.15
  93.1 5.1 %fusion.18 = (bf16[640,512]{1,0:T(8,128)(2,1)S(1)}, f32[640,512]{1,0:T(8,128)}) fusion(bf16[640,512]{1,0:T(8,128)(2,1)S(1)} %get-tuple-element.122.refs_7_, f32[512]{0:T(512)S(1)} %convert_element_type.105, f32[640]{0:T(1024)S(1)} %add_rsqrt_fusion, bf16[640,2048]{1,0:T(8,128)(2,1)S(1)} %copy-done.15, bf16[2048,512]{1,0:T(8,128)(2,1)} %refs_13_.1), kind=kOutput, calls=%fused_computation.36 | convolution fusion | flops 1345126400 | bytes 7344640 | tf_op jit(solution)/shard_map/dot_general | solution.py:30
  98.2 1.5 convolution_convert_fusion.2.refs_0_
  99.8 74.0 %line_norm.1 = (bf16[640,2048]{1,0:T(8,128)(2,1)S(1)}, f32[320,2048]{1,0:T(8,128)S(1)}) custom-call(bf16[640,2048]{1,0:T(8,128)(2,1)S(1)} %convolution_convert_fusion.2.refs_0_, bf16[320,2048]{1,0:T(8,128)(2,1)S(1)} %get-tuple-element.128.refs_1_.refs_2_, bf16[320,2048]{1,0:T(8,128)(2,1)S(1)} %get-tuple-element.128.refs_1_.refs_2_, f32[1,2048]{1,0:T(1,128)S(1)} %bitcast.48), custom_call_target="tpu_custom_call" | custom-call | flops 10000000 | bytes 200000000 | tf_op jit(solution)/shard_map/line_norm/pallas_call | solution.py:451
  173.9 6.0 %fusion.52 = f32[640,1408]{1,0:T(8,128)} fusion(bf16[640,2048]{1,0:T(8,128)(2,1)S(1)} %get-tuple-element.42.refs_4_, bf16[2048,1408]{1,0:T(8,128)(2,1)S(1)} %bitcast.63), kind=kOutput, calls=%fused_computation.107 | convolution fusion | flops 3690987520 | bytes 11993088 | tf_op jit(solution)/shard_map/dot_general | solution.py:30
  179.9 8.0 %multiply_convert_fusion = (bf16[640,1408]{1,0:T(8,128)(2,1)S(1)}, bf16[640,1408]{1,0:T(8,128)(2,1)S(1)}, bf16[640,1408]{1,0:T(8,128)(2,1)}) fusion(f32[640,1408]{1,0:T(8,128)} %fusion.52, f32[640,1408]{1,0:T(8,128)S(1)} %copy-done.39, bf16[640,2048]{1,0:T(8,128)(2,1)S(1)} %get-tuple-element.42.refs_4_, bf16[2048,1408]{1,0:T(8,128)(2,1)S(1)} %bitcast.67), kind=kOutput, calls=%fused_computation.7 | convolution fusion | flops 3704504320 | bytes 21004288 | tf_op jit(solution)/shard_map/dot_general | solution.py:30
  187.9 4.2 fusion.53
  192.2 5.6 %convolution_convert_fusion.1.refs_13_ = bf16[640,2048]{1,0:T(8,128)(2,1)} fusion(bf16[640,1408]{1,0:T(8,128)(2,1)S(1)} %get-tuple-element.114.refs_17_, bf16[1408,2048]{1,0:T(8,128)(2,1)S(1)} %bitcast.65), kind=kOutput, calls=%fused_computation.12 | convolution fusion | flops 3692298240 | bytes 10190848 | tf_op jit(solution)/shard_map/dot_general | solution.py:30
  197.8 5.5 %add_convert_fusion.refs_0_ = bf16[640,2048]{1,0:T(8,128)(2,1)} fusion(f32[640,2048]{1,0:T(8,128)S(1)} %fusion.53, bf16[640,1408]{1,0:T(8,128)(2,1)S(1)} %copy-done.41, bf16[2048,1408]{1,0:T(8,128)(2,1)S(1)} %bitcast.67), kind=kOutput, calls=%fused_computation.5 | convolution fusion | flops 3693608960 | bytes 15433728 | tf_op jit(solution)/shard_map/dot_general | solution.py:26
  203.3 82.4 %back_feed.1 = (bf16[640,2048]{1,0:T(8,128)(2,1)}, f32[320,2048]{1,0:T(8,128)}, f32[8,2048]{1,0:T(8,128)}, f32[256,1408]{1,0:T(8,128)}, f32[256,1408]{1,0:T(8,128)}) custom-call(bf16[640,2048]{1,0:T(8,128)(2,1)} %add_convert_fusion.refs_0_, f32[1,2048]{1,0:T(1,128)} %bitcast.49, f32[320,2048]{1,0:T(8,128)} %copy-done.5, ...), custom_call_target="tpu_custom_call" | custom-call | flops 12000000000 | bytes 200000000 | tf_op jit(solution)/shard_map/back_feed/pallas_call | solution.py:795
  285.7 99.0 %recur_back.1 = (bf16[640,1152]{1,0:T(8,128)(2,1)}, bf16[640,512]{1,0:T(8,128)(2,1)}, f32[8,512]{1,0:T(8,128)}, f32[256,128]{1,0:T(8,128)}, f32[8,256]{1,0:T(8,1...) custom-call(s32[1,3]{1,0:T(1,128)} %refs_0_.1, s32[1,640]{1,0:T(1,128)} %reshape.161.refs_1_, ...), custom_call_target="tpu_custom_call" | custom-call | flops 12000000000 | bytes 200000000 | tf_op jit(solution)/shard_map/recur_back/pallas_call | solution.py:1290
  384.8 1.2 slice_add_fusion
  388.4 91.0 %back_mixer.1 = (bf16[640,2048]{1,0:T(8,128)(2,1)}, f32[24,256]{1,0:T(8,128)}, f32[8,128]{1,0:T(8,128)}, f32[256,256]{1,0:T(8,128)}, f32[256,256]{1,0:T(8,128)},...) custom-call(f32[1,2048]{1,0:T(1,128)} %bitcast.58, f32[8,8,128]{2,1,0:T(8,128)} %bitcast.59, ...), custom_call_target="tpu_custom_call" | custom-call | flops 12000000000 | bytes 200000000 | tf_op jit(solution)/shard_map/back_mixer/pallas_call | solution.py:1061
  480.0 1.2 slice_bitcast_fusion.1
  481.3 1.3 slice_bitcast_fusion
  482.6 1.3 slice_reduce_fusion
  483.9 1.2 slice.53
  485.8 1.2 slice.54
  487.0 1.5 copy.74
  488.5 1.2 copy-done.13
  489.7 1.5 copy.75
  492.6 0.8 copy.78
  493.4 0.8 copy.79
  494.2 0.8 copy.80
  495.0 1.1 copy.81
  496.1 1.1 copy.82
  497.2 1.1 copy.83
  (140 shorter events, 11.1 us)
Async XLA Ops:
  0.6 6.1 %copy-start.11 = (bf16[640,2048]{1,0:T(8,128)(2,1)S(1)}, bf16[640,2048]{1,0:T(8,128)(2,1)}, u32[]{:S(2)}) copy-start(bf16[640,2048]{1,0:T(8,128)(2,1)} %param.18) | copy-start | bytes 7864324
  0.7 5.8 %copy-start.25 = (bf16[2048,16]{0,1:T(8,128)(2,1)S(1)}, bf16[2048,16]{0,1:T(8,128)(2,1)}, u32[]{:S(2)}) copy-start(bf16[2048,16]{0,1:T(8,128)(2,1)} %param.27) | copy-start | bytes 196612
  4.1 3.3 copy-start.27
  6.8 1.6 copy-start.33
  8.4 4.5 copy-start.14
  8.4 2.0 copy-start.34
  17.6 7.0 %copy-start.24 = (s32[5120]{0:T(1024)S(1)}, s32[5120]{0:T(1024)}, u32[]{:S(2)}) copy-start(s32[5120]{0:T(1024)} %param.20) | copy-start | bytes 61444
  17.6 8.0 %copy-start.28 = (bf16[256,16]{0,1:T(8,128)(2,1)S(1)}, bf16[256,16]{0,1:T(8,128)(2,1)}, u32[]{:S(2)}) copy-start(bf16[256,16]{0,1:T(8,128)(2,1)} %param.28) | copy-start | bytes 24580
  17.6 9.0 %copy-start.36 = (bf16[256]{0:T(256)(128)(2,1)S(1)}, bf16[256]{0:T(256)(128)(2,1)}, u32[]{:S(2)}) copy-start(bf16[256]{0:T(256)(128)(2,1)} %param.29) | copy-start | bytes 1540
  17.6 9.1 %copy-start.31 = (bf16[512]{0:T(512)(128)(2,1)S(1)}, bf16[512]{0:T(512)(128)(2,1)}, u32[]{:S(2)}) copy-start(bf16[512]{0:T(512)(128)(2,1)} %param.30) | copy-start | bytes 3076
  17.6 9.1 %copy-start.29 = (bf16[2048]{0:T(1024)(128)(2,1)S(1)}, bf16[2048]{0:T(1024)(128)(2,1)}, u32[]{:S(2)}) copy-start(bf16[2048]{0:T(1024)(128)(2,1)} %param.32) | copy-start | bytes 12292
  17.7 35.1 %all-to-all-start = ((bf16[8,128,1152]{2,1,0:T(8,128)(2,1)}), bf16[8,128,1152]{2,1,0:T(8,128)(2,1)}, u32[]{:S(2)}, u32[]{:S(2)}) async-start(bf16[8,128,1152]{2,1,0:T(8,128)(2,1)} %bitcast.4), calls=%async_computation | async-start | bytes 4718592 | tf_op jit(solution)/shard_map/all_to_all | solution.py:1493
  25.3 27.4 %copy-start.4 = (s32[8,128]{1,0:T(8,128)}, s32[8,128]{1,0:T(8,128)S(1)}, u32[]{:S(2)}) copy-start(s32[8,128]{1,0:T(8,128)S(1)} %broadcast_add_fusion) | copy-start | bytes 12292
  25.6 27.1 %copy-start.1 = (s32[1024,1]{1,0:T(8,128)}, s32[1024,1]{1,0:T(8,128)S(1)}, u32[]{:S(2)}) copy-start(s32[1024,1]{1,0:T(8,128)S(1)} %copy.57.slot_column_ref.refs_4_) | copy-start | bytes 12292
  26.7 26.0 %copy-start.2 = (bf16[128,256]{1,0:T(8,128)(2,1)}, bf16[128,256]{1,0:T(8,128)(2,1)S(1)}, u32[]{:S(2)}) copy-start(bf16[128,256]{1,0:T(8,128)(2,1)S(1)} %copy.54.up_ref.refs_10_) | copy-start | bytes 196612
  26.7 26.0 %copy-start.8 = (f32[256]{0:T(256)}, f32[256]{0:T(256)S(1)}, u32[]{:S(2)}) copy-start(f32[256]{0:T(256)S(1)} %reshape.177) | copy-start | bytes 3076
  26.7 65.6 %copy-start.30 = (f32[512]{0:T(512)}, f32[512]{0:T(512)S(1)}, u32[]{:S(2)}) copy-start(f32[512]{0:T(512)S(1)} %convert_element_type.105) | copy-start | bytes 6148
  26.8 73.0 %copy-start.3 = (f32[2048]{0:T(1024)}, f32[2048]{0:T(1024)S(1)}, u32[]{:S(2)}) copy-start(f32[2048]{0:T(1024)S(1)} %reshape.179) | copy-start | bytes 24580
  26.8 25.9 %copy-start.7 = (s32[1,3]{1,0:T(1,128)S(1)}, s32[1,3]{1,0:T(1,128)}, u32[]{:S(2)}) copy-start(s32[1,3]{1,0:T(1,128)} %refs_0_.1) | copy-start | bytes 40
  29.9 69.9 %copy-start = (bf16[320,2048]{1,0:T(8,128)(2,1)}, bf16[320,2048]{1,0:T(8,128)(2,1)S(1)}, u32[]{:S(2)}) copy-start(bf16[320,2048]{1,0:T(8,128)(2,1)S(1)} %get-tuple-element.128.refs_1_.refs_2_) | copy-start | bytes 3932164
  72.4 18.9 %all-to-all-start.1 = ((bf16[8,128,512]{2,1,0:T(8,128)(2,1)}), bf16[8,128,512]{2,1,0:T(8,128)(2,1)S(1)}, u32[]{:S(2)}, u32[]{:S(2)}) async-start(bf16[8,128,512]{2,1,0:T(8,128)(2,1)} %bitcast.6), calls=%async_computation.1 | async-start | bytes 2097152 | tf_op jit(solution)/shard_map/all_to_all | solution.py:1493
  91.3 1.7 copy-start.15
  91.3 82.5 %slice-start = ((s8[5767168]{0:T(1024)(128)(4,1)}), s8[4194304]{0:T(1024)(128)(4,1)S(1)}, s32[]{:S(2)}) async-start(s8[5767168]{0:T(1024)(128)(4,1)} %bitcast.62), calls=%async_computation.2 | async-start | bytes 8388608
  92.3 5.9 %copy-start.37 = (bf16[640,512]{1,0:T(8,128)(2,1)}, bf16[640,512]{1,0:T(8,128)(2,1)S(1)}, u32[]{:S(2)}) copy-start(bf16[640,512]{1,0:T(8,128)(2,1)S(1)} %get-tuple-element.122.refs_7_) | copy-start | bytes 1966084
  93.1 5.1 %copy-start.32 = (bf16[512,2048]{1,0:T(8,128)(2,1)S(1)}, bf16[512,2048]{1,0:T(8,128)(2,1)}, u32[]{:S(2)}) copy-start(bf16[512,2048]{1,0:T(8,128)(2,1)} %refs_6_.1) | copy-start | bytes 6291460
  93.1 80.7 %slice-start.1 = ((s8[5767168]{0:T(1024)(128)(4,1)}), s8[1572864]{0:T(1024)(128)(4,1)S(1)}, s32[]{:S(2)}) async-start(s8[5767168]{0:T(1024)(128)(4,1)} %bitcast.62), calls=%async_computation.3 | async-start | bytes 3145728
  98.2 1.5 copy-start.38
  99.8 80.1 %slice-start.4 = ((s8[5767168]{0:T(1024)(128)(4,1)}), s8[4194304]{0:T(1024)(128)(4,1)S(1)}, s32[]{:S(2)}) async-start(s8[5767168]{0:T(1024)(128)(4,1)} %bitcast.66), calls=%async_computation.6 | async-start | bytes 8388608
  173.8 6.1 %copy-start.5 = (f32[320,2048]{1,0:T(8,128)}, f32[320,2048]{1,0:T(8,128)S(1)}, u32[]{:S(2)}) copy-start(f32[320,2048]{1,0:T(8,128)S(1)} %get-tuple-element.43.refs_2_.refs_16_) | copy-start | bytes 7864324
  173.8 6.1 %copy-start.6 = (bf16[640,2048]{1,0:T(8,128)(2,1)}, bf16[640,2048]{1,0:T(8,128)(2,1)S(1)}, u32[]{:S(2)}) copy-start(bf16[640,2048]{1,0:T(8,128)(2,1)S(1)} %get-tuple-element.42.refs_4_) | copy-start | bytes 7864324
  173.8 6.0 %slice-start.5 = ((s8[5767168]{0:T(1024)(128)(4,1)}), s8[1572864]{0:T(1024)(128)(4,1)S(1)}, s32[]{:S(2)}) async-start(s8[5767168]{0:T(1024)(128)(4,1)} %bitcast.66), calls=%async_computation.7 | async-start | bytes 3145728
  173.8 6.0 %copy-start.39 = (f32[640,1408]{1,0:T(8,128)S(1)}, f32[640,1408]{1,0:T(8,128)}, u32[]{:S(2)}) copy-start(f32[640,1408]{1,0:T(8,128)} %fusion.51) | copy-start | bytes 10813444
  173.9 18.3 %slice-start.2 = ((s8[5767168]{0:T(1024)(128)(4,1)}), s8[4194304]{0:T(1024)(128)(4,1)S(1)}, s32[]{:S(2)}) async-start(s8[5767168]{0:T(1024)(128)(4,1)} %bitcast.64), calls=%async_computation.4 | async-start | bytes 8388608
  179.9 12.3 %slice-start.3 = ((s8[5767168]{0:T(1024)(128)(4,1)}), s8[1572864]{0:T(1024)(128)(4,1)S(1)}, s32[]{:S(2)}) async-start(s8[5767168]{0:T(1024)(128)(4,1)} %bitcast.64), calls=%async_computation.5 | async-start | bytes 3145728
  187.9 4.3 copy-start.40
  187.9 4.3 copy-start.42
  192.2 5.6 %copy-start.41 = (bf16[640,1408]{1,0:T(8,128)(2,1)S(1)}, bf16[640,1408]{1,0:T(8,128)(2,1)}, u32[]{:S(2)}) copy-start(bf16[640,1408]{1,0:T(8,128)(2,1)} %get-tuple-element.116.refs_6_) | copy-start | bytes 5406724
  285.7 102.0 %copy-start.26 = (f32[8,2048]{1,0:T(8,128)S(1)}, f32[8,2048]{1,0:T(8,128)}, u32[]{:S(2)}) copy-start(f32[8,2048]{1,0:T(8,128)} %get-tuple-element.48) | copy-start | bytes 196612
  388.4 98.6 %copy-start.12 = (bf16[640,2048]{1,0:T(8,128)(2,1)S(1)}, bf16[640,2048]{1,0:T(8,128)(2,1)}, u32[]{:S(2)}) copy-start(bf16[640,2048]{1,0:T(8,128)(2,1)} %get-tuple-element.145) | copy-start | bytes 7864324
  487.0 2.7 copy-start.13
  489.7 1.5 copy-start.23
  489.7 2.2 copy-start.22
  489.7 2.9 copy-start.21
  489.7 3.7 copy-start.20
  491.2 3.0 copy-start.19
  491.2 3.8 copy-start.17
  493.4 2.7 copy-start.16
  495.0 2.2 copy-start.18
  (3 other events, 3.9 us)

commit v6 on v5

--- a/solution.py
+++ b/solution.py
@@ -59,32 +59,14 @@
     return log_decay, cumulative, total, middle, carried, tail, keep, allowed
 
 
-def recur_forward_kernel(
-    dk, dv, slot_row_ref, slot_column_ref, lengths_ref, up_ref, bias_ref, arrived_ref,
-    out_ref, held_ref, states_ref, state, result,
-):
-    step = pl.program_id(0)
+def span_forward(dk, dv, step, ends, held_ref, up_ref, bias_ref, state, states_ref, result):
     first = step * SPAN
-    end0 = lengths_ref[0, 0]
-    end1 = end0 + lengths_ref[0, 1]
-    end2 = end1 + lengths_ref[0, 2]
-    slots = slot_row_ref.shape[1]
-
-    @pl.when(step == 0)
-    def _():
-        state[...] = jnp.zeros_like(state)
-
-    position = first + lax.broadcasted_iota(jnp.int32, (SPAN, slots), 0)
-    place = (slot_row_ref[...] == position).astype(f32).astype(bf16)
-    held = dot(place, arrived_ref[...]).astype(bf16)
-    held_ref[...] = held
-    queries = held[:, :dk].astype(f32) * (float(dk) ** -0.5)
-    keys = held[:, dk : 2 * dk].astype(f32)
-    values = held[:, 2 * dk : 2 * dk + dv]
-    logits = dot(held[:, 2 * dk + dv :], up_ref[...]) + bias_ref[...]
-    _, cumulative, total, middle, carried, tail, keep, allowed = span_terms(
-        first, (end0, end1, end2), logits
-    )
+    at = pl.ds(pl.multiple_of(first, SPAN), SPAN)
+    queries = held_ref[at, :dk].astype(f32) * (float(dk) ** -0.5)
+    keys = held_ref[at, dk : 2 * dk].astype(f32)
+    values = held_ref[at, 2 * dk : 2 * dk + dv]
+    logits = dot(held_ref[at, 2 * dk + dv :], up_ref[...]) + bias_ref[...]
+    _, cumulative, total, middle, carried, tail, keep, allowed = span_terms(first, ends, logits)
     query_mid = (queries * jnp.exp(cumulative - middle)).astype(bf16)
     key_mid = (keys * jnp.exp(middle - cumulative)).astype(bf16)
     query_start = (queries * jnp.exp(cumulative) * carried).astype(bf16)
@@ -92,29 +74,11 @@
     scores = jnp.where(allowed, dot_t(query_mid, key_mid), 0.0).astype(bf16)
     entering = state[...]
     entering_low = entering.astype(bf16)
-    states_ref[0] = entering_low
+    states_ref[step] = entering_low
     attended = dot(scores, values) + dot(query_start, entering_low)
-    result[pl.ds(pl.multiple_of(first, SPAN), SPAN), :] = attended.astype(bf16)
+    result[at, :] = attended.astype(bf16)
     decay_column = jnp.transpose(jnp.broadcast_to(keep * jnp.exp(total), (8, dk)))[:, :1]
     state[...] = decay_column * entering + rows_dot(key_end, values)
-
-    @pl.when(step == pl.num_programs(0) - 1)
-    def _():
-        return_rows(slot_column_ref, result, out_ref)
-
-
-def return_rows(slot_column_ref, source, out_ref):
-    positions = source.shape[0]
-    block = 256
-
-    def body(i, carry):
-        at = pl.ds(pl.multiple_of(i * block, block), block)
-        column = lax.broadcasted_iota(jnp.int32, (block, positions), 1)
-        pick = (slot_column_ref[at, :] == column).astype(f32).astype(bf16)
-        out_ref[at, :] = dot(pick, source[...]).astype(out_ref.dtype)
-        return carry
-
-    lax.fori_loop(0, out_ref.shape[0] // block, body, 0)
 
 
 def span_backward(
@@ -175,43 +139,6 @@
     d_state[...] = kept_column * leaving + rows_dot(query_start, d_out)
 
 
-def whole(shape):
-    return pl.BlockSpec(shape, lambda i: (0,) * len(shape))
-
-
-def recur_forward(slot_map, lengths, up_wide, bias, arrived, dk, dv):
-    slots, width = arrived.shape
-    steps = OWN_CAP // SPAN
-    return pl.pallas_call(
-        functools.partial(recur_forward_kernel, dk, dv),
-        grid=(steps,),
-        in_specs=[
-            whole((1, slots)),
-            whole((slots, 1)),
-            pl.BlockSpec(memory_space=pltpu.SMEM),
-            whole((LANES, dk)),
-            whole((1, dk)),
-            whole((slots, width)),
-        ],
-        out_specs=[
-            whole((slots, dv)),
-            pl.BlockSpec((SPAN, width), lambda i: (i, 0)),
-            pl.BlockSpec((1, dk, dv), lambda i: (i, 0, 0)),
-        ],
-        out_shape=[
-            jax.ShapeDtypeStruct((slots, dv), bf16),
-            jax.ShapeDtypeStruct((OWN_CAP, width), bf16),
-            jax.ShapeDtypeStruct((steps, dk, dv), bf16),
-        ],
-        scratch_shapes=[pltpu.VMEM((dk, dv), f32), pltpu.VMEM((OWN_CAP, dv), bf16)],
-        compiler_params=pltpu.CompilerParams(vmem_limit_bytes=40 << 20),
-        cost_estimate=pl.CostEstimate(
-            flops=6_000_000_000, bytes_accessed=10_000_000, transcendentals=2_000_000
-        ),
-        name="recur_forward",
-    )(slot_map.reshape(1, -1), slot_map.reshape(-1, 1), lengths, up_wide, bias, arrived)
-
-
 FINE = 16
 SKEW = 2
 
@@ -302,8 +229,8 @@
         rows = self.out.at[self.low(g), :]
         return self.right(rows, rows, 3, g)
 
-    def prime(self):
-        @pl.when(self.me == 0)
+    def prime(self, top=True, bottom=True):
+        @pl.when((self.me == 0) & top)
         def _():
             @pl.loop(0, self.count)
             def _(g):
@@ -311,7 +238,7 @@
                     self.share.at[self.at(g), :], self.up_in.at[self.at(g), :], 0, g
                 ).start()
 
-        @pl.when(self.me == self.n - 1)
+        @pl.when((self.me == self.n - 1) & bottom)
         def _():
             @pl.loop(0, self.count)
             def _(g):
@@ -421,19 +348,10 @@
     return finish
 
 
-def line_kernel(mode, n, *refs):
-    share_ref, x_ref, base_ref, gain_ref, out_ref, kept_ref = refs[:6]
-    if mode == "norm":
-        up_in, down_in, sems = refs[6:]
-
-        def finish(total, own, place):
-            hidden = base_ref[own, :].astype(f32) + total
-            kept_ref[own, :] = hidden
-            scaling = lax.rsqrt(jnp.mean(hidden * hidden, axis=1, keepdims=True) + epsilon)
-            out_ref[place, :] = (hidden * scaling * gain_ref[...]).astype(out_ref.dtype)
-    else:
-        gain_grad_ref, up_in, down_in, sems = refs[6:]
-        finish = norm_back(x_ref, base_ref, gain_ref, out_ref, kept_ref, gain_grad_ref)
+def line_kernel(n, *refs):
+    share_ref, x_ref, base_ref, gain_ref, out_ref, kept_ref, gain_grad_ref = refs[:7]
+    up_in, down_in, sems = refs[7:]
+    finish = norm_back(x_ref, base_ref, gain_ref, out_ref, kept_ref, gain_grad_ref)
     line = Line(n, share_ref, up_in, down_in, out_ref, sems, finish)
     line.greet(pltpu.get_barrier_semaphore(), 0)
     line.prime()
@@ -441,26 +359,24 @@
     line.drain()
 
 
-def line_sum(mode, call, n, share, x_own, base_own, gain):
+def line_sum(call, n, share, x_own, base_own, gain):
     rows, width = share.shape
     half = rows // 2
     vmem = pl.BlockSpec(memory_space=pltpu.VMEM)
-    outs = [jax.ShapeDtypeStruct((rows, width), bf16), jax.ShapeDtypeStruct((half, width), f32)]
-    if mode == "back":
-        outs.append(jax.ShapeDtypeStruct((8, width), f32))
     return pl.pallas_call(
-        functools.partial(line_kernel, mode, n),
+        functools.partial(line_kernel, n),
         in_specs=[vmem] * 4,
-        out_specs=[vmem] * len(outs),
-        out_shape=outs,
+        out_specs=[vmem] * 3,
+        out_shape=[
+            jax.ShapeDtypeStruct((rows, width), bf16),
+            jax.ShapeDtypeStruct((half, width), f32),
+            jax.ShapeDtypeStruct((8, width), f32),
+        ],
         scratch_shapes=Line.scratch(half, width) + [Line.semaphores(half)],
         compiler_params=pltpu.CompilerParams(
             collective_id=call, has_side_effects=True, vmem_limit_bytes=40 << 20
         ),
-        cost_estimate=pl.CostEstimate(
-            flops=10_000_000, bytes_accessed=200_000_000, transcendentals=0
-        ),
-        name="line_" + mode,
+        name="line_back",
     )(share, x_own, base_own, gain)
 
 
@@ -586,25 +502,22 @@
 
 
 class RowGrads:
-    def __init__(self, groups, left, parts, tiles, outs, outputs, refs):
+    def __init__(self, groups, left, tiles, outs, outputs, refs):
         (
             self.left, self.all, self.left_in, self.all_in, self.send, self.recv,
-            self.load_sems, self.left_sems, self.part_sems, self.sems,
+            self.load_sems, self.left_sems, self.piece_sems, self.sems,
         ) = refs
-        self.left_far, self.parts, self.tiles = left, parts, tiles
+        self.left_far, self.tiles = left, tiles
         self.outs, self.outputs = outs, outputs
         self.member = lax.axis_index("dp")
         self.parity = lax.rem(self.member, 2)
         self.mine = self.member // 2
         self.team = groups // 2
         self.block = left.shape[1] // groups
-        self.offsets = [0]
-        for part in parts:
-            self.offsets.append(self.offsets[-1] + part.shape[1])
         self.items = self.team * len(tiles)
 
     @staticmethod
-    def scratch(groups, count, width, total, parts, tiles):
+    def scratch(groups, count, width, total, pieces, tiles):
         team = groups // 2
         return [
             pltpu.VMEM((count, width), bf16),
@@ -613,9 +526,9 @@
             pltpu.VMEM((count, total), bf16),
             pltpu.VMEM((team, width // groups, total), bf16),
             pltpu.VMEM((team, width // groups, total), bf16),
-            pltpu.SemaphoreType.DMA((1 + parts,)),
+            pltpu.SemaphoreType.DMA((1 + pieces,)),
             pltpu.SemaphoreType.DMA((2, team)),
-            pltpu.SemaphoreType.DMA((2, parts)),
+            pltpu.SemaphoreType.DMA((2, pieces)),
             pltpu.SemaphoreType.DMA((2, tiles, team)),
         ]
 
@@ -625,13 +538,8 @@
     def left_load(self):
         return pltpu.make_async_copy(self.left_far, self.left, self.load_sems.at[0])
 
-    def part_columns(self, i):
-        return pl.ds(self.offsets[i], self.offsets[i + 1] - self.offsets[i])
-
-    def part_load(self, i):
-        return pltpu.make_async_copy(
-            self.parts[i], self.all.at[:, self.part_columns(i)], self.load_sems.at[1 + i]
-        )
+    def piece_load(self, p, source, span):
+        return pltpu.make_async_copy(source, self.all.at[:, span], self.load_sems.at[1 + p])
 
     def left_copy(self, q):
         return to_dp(
@@ -640,10 +548,10 @@
             self.left_sems.at[0, q], self.left_sems.at[1, q], partner_of(self.member),
         )
 
-    def part_copy(self, i):
+    def piece_copy(self, p, source, span):
         return to_dp(
-            self.parts[i], self.all_in.at[:, self.part_columns(i)],
-            self.part_sems.at[0, i], self.part_sems.at[1, i], partner_of(self.member),
+            source, self.all_in.at[:, span], self.piece_sems.at[0, p], self.piece_sems.at[1, p],
+            partner_of(self.member),
         )
 
     def start_left(self):
@@ -652,10 +560,6 @@
             self.left_copy(q).start()
 
         self.left_load().start()
-
-    def start_part(self, i):
-        self.part_copy(i).start()
-        self.part_load(i).start()
 
     def ready_left(self):
         self.left_load().wait()
@@ -714,8 +618,6 @@
         def _(q):
             self.left_copy(q).wait_send()
 
-        for i in range(len(self.parts)):
-            self.part_copy(i).wait_send()
         for t in range(len(self.tiles)):
             @pl.loop(1, self.team)
             def _(k):
@@ -733,60 +635,473 @@
     return take
 
 
+def one_hot(index, base, shape, dim):
+    return (index == base + lax.broadcasted_iota(jnp.int32, shape, dim)).astype(f32).astype(bf16)
+
+
+class Exchange:
+    def __init__(self, groups, sent, came, sems):
+        self.groups, self.sent, self.came, self.sems = groups, sent, came, sems
+        self.member = lax.axis_index("dp")
+        self.cap = sent.shape[0] // groups
+
+    @staticmethod
+    def scratch(groups, slots, width):
+        return [
+            pltpu.VMEM((slots, width), bf16),
+            pltpu.VMEM((slots, width), bf16),
+            pltpu.SemaphoreType.DMA((2, groups)),
+        ]
+
+    def part(self, j):
+        return pl.ds(pl.multiple_of(j * self.cap, self.cap), self.cap)
+
+    def copy(self, to, source):
+        return to_dp(
+            self.sent.at[self.part(to), :], self.came.at[self.part(source), :],
+            self.sems.at[0, to], self.sems.at[1, source], to,
+        )
+
+    def send(self, index_ref, dim, source):
+        groups, count = self.groups, source.shape[0]
+        rows = self.sent.shape[0] // 2
+
+        @pl.loop(0, 2)
+        def _(h):
+            at = pl.ds(pl.multiple_of(h * rows, rows), rows)
+            if dim == 0:
+                pick = one_hot(index_ref[...], h * rows, (rows, count), 0)
+            else:
+                pick = one_hot(index_ref[at, :], 0, (rows, count), 1)
+            self.sent[at, :] = dot(pick, source[...]).astype(bf16)
+
+            @pl.loop(0, groups // 2)
+            def _(k):
+                to = h * (groups // 2) + lax.rem(self.member + k, groups // 2)
+
+                @pl.when(to != self.member)
+                def _():
+                    self.copy(to, self.member).start()
+
+        self.came[self.part(self.member), :] = self.sent[self.part(self.member), :]
+
+    def receive(self):
+        @pl.loop(1, self.groups)
+        def _(k):
+            self.copy(0, lax.rem(self.member + k, self.groups)).wait_recv()
+
+    def drain(self):
+        @pl.loop(1, self.groups)
+        def _(k):
+            self.copy(lax.rem(self.member + k, self.groups), self.member).wait_send()
+
+
+def place_rows(slot_row_ref, came, held):
+    positions, slots = held.shape[0], came.shape[0]
+    rows = positions // 2
+
+    @pl.loop(0, 2)
+    def _(h):
+        at = pl.ds(pl.multiple_of(h * rows, rows), rows)
+        pick = one_hot(slot_row_ref[...], h * rows, (rows, slots), 0)
+        held[at, :] = dot(pick, came[...]).astype(bf16)
+
+
+def front_kernel(n, groups, dk, dv, *refs):
+    take = splitter(refs)
+    lengths_ref, slots_ref, tokens_ref, mixer_gain_ref, feed_gain_ref, head_gain_ref = take(6)
+    up_ref, bias_ref = take(2)
+    weights_far = take(4)
+    gate_far, out_far, cotangent_far, down_far = take(4)
+    normed_ref, gate_ref, attended_ref, gated_ref, feed_ref, hidden_ref, d_active_ref = take(7)
+    held_ref, states_ref, send_row_ref, send_column_ref, slot_row_ref, slot_column_ref = take(6)
+    up_in, down_in, weight_ref, gate_weight_ref, out_weight_ref, cotangent_ref, down_ref = take(7)
+    rows_out, share_ref, state, result, rank_ref, load_sems, sems = take(7)
+    go = Exchange(groups, *take(3))
+    back = Exchange(groups, *take(3))
+    member = lax.axis_index("dp")
+    count, width = tokens_ref.shape
+    cap = OWN_CAP // groups
+    half = count // 2
+    end0 = lengths_ref[0, 0]
+    end1 = end0 + lengths_ref[0, 1]
+    ends = (end0, end1, end1 + lengths_ref[0, 2])
+    third = LANES // 4
+
+    def finish(total, own, place):
+        hidden = tokens_ref[place, :].astype(f32) + total
+        hidden_ref[own, :] = hidden
+        scaling = lax.rsqrt(jnp.mean(hidden * hidden, axis=1, keepdims=True) + epsilon)
+        feed_ref[place, :] = (hidden * scaling * feed_gain_ref[...]).astype(bf16)
+
+    line = Line(n, share_ref, up_in, down_in, feed_ref, sems, finish)
+    loads = []
+    offset = 0
+    for i, far in enumerate(weights_far):
+        wide = far.shape[1]
+        loads.append(
+            pltpu.make_async_copy(far, weight_ref.at[:, pl.ds(offset, wide)], load_sems.at[i])
+        )
+        offset += wide
+    later = [
+        pltpu.make_async_copy(gate_far, gate_weight_ref, load_sems.at[4]),
+        pltpu.make_async_copy(out_far, out_weight_ref, load_sems.at[5]),
+    ]
+    latest = [
+        pltpu.make_async_copy(cotangent_far, cotangent_ref, load_sems.at[6]),
+        pltpu.make_async_copy(down_far, down_ref, load_sems.at[7]),
+    ]
+    for c in loads + later + latest:
+        c.start()
+    barrier = pltpu.get_barrier_semaphore()
+    greet_dp(barrier, groups)
+    line.greet(barrier, groups - 1)
+
+    owners = slots_ref[...] // OWN_CAP
+    mine = owners == member
+    my_slots = slots_ref[pl.ds(member, 1), :]
+    my_owner = my_slots // OWN_CAP
+    device = lax.broadcasted_iota(jnp.int32, (groups, count), 0)
+    chosen = (my_owner == device).astype(f32)
+    before = (
+        lax.broadcasted_iota(jnp.int32, (count, count), 0)
+        < lax.broadcasted_iota(jnp.int32, (count, count), 1)
+    ).astype(f32).astype(bf16)
+    send_rank = jnp.sum(chosen * dot(chosen.astype(bf16), before), axis=0, keepdims=True)
+    send_row = my_owner * cap + send_rank.astype(jnp.int32)
+    send_row_ref[...] = send_row
+    send_column_ref[...] = jnp.transpose(
+        jnp.broadcast_to(send_row.astype(f32), (8, count))
+    )[:, :1].astype(jnp.int32)
+    rank_ref[...] = jnp.where(mine, dot(mine.astype(f32).astype(bf16), before), -1.0)
+
+    tile = count // 5
+
+    @pl.loop(0, 5)
+    def _(i):
+        at = pl.ds(pl.multiple_of(i * tile, tile), tile)
+        rows = tokens_ref[at, :].astype(f32)
+        scaling = lax.rsqrt(jnp.mean(rows * rows, axis=1, keepdims=True) + epsilon)
+        normed_ref[at, :] = (rows * scaling * mixer_gain_ref[...]).astype(bf16)
+
+    for c in loads:
+        c.wait()
+    body = 2 * dk + dv
+
+    @pl.loop(0, body // 256)
+    def _(i):
+        to = pl.ds(pl.multiple_of(i * 256, 256), 256)
+        rows_out[:, to] = dot(normed_ref[...], weight_ref[:, to]).astype(bf16)
+
+    latent = dot(normed_ref[...], weight_ref[:, body:])
+    high = latent.astype(bf16).astype(f32)
+    middle = (latent - high).astype(bf16).astype(f32)
+    lane = lax.broadcasted_iota(jnp.int32, latent.shape, 1)
+    rows_out[:, body:] = jnp.where(
+        lane < third, high, jnp.where(lane < 2 * third, middle, latent - high - middle)
+    ).astype(bf16)
+    go.send(send_row_ref, 0, rows_out)
+
+    for c in later:
+        c.wait()
+
+    @pl.loop(0, dv // 256)
+    def _(i):
+        to = pl.ds(pl.multiple_of(i * 256, 256), 256)
+        gate_ref[:, to] = dot(normed_ref[...], gate_weight_ref[:, to])
+
+    @pl.loop(0, groups)
+    def _(j):
+        rank = rank_ref[pl.ds(j, 1), :]
+        local = (lax.rem(slots_ref[pl.ds(j, 1), :], OWN_CAP) - OWN_CAP).astype(f32)
+        wanted = lax.broadcasted_iota(jnp.int32, (cap, count), 0).astype(f32)
+        at = jnp.sum(jnp.where(rank == wanted, local, 0.0), axis=1, keepdims=True)
+        slot_column_ref[go.part(j), :] = at.astype(jnp.int32) + OWN_CAP
+
+    slots = slot_row_ref.shape[1]
+    slot_row_ref[...] = jnp.transpose(
+        jnp.broadcast_to(slot_column_ref[...].astype(f32), (slots, LANES))
+    )[:1, :].astype(jnp.int32)
+    state[...] = jnp.zeros_like(state)
+    go.receive()
+    place_rows(slot_row_ref, go.came, held_ref)
+
+    @pl.loop(0, held_ref.shape[0] // SPAN)
+    def _(step):
+        span_forward(dk, dv, step, ends, held_ref, up_ref, bias_ref, state, states_ref, result)
+
+    back.send(slot_column_ref, 1, result)
+    back.receive()
+
+    def head_rows(at):
+        pick = one_hot(send_column_ref[at, :], 0, (half, slots), 1)
+        attended = dot(pick, back.came[...])
+        attended_ref[at, :] = attended.astype(bf16)
+        gate = gate_ref[at, :]
+        scaling = lax.rsqrt(jnp.mean(attended * attended, axis=1, keepdims=True) + head_floor)
+        gated = attended * scaling * head_gain_ref[...] * (gate * jax.nn.sigmoid(gate))
+        gated_ref[at, :] = gated.astype(bf16)
+
+        @pl.loop(0, width // 512)
+        def _(i):
+            to = pl.ds(pl.multiple_of(i * 512, 512), 512)
+            share_ref[at, to] = dot(gated_ref[at, :], out_weight_ref[:, to]).astype(bf16)
+
+    last = line.me == n - 1
+
+    @pl.loop(0, 2)
+    def _(i):
+        bottom = jnp.where(last, 1 - i, i)
+        head_rows(pl.ds(pl.multiple_of(bottom * half, half), half))
+        line.prime(i == 0, i == 0)
+
+    wide = d_active_ref.shape[1]
+    full, rest = wide // 256, wide % 256
+
+    def hidden_units(i, size):
+        at = pl.ds(pl.multiple_of(i * 256, 256), size)
+        d_active_ref[:, at] = dot_t(cotangent_ref[...], down_ref[at, :]).astype(bf16)
+
+    for c in latest:
+        c.wait()
+
+    @pl.loop(0, line.steps)
+    def _(step):
+        line.step(step)
+        i = step // 2 - 2
+
+        @pl.when((lax.rem(step, 2) == 0) & (i >= 0) & (i < full))
+        def _():
+            hidden_units(i, 256)
+
+        if rest:
+            @pl.when(step == 2 * full + 4)
+            def _():
+                hidden_units(full, rest)
+
+    line.drain()
+    go.drain()
+    back.drain()
+
+
+def front(
+    call, n, groups, lengths, slots, tokens, mixer_gain, feed_gain, head_gain, up_wide, bias, weights,
+    gate_weight, out_weight, cotangent, feed_down,
+):
+    count, width = tokens.shape
+    dk, dv = weights[0].shape[1], weights[2].shape[1]
+    wide = sum(w.shape[1] for w in weights)
+    half = count // 2
+    spans = OWN_CAP // SPAN
+    vmem = pl.BlockSpec(memory_space=pltpu.VMEM)
+    far = pl.BlockSpec(memory_space=pl.ANY)
+    smem = pl.BlockSpec(memory_space=pltpu.SMEM)
+    shape = jax.ShapeDtypeStruct
+    return pl.pallas_call(
+        functools.partial(front_kernel, n, groups, dk, dv),
+        in_specs=[smem] + [vmem] * 7 + [far] * 8,
+        out_specs=[vmem] * 13,
+        out_shape=[
+            shape((count, width), bf16),
+            shape((count, dv), f32),
+            shape((count, dv), bf16),
+            shape((count, dv), bf16),
+            shape((count, width), bf16),
+            shape((half, width), f32),
+            shape((count, feed_down.shape[0]), bf16),
+            shape((OWN_CAP, wide), bf16),
+            shape((spans, dk, dv), bf16),
+            shape((1, count), jnp.int32),
+            shape((count, 1), jnp.int32),
+            shape((1, OWN_CAP), jnp.int32),
+            shape((OWN_CAP, 1), jnp.int32),
+        ],
+        scratch_shapes=Line.scratch(half, width)
+        + [
+            pltpu.VMEM((width, wide), bf16),
+            pltpu.VMEM((width, dv), bf16),
+            pltpu.VMEM((dv, width), bf16),
+            pltpu.VMEM((count, width), bf16),
+            pltpu.VMEM(feed_down.shape, bf16),
+            pltpu.VMEM((count, wide), bf16),
+            pltpu.VMEM((count, width), bf16),
+            pltpu.VMEM((dk, dv), f32),
+            pltpu.VMEM((OWN_CAP, dv), bf16),
+            pltpu.VMEM((groups, count), f32),
+            pltpu.SemaphoreType.DMA((8,)),
+            Line.semaphores(half),
+        ]
+        + Exchange.scratch(groups, OWN_CAP, wide)
+        + Exchange.scratch(groups, OWN_CAP, dv),
+        compiler_params=pltpu.CompilerParams(
+            collective_id=call, has_side_effects=True, vmem_limit_bytes=60 << 20
+        ),
+        cost_estimate=pl.CostEstimate(
+            flops=12_000_000_000, bytes_accessed=200_000_000, transcendentals=4_000_000
+        ),
+        name="front",
+    )(
+        lengths, slots, tokens, mixer_gain, feed_gain, head_gain, up_wide, bias, *weights,
+        gate_weight, out_weight, cotangent, feed_down,
+    )
+
+
 def back_feed_kernel(n, groups, tiles, outs, *refs):
     take = splitter(refs)
-    share_ref, gain_ref, x_far, base_far, left_far = take(5)
-    parts = take(2)
+    gain_ref, x_far, base_far, left_far, d_active_far, gate_far, up_far, down_far = take(8)
     out_ref, kept_ref, gain_grad_ref = take(3)
     outputs = take(2)
-    up_in, down_in, x_ref, base_ref, load_sems, sems = take(6)
-    rows = RowGrads(groups, left_far, parts, tiles, outs, outputs, take(10))
+    active_ref, layer_ref = take(2)
+    up_in, down_in, x_ref, base_ref, share_ref, weight_ref, d_active_ref = take(7)
+    load_sems, weight_sems, sems = take(3)
+    rows = RowGrads(groups, left_far, tiles, outs, outputs, take(10))
     finish = norm_back(x_ref, base_ref, gain_ref, out_ref, kept_ref, gain_grad_ref)
     line = Line(n, share_ref, up_in, down_in, out_ref, sems, finish)
+    count, width = share_ref.shape
+    wide = active_ref.shape[1]
+    full, rest = wide // 256, wide % 256
+    pieces = full + (rest > 0)
     loads = (
+        pltpu.make_async_copy(d_active_far, d_active_ref, load_sems.at[2]),
         pltpu.make_async_copy(x_far, x_ref, load_sems.at[0]),
         pltpu.make_async_copy(base_far, base_ref, load_sems.at[1]),
     )
+    down_load = pltpu.make_async_copy(
+        down_far, weight_ref.at[pl.ds(0, wide), pl.ds(0, width)], load_sems.at[3]
+    )
+
+    def spans(i, size):
+        start = pl.multiple_of(i * 256, 256)
+        return pl.ds(start, size), pl.ds(pl.multiple_of(wide + start, LANES), size)
+
+    def weight_loads(i, size):
+        gate_span, up_span = spans(i, size)
+        return (
+            pltpu.make_async_copy(
+                gate_far.at[:, gate_span], weight_ref.at[:, gate_span], weight_sems.at[0, i]
+            ),
+            pltpu.make_async_copy(
+                up_far.at[:, gate_span], weight_ref.at[:, up_span], weight_sems.at[1, i]
+            ),
+        )
+
+    def piece_copies(i, size):
+        gate_span, up_span = spans(i, size)
+        return (
+            rows.piece_copy(2 * i, rows.all.at[:, gate_span], gate_span),
+            rows.piece_copy(2 * i + 1, rows.all.at[:, up_span], up_span),
+        )
+
+    def each(action):
+        @pl.loop(0, full)
+        def _(i):
+            action(i, 256)
+
+        if rest:
+            action(full, rest)
+
+    def start_weights(i, size):
+        for c in weight_loads(i, size):
+            c.start()
+
+    rows.left_load().start()
+    each(start_weights)
+    for c in loads:
+        c.start()
     barrier = pltpu.get_barrier_semaphore()
     greet_dp(barrier, groups)
     line.greet(barrier, groups - 1)
-    line.prime()
-    rows.start_left()
-    for i in range(2):
-        rows.start_part(i)
-    for c in loads:
-        c.start()
+
+    @pl.loop(0, rows.team)
+    def _(q):
+        rows.left_copy(q).start()
+
+    rows.left_load().wait()
     for c in loads:
         c.wait()
-    first_work = 3
+
+    def hidden_units(i, size):
+        for c in weight_loads(i, size):
+            c.wait()
+        gate_span, up_span = spans(i, size)
+        gate = dot(rows.left[...], weight_ref[:, gate_span])
+        up = dot(rows.left[...], weight_ref[:, up_span])
+        d_active = d_active_ref[:, gate_span].astype(f32)
+        sigmoid = jax.nn.sigmoid(gate)
+        swish = gate * sigmoid
+        active_ref[:, gate_span] = (swish * up).astype(bf16)
+        rows.all[:, gate_span] = (
+            d_active * up * sigmoid * (1.0 + gate * (1.0 - sigmoid))
+        ).astype(bf16)
+        rows.all[:, up_span] = (d_active * swish).astype(bf16)
+        for c in piece_copies(i, size):
+            c.start()
+
+    each(hidden_units)
+
+    half = count // 2
+    last = line.me == n - 1
+
+    @pl.loop(0, 2)
+    def _(i):
+        bottom = jnp.where(last, 1 - i, i)
+        at = pl.ds(pl.multiple_of(bottom * half, half), half)
+
+        @pl.loop(0, width // 256)
+        def _(j):
+            to = pl.ds(pl.multiple_of(j * 256, 256), 256)
+            share_ref[at, to] = dot_t(rows.all[at, :], weight_ref[to, :]).astype(bf16)
+
+        line.prime(i == 0, i == 0)
+
+    down_load.start()
+
+    def piece_arrived(i, size):
+        for c in piece_copies(i, size):
+            c.wait_recv()
+
+    layer_items = width // 512
 
     @pl.loop(0, line.steps)
     def _(step):
         line.step(step)
-        w = step - first_work
-
-        @pl.when(w == 0)
-        def _():
-            rows.ready_left()
-            rows.part_load(0).wait()
-            rows.part_copy(0).wait_recv()
-
-        @pl.when(w == len(tiles) // 2)
-        def _():
-            rows.part_load(1).wait()
-            rows.part_copy(1).wait_recv()
-
-        rows.item(w)
+
+        @pl.when(step == 0)
+        def _():
+            @pl.loop(0, rows.team)
+            def _(q):
+                rows.left_copy(q).wait_recv()
+
+            each(piece_arrived)
+
+        rows.item(step)
+        layer_item = step - rows.items
+
+        @pl.when(layer_item == 0)
+        def _():
+            down_load.wait()
+
+        @pl.when((layer_item >= 0) & (layer_item < layer_items))
+        def _():
+            to = pl.ds(pl.multiple_of(layer_item * 512, 512), 512)
+            layer_ref[:, to] = dot(active_ref[...], weight_ref[pl.ds(0, wide), to]).astype(bf16)
 
     rows.receive()
     line.drain()
     rows.drain()
 
-
-def back_feed(call, n, groups, share, gain, x_own, base_own, left, parts):
-    count, width = share.shape
+    def piece_sent(i, size):
+        for c in piece_copies(i, size):
+            c.wait_send()
+
+    each(piece_sent)
+
+
+def back_feed(call, n, groups, gain, x_own, base_own, left, d_active, feed_gate, feed_up, feed_down):
+    count, width = left.shape
     half = count // 2
-    wide = parts[0].shape[1]
+    wide = feed_gate.shape[1]
+    pieces = (wide + 255) // 256
     cut = (wide // 2 + LANES - 1) // LANES * LANES
     tiles = [(0, cut), (cut, wide - cut), (wide, cut), (wide + cut, wide - cut)]
     outs = [(0, wide), (wide, wide)]
@@ -794,31 +1109,37 @@
     far = pl.BlockSpec(memory_space=pl.ANY)
     return pl.pallas_call(
         functools.partial(back_feed_kernel, n, groups, tiles, outs),
-        in_specs=[vmem] * 2 + [far] * 5,
-        out_specs=[vmem] * 5,
+        in_specs=[vmem] + [far] * 7,
+        out_specs=[vmem] * 7,
         out_shape=[
             jax.ShapeDtypeStruct((count, width), bf16),
             jax.ShapeDtypeStruct((half, width), f32),
             jax.ShapeDtypeStruct((8, width), f32),
             jax.ShapeDtypeStruct((width // groups, wide), f32),
             jax.ShapeDtypeStruct((width // groups, wide), f32),
+            jax.ShapeDtypeStruct((count, wide), bf16),
+            jax.ShapeDtypeStruct((count, width), bf16),
         ],
         scratch_shapes=Line.scratch(half, width)
         + [
             pltpu.VMEM((half, width), x_own.dtype),
             pltpu.VMEM((half, width), base_own.dtype),
-            pltpu.SemaphoreType.DMA((2,)),
+            pltpu.VMEM((count, width), bf16),
+            pltpu.VMEM((width, 2 * wide), bf16),
+            pltpu.VMEM((count, wide), bf16),
+            pltpu.SemaphoreType.DMA((4,)),
+            pltpu.SemaphoreType.DMA((2, pieces)),
             Line.semaphores(half),
         ]
-        + RowGrads.scratch(groups, count, width, 2 * wide, 2, len(tiles)),
+        + RowGrads.scratch(groups, count, width, 2 * wide, 2 * pieces, len(tiles)),
         compiler_params=pltpu.CompilerParams(
-            collective_id=call, has_side_effects=True, vmem_limit_bytes=60 << 20
+            collective_id=call, has_side_effects=True, vmem_limit_bytes=61 << 20
         ),
         cost_estimate=pl.CostEstimate(
-            flops=12_000_000_000, bytes_accessed=200_000_000, transcendentals=0
+            flops=30_000_000_000, bytes_accessed=200_000_000, transcendentals=0
         ),
         name="back_feed",
-    )(share, gain, x_own, base_own, left, *parts)
+    )(gain, x_own, base_own, left, d_active, feed_gate, feed_up, feed_down)
 
 
 class SmallSum:
@@ -948,7 +1269,12 @@
     (col_out,) = take(1)
     up_in, down_in, x_ref, base_ref, kept_ref, share_ref, wide_ref, gain_grad_ref = take(8)
     weight_ref, load_sems, sems = take(3)
-    rows = RowGrads(groups, left_far, parts, tiles, outs, outputs, take(10))
+    rows = RowGrads(groups, left_far, tiles, outs, outputs, take(10))
+    part_spans = [
+        pl.ds(0, parts[0].shape[1]), pl.ds(parts[0].shape[1], parts[1].shape[1])
+    ]
+    part_loads = [rows.piece_load(i, parts[i], part_spans[i]) for i in range(2)]
+    part_copies = [rows.piece_copy(i, parts[i], part_spans[i]) for i in range(2)]
     cols = ColGrad(groups, col_left, col_right, col_out, take(9))
     small = SmallSum(n, groups, wide_ref, near_ref, near_all, wide_out, near_out, take(6))
     finish = norm_back(x_ref, base_ref, gain_ref, out_ref, kept_ref, gain_grad_ref)
@@ -966,23 +1292,19 @@
             )
         )
         offset += wide
-    for i in range(2):
-        rows.part_load(i).start()
-    for c in weight_loads:
+    for c in part_loads + weight_loads:
         c.start()
     barrier = pltpu.get_barrier_semaphore()
     greet_dp(barrier, groups)
     small.greet(barrier)
     line.greet_all(barrier, groups - 1)
     rows.start_left()
-    for i in range(2):
-        rows.part_copy(i).start()
+    for c in part_copies:
+        c.start()
     cols.start()
     for c in loads:
         c.start()
-    for i in range(2):
-        rows.part_load(i).wait()
-    for c in weight_loads:
+    for c in part_loads + weight_loads:
         c.wait()
 
     count, width = share_ref.shape
@@ -1010,8 +1332,8 @@
         @pl.when(step == 0)
         def _():
             rows.ready_left()
-            for i in range(2):
-                rows.part_copy(i).wait_recv()
+            for c in part_copies:
+                c.wait_recv()
 
         rows.item(step)
 
@@ -1043,6 +1365,8 @@
     small.receive()
     line.drain()
     rows.drain()
+    for c in part_copies:
+        c.wait_send()
     cols.drain()
     small.drain()
 
@@ -1094,24 +1418,20 @@
     )(gain, near, x_own, base_own, left, *parts, *pair, *weights)
 
 
-def one_hot(index, base, shape, dim):
-    return (index == base + lax.broadcasted_iota(jnp.int32, shape, dim)).astype(f32).astype(bf16)
-
-
 def recur_back_kernel(n, groups, dk, dv, beside, *refs):
     (
         lengths_ref, send_row_ref, send_column_ref, slot_row_ref, slot_column_ref,
         d_mixed_ref, out_weight_ref, attended_ref, gate_ref, gain_ref, up_ref, bias_ref, down_ref,
         share_ref, held_far, states_far, hidden_far, active_far, cotangent_far,
         d_rows_ref, d_gate_ref, head_gain_ref, grad_up_ref, grad_bias_ref, layer_ref, grad_down_ref,
-        up_in, down_in, d_attended, sent, came, d_state, result, back_sent, back_came,
-        held_ref, states_ref, hidden_ref, load_sems, sems, go_sems, back_sems,
-    ) = refs[:42]
-    cols = ColGrad(groups, active_far, cotangent_far, grad_down_ref, refs[42:]) if beside else None
-    member = lax.axis_index("dp")
+        up_in, down_in, d_attended, d_placed, d_state, result,
+        held_ref, states_ref, hidden_ref, load_sems, sems,
+    ) = refs[:37]
+    go = Exchange(groups, *refs[37:40])
+    back = Exchange(groups, *refs[40:43])
+    cols = ColGrad(groups, active_far, cotangent_far, grad_down_ref, refs[43:]) if beside else None
     count = d_mixed_ref.shape[0]
     slots = slot_row_ref.shape[1]
-    cap = slots // groups
     end0 = lengths_ref[0, 0]
     end1 = end0 + lengths_ref[0, 1]
     ends = (end0, end1, end1 + lengths_ref[0, 2])
@@ -1135,25 +1455,10 @@
         cols.start()
     loads[0].wait()
 
-    def part(j):
-        return pl.ds(pl.multiple_of(j * cap, cap), cap)
-
-    def go_copy(to, source):
-        return pltpu.make_async_remote_copy(
-            sent.at[part(to), :], came.at[part(source), :], go_sems.at[0, to],
-            go_sems.at[1, source], device_id={"dp": to}, device_id_type=MESH,
-        )
-
-    def back_copy(to, source):
-        return pltpu.make_async_remote_copy(
-            back_sent.at[part(to), :], back_came.at[part(source), :], back_sems.at[0, to],
-            back_sems.at[1, source], device_id={"dp": to}, device_id_type=MESH,
-        )
-
     head_gain_ref[...] = jnp.zeros_like(head_gain_ref)
-    tile = count // 5
-
-    @pl.loop(0, 5)
+    tile = count // 2
+
+    @pl.loop(0, 2)
     def _(i):
         rows = pl.ds(pl.multiple_of(i * tile, tile), tile)
         d_gated = dot_t(d_mixed_ref[rows, :], out_weight_ref[...])
@@ -1176,54 +1481,38 @@
         for r in range(1, tile // 8):
             piece = piece + term[8 * r : 8 * r + 8, :]
         head_gain_ref[...] += piece
-        line.step(i)
-
-    @pl.loop(1, groups + 1)
-    def _(k):
-        to = lax.rem(member + k, groups)
-        pick = one_hot(send_row_ref[...], to * cap, (cap, count), 0)
-        block = dot(pick, d_attended[...]).astype(bf16)
-
-        @pl.when(k < groups)
-        def _():
-            sent[part(to), :] = block
-            go_copy(to, member).start()
-
-        @pl.when(k == groups)
-        def _():
-            came[part(member), :] = block
-
+        line.step(2 * i)
+        line.step(2 * i + 1)
+
+    go.send(send_row_ref, 0, d_attended)
     d_state[...] = jnp.zeros_like(d_state)
     grad_up_ref[...] = jnp.zeros_like(grad_up_ref)
     grad_bias_ref[...] = jnp.zeros_like(grad_bias_ref)
-    done = 13
+    done = 12
     if beside:
         cols.ready()
 
         @pl.loop(0, cols.items)
         def _(i):
             cols.item(i)
+            line.step(4 + 2 * i)
             line.step(5 + 2 * i)
-            line.step(6 + 2 * i)
-
-        done = 5 + 2 * cols.items
+
+        done = 4 + 2 * cols.items
         cols.send_all()
     else:
-        line.run(5, done)
+        line.run(4, done)
     for c in loads[1:]:
         c.wait()
 
-    @pl.loop(1, groups)
-    def _(k):
-        go_copy(0, lax.rem(member + k, groups)).wait_recv()
-
+    go.receive()
+    place_rows(slot_row_ref, go.came, d_placed)
     spans = held_ref.shape[0] // SPAN
 
     @pl.loop(0, spans)
     def _(i):
         step = spans - 1 - i
-        place = one_hot(slot_row_ref[...], step * SPAN, (SPAN, slots), 0)
-        d_out = dot(place, came[...]).astype(bf16)
+        d_out = d_placed[pl.ds(pl.multiple_of(step * SPAN, SPAN), SPAN), :]
         span_backward(
             dk, dv, step, ends, d_out, held_ref, states_ref[step], up_ref, bias_ref, down_ref,
             d_state, result, grad_up_ref, grad_bias_ref,
@@ -1231,50 +1520,28 @@
         line.step(done + 2 * i)
         line.step(done + 1 + 2 * i)
 
-    positions = result.shape[0]
-
-    @pl.loop(1, groups + 1)
-    def _(k):
-        to = lax.rem(member + k, groups)
-        pick = one_hot(slot_column_ref[part(to), :], 0, (cap, positions), 1)
-        block = dot(pick, result[...]).astype(bf16)
-
-        @pl.when(k < groups)
-        def _():
-            back_sent[part(to), :] = block
-            back_copy(to, member).start()
-
-        @pl.when(k == groups)
-        def _():
-            back_came[part(member), :] = block
-
+    back.send(slot_column_ref, 1, result)
     line.run(done + 2 * spans, line.steps)
     if beside:
         cols.receive()
 
-    @pl.loop(1, groups)
-    def _(k):
-        back_copy(0, lax.rem(member + k, groups)).wait_recv()
-
-    @pl.loop(0, 5)
+    back.receive()
+
+    @pl.loop(0, 2)
     def _(i):
         rows = pl.ds(pl.multiple_of(i * tile, tile), tile)
         pick = one_hot(send_column_ref[rows, :], 0, (tile, slots), 1)
-        d_rows_ref[rows, :] = dot(pick, back_came[...]).astype(bf16)
+        d_rows_ref[rows, :] = dot(pick, back.came[...]).astype(bf16)
 
     line.drain()
     if beside:
         cols.drain()
-
-    @pl.loop(1, groups)
-    def _(k):
-        to = lax.rem(member + k, groups)
-        go_copy(to, member).wait_send()
-        back_copy(to, member).wait_send()
+    go.drain()
+    back.drain()
 
 
 def recur_back(
-    call, n, groups, dk, dv, beside, lengths, send_pos, slot_map, d_mixed, out_weight, attended, gate_pre,
+    call, n, groups, dk, dv, beside, lengths, send_row, send_column, slot_row, slot_column, d_mixed, out_weight, attended, gate_pre,
     head_gain, up_wide, bias, down_wide, share, held, states, hidden_own, active, cotangent,
 ):
     count, width = d_mixed.shape
@@ -1282,8 +1549,7 @@
     half = count // 2
     vmem = pl.BlockSpec(memory_space=pltpu.VMEM)
     operands = [
-        lengths, send_pos.reshape(1, -1), send_pos.reshape(-1, 1), slot_map.reshape(1, -1),
-        slot_map.reshape(-1, 1), d_mixed, out_weight, attended, gate_pre, head_gain, up_wide, bias,
+        lengths, send_row, send_column, slot_row, slot_column, d_mixed, out_weight, attended, gate_pre, head_gain, up_wide, bias,
         down_wide, share, held, states, hidden_own, active, cotangent,
     ]
     far = pl.BlockSpec(memory_space=pl.ANY)
@@ -1304,19 +1570,16 @@
         + [
             pltpu.VMEM((count, dv), bf16),
             pltpu.VMEM((slots, dv), bf16),
-            pltpu.VMEM((slots, dv), bf16),
             pltpu.VMEM((dk, dv), f32),
-            pltpu.VMEM((slots, wide), bf16),
-            pltpu.VMEM((slots, wide), bf16),
             pltpu.VMEM((slots, wide), bf16),
             pltpu.VMEM(held.shape, bf16),
             pltpu.VMEM(states.shape, bf16),
             pltpu.VMEM((half, width), f32),
             pltpu.SemaphoreType.DMA((3,)),
             Line.semaphores(half),
-            pltpu.SemaphoreType.DMA((2, groups)),
-            pltpu.SemaphoreType.DMA((2, groups)),
         ]
+        + Exchange.scratch(groups, slots, dv)
+        + Exchange.scratch(groups, slots, wide)
         + (ColGrad.scratch(groups, count, active.shape[1], width) if beside else []),
         compiler_params=pltpu.CompilerParams(
             collective_id=call, has_side_effects=True, vmem_limit_bytes=60 << 20
@@ -1456,8 +1719,6 @@
     member = lax.axis_index("dp")
     place = lax.axis_index("tensor")
     count, width = tokens.shape
-    cap = OWN_CAP // groups
-    slots = groups * cap
     dk = query_weight.shape[1]
     dv = value_weight.shape[1]
     rank = decay_up.shape[1]
@@ -1465,121 +1726,65 @@
     pairs = [(i, i ^ 1) for i in range(groups)]
     same_parity = [[i for i in range(groups) if i % 2 == b] for b in range(2)]
 
-    owners = (token_slots // OWN_CAP).reshape(groups, count)
-    mine = (owners == member).astype(bf16)
-    my_slots = lax.dynamic_slice_in_dim(token_slots, member * count, count)
-    my_owner = my_slots // OWN_CAP
-    chosen = (my_owner[None, :] == jnp.arange(groups, dtype=jnp.int32)[:, None]).astype(bf16)
-    index = jnp.arange(count, dtype=jnp.int32)
-    before = (index[:, None] < index[None, :]).astype(bf16)
-    ranks = dot(jnp.concatenate([mine, chosen], axis=0), before).astype(jnp.int32)
-    recv_rank, send_rank = ranks[:groups], ranks[groups:]
-    hit = (recv_rank[:, None, :] == jnp.arange(cap, dtype=jnp.int32)[None, :, None]) & (
-        owners == member
-    )[:, None, :]
-    local = (token_slots % OWN_CAP).reshape(groups, count)
-    slot_map = (
-        jnp.sum(jnp.where(hit, local[:, None, :] - OWN_CAP, 0), axis=2) + OWN_CAP
-    ).reshape(slots)
-    send_pos = my_owner * cap + jnp.sum(
-        jnp.where(chosen > 0, send_rank, 0), axis=0, dtype=jnp.int32
-    )
-    slot_ids = jnp.arange(slots, dtype=jnp.int32)
-    pack = (slot_ids[:, None] == send_pos[None, :]).astype(bf16)
-    unpack = (send_pos[:, None] == slot_ids[None, :]).astype(bf16)
-
-    def exchange(row_block):
-        blocks = row_block.reshape(groups, cap, row_block.shape[1])
-        moved = lax.all_to_all(blocks, "dp", split_axis=0, concat_axis=0, tiled=True)
-        return moved.reshape(slots, row_block.shape[1])
-
     half = count // 2
     own_at = jnp.where(place == 0, half, 0)
     tokens_own = lax.dynamic_slice_in_dim(tokens, own_at, half)
     cotangent_own = lax.dynamic_slice_in_dim(cotangent, own_at, half)
 
-    tokens_wide = tokens.astype(f32)
     mixer_gain_wide = mixer_gain.astype(f32)
     feed_gain_wide = feed_gain.astype(f32)
-    normed = (
-        tokens_wide
-        * lax.rsqrt(jnp.mean(tokens_wide * tokens_wide, axis=-1, keepdims=True) + epsilon)
-        * mixer_gain_wide
-    ).astype(bf16)
-    queries = dot(normed, query_weight).astype(bf16)
-    keys_low = dot(normed, key_weight).astype(bf16)
-    value_rows = dot(normed, value_weight).astype(bf16)
-    gate_pre = dot(normed, gate_weight)
+    head_gain_wide = head_gain.astype(f32)
     third = LANES // 4
     down_pad = jnp.pad(decay_down, ((0, 0), (0, third - rank)))
-    latent = dot(
-        normed,
-        jnp.concatenate([down_pad, down_pad, down_pad, jnp.zeros_like(down_pad)], axis=1),
+    down_none = jnp.zeros_like(down_pad)
+    down_all = jnp.concatenate([down_pad, down_pad, down_pad, down_none], axis=1)
+    up_pad = jnp.pad(decay_up, ((0, 0), (0, third - rank)))
+    up_none = jnp.zeros_like(up_pad)
+    up_wide = jnp.concatenate([up_pad, up_pad, up_pad, up_none], axis=1).T
+    down_wide = jnp.concatenate([up_pad, up_pad, up_none, up_none], axis=1)
+    bias = decay_bias.astype(f32).reshape(1, dk)
+    (
+        normed, gate_pre, attended, gated, feed_normed, hidden_own, d_active, held, states,
+        send_row, send_column, slot_row, slot_column,
+    ) = front(
+        1, lines, groups, lengths, token_slots.reshape(groups, count), tokens,
+        mixer_gain_wide.reshape(1, -1), feed_gain_wide.reshape(1, -1),
+        head_gain_wide.reshape(1, -1), up_wide, bias,
+        [query_weight, key_weight, value_weight, down_all], gate_weight, out_weight, cotangent,
+        feed_down,
     )
-    latent_high = latent.astype(bf16)
-    latent_rest = latent - latent_high.astype(f32)
-    latent_mid = latent_rest.astype(bf16)
-    latent_low = (latent_rest - latent_mid.astype(f32)).astype(bf16)
-    lane = jnp.arange(LANES, dtype=jnp.int32)[None, :]
-    latent_packed = jnp.where(
-        lane < third, latent_high, jnp.where(lane < 2 * third, latent_mid, latent_low)
-    )
-    rows_out = jnp.concatenate([queries, keys_low, value_rows, latent_packed], axis=1)
-    arrived = exchange(dot(pack, rows_out).astype(bf16))
-    up_pad = jnp.pad(decay_up, ((0, 0), (0, third - rank)))
-    up_wide = jnp.concatenate([up_pad, up_pad, up_pad, jnp.zeros_like(up_pad)], axis=1).T
-    down_wide = jnp.concatenate(
-        [up_pad, up_pad, jnp.zeros_like(up_pad), jnp.zeros_like(up_pad)], axis=1
-    )
-    bias = decay_bias.astype(f32).reshape(1, dk)
-    attended_slots, held, states = recur_forward(
-        slot_map, lengths, up_wide, bias, arrived, dk, dv
-    )
-    attended = dot(unpack, exchange(attended_slots)).astype(bf16)
-    head_gain_wide = head_gain.astype(f32)
-    attended_wide = attended.astype(f32)
-    gated = (
-        attended_wide
-        * lax.rsqrt(jnp.mean(attended_wide * attended_wide, axis=-1, keepdims=True) + head_floor)
-        * head_gain_wide
-        * jax.nn.silu(gate_pre)
-    ).astype(bf16)
-    mixer_share = dot(gated, out_weight).astype(bf16)
-    feed_normed, hidden_own = line_sum(
-        "norm", 1, lines, mixer_share, tokens_own, tokens_own, feed_gain_wide.reshape(1, -1)
-    )
-
-    gate_hidden = dot(feed_normed, feed_gate)
-    up_hidden = dot(feed_normed, feed_up)
-    d_active = dot_t(cotangent, feed_down)
-    sigmoid_gate = jax.nn.sigmoid(gate_hidden)
-    swish_gate = gate_hidden * sigmoid_gate
-    active = (swish_gate * up_hidden).astype(bf16)
-    d_gate_hidden = (
-        d_active * up_hidden * sigmoid_gate * (1.0 + gate_hidden * (1.0 - sigmoid_gate))
-    ).astype(bf16)
-    d_up_hidden = (d_active * swish_gate).astype(bf16)
-    feed_share = (dot_t(d_gate_hidden, feed_gate) + dot_t(d_up_hidden, feed_up)).astype(bf16)
+
     fused = (width // groups) % LANES == 0
     if fused:
-        d_mixed, d_hidden_own, feed_gain_part, grad_feed_gate, grad_feed_up = back_feed(
-            2, lines, groups, feed_share, feed_gain_wide.reshape(1, -1), hidden_own, cotangent_own,
-            feed_normed, [d_gate_hidden, d_up_hidden],
+        (
+            d_mixed, d_hidden_own, feed_gain_part, grad_feed_gate, grad_feed_up, active, layer_share,
+        ) = back_feed(
+            2, lines, groups, feed_gain_wide.reshape(1, -1), hidden_own, cotangent_own, feed_normed,
+            d_active, feed_gate, feed_up, feed_down,
         )
     else:
+        gate_hidden = dot(feed_normed, feed_gate)
+        up_hidden = dot(feed_normed, feed_up)
+        d_active = d_active.astype(f32)
+        sigmoid_gate = jax.nn.sigmoid(gate_hidden)
+        swish_gate = gate_hidden * sigmoid_gate
+        active = (swish_gate * up_hidden).astype(bf16)
+        d_gate_hidden = (
+            d_active * up_hidden * sigmoid_gate * (1.0 + gate_hidden * (1.0 - sigmoid_gate))
+        ).astype(bf16)
+        d_up_hidden = (d_active * swish_gate).astype(bf16)
+        feed_share = (dot_t(d_gate_hidden, feed_gate) + dot_t(d_up_hidden, feed_up)).astype(bf16)
         d_mixed, d_hidden_own, feed_gain_part = line_sum(
-            "back", 2, lines, feed_share, hidden_own, cotangent_own, feed_gain_wide.reshape(1, -1)
-        )
-
-    layer_share = dot(active, feed_down).astype(bf16)
+            2, lines, feed_share, hidden_own, cotangent_own, feed_gain_wide.reshape(1, -1)
+        )
+        layer_share = dot(active, feed_down).astype(bf16)
+
     d_rows, d_gate_low, head_gain_part, up_part, bias_part, layer_out, grad_feed_down = recur_back(
-        4, lines, groups, dk, dv, fused, lengths, send_pos, slot_map, d_mixed, out_weight, attended,
-        gate_pre, head_gain_wide.reshape(1, -1), up_wide, bias, down_wide, layer_share, held, states,
+        4, lines, groups, dk, dv, fused, lengths, send_row, send_column, slot_row, slot_column, d_mixed,
+        out_weight, attended, gate_pre, head_gain_wide.reshape(1, -1), up_wide, bias, down_wide, layer_share, held, states,
         hidden_own, active, cotangent,
     )
-    down_both = jnp.concatenate(
-        [down_pad, down_pad, jnp.zeros_like(down_pad), jnp.zeros_like(down_pad)], axis=1
-    )
+    down_both = jnp.concatenate([down_pad, down_pad, down_none, down_none], axis=1)
     up_part = up_part[:, :rank] + up_part[:, third : third + rank] + (
         up_part[:, 2 * third : 2 * third + rank]
     )
@@ -1628,7 +1833,7 @@
             + dot_t(d_latent_low, down_both)
         ).astype(bf16)
         token_grad, _, mixer_gain_part = line_sum(
-            "back", 3, lines, normed_share, tokens_own, d_hidden_own,
+            3, lines, normed_share, tokens_own, d_hidden_own,
             mixer_gain_wide.reshape(1, -1),
         )
         down_part = rows_dot(normed, d_latent_low)

time: 507 us -> 474 us (0.935); the launches traced: 498 us -> 474 us
  Pallas kernels: 363 us -> 436 us
  matrix products: 55.3 us -> 0 us
  waiting for transfers between devices: 27.5 us -> 0 us
  starting transfers between devices: 9.1 us -> 0 us
    pallas_call x2 -> x1, Pallas kernels: 91 us -> 147 us  [front(): pl.pallas_call(functools.partial(front_kernel, n, groups, dk, dv), in_spe...]
    dot_general x15 -> x0, matrix products: 55.3 us -> none  [the longest x12 36.1 us: dot(): return jnp.dot(left, right, preferred_element_type=f32)]
    all_to_all x2 -> x0, waiting for transfers between devices: 27.5 us -> none  [exchange(): lax.all_to_all(blocks, 'dp', split_axis=0, concat_axis=0, tiled=True)]
    pallas_call x1, Pallas kernels: 82.4 us -> 105 us  [back_feed(): pl.pallas_call(functools.partial(back_feed_kernel, n, groups, tiles, outs...]
    all_to_all x2 -> x0, starting transfers between devices: 9.1 us -> none  [exchange(): lax.all_to_all(blocks, 'dp', split_axis=0, concat_axis=0, tiled=True)]
    unnamed x112 -> x38, local copies, waits for them, and re-layouts: 17.8 us -> 14.5 us
  transfers between devices with their start and end apart: 2 -> 0, of which waited for: 2 -> 0; matrix products, arithmetic and copies ran while one was open for 3% -> 0% of each run, Pallas kernels for 0% -> 0%
where the time goes in v6:
time: 474 us
  Pallas kernels  436 us (92%)
  local copies, waits for them, and re-layouts  26.6 us (6%)
  other arithmetic  10.6 us (2%)
    pallas_call x1, Pallas kernels, front(): pl.pallas_call(functools.partial(front_kernel, n, groups, dk, dv), in_spe...  147 us
    pallas_call x1, Pallas kernels, back_feed(): pl.pallas_call(functools.partial(back_feed_kernel, n, groups, tiles, outs...  105 us
    pallas_call x1, Pallas kernels, recur_back(): pl.pallas_call(functools.partial(recur_back_kernel, n, groups, dk, dv, be...  94.1 us
    pallas_call x1, Pallas kernels, back_mixer(): pl.pallas_call(functools.partial(back_mixer_kernel, n, groups, widths, ne...  90.2 us
    unnamed x38, local copies, waits for them, and re-layouts  14.5 us

profile of v6, /device:TPU:0, one launch (start us, length us, event | category | flops | bytes accessed | tf_op | source)
XLA Modules:
  0.0 473.5 jit_solution(14330248690987439894)
XLA Ops:
  0.6 0.0 copy-start.5
  0.7 0.1 pad.29.clone
  0.8 0.1 pad.37.clone
  0.8 1.4 reshape.104
  2.2 1.3 reshape.102
  3.5 1.3 reshape.98
  4.7 1.3 reshape.100
  6.0 1.3 reshape.83.refs_1_
  7.4 0.8 copy.39
  8.2 0.7 fusion.1
  8.9 0.7 copy.41.refs_6_.refs_10_
  9.7 1.1 copy.40
  10.8 0.1 pad.17
  10.9 1.5 fusion
  12.4 0.0 copy-done.5
  12.4 3.0 constant_dynamic-slice_fusion
  15.4 146.5 %front.1 = (bf16[640,2048]{1,0:T(8,128)(2,1)}, f32[640,512]{1,0:T(8,128)}, bf16[640,512]{1,0:T(8,128)(2,1)}, bf16[640,512]{1,0:T(8,128)(2,1)}, bf16[640,2048]{1,...) custom-call(s32[1,3]{1,0:T(1,128)} %refs_0_.3, ...), custom_call_target="tpu_custom_call" | custom-call | flops 12000000000 | bytes 200000000 | tf_op jit(solution)/shard_map/front/pallas_call | solution.py:900
  162.0 104.7 %back_feed.1 = (bf16[640,2048]{1,0:T(8,128)(2,1)}, f32[320,2048]{1,0:T(8,128)}, f32[8,2048]{1,0:T(8,128)}, f32[256,1408]{1,0:T(8,128)}, f32[256,1408]{1,0:T(8,12...) custom-call(f32[1,2048]{1,0:T(1,128)} %bitcast.24, f32[320,2048]{1,0:T(8,128)} %get-tuple-element.55.refs_1_.refs_16_, ...), custom_call_target="tpu_custom_call" | custom-call | flops 30000001024 | bytes 200000000 | tf_op jit(solution)/shard_map/back_feed/pallas_call | solution.py:1110
  266.7 94.1 %recur_back.1 = (bf16[640,1152]{1,0:T(8,128)(2,1)}, bf16[640,512]{1,0:T(8,128)(2,1)}, f32[8,512]{1,0:T(8,128)}, f32[256,128]{1,0:T(8,128)}, f32[8,256]{1,0:T(8,1...) custom-call(s32[1,3]{1,0:T(1,128)} %refs_0_.3, s32[1,640]{1,0:T(1,128)} %get-tuple-element.51.refs_1_, ...), custom_call_target="tpu_custom_call" | custom-call | flops 12000000000 | bytes 200000000 | tf_op jit(solution)/shard_map/recur_back/pallas_call | solution.py:1556
  360.8 0.7 slice_reduce_fusion.1
  361.5 0.7 reduce_sum.28
  362.3 0.1 reshape.93
  362.4 0.1 reshape_squeeze.3
  362.4 1.2 slice_add_fusion
  363.6 0.1 reshape.94
  363.8 0.6 copy.46
  364.4 90.2 %back_mixer.1 = (bf16[640,2048]{1,0:T(8,128)(2,1)}, f32[24,256]{1,0:T(8,128)}, f32[8,128]{1,0:T(8,128)}, f32[256,256]{1,0:T(8,128)}, f32[256,256]{1,0:T(8,128)},...) custom-call(f32[1,2048]{1,0:T(1,128)} %bitcast.22, f32[8,8,128]{2,1,0:T(8,128)} %bitcast.20, ...), custom_call_target="tpu_custom_call" | custom-call | flops 12000000000 | bytes 200000000 | tf_op jit(solution)/shard_map/back_mixer/pallas_call | solution.py:1385
  454.6 1.2 slice.46
  455.8 1.2 slice.45
  457.0 1.3 slice_reduce_fusion
  458.2 1.3 slice_bitcast_fusion
  459.6 1.2 slice_bitcast_fusion.1
  460.8 0.7 slice.44
  461.5 0.1 reshape.96
  461.5 0.7 copy.43
  462.2 1.5 copy.57
  463.7 1.2 copy-done.1
  464.9 1.5 copy.58
  466.4 0.7 copy.59
  467.1 0.7 copy.60
  467.8 0.8 copy.61
  468.6 0.0 copy-done.7
  468.6 0.8 copy.62
  469.4 0.0 copy-done.6
  469.4 0.8 copy.63
  470.2 1.1 copy.64
  471.3 1.1 copy.65
  472.4 1.1 copy.66
  (25 shorter events, 0.1 us)
Async XLA Ops:
  0.6 11.7 %copy-start.5 = (bf16[640,2048]{1,0:T(8,128)(2,1)S(1)}, bf16[640,2048]{1,0:T(8,128)(2,1)}, u32[]{:S(2)}) copy-start(bf16[640,2048]{1,0:T(8,128)(2,1)} %refs_2_.1) | copy-start | bytes 7864324
  266.7 95.5 %copy-start.11 = (f32[8,2048]{1,0:T(8,128)S(1)}, f32[8,2048]{1,0:T(8,128)}, u32[]{:S(2)}) copy-start(f32[8,2048]{1,0:T(8,128)} %get-tuple-element.66) | copy-start | bytes 196612
  364.4 97.8 %copy-start = (bf16[640,2048]{1,0:T(8,128)(2,1)S(1)}, bf16[640,2048]{1,0:T(8,128)(2,1)}, u32[]{:S(2)}) copy-start(bf16[640,2048]{1,0:T(8,128)(2,1)} %get-tuple-element.140) | copy-start | bytes 7864324
  462.2 2.7 copy-start.1
  464.9 1.5 copy-start.10
  464.9 2.2 copy-start.9
  464.9 2.9 copy-start.8
  464.9 3.7 copy-start.7
  466.4 3.0 copy-start.6
  466.4 3.8 copy-start.3
  468.6 2.7 copy-start.2
  470.2 2.2 copy-start.4

commit v7 on v6

--- a/solution.py
+++ b/solution.py
@@ -127,7 +127,7 @@
     d_logits_high = d_logits.astype(bf16)
     d_logits_low = (d_logits - d_logits_high.astype(f32)).astype(bf16)
     grad_up_ref[...] += rows_dot(d_logits_high, latent) + rows_dot(d_logits_low, latent)
-    d_latent = dot(d_logits_high, down_ref[...]) + dot(d_logits_low, down_ref[...])
+    d_latent = dot_t(d_logits_high, down_ref[...]) + dot_t(d_logits_low, down_ref[...])
     high = d_latent.astype(bf16).astype(f32)
     lane = lax.broadcasted_iota(jnp.int32, d_latent.shape, 1)
     d_latent_packed = jnp.where(lane < LANES // 4, high, d_latent - high)
@@ -161,6 +161,9 @@
     def semaphores(half):
         return pltpu.SemaphoreType.DMA((8, half // FINE))
 
+    def own_half(self):
+        return pl.ds(pl.multiple_of(jnp.where(self.me == 0, self.half, 0), self.half), self.half)
+
     def greet(self, barrier, others):
         n, me = self.n, self.me
 
@@ -326,18 +329,19 @@
                 self.up_back_copy(g).wait_send()
 
 
-def norm_back(x_ref, base_ref, gain_ref, out_ref, kept_ref, gain_grad_ref):
+def norm_back(x_ref, base_ref, gain, out_ref, kept_ref, gain_grad_ref):
     gain_grad_ref[...] = jnp.zeros_like(gain_grad_ref)
 
     def finish(total, own, place):
         rows = x_ref[own, :].astype(f32)
         scaling = lax.rsqrt(jnp.mean(rows * rows, axis=1, keepdims=True) + epsilon)
         unit = rows * scaling
-        gained = gain_ref[...] * total
+        gained = gain() * total
         grad = base_ref[own, :].astype(f32) + scaling * (
             gained - unit * jnp.mean(gained * unit, axis=1, keepdims=True)
         )
-        kept_ref[own, :] = grad.astype(kept_ref.dtype)
+        if kept_ref is not None:
+            kept_ref[own, :] = grad
         out_ref[place, :] = grad.astype(out_ref.dtype)
         term = total * unit
         part = term[0:8, :]
@@ -351,7 +355,7 @@
 def line_kernel(n, *refs):
     share_ref, x_ref, base_ref, gain_ref, out_ref, kept_ref, gain_grad_ref = refs[:7]
     up_in, down_in, sems = refs[7:]
-    finish = norm_back(x_ref, base_ref, gain_ref, out_ref, kept_ref, gain_grad_ref)
+    finish = norm_back(x_ref, base_ref, lambda: gain_ref[...], out_ref, kept_ref, gain_grad_ref)
     line = Line(n, share_ref, up_in, down_in, out_ref, sems, finish)
     line.greet(pltpu.get_barrier_semaphore(), 0)
     line.prime()
@@ -403,35 +407,35 @@
 class ColGrad:
     TILE = 256
 
-    def __init__(self, groups, left, right, out, refs):
+    def __init__(self, groups, left, right, first, recv, refs):
         (
-            self.left, self.right, self.left_in, self.right_in, self.send, self.recv,
+            self.left, self.right, self.left_in, self.right_in, self.send,
             self.load_sems, self.pair_sems, self.sems,
         ) = refs
-        self.left_far, self.right_far, self.out, self.groups = left, right, out, groups
+        self.left_far, self.right_far, self.recv, self.groups = left, right, recv, groups
         self.member = lax.axis_index("dp")
         self.parity = lax.rem(self.member, 2)
-        self.half = self.right_in.shape[1]
+        self.half = right.shape[1] // 2
+        self.first, self.wide = first, self.right_in.shape[1]
         self.size = self.send.shape[0] // groups
-        self.items = self.half // self.TILE
+        self.items = self.wide // self.TILE
 
     @staticmethod
-    def scratch(groups, count, rows, width):
-        half = width // 2
+    def scratch(groups, count, rows, wide):
         return [
             pltpu.VMEM((count, rows), bf16),
-            pltpu.VMEM((count, half), bf16),
+            pltpu.VMEM((count, wide), bf16),
             pltpu.VMEM((count, rows), bf16),
-            pltpu.VMEM((count, half), bf16),
-            pltpu.VMEM((rows, half), bf16),
-            pltpu.VMEM((groups, rows // groups, half), bf16),
-            pltpu.SemaphoreType.DMA((2,)),
+            pltpu.VMEM((count, wide), bf16),
+            pltpu.VMEM((rows, wide), bf16),
+            pltpu.SemaphoreType.DMA((3,)),
             pltpu.SemaphoreType.DMA((2, 2)),
             pltpu.SemaphoreType.DMA((2, groups)),
         ]
 
     def halves(self, parity):
-        return self.right_far.at[:, pl.ds(pl.multiple_of(parity * self.half, self.half), self.half)]
+        start = pl.multiple_of(parity * self.half + self.first, self.TILE)
+        return self.right_far.at[:, pl.ds(start, self.wide)]
 
     def loads(self):
         return (
@@ -478,20 +482,21 @@
         def _(k):
             self.copy(lax.rem(self.member + k, self.groups), self.member).start()
 
+        self.keep().start()
+
+    def keep(self):
         own = pl.ds(pl.multiple_of(self.member * self.size, 16), self.size)
-        self.recv[pl.ds(self.member, 1)] = self.send[own, :][None]
+        return pltpu.make_async_copy(
+            self.send.at[own, :], self.recv.at[self.member], self.load_sems.at[2]
+        )
 
     def receive(self):
+        self.keep().wait()
+
         @pl.loop(1, self.groups)
         def _(k):
             self.copy(0, lax.rem(self.member + k, self.groups)).wait_recv()
 
-        for b in range(2):
-            total = self.recv[b].astype(f32)
-            for q in range(1, self.groups // 2):
-                total = total + self.recv[2 * q + b].astype(f32)
-            self.out[:, b * self.half : (b + 1) * self.half] = total
-
     def drain(self):
         for c in self.pair_copies():
             c.wait_send()
@@ -502,13 +507,12 @@
 
 
 class RowGrads:
-    def __init__(self, groups, left, tiles, outs, outputs, refs):
+    def __init__(self, groups, left, tiles, recv, refs):
         (
-            self.left, self.all, self.left_in, self.all_in, self.send, self.recv,
-            self.load_sems, self.left_sems, self.piece_sems, self.sems,
+            self.left, self.all, self.left_in, self.all_in, self.send,
+            self.load_sems, self.left_sems, self.piece_sems, self.sems, self.keep_sems,
         ) = refs
-        self.left_far, self.tiles = left, tiles
-        self.outs, self.outputs = outs, outputs
+        self.left_far, self.tiles, self.recv = left, tiles, recv
         self.member = lax.axis_index("dp")
         self.parity = lax.rem(self.member, 2)
         self.mine = self.member // 2
@@ -525,11 +529,11 @@
             pltpu.VMEM((count, width // 2), bf16),
             pltpu.VMEM((count, total), bf16),
             pltpu.VMEM((team, width // groups, total), bf16),
-            pltpu.VMEM((team, width // groups, total), bf16),
             pltpu.SemaphoreType.DMA((1 + pieces,)),
             pltpu.SemaphoreType.DMA((2, team)),
             pltpu.SemaphoreType.DMA((2, pieces)),
             pltpu.SemaphoreType.DMA((2, tiles, team)),
+            pltpu.SemaphoreType.DMA((tiles,)),
         ]
 
     def columns(self, j):
@@ -589,29 +593,30 @@
                 product = rows_dot(
                     self.left[:, self.columns(2 * to + self.parity)], self.all[:, span]
                 ) + rows_dot(self.left_in[:, self.columns(to)], self.all_in[:, span])
-                low_product = product.astype(bf16)
+                self.send[to, :, span] = product.astype(bf16)
 
                 @pl.when(k < self.team - 1)
                 def _():
-                    self.send[to, :, span] = low_product
                     self.copy(t, to, self.mine).start()
 
                 @pl.when(k == self.team - 1)
                 def _():
-                    self.recv[self.mine, :, span] = low_product
+                    self.keep(t).start()
+
+    def keep(self, t):
+        start, wide = self.tiles[t]
+        span = pl.ds(start, wide)
+        return pltpu.make_async_copy(
+            self.send.at[self.mine, :, span], self.recv.at[self.mine, :, span], self.keep_sems.at[t]
+        )
 
     def receive(self):
         for t in range(len(self.tiles)):
+            self.keep(t).wait()
+
             @pl.loop(1, self.team)
             def _(k):
                 self.copy(t, 0, lax.rem(self.mine + k, self.team)).wait_recv()
-
-        for (start, wide), output in zip(self.outs, self.outputs):
-            span = pl.ds(start, wide)
-            total = self.recv[0, :, span].astype(f32)
-            for q in range(1, self.team):
-                total = total + self.recv[q, :, span].astype(f32)
-            output[...] = total
 
     def drain(self):
         @pl.loop(0, self.team)
@@ -639,30 +644,41 @@
     return (index == base + lax.broadcasted_iota(jnp.int32, shape, dim)).astype(f32).astype(bf16)
 
 
+def thirds(source, terms, target):
+    third = LANES // 4
+    size = source.shape[0]
+    target[...] = jnp.zeros_like(target)
+    for i in range(terms):
+        target[i * third : i * third + size, :] = source[...]
+
+
 class Exchange:
-    def __init__(self, groups, sent, came, sems):
+    def __init__(self, groups, cuts, sent, came, sems):
         self.groups, self.sent, self.came, self.sems = groups, sent, came, sems
+        self.spans = [pl.ds(a, b - a) for a, b in zip((0,) + cuts, cuts + (sent.shape[1],))]
         self.member = lax.axis_index("dp")
         self.cap = sent.shape[0] // groups
 
     @staticmethod
-    def scratch(groups, slots, width):
+    def scratch(groups, slots, width, pieces):
         return [
             pltpu.VMEM((slots, width), bf16),
             pltpu.VMEM((slots, width), bf16),
-            pltpu.SemaphoreType.DMA((2, groups)),
+            pltpu.SemaphoreType.DMA((2, pieces, groups)),
         ]
 
     def part(self, j):
         return pl.ds(pl.multiple_of(j * self.cap, self.cap), self.cap)
 
-    def copy(self, to, source):
+    def copy(self, p, to, source):
+        span = self.spans[p]
         return to_dp(
-            self.sent.at[self.part(to), :], self.came.at[self.part(source), :],
-            self.sems.at[0, to], self.sems.at[1, source], to,
-        )
-
-    def send(self, index_ref, dim, source):
+            self.sent.at[self.part(to), span], self.came.at[self.part(source), span],
+            self.sems.at[0, p, to], self.sems.at[1, p, source], to,
+        )
+
+    def send(self, p, index_ref, dim, source):
+        span = self.spans[p]
         groups, count = self.groups, source.shape[0]
         rows = self.sent.shape[0] // 2
 
@@ -673,7 +689,7 @@
                 pick = one_hot(index_ref[...], h * rows, (rows, count), 0)
             else:
                 pick = one_hot(index_ref[at, :], 0, (rows, count), 1)
-            self.sent[at, :] = dot(pick, source[...]).astype(bf16)
+            self.sent[at, span] = dot(pick, source[:, span]).astype(bf16)
 
             @pl.loop(0, groups // 2)
             def _(k):
@@ -681,22 +697,24 @@
 
                 @pl.when(to != self.member)
                 def _():
-                    self.copy(to, self.member).start()
-
-        self.came[self.part(self.member), :] = self.sent[self.part(self.member), :]
-
-    def receive(self):
+                    self.copy(p, to, self.member).start()
+
+        own = self.part(self.member)
+        self.came[own, span] = self.sent[own, span]
+
+    def receive(self, p):
         @pl.loop(1, self.groups)
         def _(k):
-            self.copy(0, lax.rem(self.member + k, self.groups)).wait_recv()
+            self.copy(p, 0, lax.rem(self.member + k, self.groups)).wait_recv()
 
     def drain(self):
-        @pl.loop(1, self.groups)
-        def _(k):
-            self.copy(lax.rem(self.member + k, self.groups), self.member).wait_send()
-
-
-def place_rows(slot_row_ref, came, held):
+        for p in range(len(self.spans)):
+            @pl.loop(1, self.groups)
+            def _(k):
+                self.copy(p, lax.rem(self.member + k, self.groups), self.member).wait_send()
+
+
+def place_rows(slot_row_ref, came, held, span):
     positions, slots = held.shape[0], came.shape[0]
     rows = positions // 2
 
@@ -704,25 +722,36 @@
     def _(h):
         at = pl.ds(pl.multiple_of(h * rows, rows), rows)
         pick = one_hot(slot_row_ref[...], h * rows, (rows, slots), 0)
-        held[at, :] = dot(pick, came[...]).astype(bf16)
+        held[at, span] = dot(pick, came[:, span]).astype(bf16)
 
 
 def front_kernel(n, groups, dk, dv, *refs):
     take = splitter(refs)
-    lengths_ref, slots_ref, tokens_ref, mixer_gain_ref, feed_gain_ref, head_gain_ref = take(6)
-    up_ref, bias_ref = take(2)
-    weights_far = take(4)
+    lengths_ref, slots_ref, tokens_ref, gains_ref, up_rows_ref, down_rows_ref = take(6)
+    weights_far = take(3)
     gate_far, out_far, cotangent_far, down_far = take(4)
-    normed_ref, gate_ref, attended_ref, gated_ref, feed_ref, hidden_ref, d_active_ref = take(7)
-    held_ref, states_ref, send_row_ref, send_column_ref, slot_row_ref, slot_column_ref = take(6)
+    spilled = take(6)
+    feed_ref, hidden_ref, d_active_ref = take(3)
+    send_row_ref, send_column_ref, slot_row_ref, slot_column_ref = take(4)
+    normed_ref, gate_ref, attended_ref, gated_ref, held_ref, states_ref = kept = take(6)
     up_in, down_in, weight_ref, gate_weight_ref, out_weight_ref, cotangent_ref, down_ref = take(7)
-    rows_out, share_ref, state, result, rank_ref, load_sems, sems = take(7)
-    go = Exchange(groups, *take(3))
-    back = Exchange(groups, *take(3))
+    rows_out, share_ref, state, result, rank_ref, up_ref, bias_ref, latent_ref = take(8)
+    load_sems, sems = take(2)
+    go = Exchange(groups, (2 * dk,), *take(3))
+    back = Exchange(groups, (), *take(3))
+    (spill_sems,) = take(1)
     member = lax.axis_index("dp")
     count, width = tokens_ref.shape
     cap = OWN_CAP // groups
     half = count // 2
+    spills = [
+        pltpu.make_async_copy(kept[i], spilled[i], spill_sems.at[i]) for i in range(6)
+    ]
+
+    def spill(*which):
+        for i in which:
+            spills[i].start()
+
     end0 = lengths_ref[0, 0]
     end1 = end0 + lengths_ref[0, 1]
     ends = (end0, end1, end1 + lengths_ref[0, 2])
@@ -732,7 +761,7 @@
         hidden = tokens_ref[place, :].astype(f32) + total
         hidden_ref[own, :] = hidden
         scaling = lax.rsqrt(jnp.mean(hidden * hidden, axis=1, keepdims=True) + epsilon)
-        feed_ref[place, :] = (hidden * scaling * feed_gain_ref[...]).astype(bf16)
+        feed_ref[place, :] = (hidden * scaling * gains_ref[1:2, :]).astype(bf16)
 
     line = Line(n, share_ref, up_in, down_in, feed_ref, sems, finish)
     loads = []
@@ -775,6 +804,10 @@
     )[:, :1].astype(jnp.int32)
     rank_ref[...] = jnp.where(mine, dot(mine.astype(f32).astype(bf16), before), -1.0)
 
+    bias_ref[...] = gains_ref[2:3, dv : dv + dk]
+    thirds(up_rows_ref, 3, up_ref)
+    thirds(down_rows_ref, 3, latent_ref)
+
     tile = count // 5
 
     @pl.loop(0, 5)
@@ -782,25 +815,33 @@
         at = pl.ds(pl.multiple_of(i * tile, tile), tile)
         rows = tokens_ref[at, :].astype(f32)
         scaling = lax.rsqrt(jnp.mean(rows * rows, axis=1, keepdims=True) + epsilon)
-        normed_ref[at, :] = (rows * scaling * mixer_gain_ref[...]).astype(bf16)
-
-    for c in loads:
+        normed_ref[at, :] = (rows * scaling * gains_ref[0:1, :]).astype(bf16)
+
+    for c in loads[:2]:
         c.wait()
     body = 2 * dk + dv
 
-    @pl.loop(0, body // 256)
-    def _(i):
-        to = pl.ds(pl.multiple_of(i * 256, 256), 256)
-        rows_out[:, to] = dot(normed_ref[...], weight_ref[:, to]).astype(bf16)
-
-    latent = dot(normed_ref[...], weight_ref[:, body:])
+    spill(0)
+
+    def project(first, last):
+        @pl.loop(first // 256, last // 256)
+        def _(i):
+            to = pl.ds(pl.multiple_of(i * 256, 256), 256)
+            rows_out[:, to] = dot(normed_ref[...], weight_ref[:, to]).astype(bf16)
+
+    project(0, 2 * dk)
+    go.send(0, send_row_ref, 0, rows_out)
+    for c in loads[2:]:
+        c.wait()
+    project(2 * dk, body)
+    latent = dot_t(normed_ref[...], latent_ref[...])
     high = latent.astype(bf16).astype(f32)
     middle = (latent - high).astype(bf16).astype(f32)
     lane = lax.broadcasted_iota(jnp.int32, latent.shape, 1)
     rows_out[:, body:] = jnp.where(
         lane < third, high, jnp.where(lane < 2 * third, middle, latent - high - middle)
     ).astype(bf16)
-    go.send(send_row_ref, 0, rows_out)
+    go.send(1, send_row_ref, 0, rows_out)
 
     for c in later:
         c.wait()
@@ -809,6 +850,8 @@
     def _(i):
         to = pl.ds(pl.multiple_of(i * 256, 256), 256)
         gate_ref[:, to] = dot(normed_ref[...], gate_weight_ref[:, to])
+
+    spill(1)
 
     @pl.loop(0, groups)
     def _(j):
@@ -823,15 +866,17 @@
         jnp.broadcast_to(slot_column_ref[...].astype(f32), (slots, LANES))
     )[:1, :].astype(jnp.int32)
     state[...] = jnp.zeros_like(state)
-    go.receive()
-    place_rows(slot_row_ref, go.came, held_ref)
+    for p in range(2):
+        go.receive(p)
+        place_rows(slot_row_ref, go.came, held_ref, go.spans[p])
 
     @pl.loop(0, held_ref.shape[0] // SPAN)
     def _(step):
         span_forward(dk, dv, step, ends, held_ref, up_ref, bias_ref, state, states_ref, result)
 
-    back.send(slot_column_ref, 1, result)
-    back.receive()
+    back.send(0, slot_column_ref, 1, result)
+    spill(4, 5)
+    back.receive(0)
 
     def head_rows(at):
         pick = one_hot(send_column_ref[at, :], 0, (half, slots), 1)
@@ -839,7 +884,7 @@
         attended_ref[at, :] = attended.astype(bf16)
         gate = gate_ref[at, :]
         scaling = lax.rsqrt(jnp.mean(attended * attended, axis=1, keepdims=True) + head_floor)
-        gated = attended * scaling * head_gain_ref[...] * (gate * jax.nn.sigmoid(gate))
+        gated = attended * scaling * gains_ref[2:3, :dv] * (gate * jax.nn.sigmoid(gate))
         gated_ref[at, :] = gated.astype(bf16)
 
         @pl.loop(0, width // 512)
@@ -855,6 +900,7 @@
         head_rows(pl.ds(pl.multiple_of(bottom * half, half), half))
         line.prime(i == 0, i == 0)
 
+    spill(2, 3)
     wide = d_active_ref.shape[1]
     full, rest = wide // 256, wide % 256
 
@@ -882,43 +928,50 @@
     line.drain()
     go.drain()
     back.drain()
+    for c in spills:
+        c.wait()
 
 
 def front(
-    call, n, groups, lengths, slots, tokens, mixer_gain, feed_gain, head_gain, up_wide, bias, weights,
-    gate_weight, out_weight, cotangent, feed_down,
+    call, n, groups, lengths, slots, tokens, gains, up_rows, down_rows, weights, gate_weight,
+    out_weight, cotangent, feed_down,
 ):
     count, width = tokens.shape
     dk, dv = weights[0].shape[1], weights[2].shape[1]
-    wide = sum(w.shape[1] for w in weights)
+    body = 2 * dk + dv
+    wide = body + LANES
     half = count // 2
     spans = OWN_CAP // SPAN
     vmem = pl.BlockSpec(memory_space=pltpu.VMEM)
     far = pl.BlockSpec(memory_space=pl.ANY)
     smem = pl.BlockSpec(memory_space=pltpu.SMEM)
     shape = jax.ShapeDtypeStruct
+    saved = [
+        shape((count, width), bf16),
+        shape((count, dv), f32),
+        shape((count, dv), bf16),
+        shape((count, dv), bf16),
+        shape((OWN_CAP, wide), bf16),
+        shape((spans, dk, dv), bf16),
+    ]
     return pl.pallas_call(
         functools.partial(front_kernel, n, groups, dk, dv),
-        in_specs=[smem] + [vmem] * 7 + [far] * 8,
-        out_specs=[vmem] * 13,
+        in_specs=[smem] + [vmem] * 5 + [far] * 7,
+        out_specs=[far] * 6 + [vmem] * 7,
         out_shape=[
-            shape((count, width), bf16),
-            shape((count, dv), f32),
-            shape((count, dv), bf16),
-            shape((count, dv), bf16),
+            *saved,
             shape((count, width), bf16),
             shape((half, width), f32),
             shape((count, feed_down.shape[0]), bf16),
-            shape((OWN_CAP, wide), bf16),
-            shape((spans, dk, dv), bf16),
             shape((1, count), jnp.int32),
             shape((count, 1), jnp.int32),
             shape((1, OWN_CAP), jnp.int32),
             shape((OWN_CAP, 1), jnp.int32),
         ],
-        scratch_shapes=Line.scratch(half, width)
+        scratch_shapes=[pltpu.VMEM(a.shape, a.dtype) for a in saved]
+        + Line.scratch(half, width)
         + [
-            pltpu.VMEM((width, wide), bf16),
+            pltpu.VMEM((width, body), bf16),
             pltpu.VMEM((width, dv), bf16),
             pltpu.VMEM((dv, width), bf16),
             pltpu.VMEM((count, width), bf16),
@@ -928,11 +981,15 @@
             pltpu.VMEM((dk, dv), f32),
             pltpu.VMEM((OWN_CAP, dv), bf16),
             pltpu.VMEM((groups, count), f32),
+            pltpu.VMEM((LANES, dk), bf16),
+            pltpu.VMEM((1, dk), f32),
+            pltpu.VMEM((LANES, width), bf16),
             pltpu.SemaphoreType.DMA((8,)),
             Line.semaphores(half),
         ]
-        + Exchange.scratch(groups, OWN_CAP, wide)
-        + Exchange.scratch(groups, OWN_CAP, dv),
+        + Exchange.scratch(groups, OWN_CAP, wide, 2)
+        + Exchange.scratch(groups, OWN_CAP, dv, 1)
+        + [pltpu.SemaphoreType.DMA((6,))],
         compiler_params=pltpu.CompilerParams(
             collective_id=call, has_side_effects=True, vmem_limit_bytes=60 << 20
         ),
@@ -941,21 +998,24 @@
         ),
         name="front",
     )(
-        lengths, slots, tokens, mixer_gain, feed_gain, head_gain, up_wide, bias, *weights,
-        gate_weight, out_weight, cotangent, feed_down,
+        lengths, slots, tokens, gains, up_rows, down_rows, *weights, gate_weight, out_weight,
+        cotangent, feed_down,
     )
 
 
-def back_feed_kernel(n, groups, tiles, outs, *refs):
+def back_feed_kernel(n, groups, tiles, *refs):
     take = splitter(refs)
-    gain_ref, x_far, base_far, left_far, d_active_far, gate_far, up_far, down_far = take(8)
-    out_ref, kept_ref, gain_grad_ref = take(3)
-    outputs = take(2)
+    gains_ref, x_far, base_far, left_far, d_active_far, gate_far, up_far, down_far = take(8)
+    out_ref, kept_ref, gain_grad_ref, recv, active_far, layer_far = take(6)
     active_ref, layer_ref = take(2)
     up_in, down_in, x_ref, base_ref, share_ref, weight_ref, d_active_ref = take(7)
     load_sems, weight_sems, sems = take(3)
-    rows = RowGrads(groups, left_far, tiles, outs, outputs, take(10))
-    finish = norm_back(x_ref, base_ref, gain_ref, out_ref, kept_ref, gain_grad_ref)
+    active_spill = pltpu.make_async_copy(active_ref, active_far, load_sems.at[4])
+    layer_spill = pltpu.make_async_copy(layer_ref, layer_far, load_sems.at[5])
+    rows = RowGrads(groups, left_far, tiles, recv, take(10))
+    finish = norm_back(
+        x_ref, base_ref, lambda: gains_ref[1:2, :], out_ref, kept_ref, gain_grad_ref
+    )
     line = Line(n, share_ref, up_in, down_in, out_ref, sems, finish)
     count, width = share_ref.shape
     wide = active_ref.shape[1]
@@ -964,7 +1024,7 @@
     loads = (
         pltpu.make_async_copy(d_active_far, d_active_ref, load_sems.at[2]),
         pltpu.make_async_copy(x_far, x_ref, load_sems.at[0]),
-        pltpu.make_async_copy(base_far, base_ref, load_sems.at[1]),
+        pltpu.make_async_copy(base_far.at[line.own_half(), :], base_ref, load_sems.at[1]),
     )
     down_load = pltpu.make_async_copy(
         down_far, weight_ref.at[pl.ds(0, wide), pl.ds(0, width)], load_sems.at[3]
@@ -1038,6 +1098,7 @@
             c.start()
 
     each(hidden_units)
+    active_spill.start()
 
     half = count // 2
     last = line.me == n - 1
@@ -1086,9 +1147,15 @@
             to = pl.ds(pl.multiple_of(layer_item * 512, 512), 512)
             layer_ref[:, to] = dot(active_ref[...], weight_ref[pl.ds(0, wide), to]).astype(bf16)
 
+        @pl.when(layer_item == layer_items)
+        def _():
+            layer_spill.start()
+
     rows.receive()
     line.drain()
     rows.drain()
+    active_spill.wait()
+    layer_spill.wait()
 
     def piece_sent(i, size):
         for c in piece_copies(i, size):
@@ -1097,37 +1164,36 @@
     each(piece_sent)
 
 
-def back_feed(call, n, groups, gain, x_own, base_own, left, d_active, feed_gate, feed_up, feed_down):
+def back_feed(call, n, groups, gains, x_own, base, left, d_active, feed_gate, feed_up, feed_down):
     count, width = left.shape
     half = count // 2
     wide = feed_gate.shape[1]
     pieces = (wide + 255) // 256
     cut = (wide // 2 + LANES - 1) // LANES * LANES
     tiles = [(0, cut), (cut, wide - cut), (wide, cut), (wide + cut, wide - cut)]
-    outs = [(0, wide), (wide, wide)]
     vmem = pl.BlockSpec(memory_space=pltpu.VMEM)
     far = pl.BlockSpec(memory_space=pl.ANY)
     return pl.pallas_call(
-        functools.partial(back_feed_kernel, n, groups, tiles, outs),
+        functools.partial(back_feed_kernel, n, groups, tiles),
         in_specs=[vmem] + [far] * 7,
-        out_specs=[vmem] * 7,
+        out_specs=[vmem] * 3 + [far] * 3,
         out_shape=[
             jax.ShapeDtypeStruct((count, width), bf16),
             jax.ShapeDtypeStruct((half, width), f32),
             jax.ShapeDtypeStruct((8, width), f32),
-            jax.ShapeDtypeStruct((width // groups, wide), f32),
-            jax.ShapeDtypeStruct((width // groups, wide), f32),
+            jax.ShapeDtypeStruct((groups // 2, width // groups, 2 * wide), bf16),
             jax.ShapeDtypeStruct((count, wide), bf16),
             jax.ShapeDtypeStruct((count, width), bf16),
         ],
-        scratch_shapes=Line.scratch(half, width)
+        scratch_shapes=[pltpu.VMEM((count, wide), bf16), pltpu.VMEM((count, width), bf16)]
+        + Line.scratch(half, width)
         + [
             pltpu.VMEM((half, width), x_own.dtype),
-            pltpu.VMEM((half, width), base_own.dtype),
+            pltpu.VMEM((half, width), base.dtype),
             pltpu.VMEM((count, width), bf16),
             pltpu.VMEM((width, 2 * wide), bf16),
             pltpu.VMEM((count, wide), bf16),
-            pltpu.SemaphoreType.DMA((4,)),
+            pltpu.SemaphoreType.DMA((6,)),
             pltpu.SemaphoreType.DMA((2, pieces)),
             Line.semaphores(half),
         ]
@@ -1139,7 +1205,7 @@
             flops=30_000_000_000, bytes_accessed=200_000_000, transcendentals=0
         ),
         name="back_feed",
-    )(gain, x_own, base_own, left, d_active, feed_gate, feed_up, feed_down)
+    )(gains, x_own, base, left, d_active, feed_gate, feed_up, feed_down)
 
 
 class SmallSum:
@@ -1258,34 +1324,35 @@
                 c.wait_send()
 
 
-def back_mixer_kernel(n, groups, widths, near_all, tiles, outs, *refs):
+def back_mixer_kernel(n, groups, widths, near_all, tiles, *refs):
     take = splitter(refs)
-    gain_ref, near_ref, x_far, base_far, left_far = take(5)
+    gains_ref, near_ref, down_rows_ref, x_far, base_far, left_far = take(6)
     parts = take(2)
     col_left, col_right = take(2)
     weights = take(len(widths))
-    out_ref, wide_out, near_out = take(3)
-    outputs = take(len(outs))
-    (col_out,) = take(1)
-    up_in, down_in, x_ref, base_ref, kept_ref, share_ref, wide_ref, gain_grad_ref = take(8)
-    weight_ref, load_sems, sems = take(3)
-    rows = RowGrads(groups, left_far, tiles, outs, outputs, take(10))
+    out_ref, wide_out, near_out, recv, col_recv = take(5)
+    up_in, down_in, x_ref, base_ref, share_ref, wide_ref, gain_grad_ref = take(7)
+    weight_ref, latent_ref, load_sems, sems = take(4)
+    rows = RowGrads(groups, left_far, tiles, recv, take(10))
     part_spans = [
         pl.ds(0, parts[0].shape[1]), pl.ds(parts[0].shape[1], parts[1].shape[1])
     ]
     part_loads = [rows.piece_load(i, parts[i], part_spans[i]) for i in range(2)]
     part_copies = [rows.piece_copy(i, parts[i], part_spans[i]) for i in range(2)]
-    cols = ColGrad(groups, col_left, col_right, col_out, take(9))
+    cols = ColGrad(groups, col_left, col_right, 0, col_recv, take(8))
     small = SmallSum(n, groups, wide_ref, near_ref, near_all, wide_out, near_out, take(6))
-    finish = norm_back(x_ref, base_ref, gain_ref, out_ref, kept_ref, gain_grad_ref)
+    finish = norm_back(x_ref, base_ref, lambda: gains_ref[0:1, :], out_ref, None, gain_grad_ref)
     line = Line(n, share_ref, up_in, down_in, out_ref, sems, finish)
     loads = [
-        pltpu.make_async_copy(x_far, x_ref, load_sems.at[0]),
+        pltpu.make_async_copy(x_far.at[line.own_half(), :], x_ref, load_sems.at[0]),
         pltpu.make_async_copy(base_far, base_ref, load_sems.at[1]),
     ]
     weight_loads = []
     offset = 0
     for i, wide in enumerate(widths):
+        if i == len(widths) - 1:
+            latent_at = offset
+            offset += LANES
         weight_loads.append(
             pltpu.make_async_copy(
                 weights[i], weight_ref.at[:, pl.ds(offset, wide)], load_sems.at[2 + i]
@@ -1294,6 +1361,8 @@
         offset += wide
     for c in part_loads + weight_loads:
         c.start()
+    thirds(down_rows_ref, 2, latent_ref)
+    weight_ref[:, pl.ds(latent_at, LANES)] = jnp.transpose(latent_ref[...].astype(f32)).astype(bf16)
     barrier = pltpu.get_barrier_semaphore()
     greet_dp(barrier, groups)
     small.greet(barrier)
@@ -1321,7 +1390,6 @@
     for c in loads:
         c.wait()
     third = LANES // 4
-    latent_at = offset - widths[-1] - LANES
     first_cols = rows.items
     last_item = first_cols + cols.items
 
@@ -1371,7 +1439,9 @@
     small.drain()
 
 
-def back_mixer(call, n, groups, gain, near, near_all, x_own, base_own, left, parts, outs, pair, weights):
+def back_mixer(
+    call, n, groups, gains, near, near_all, down_rows, x, base_own, left, parts, pair, weights
+):
     count, width = left.shape
     half = count // 2
     widths = [w.shape[1] for w in weights]
@@ -1383,30 +1453,30 @@
     far = pl.BlockSpec(memory_space=pl.ANY)
     wide_shape = (24, width)
     return pl.pallas_call(
-        functools.partial(back_mixer_kernel, n, groups, widths, near_all, tiles, outs),
-        in_specs=[vmem] * 2 + [far] * (7 + len(weights)),
-        out_specs=[vmem] * (4 + len(outs)),
+        functools.partial(back_mixer_kernel, n, groups, widths, near_all, tiles),
+        in_specs=[vmem] * 3 + [far] * (7 + len(weights)),
+        out_specs=[vmem] * 3 + [far] * 2,
         out_shape=[
             jax.ShapeDtypeStruct((count, width), bf16),
             jax.ShapeDtypeStruct((24, width // groups), f32),
             jax.ShapeDtypeStruct(near.shape[1:], f32),
-        ]
-        + [jax.ShapeDtypeStruct((width // groups, wide), f32) for _, wide in outs]
-        + [jax.ShapeDtypeStruct((col_rows // groups, width), f32)],
+            jax.ShapeDtypeStruct((groups // 2, width // groups, total), bf16),
+            jax.ShapeDtypeStruct((groups, col_rows // groups, width // 2), bf16),
+        ],
         scratch_shapes=Line.scratch(half, width)
         + [
-            pltpu.VMEM((half, width), x_own.dtype),
+            pltpu.VMEM((half, width), x.dtype),
             pltpu.VMEM((half, width), base_own.dtype),
-            pltpu.VMEM((half, width), bf16),
             pltpu.VMEM((count, width), bf16),
             pltpu.VMEM(wide_shape, f32),
             pltpu.VMEM((8, width), f32),
             pltpu.VMEM((width, total), bf16),
+            pltpu.VMEM((LANES, width), bf16),
             pltpu.SemaphoreType.DMA((2 + len(weights),)),
             Line.semaphores(half),
         ]
         + RowGrads.scratch(groups, count, width, total, 2, len(tiles))
-        + ColGrad.scratch(groups, count, col_rows, width)
+        + ColGrad.scratch(groups, count, col_rows, width // 2)
         + SmallSum.scratch(n, groups, wide_shape, near.shape),
         compiler_params=pltpu.CompilerParams(
             collective_id=call, has_side_effects=True, vmem_limit_bytes=61 << 20
@@ -1415,21 +1485,124 @@
             flops=12_000_000_000, bytes_accessed=200_000_000, transcendentals=0
         ),
         name="back_mixer",
-    )(gain, near, x_own, base_own, left, *parts, *pair, *weights)
+    )(gains, near, down_rows, x, base_own, left, *parts, *pair, *weights)
+
+
+def outputs_kernel(dk, dv, rank, near_all, *refs):
+    take = splitter(refs)
+    feed_ref, rows_ref, down_ref, out_ref = take(4)
+    wide_ref, near_ref, token_ref, layer_ref = take(4)
+    token_out, layer_out, query_out, key_out, value_out, gate_out = take(6)
+    feed_gate_out, feed_up_out, feed_down_out, out_out, decay_out, vector_out = take(6)
+    step = pl.program_id(0)
+
+    def total(ref, start, wide):
+        span = pl.ds(start, wide)
+        result = ref[0, :, span].astype(f32)
+        for q in range(1, ref.shape[0]):
+            result = result + ref[q, :, span].astype(f32)
+        return result
+
+    wide = feed_gate_out.shape[1]
+    feed_gate_out[...] = total(feed_ref, 0, wide)
+    feed_up_out[...] = total(feed_ref, wide, wide)
+    query_out[...] = total(rows_ref, 0, dk)
+    key_out[...] = total(rows_ref, dk, dk)
+    value_out[...] = total(rows_ref, 2 * dk, dv)
+    gate_out[...] = total(rows_ref, 2 * dk + dv + LANES, dv)
+    token_out[...] = token_ref[...]
+    layer_out[...] = layer_ref[...]
+
+    @pl.when(lax.rem(step, 4) == 0)
+    def _():
+        half = out_out.shape[2] // 2
+        for ref, out in ((down_ref, feed_down_out), (out_ref, out_out)):
+            for b in range(2):
+                result = ref[b].astype(f32)
+                for q in range(1, ref.shape[0] // 2):
+                    result = result + ref[2 * q + b].astype(f32)
+                out[0, :, b * half : (b + 1) * half] = result
+
+    @pl.when(step == 0)
+    def _():
+        decay_out[...] = wide_ref[:rank, :]
+        vector_out[...] = jnp.sum(wide_ref[rank:, :], axis=0, keepdims=True)
+
+
+def outputs(
+    groups, dk, dv, rank, near_all, feed, rows, down, out, wide_sum, near_sum, token, layer
+):
+    steps = 8
+    count, width = token.shape
+    wide = feed.shape[2] // 2
+    per = width // groups
+    block = per // steps
+    shape = jax.ShapeDtypeStruct
+
+    def rows_of(columns):
+        return pl.BlockSpec((block, columns), lambda i: (i, 0))
+
+    def fixed(array):
+        return pl.BlockSpec(array.shape, lambda i: (0,) * array.ndim)
+
+    def recv(array):
+        return pl.BlockSpec((array.shape[0], block, array.shape[2]), lambda i: (0, i, 0))
+
+    def recv_half(array):
+        return pl.BlockSpec(
+            (array.shape[0], array.shape[1] // 2, array.shape[2]), lambda i: (0, i // 4, 0)
+        )
+
+    def out_half(array):
+        return pl.BlockSpec((1, array.shape[1] // 2, width), lambda i: (0, i // 4, 0))
+
+    tokens_block = pl.BlockSpec((count // steps, width), lambda i: (i, 0))
+    return pl.pallas_call(
+        functools.partial(outputs_kernel, dk, dv, rank, near_all),
+        grid=(steps,),
+        in_specs=[
+            recv(feed), recv(rows), recv_half(down), recv_half(out), fixed(wide_sum),
+            fixed(near_sum), tokens_block, tokens_block,
+        ],
+        out_specs=[
+            tokens_block, tokens_block, rows_of(dk), rows_of(dk), rows_of(dv), rows_of(dv),
+            rows_of(wide), rows_of(wide), out_half(down), out_half(out),
+            pl.BlockSpec((rank, per), lambda i: (0, 0)),
+            pl.BlockSpec((1, per), lambda i: (0, 0)),
+        ],
+        out_shape=[
+            shape((count, width), bf16),
+            shape((count, width), bf16),
+            shape((per, dk), f32),
+            shape((per, dk), f32),
+            shape((per, dv), f32),
+            shape((per, dv), f32),
+            shape((per, wide), f32),
+            shape((per, wide), f32),
+            shape((1, down.shape[1], width), f32),
+            shape((1, out.shape[1], width), f32),
+            shape((rank, per), f32),
+            shape((1, per), f32),
+        ],
+        compiler_params=pltpu.CompilerParams(vmem_limit_bytes=60 << 20),
+        name="outputs",
+    )(feed, rows, down, out, wide_sum, near_sum, token, layer)
 
 
 def recur_back_kernel(n, groups, dk, dv, beside, *refs):
     (
         lengths_ref, send_row_ref, send_column_ref, slot_row_ref, slot_column_ref,
-        d_mixed_ref, out_weight_ref, attended_ref, gate_ref, gain_ref, up_ref, bias_ref, down_ref,
+        d_mixed_ref, out_weight_ref, attended_ref, gate_ref, gains_ref, up_rows_ref,
         share_ref, held_far, states_far, hidden_far, active_far, cotangent_far,
         d_rows_ref, d_gate_ref, head_gain_ref, grad_up_ref, grad_bias_ref, layer_ref, grad_down_ref,
         up_in, down_in, d_attended, d_placed, d_state, result,
-        held_ref, states_ref, hidden_ref, load_sems, sems,
-    ) = refs[:37]
-    go = Exchange(groups, *refs[37:40])
-    back = Exchange(groups, *refs[40:43])
-    cols = ColGrad(groups, active_far, cotangent_far, grad_down_ref, refs[43:]) if beside else None
+        held_ref, states_ref, hidden_ref, up_ref, down_ref, bias_ref, load_sems, sems,
+    ) = refs[:38]
+    go = Exchange(groups, (), *refs[38:41])
+    back = Exchange(groups, (2 * dk,), *refs[41:44])
+    cols = None
+    if beside:
+        cols = ColGrad(groups, active_far, cotangent_far, 0, grad_down_ref, refs[44:])
     count = d_mixed_ref.shape[0]
     slots = slot_row_ref.shape[1]
     end0 = lengths_ref[0, 0]
@@ -1455,6 +1628,10 @@
         cols.start()
     loads[0].wait()
 
+    bias_ref[...] = gains_ref[2:3, dv : dv + dk]
+    thirds(up_rows_ref, 3, up_ref)
+    thirds(up_rows_ref, 2, down_ref)
+
     head_gain_ref[...] = jnp.zeros_like(head_gain_ref)
     tile = count // 2
 
@@ -1468,7 +1645,7 @@
         unit = attended * scaling
         sigmoid = jax.nn.sigmoid(gate)
         swish = gate * sigmoid
-        gained = d_gated * gain_ref[...]
+        gained = d_gated * gains_ref[2:3, :dv]
         d_gate_ref[rows, :] = (
             gained * unit * sigmoid * (1.0 + gate * (1.0 - sigmoid))
         ).astype(bf16)
@@ -1484,7 +1661,7 @@
         line.step(2 * i)
         line.step(2 * i + 1)
 
-    go.send(send_row_ref, 0, d_attended)
+    go.send(0, send_row_ref, 0, d_attended)
     d_state[...] = jnp.zeros_like(d_state)
     grad_up_ref[...] = jnp.zeros_like(grad_up_ref)
     grad_bias_ref[...] = jnp.zeros_like(grad_bias_ref)
@@ -1505,8 +1682,8 @@
     for c in loads[1:]:
         c.wait()
 
-    go.receive()
-    place_rows(slot_row_ref, go.came, d_placed)
+    go.receive(0)
+    place_rows(slot_row_ref, go.came, d_placed, go.spans[0])
     spans = held_ref.shape[0] // SPAN
 
     @pl.loop(0, spans)
@@ -1520,18 +1697,21 @@
         line.step(done + 2 * i)
         line.step(done + 1 + 2 * i)
 
-    back.send(slot_column_ref, 1, result)
+    for p in range(2):
+        back.send(p, slot_column_ref, 1, result)
     line.run(done + 2 * spans, line.steps)
     if beside:
         cols.receive()
 
-    back.receive()
-
-    @pl.loop(0, 2)
-    def _(i):
-        rows = pl.ds(pl.multiple_of(i * tile, tile), tile)
-        pick = one_hot(send_column_ref[rows, :], 0, (tile, slots), 1)
-        d_rows_ref[rows, :] = dot(pick, back.came[...]).astype(bf16)
+    for p in range(2):
+        back.receive(p)
+        span = back.spans[p]
+
+        @pl.loop(0, 2)
+        def _(i):
+            rows = pl.ds(pl.multiple_of(i * tile, tile), tile)
+            pick = one_hot(send_column_ref[rows, :], 0, (tile, slots), 1)
+            d_rows_ref[rows, span] = dot(pick, back.came[:, span]).astype(bf16)
 
     line.drain()
     if beside:
@@ -1542,21 +1722,20 @@
 
 def recur_back(
     call, n, groups, dk, dv, beside, lengths, send_row, send_column, slot_row, slot_column, d_mixed, out_weight, attended, gate_pre,
-    head_gain, up_wide, bias, down_wide, share, held, states, hidden_own, active, cotangent,
+    gains, up_rows, share, held, states, hidden_own, active, cotangent,
 ):
     count, width = d_mixed.shape
     slots, wide = held.shape
     half = count // 2
     vmem = pl.BlockSpec(memory_space=pltpu.VMEM)
     operands = [
-        lengths, send_row, send_column, slot_row, slot_column, d_mixed, out_weight, attended, gate_pre, head_gain, up_wide, bias,
-        down_wide, share, held, states, hidden_own, active, cotangent,
+        lengths, send_row, send_column, slot_row, slot_column, d_mixed, out_weight, attended, gate_pre, gains, up_rows, share, held, states, hidden_own, active, cotangent,
     ]
     far = pl.BlockSpec(memory_space=pl.ANY)
     return pl.pallas_call(
         functools.partial(recur_back_kernel, n, groups, dk, dv, beside),
         in_specs=[pl.BlockSpec(memory_space=pltpu.SMEM)] + [vmem] * (len(operands) - 6) + [far] * 5,
-        out_specs=[vmem] * 7,
+        out_specs=[vmem] * 6 + [far],
         out_shape=[
             jax.ShapeDtypeStruct((count, wide), bf16),
             jax.ShapeDtypeStruct((count, dv), bf16),
@@ -1564,7 +1743,9 @@
             jax.ShapeDtypeStruct((dk, LANES), f32),
             jax.ShapeDtypeStruct((8, dk), f32),
             jax.ShapeDtypeStruct((count, width), bf16),
-            jax.ShapeDtypeStruct((active.shape[1] // groups if beside else 8, width), f32),
+            jax.ShapeDtypeStruct(
+                (groups, active.shape[1] // groups if beside else 8, width // 2), bf16
+            ),
         ],
         scratch_shapes=Line.scratch(half, width)
         + [
@@ -1575,12 +1756,15 @@
             pltpu.VMEM(held.shape, bf16),
             pltpu.VMEM(states.shape, bf16),
             pltpu.VMEM((half, width), f32),
+            pltpu.VMEM((LANES, dk), bf16),
+            pltpu.VMEM((LANES, dk), bf16),
+            pltpu.VMEM((1, dk), f32),
             pltpu.SemaphoreType.DMA((3,)),
             Line.semaphores(half),
         ]
-        + Exchange.scratch(groups, slots, dv)
-        + Exchange.scratch(groups, slots, wide)
-        + (ColGrad.scratch(groups, count, active.shape[1], width) if beside else []),
+        + Exchange.scratch(groups, slots, dv, 1)
+        + Exchange.scratch(groups, slots, wide, 2)
+        + (ColGrad.scratch(groups, count, active.shape[1], width // 2) if beside else []),
         compiler_params=pltpu.CompilerParams(
             collective_id=call, has_side_effects=True, vmem_limit_bytes=60 << 20
         ),
@@ -1726,43 +1910,31 @@
     pairs = [(i, i ^ 1) for i in range(groups)]
     same_parity = [[i for i in range(groups) if i % 2 == b] for b in range(2)]
 
-    half = count // 2
-    own_at = jnp.where(place == 0, half, 0)
-    tokens_own = lax.dynamic_slice_in_dim(tokens, own_at, half)
-    cotangent_own = lax.dynamic_slice_in_dim(cotangent, own_at, half)
-
-    mixer_gain_wide = mixer_gain.astype(f32)
-    feed_gain_wide = feed_gain.astype(f32)
-    head_gain_wide = head_gain.astype(f32)
+    fused = (width // groups) % LANES == 0
     third = LANES // 4
-    down_pad = jnp.pad(decay_down, ((0, 0), (0, third - rank)))
-    down_none = jnp.zeros_like(down_pad)
-    down_all = jnp.concatenate([down_pad, down_pad, down_pad, down_none], axis=1)
-    up_pad = jnp.pad(decay_up, ((0, 0), (0, third - rank)))
-    up_none = jnp.zeros_like(up_pad)
-    up_wide = jnp.concatenate([up_pad, up_pad, up_pad, up_none], axis=1).T
-    down_wide = jnp.concatenate([up_pad, up_pad, up_none, up_none], axis=1)
-    bias = decay_bias.astype(f32).reshape(1, dk)
+    down_rows = decay_down.T
+    up_rows = decay_up.T
+    last = jnp.pad(jnp.concatenate([head_gain, decay_bias]), (0, width - dv - dk))
+    gains = jnp.stack([mixer_gain, feed_gain, last]).astype(f32)
     (
-        normed, gate_pre, attended, gated, feed_normed, hidden_own, d_active, held, states,
-        send_row, send_column, slot_row, slot_column,
+        normed, gate_pre, attended, gated, held, states, feed_normed, hidden_own, d_active, send_row,
+        send_column, slot_row, slot_column,
     ) = front(
-        1, lines, groups, lengths, token_slots.reshape(groups, count), tokens,
-        mixer_gain_wide.reshape(1, -1), feed_gain_wide.reshape(1, -1),
-        head_gain_wide.reshape(1, -1), up_wide, bias,
-        [query_weight, key_weight, value_weight, down_all], gate_weight, out_weight, cotangent,
+        1, lines, groups, lengths, token_slots.reshape(groups, count), tokens, gains, up_rows,
+        down_rows, [query_weight, key_weight, value_weight], gate_weight, out_weight, cotangent,
         feed_down,
     )
 
-    fused = (width // groups) % LANES == 0
     if fused:
-        (
-            d_mixed, d_hidden_own, feed_gain_part, grad_feed_gate, grad_feed_up, active, layer_share,
-        ) = back_feed(
-            2, lines, groups, feed_gain_wide.reshape(1, -1), hidden_own, cotangent_own, feed_normed,
+        d_mixed, d_hidden_own, feed_gain_part, feed_recv, active, layer_share = back_feed(
+            2, lines, groups, gains, hidden_own, cotangent, feed_normed,
             d_active, feed_gate, feed_up, feed_down,
         )
     else:
+        half = count // 2
+        own_at = jnp.where(place == 0, half, 0)
+        tokens_own = lax.dynamic_slice_in_dim(tokens, own_at, half)
+        cotangent_own = lax.dynamic_slice_in_dim(cotangent, own_at, half)
         gate_hidden = dot(feed_normed, feed_gate)
         up_hidden = dot(feed_normed, feed_up)
         d_active = d_active.astype(f32)
@@ -1775,16 +1947,15 @@
         d_up_hidden = (d_active * swish_gate).astype(bf16)
         feed_share = (dot_t(d_gate_hidden, feed_gate) + dot_t(d_up_hidden, feed_up)).astype(bf16)
         d_mixed, d_hidden_own, feed_gain_part = line_sum(
-            2, lines, feed_share, hidden_own, cotangent_own, feed_gain_wide.reshape(1, -1)
+            2, lines, feed_share, hidden_own, cotangent_own, gains[1:2]
         )
         layer_share = dot(active, feed_down).astype(bf16)
 
-    d_rows, d_gate_low, head_gain_part, up_part, bias_part, layer_out, grad_feed_down = recur_back(
+    d_rows, d_gate_low, head_gain_part, up_part, bias_part, layer_out, down_recv = recur_back(
         4, lines, groups, dk, dv, fused, lengths, send_row, send_column, slot_row, slot_column, d_mixed,
-        out_weight, attended, gate_pre, head_gain_wide.reshape(1, -1), up_wide, bias, down_wide, layer_share, held, states,
-        hidden_own, active, cotangent,
+        out_weight, attended, gate_pre, gains, up_rows, layer_share, held, states, hidden_own, active,
+        cotangent,
     )
-    down_both = jnp.concatenate([down_pad, down_pad, down_none, down_none], axis=1)
     up_part = up_part[:, :rank] + up_part[:, third : third + rank] + (
         up_part[:, 2 * third : 2 * third + rank]
     )
@@ -1805,22 +1976,29 @@
         near_all = (per + head_per + LANES - 1) // LANES
         near = jnp.concatenate(near, axis=1)
         near = jnp.pad(near, ((0, 0), (0, -near.shape[1] % (8 * LANES))))
+        token_grad, wide_sum, near_sum, rows_recv, out_recv = back_mixer(
+            3, lines, groups, gains, near.reshape(groups, -1, LANES), near_all, down_rows, tokens,
+            d_hidden_own, normed, [d_rows, d_gate_low], (gated, d_mixed),
+            [query_weight, key_weight, value_weight, gate_weight],
+        )
         (
-            token_grad, wide_sum, near_sum, grad_query, grad_key, grad_value, grad_gate, grad_out,
-        ) = back_mixer(
-            3, lines, groups, mixer_gain_wide.reshape(1, -1), near.reshape(groups, -1, LANES),
-            near_all, tokens_own, d_hidden_own, normed, [d_rows, d_gate_low],
-            [(0, dk), (dk, dk), (2 * dk, dv), (2 * dk + dv + LANES, dv)], (gated, d_mixed),
-            [query_weight, key_weight, value_weight, down_both, gate_weight],
+            token_grad, layer_out, grad_query, grad_key, grad_value, grad_gate, grad_feed_gate,
+            grad_feed_up, grad_feed_down, grad_out, down_sum, mixer_sum,
+        ) = outputs(
+            groups, dk, dv, rank, near_all, feed_recv, rows_recv, down_recv, out_recv,
+            wide_sum, near_sum, token_grad, layer_out,
         )
         near_sum = near_sum.reshape(-1)
-        mixer_sum = jnp.sum(wide_sum[16:], axis=0)
+        mixer_sum = mixer_sum.reshape(-1)
+        down_sum = down_sum.T
         feed_sum = near_sum[:per]
         head_sum = near_sum[per : per + head_per]
-        down_sum = wide_sum[:16].T
         up_sum = near_sum[near_all * LANES : near_all * LANES + up_per]
         bias_sum = near_sum[near_all * LANES + up_per :][: dk // groups]
     else:
+        down_pad = jnp.pad(decay_down, ((0, 0), (0, third - rank)))
+        down_none = jnp.zeros_like(down_pad)
+        down_both = jnp.concatenate([down_pad, down_pad, down_none, down_none], axis=1)
         d_query_low = d_rows[:, :dk]
         d_key_low = d_rows[:, dk : 2 * dk]
         d_value_low = d_rows[:, 2 * dk : 2 * dk + dv]
@@ -1833,8 +2011,7 @@
             + dot_t(d_latent_low, down_both)
         ).astype(bf16)
         token_grad, _, mixer_gain_part = line_sum(
-            3, lines, normed_share, tokens_own, d_hidden_own,
-            mixer_gain_wide.reshape(1, -1),
+            3, lines, normed_share, tokens_own, d_hidden_own, gains[0:1],
         )
         down_part = rows_dot(normed, d_latent_low)
         down_part = down_part[:, :rank] + down_part[:, third : third + rank]
@@ -1877,12 +2054,12 @@
         return jnp.sum(moved.astype(f32), axis=0)
 
     if not fused:
-        grad_feed_down = summed_share(halves(active, active.shape[1]), partner(cotangent))
+        grad_feed_down = summed_share(halves(active, active.shape[1]), partner(cotangent))[None]
         feed_halves = halves(feed_normed, width)
         normed_halves = halves(normed, width)
         grad_feed_gate = summed_share(feed_halves, partner(d_gate_hidden))
         grad_feed_up = summed_share(feed_halves, partner(d_up_hidden))
-        grad_out = summed_share(halves(gated, dv), partner(d_mixed))
+        grad_out = summed_share(halves(gated, dv), partner(d_mixed))[None]
         grad_query = summed_share(normed_halves, partner(d_query_low))
         grad_key = summed_share(normed_halves, partner(d_key_low))
         grad_value = summed_share(normed_halves, partner(d_value_low))
@@ -1900,11 +2077,11 @@
         up_sum.reshape(1, dk // groups, rank),
         bias_sum.reshape(1, dk // groups),
         head_sum,
-        grad_out[None],
+        grad_out,
         feed_sum,
         grad_feed_gate,
         grad_feed_up,
-        grad_feed_down[None],
+        grad_feed_down,
     )
 
 

time: 474 us -> 450 us (0.949)
  local copies, waits for them, and re-layouts: 26.6 us -> 6.69 us
  other arithmetic: 10.6 us -> 3.3 us
    unnamed x38 -> x6, local copies, waits for them, and re-layouts: 14.5 us -> 1.31 us
    pallas_call x1 -> x2, Pallas kernels: 105 us -> 115 us  [the longest x1 102 us: back_feed(): pl.pallas_call(functools.partial(back_feed_kernel, n, groups, tiles), in_...]
    pallas_call x1, Pallas kernels: 147 us -> 139 us  [front(): pl.pallas_call(functools.partial(front_kernel, n, groups, dk, dv), in_spe...]
    reshape x4 -> x0, other arithmetic: 5.19 us -> none  [the longest x1 1.36 us: per_device(): bias = decay_bias.astype(f32).reshape(1, dk)]
where the time goes in v7:
time: 450 us
  Pallas kernels  439 us (98%)
  local copies, waits for them, and re-layouts  6.69 us (1%)
    pallas_call x1, Pallas kernels, front(): pl.pallas_call(functools.partial(front_kernel, n, groups, dk, dv), in_spe...  139 us
    pallas_call x1, Pallas kernels, back_feed(): pl.pallas_call(functools.partial(back_feed_kernel, n, groups, tiles), in_...  102 us
    pallas_call x1, Pallas kernels, recur_back(): pl.pallas_call(functools.partial(recur_back_kernel, n, groups, dk, dv, be...  95.8 us
    pallas_call x1, Pallas kernels, back_mixer(): pl.pallas_call(functools.partial(back_mixer_kernel, n, groups, widths, ne...  89.3 us
    pallas_call x1, Pallas kernels, outputs(): pl.pallas_call(functools.partial(outputs_kernel, dk, dv, rank, near_all),...  13.4 us

profile of v7, /device:TPU:0, one launch (start us, length us, event | category | flops | bytes accessed | tf_op | source)
XLA Modules:
  0.0 449.8 jit_solution(17864784556609901698)
XLA Ops:
  0.6 0.7 fusion.5
  1.4 0.7 stack.12
  2.1 0.7 stack.13
  2.7 0.6 maximum_convert_fusion.refs_3_.refs_0_.refs_9_
  3.4 1.3 reshape.63.refs_1_
  4.7 138.5 %front.1 = (bf16[640,2048]{1,0:T(8,128)(2,1)}, f32[640,512]{1,0:T(8,128)}, bf16[640,512]{1,0:T(8,128)(2,1)}, bf16[640,512]{1,0:T(8,128)(2,1)}, bf16[1024,1152]{1...) custom-call(s32[1,3]{1,0:T(1,128)} %refs_0_.3, ...), custom_call_target="tpu_custom_call" | custom-call | flops 12000000000 | bytes 200000000 | tf_op jit(solution)/shard_map/front/pallas_call | solution.py:957
  143.2 102.0 %back_feed.1 = (bf16[640,2048]{1,0:T(8,128)(2,1)}, f32[320,2048]{1,0:T(8,128)}, f32[8,2048]{1,0:T(8,128)}, bf16[4,256,2816]{2,1,0:T(8,128)(2,1)}, bf16[640,1408]{1,0:T(8,128)(2,1)}, /*index=5*/bf16[640,2048]{1,0:T(8,128)(2,1)}) custom-call(f32[3,2048]{1,0:T(4,128)} %maximum_convert_fusion.refs_3_.refs_0_.refs_9_, ...), custom_call_target="tpu_custom_call" | custom-call | flops 30000001024 | bytes 200000000 | tf_op jit(solution)/shard_map/back_feed/pallas_call | solution.py:1176
  245.2 0.0 copy-start
  245.2 95.8 %recur_back.1 = (bf16[640,1152]{1,0:T(8,128)(2,1)}, bf16[640,512]{1,0:T(8,128)(2,1)}, f32[8,512]{1,0:T(8,128)}, f32[256,128]{1,0:T(8,128)}, f32[8,256]{1,0:T(8,1...) custom-call(s32[1,3]{1,0:T(1,128)} %refs_0_.3, s32[1,640]{1,0:T(1,128)} %get-tuple-element.64.refs_1_, ...), custom_call_target="tpu_custom_call" | custom-call | flops 12000000000 | bytes 200000000 | tf_op jit(solution)/shard_map/recur_back/pallas_call | solution.py:1735
  341.1 0.7 reduce_sum.19
  341.8 0.7 slice_reduce_fusion
  342.5 0.1 reshape.65
  342.6 0.1 reshape_squeeze.3
  342.7 0.0 copy-done
  342.7 1.2 slice_add_fusion
  343.9 0.1 reshape.66
  344.1 0.6 copy.38
  344.7 89.3 %back_mixer.1 = (bf16[640,2048]{1,0:T(8,128)(2,1)}, f32[24,256]{1,0:T(8,128)}, f32[8,128]{1,0:T(8,128)}, bf16[4,256,1664]{2,1,0:T(8,128)(2,1)}, bf16[8,64,1024]{2,1,0:T(8,128)(2,1)}) custom-call(f32[3,2048]{1,0:T(4,128)} %maximum_convert_fusion.refs_3_.refs_0_.refs_9_, f32[8,8,128]{2,1,0:T(8,128)} %bitcast.12, bf16[16,2048]{1,0:T(8,128)(2,1)} %bitcast.15, ...), custom_call_target="tpu_custom_call" | custom-call | flops 12000000000 | bytes 200000000 | tf_op jit(solution)/shard_map/back_mixer/pallas_call | solution.py:1455
  434.0 0.0 copy-start.1
  434.0 13.4 %outputs.1 = (bf16[640,2048]{1,0:T(8,128)(2,1)}, bf16[640,2048]{1,0:T(8,128)(2,1)}, f32[256,256]{1,0:T(8,128)}, f32[256,256]{1,0:T(8,128)}, f32[256,512]{1,0:T(8...) custom-call(bf16[4,256,2816]{2,1,0:T(8,128)(2,1)} %get-tuple-element, ...), custom_call_target="tpu_custom_call" | custom-call | tf_op jit(solution)/shard_map/outputs/pallas_call | solution.py:1560
  447.5 0.0 copy-done.1
  447.5 0.5 slice.38
  448.0 0.5 slice.37
  448.5 0.6 slice_bitcast_fusion
  449.1 0.1 reshape.69
  449.1 0.7 copy.35
  (5 shorter events, 0.0 us)
Async XLA Ops:
  245.2 97.5 %copy-start = (f32[8,2048]{1,0:T(8,128)S(1)}, f32[8,2048]{1,0:T(8,128)}, u32[]{:S(2)}) copy-start(f32[8,2048]{1,0:T(8,128)} %get-tuple-element.63) | copy-start | bytes 196612
  434.0 13.5 %copy-start.1 = (f32[8,128]{1,0:T(8,128)S(1)}, f32[8,128]{1,0:T(8,128)}, u32[]{:S(2)}) copy-start(f32[8,128]{1,0:T(8,128)} %get-tuple-element.87.refs_5_) | copy-start | bytes 12292

commit v8 on v7

--- a/solution.py
+++ b/solution.py
@@ -140,7 +140,7 @@
 
 
 FINE = 16
-SKEW = 2
+SKEW = 3
 
 
 class Line:
@@ -149,6 +149,7 @@
         self.share, self.up_in, self.down_in, self.out = share_ref, up_in, down_in, out_ref
         self.sems, self.finish = sems, finish
         self.half = up_in.shape[0]
+        self.block = self.half // 2
         self.count = self.half // FINE
         self.second = self.count + 2
         self.steps = self.second + self.count + SKEW * (n - 2)
@@ -161,8 +162,22 @@
     def semaphores(half):
         return pltpu.SemaphoreType.DMA((8, half // FINE))
 
-    def own_half(self):
-        return pl.ds(pl.multiple_of(jnp.where(self.me == 0, self.half, 0), self.half), self.half)
+    def own_copies(self, source, target, sems):
+        block = self.block
+        return [
+            pltpu.make_async_copy(
+                source.at[
+                    pl.ds(
+                        pl.multiple_of(2 * i * block + jnp.where(self.me == 0, block, 0), block),
+                        block,
+                    ),
+                    :,
+                ],
+                target.at[pl.ds(i * block, block), :],
+                sems[i],
+            )
+            for i in range(2)
+        ]
 
     def greet(self, barrier, others):
         n, me = self.n, self.me
@@ -198,11 +213,19 @@
 
         pl.semaphore_wait(barrier, others + n - 1)
 
+    def own(self, g):
+        return pl.ds(pl.multiple_of(g * FINE, FINE), FINE)
+
     def at(self, g):
-        return pl.ds(pl.multiple_of(g * FINE, FINE), FINE)
+        per = self.block // FINE
+        return pl.ds(
+            pl.multiple_of((g // per) * 2 * self.block + lax.rem(g, per) * FINE, FINE), FINE
+        )
 
     def low(self, g):
-        return pl.ds(pl.multiple_of(self.half + g * FINE, FINE), FINE)
+        per = self.block // FINE
+        start = (g // per) * 2 * self.block + self.block + lax.rem(g, per) * FINE
+        return pl.ds(pl.multiple_of(start, FINE), FINE)
 
     def right(self, source, target, lane, g):
         return pltpu.make_async_remote_copy(
@@ -217,11 +240,11 @@
         )
 
     def up_copy(self, g):
-        rows = self.up_in.at[self.at(g), :]
+        rows = self.up_in.at[self.own(g), :]
         return self.right(rows, rows, 0, g)
 
     def down_copy(self, g):
-        rows = self.down_in.at[self.at(g), :]
+        rows = self.down_in.at[self.own(g), :]
         return self.left(rows, rows, 1, g)
 
     def up_back_copy(self, g):
@@ -232,41 +255,46 @@
         rows = self.out.at[self.low(g), :]
         return self.right(rows, rows, 3, g)
 
-    def prime(self, top=True, bottom=True):
-        @pl.when((self.me == 0) & top)
-        def _():
-            @pl.loop(0, self.count)
+    def prime(self, block=None):
+        first, last = (0, self.count)
+        if block is not None:
+            per = self.block // FINE
+            first, last = block * per, block * per + per
+
+        @pl.when(self.me == 0)
+        def _():
+            @pl.loop(first, last)
             def _(g):
                 self.right(
-                    self.share.at[self.at(g), :], self.up_in.at[self.at(g), :], 0, g
+                    self.share.at[self.at(g), :], self.up_in.at[self.own(g), :], 0, g
                 ).start()
 
-        @pl.when((self.me == self.n - 1) & bottom)
-        def _():
-            @pl.loop(0, self.count)
+        @pl.when(self.me == self.n - 1)
+        def _():
+            @pl.loop(first, last)
             def _(g):
                 self.left(
-                    self.share.at[self.low(g), :], self.down_in.at[self.at(g), :], 1, g
+                    self.share.at[self.low(g), :], self.down_in.at[self.own(g), :], 1, g
                 ).start()
 
     def step(self, step):
         n, me, count = self.n, self.me, self.count
-        at, low = self.at, self.low
+        at, low, own = self.at, self.low, self.own
         g_up = step - SKEW * (me - 1)
 
         @pl.when((me > 0) & (g_up >= 0) & (g_up < count))
         def _():
             self.up_copy(g_up).wait_recv()
-            total = self.up_in[at(g_up), :].astype(f32) + self.share[at(g_up), :].astype(f32)
+            total = self.up_in[own(g_up), :].astype(f32) + self.share[at(g_up), :].astype(f32)
 
             @pl.when(me < n - 1)
             def _():
-                self.up_in[at(g_up), :] = total.astype(bf16)
+                self.up_in[own(g_up), :] = total.astype(bf16)
                 self.up_copy(g_up).start()
 
             @pl.when(me == n - 1)
             def _():
-                self.finish(total, at(g_up), at(g_up))
+                self.finish(total, own(g_up), at(g_up))
                 self.up_back_copy(g_up).start()
 
         g_down = step - SKEW * (n - 2 - me)
@@ -274,18 +302,18 @@
         @pl.when((me < n - 1) & (g_down >= 0) & (g_down < count))
         def _():
             self.down_copy(g_down).wait_recv()
-            total = self.down_in[at(g_down), :].astype(f32) + (
+            total = self.down_in[own(g_down), :].astype(f32) + (
                 self.share[low(g_down), :].astype(f32)
             )
 
             @pl.when(me > 0)
             def _():
-                self.down_in[at(g_down), :] = total.astype(bf16)
+                self.down_in[own(g_down), :] = total.astype(bf16)
                 self.down_copy(g_down).start()
 
             @pl.when(me == 0)
             def _():
-                self.finish(total, at(g_down), low(g_down))
+                self.finish(total, own(g_down), low(g_down))
                 self.down_back_copy(g_down).start()
 
         g_up_back = step - self.second - SKEW * (n - 2 - me)
@@ -329,7 +357,7 @@
                 self.up_back_copy(g).wait_send()
 
 
-def norm_back(x_ref, base_ref, gain, out_ref, kept_ref, gain_grad_ref):
+def norm_back(x_ref, base, gain, out_ref, kept_ref, gain_grad_ref):
     gain_grad_ref[...] = jnp.zeros_like(gain_grad_ref)
 
     def finish(total, own, place):
@@ -337,7 +365,7 @@
         scaling = lax.rsqrt(jnp.mean(rows * rows, axis=1, keepdims=True) + epsilon)
         unit = rows * scaling
         gained = gain() * total
-        grad = base_ref[own, :].astype(f32) + scaling * (
+        grad = base(own, place).astype(f32) + scaling * (
             gained - unit * jnp.mean(gained * unit, axis=1, keepdims=True)
         )
         if kept_ref is not None:
@@ -352,10 +380,31 @@
     return finish
 
 
-def line_kernel(n, *refs):
+def norm_forward(base, gain, out_ref, kept_ref):
+    def finish(total, own, place):
+        hidden = base(own, place).astype(f32) + total
+        kept_ref[own, :] = hidden
+        scaling = lax.rsqrt(jnp.mean(hidden * hidden, axis=1, keepdims=True) + epsilon)
+        out_ref[place, :] = (hidden * scaling * gain()).astype(bf16)
+
+    return finish
+
+
+def line_kernel(mode, n, *refs):
     share_ref, x_ref, base_ref, gain_ref, out_ref, kept_ref, gain_grad_ref = refs[:7]
     up_in, down_in, sems = refs[7:]
-    finish = norm_back(x_ref, base_ref, lambda: gain_ref[...], out_ref, kept_ref, gain_grad_ref)
+
+    def base(own, place):
+        return base_ref[own, :]
+
+    def gain():
+        return gain_ref[...]
+
+    gain_grad_ref[...] = jnp.zeros_like(gain_grad_ref)
+    if mode == "norm":
+        finish = norm_forward(base, gain, out_ref, kept_ref)
+    else:
+        finish = norm_back(x_ref, base, gain, out_ref, kept_ref, gain_grad_ref)
     line = Line(n, share_ref, up_in, down_in, out_ref, sems, finish)
     line.greet(pltpu.get_barrier_semaphore(), 0)
     line.prime()
@@ -363,12 +412,12 @@
     line.drain()
 
 
-def line_sum(call, n, share, x_own, base_own, gain):
+def line_sum(mode, call, n, share, x_own, base_own, gain):
     rows, width = share.shape
     half = rows // 2
     vmem = pl.BlockSpec(memory_space=pltpu.VMEM)
     return pl.pallas_call(
-        functools.partial(line_kernel, n),
+        functools.partial(line_kernel, mode, n),
         in_specs=[vmem] * 4,
         out_specs=[vmem] * 3,
         out_shape=[
@@ -380,7 +429,7 @@
         compiler_params=pltpu.CompilerParams(
             collective_id=call, has_side_effects=True, vmem_limit_bytes=40 << 20
         ),
-        name="line_back",
+        name="line_" + mode,
     )(share, x_own, base_own, gain)
 
 
@@ -507,17 +556,20 @@
 
 
 class RowGrads:
-    def __init__(self, groups, left, tiles, recv, refs):
+    def __init__(self, groups, left, tiles, recv, refs, deferred=0):
         (
             self.left, self.all, self.left_in, self.all_in, self.send,
             self.load_sems, self.left_sems, self.piece_sems, self.sems, self.keep_sems,
         ) = refs
         self.left_far, self.tiles, self.recv = left, tiles, recv
+        self.live = len(tiles) - deferred
+        if left is None:
+            self.left_far = self.left
         self.member = lax.axis_index("dp")
         self.parity = lax.rem(self.member, 2)
         self.mine = self.member // 2
         self.team = groups // 2
-        self.block = left.shape[1] // groups
+        self.block = self.left.shape[1] // groups
         self.items = self.team * len(tiles)
 
     @staticmethod
@@ -552,9 +604,9 @@
             self.left_sems.at[0, q], self.left_sems.at[1, q], partner_of(self.member),
         )
 
-    def piece_copy(self, p, source, span):
+    def piece_copy(self, p, source, span, rows=slice(None)):
         return to_dp(
-            source, self.all_in.at[:, span], self.piece_sems.at[0, p], self.piece_sems.at[1, p],
+            source, self.all_in.at[rows, span], self.piece_sems.at[0, p], self.piece_sems.at[1, p],
             partner_of(self.member),
         )
 
@@ -595,13 +647,14 @@
                 ) + rows_dot(self.left_in[:, self.columns(to)], self.all_in[:, span])
                 self.send[to, :, span] = product.astype(bf16)
 
-                @pl.when(k < self.team - 1)
-                def _():
-                    self.copy(t, to, self.mine).start()
-
-                @pl.when(k == self.team - 1)
-                def _():
-                    self.keep(t).start()
+                if t < self.live:
+                    @pl.when(k < self.team - 1)
+                    def _():
+                        self.copy(t, to, self.mine).start()
+
+                    @pl.when(k == self.team - 1)
+                    def _():
+                        self.keep(t).start()
 
     def keep(self, t):
         start, wide = self.tiles[t]
@@ -611,7 +664,7 @@
         )
 
     def receive(self):
-        for t in range(len(self.tiles)):
+        for t in range(self.live):
             self.keep(t).wait()
 
             @pl.loop(1, self.team)
@@ -623,7 +676,7 @@
         def _(q):
             self.left_copy(q).wait_send()
 
-        for t in range(len(self.tiles)):
+        for t in range(self.live):
             @pl.loop(1, self.team)
             def _(k):
                 self.copy(t, lax.rem(self.mine + k, self.team), self.mine).wait_send()
@@ -677,7 +730,7 @@
             self.sems.at[0, p, to], self.sems.at[1, p, source], to,
         )
 
-    def send(self, p, index_ref, dim, source):
+    def send(self, p, index_ref, dim, source, between=None):
         span = self.spans[p]
         groups, count = self.groups, source.shape[0]
         rows = self.sent.shape[0] // 2
@@ -699,6 +752,9 @@
                 def _():
                     self.copy(p, to, self.member).start()
 
+            if between is not None:
+                between(h)
+
         own = self.part(self.member)
         self.came[own, span] = self.sent[own, span]
 
@@ -714,7 +770,7 @@
                 self.copy(p, lax.rem(self.member + k, self.groups), self.member).wait_send()
 
 
-def place_rows(slot_row_ref, came, held, span):
+def place_rows(slot_row_ref, came, held, span, between=None):
     positions, slots = held.shape[0], came.shape[0]
     rows = positions // 2
 
@@ -723,20 +779,22 @@
         at = pl.ds(pl.multiple_of(h * rows, rows), rows)
         pick = one_hot(slot_row_ref[...], h * rows, (rows, slots), 0)
         held[at, span] = dot(pick, came[:, span]).astype(bf16)
-
-
-def front_kernel(n, groups, dk, dv, *refs):
+        if between is not None:
+            between(h)
+
+
+def front_kernel(groups, dk, dv, *refs):
     take = splitter(refs)
-    lengths_ref, slots_ref, tokens_ref, gains_ref, up_rows_ref, down_rows_ref = take(6)
+    lengths_ref, slot_rows_ref, tokens_ref, gains_ref, up_rows_ref, down_rows_ref = take(6)
     weights_far = take(3)
-    gate_far, out_far, cotangent_far, down_far = take(4)
+    gate_far, out_far = take(2)
     spilled = take(6)
-    feed_ref, hidden_ref, d_active_ref = take(3)
+    (share_ref,) = take(1)
     send_row_ref, send_column_ref, slot_row_ref, slot_column_ref = take(4)
     normed_ref, gate_ref, attended_ref, gated_ref, held_ref, states_ref = kept = take(6)
-    up_in, down_in, weight_ref, gate_weight_ref, out_weight_ref, cotangent_ref, down_ref = take(7)
-    rows_out, share_ref, state, result, rank_ref, up_ref, bias_ref, latent_ref = take(8)
-    load_sems, sems = take(2)
+    weight_ref, gate_weight_ref, out_weight_ref = take(3)
+    rows_out, state, result, rank_ref, up_ref, bias_ref, latent_ref = take(7)
+    slots_ref, load_sems = take(2)
     go = Exchange(groups, (2 * dk,), *take(3))
     back = Exchange(groups, (), *take(3))
     (spill_sems,) = take(1)
@@ -757,13 +815,6 @@
     ends = (end0, end1, end1 + lengths_ref[0, 2])
     third = LANES // 4
 
-    def finish(total, own, place):
-        hidden = tokens_ref[place, :].astype(f32) + total
-        hidden_ref[own, :] = hidden
-        scaling = lax.rsqrt(jnp.mean(hidden * hidden, axis=1, keepdims=True) + epsilon)
-        feed_ref[place, :] = (hidden * scaling * gains_ref[1:2, :]).astype(bf16)
-
-    line = Line(n, share_ref, up_in, down_in, feed_ref, sems, finish)
     loads = []
     offset = 0
     for i, far in enumerate(weights_far):
@@ -776,16 +827,15 @@
         pltpu.make_async_copy(gate_far, gate_weight_ref, load_sems.at[4]),
         pltpu.make_async_copy(out_far, out_weight_ref, load_sems.at[5]),
     ]
-    latest = [
-        pltpu.make_async_copy(cotangent_far, cotangent_ref, load_sems.at[6]),
-        pltpu.make_async_copy(down_far, down_ref, load_sems.at[7]),
-    ]
-    for c in loads + later + latest:
+    for c in loads + later:
         c.start()
     barrier = pltpu.get_barrier_semaphore()
     greet_dp(barrier, groups)
-    line.greet(barrier, groups - 1)
-
+    pl.semaphore_wait(barrier, groups - 1)
+
+    pieces = count // LANES
+    for i in range(pieces):
+        slots_ref[:, i * LANES : (i + 1) * LANES] = slot_rows_ref[pl.ds(i, groups, stride=pieces), :]
     owners = slots_ref[...] // OWN_CAP
     mine = owners == member
     my_slots = slots_ref[pl.ds(member, 1), :]
@@ -892,40 +942,11 @@
             to = pl.ds(pl.multiple_of(i * 512, 512), 512)
             share_ref[at, to] = dot(gated_ref[at, :], out_weight_ref[:, to]).astype(bf16)
 
-    last = line.me == n - 1
-
     @pl.loop(0, 2)
     def _(i):
-        bottom = jnp.where(last, 1 - i, i)
-        head_rows(pl.ds(pl.multiple_of(bottom * half, half), half))
-        line.prime(i == 0, i == 0)
+        head_rows(pl.ds(pl.multiple_of(i * half, half), half))
 
     spill(2, 3)
-    wide = d_active_ref.shape[1]
-    full, rest = wide // 256, wide % 256
-
-    def hidden_units(i, size):
-        at = pl.ds(pl.multiple_of(i * 256, 256), size)
-        d_active_ref[:, at] = dot_t(cotangent_ref[...], down_ref[at, :]).astype(bf16)
-
-    for c in latest:
-        c.wait()
-
-    @pl.loop(0, line.steps)
-    def _(step):
-        line.step(step)
-        i = step // 2 - 2
-
-        @pl.when((lax.rem(step, 2) == 0) & (i >= 0) & (i < full))
-        def _():
-            hidden_units(i, 256)
-
-        if rest:
-            @pl.when(step == 2 * full + 4)
-            def _():
-                hidden_units(full, rest)
-
-    line.drain()
     go.drain()
     back.drain()
     for c in spills:
@@ -933,14 +954,13 @@
 
 
 def front(
-    call, n, groups, lengths, slots, tokens, gains, up_rows, down_rows, weights, gate_weight,
-    out_weight, cotangent, feed_down,
+    call, groups, lengths, slots, tokens, gains, up_rows, down_rows, weights, gate_weight,
+    out_weight,
 ):
     count, width = tokens.shape
     dk, dv = weights[0].shape[1], weights[2].shape[1]
     body = 2 * dk + dv
     wide = body + LANES
-    half = count // 2
     spans = OWN_CAP // SPAN
     vmem = pl.BlockSpec(memory_space=pltpu.VMEM)
     far = pl.BlockSpec(memory_space=pl.ANY)
@@ -955,37 +975,31 @@
         shape((spans, dk, dv), bf16),
     ]
     return pl.pallas_call(
-        functools.partial(front_kernel, n, groups, dk, dv),
-        in_specs=[smem] + [vmem] * 5 + [far] * 7,
-        out_specs=[far] * 6 + [vmem] * 7,
+        functools.partial(front_kernel, groups, dk, dv),
+        in_specs=[smem] + [vmem] * 5 + [far] * 5,
+        out_specs=[far] * 6 + [vmem] * 5,
         out_shape=[
             *saved,
             shape((count, width), bf16),
-            shape((half, width), f32),
-            shape((count, feed_down.shape[0]), bf16),
             shape((1, count), jnp.int32),
             shape((count, 1), jnp.int32),
             shape((1, OWN_CAP), jnp.int32),
             shape((OWN_CAP, 1), jnp.int32),
         ],
         scratch_shapes=[pltpu.VMEM(a.shape, a.dtype) for a in saved]
-        + Line.scratch(half, width)
         + [
             pltpu.VMEM((width, body), bf16),
             pltpu.VMEM((width, dv), bf16),
             pltpu.VMEM((dv, width), bf16),
-            pltpu.VMEM((count, width), bf16),
-            pltpu.VMEM(feed_down.shape, bf16),
             pltpu.VMEM((count, wide), bf16),
-            pltpu.VMEM((count, width), bf16),
             pltpu.VMEM((dk, dv), f32),
             pltpu.VMEM((OWN_CAP, dv), bf16),
             pltpu.VMEM((groups, count), f32),
             pltpu.VMEM((LANES, dk), bf16),
             pltpu.VMEM((1, dk), f32),
             pltpu.VMEM((LANES, width), bf16),
+            pltpu.VMEM((groups, count), jnp.int32),
             pltpu.SemaphoreType.DMA((8,)),
-            Line.semaphores(half),
         ]
         + Exchange.scratch(groups, OWN_CAP, wide, 2)
         + Exchange.scratch(groups, OWN_CAP, dv, 1)
@@ -999,35 +1013,48 @@
         name="front",
     )(
         lengths, slots, tokens, gains, up_rows, down_rows, *weights, gate_weight, out_weight,
-        cotangent, feed_down,
     )
 
 
 def back_feed_kernel(n, groups, tiles, *refs):
     take = splitter(refs)
-    gains_ref, x_far, base_far, left_far, d_active_far, gate_far, up_far, down_far = take(8)
-    out_ref, kept_ref, gain_grad_ref, recv, active_far, layer_far = take(6)
-    active_ref, layer_ref = take(2)
-    up_in, down_in, x_ref, base_ref, share_ref, weight_ref, d_active_ref = take(7)
-    load_sems, weight_sems, sems = take(3)
-    active_spill = pltpu.make_async_copy(active_ref, active_far, load_sems.at[4])
-    layer_spill = pltpu.make_async_copy(layer_ref, layer_far, load_sems.at[5])
-    rows = RowGrads(groups, left_far, tiles, recv, take(10))
-    finish = norm_back(
-        x_ref, base_ref, lambda: gains_ref[1:2, :], out_ref, kept_ref, gain_grad_ref
-    )
-    line = Line(n, share_ref, up_in, down_in, out_ref, sems, finish)
+    gains_ref, first_share_ref, tokens_far, cotangent_far, gate_far, up_far, down_far = take(7)
+    out_ref, kept_ref, gain_grad_ref = take(3)
+    recv, more_far, active_far, layer_far, hidden_far = take(5)
+    active_ref, layer_ref, first_up, first_down, up_in, down_in = take(6)
+    hidden_ref, tokens_ref, cotangent_ref, share_ref, weight_ref, d_active_ref = take(6)
+    load_sems, weight_sems, first_sems, sems = take(4)
+    rows = RowGrads(groups, None, tiles, recv, take(10), deferred=1)
+    feed_ref = rows.left
     count, width = share_ref.shape
     wide = active_ref.shape[1]
     full, rest = wide // 256, wide % 256
     pieces = full + (rest > 0)
-    loads = (
-        pltpu.make_async_copy(d_active_far, d_active_ref, load_sems.at[2]),
-        pltpu.make_async_copy(x_far, x_ref, load_sems.at[0]),
-        pltpu.make_async_copy(base_far.at[line.own_half(), :], base_ref, load_sems.at[1]),
+    half = count // 2
+    first_line = Line(
+        n, first_share_ref, first_up, first_down, feed_ref, first_sems,
+        norm_forward(
+            lambda own, place: tokens_ref[own, :], lambda: gains_ref[1:2, :], feed_ref, hidden_ref
+        ),
     )
+    line = Line(
+        n, share_ref, up_in, down_in, out_ref, sems,
+        norm_back(
+            hidden_ref, lambda own, place: cotangent_ref[place, :], lambda: gains_ref[1:2, :],
+            out_ref, kept_ref, gain_grad_ref,
+        ),
+    )
+    token_loads = first_line.own_copies(tokens_far, tokens_ref, [load_sems.at[0], load_sems.at[1]])
+    cotangent_load = pltpu.make_async_copy(cotangent_far, cotangent_ref, load_sems.at[2])
     down_load = pltpu.make_async_copy(
         down_far, weight_ref.at[pl.ds(0, wide), pl.ds(0, width)], load_sems.at[3]
+    )
+    active_spill = pltpu.make_async_copy(active_ref, active_far, load_sems.at[4])
+    layer_spill = pltpu.make_async_copy(layer_ref, layer_far, load_sems.at[5])
+    hidden_spill = pltpu.make_async_copy(hidden_ref, hidden_far, load_sems.at[6])
+    more_start, more_wide = tiles[-1]
+    more_spill = pltpu.make_async_copy(
+        rows.send.at[:, :, pl.ds(more_start, more_wide)], more_far, load_sems.at[7]
     )
 
     def spans(i, size):
@@ -1045,11 +1072,15 @@
             ),
         )
 
-    def piece_copies(i, size):
+    def block_rows(b):
+        return pl.ds(b * half, half)
+
+    def piece_copies(b, i, size):
         gate_span, up_span = spans(i, size)
-        return (
-            rows.piece_copy(2 * i, rows.all.at[:, gate_span], gate_span),
-            rows.piece_copy(2 * i + 1, rows.all.at[:, up_span], up_span),
+        at = block_rows(b)
+        return tuple(
+            rows.piece_copy(2 * (b * pieces + i) + j, rows.all.at[at, span], span, at)
+            for j, span in enumerate((gate_span, up_span))
         )
 
     def each(action):
@@ -1060,87 +1091,152 @@
         if rest:
             action(full, rest)
 
-    def start_weights(i, size):
-        for c in weight_loads(i, size):
-            c.start()
-
-    rows.left_load().start()
-    each(start_weights)
-    for c in loads:
+    def at_item(w, action):
+        @pl.when((w >= 0) & (w < full))
+        def _():
+            action(w, 256)
+
+        if rest:
+            @pl.when(w == full)
+            def _():
+                action(full, rest)
+
+    down_load.start()
+    cotangent_load.start()
+    for c in token_loads:
         c.start()
     barrier = pltpu.get_barrier_semaphore()
     greet_dp(barrier, groups)
     line.greet(barrier, groups - 1)
+    first_line.prime()
+    for c in token_loads:
+        c.wait()
+
+    def make_d_active(i, size):
+        span, _ = spans(i, size)
+        d_active_ref[:, span] = dot_t(
+            cotangent_ref[...], weight_ref[span, pl.ds(0, width)]
+        ).astype(bf16)
+
+    def start_weights(i, size):
+        for c in weight_loads(i, size):
+            c.start()
+
+    def hidden_units(b, i, size):
+        if b == 0:
+            for c in weight_loads(i, size):
+                c.wait()
+        gate_span, up_span = spans(i, size)
+        at = block_rows(b)
+        gate = dot(feed_ref[at, :], weight_ref[:, gate_span])
+        up = dot(feed_ref[at, :], weight_ref[:, up_span])
+        d_active = d_active_ref[at, gate_span].astype(f32)
+        sigmoid = jax.nn.sigmoid(gate)
+        swish = gate * sigmoid
+        active_ref[at, gate_span] = (swish * up).astype(bf16)
+        rows.all[at, gate_span] = (
+            d_active * up * sigmoid * (1.0 + gate * (1.0 - sigmoid))
+        ).astype(bf16)
+        rows.all[at, up_span] = (d_active * swish).astype(bf16)
+        for c in piece_copies(b, i, size):
+            c.start()
+
+    share_items = width // 256
+
+    def make_share(b, w):
+        @pl.when((w >= 0) & (w < share_items))
+        def _():
+            to = pl.ds(pl.multiple_of(w * 256, 256), 256)
+            at = block_rows(b)
+            share_ref[at, to] = dot_t(rows.all[at, :], weight_ref[to, :]).astype(bf16)
+
+    per = first_line.block // FINE
+    arrived = first_line.second + SKEW * (n - 2) + per
+    d_first = 3
+
+    @pl.loop(0, first_line.steps)
+    def _(step):
+        first_line.step(step)
+
+        @pl.when(step == d_first)
+        def _():
+            down_load.wait()
+            cotangent_load.wait()
+
+        at_item(step - d_first, make_d_active)
+
+        @pl.when(step == d_first + pieces)
+        def _():
+            each(start_weights)
+
+        at_item(step - arrived, lambda i, size: hidden_units(0, i, size))
+        w = 2 * (step - arrived - pieces)
+        make_share(0, w)
+        make_share(0, w + 1)
+
+    done_share = 2 * (first_line.steps - arrived - pieces)
+
+    @pl.loop(done_share, max(share_items, done_share))
+    def _(w):
+        make_share(0, w)
+
+    line.prime(0)
+    hidden_spill.start()
 
     @pl.loop(0, rows.team)
     def _(q):
         rows.left_copy(q).start()
 
-    rows.left_load().wait()
-    for c in loads:
-        c.wait()
-
-    def hidden_units(i, size):
-        for c in weight_loads(i, size):
-            c.wait()
-        gate_span, up_span = spans(i, size)
-        gate = dot(rows.left[...], weight_ref[:, gate_span])
-        up = dot(rows.left[...], weight_ref[:, up_span])
-        d_active = d_active_ref[:, gate_span].astype(f32)
-        sigmoid = jax.nn.sigmoid(gate)
-        swish = gate * sigmoid
-        active_ref[:, gate_span] = (swish * up).astype(bf16)
-        rows.all[:, gate_span] = (
-            d_active * up * sigmoid * (1.0 + gate * (1.0 - sigmoid))
-        ).astype(bf16)
-        rows.all[:, up_span] = (d_active * swish).astype(bf16)
-        for c in piece_copies(i, size):
-            c.start()
-
-    each(hidden_units)
-    active_spill.start()
-
-    half = count // 2
-    last = line.me == n - 1
-
-    @pl.loop(0, 2)
-    def _(i):
-        bottom = jnp.where(last, 1 - i, i)
-        at = pl.ds(pl.multiple_of(bottom * half, half), half)
-
-        @pl.loop(0, width // 256)
-        def _(j):
-            to = pl.ds(pl.multiple_of(j * 256, 256), 256)
-            share_ref[at, to] = dot_t(rows.all[at, :], weight_ref[to, :]).astype(bf16)
-
-        line.prime(i == 0, i == 0)
-
-    down_load.start()
-
-    def piece_arrived(i, size):
-        for c in piece_copies(i, size):
-            c.wait_recv()
-
     layer_items = width // 512
-
-    @pl.loop(0, line.steps)
-    def _(step):
-        line.step(step)
-
-        @pl.when(step == 0)
+    first_work = 8
+
+    def row_work(w):
+        @pl.when(w == 0)
         def _():
             @pl.loop(0, rows.team)
             def _(q):
                 rows.left_copy(q).wait_recv()
 
-            each(piece_arrived)
-
-        rows.item(step)
-        layer_item = step - rows.items
-
-        @pl.when(layer_item == 0)
-        def _():
+            for b in range(2):
+                def arrive(i, size, b=b):
+                    for c in piece_copies(b, i, size):
+                        c.wait_recv()
+
+                each(arrive)
+
+        rows.item(w)
+
+    @pl.loop(0, per)
+    def _(step):
+        line.step(step)
+        at_item(step, lambda i, size: hidden_units(1, i, size))
+        w = 2 * (step - pieces)
+        make_share(1, w)
+        make_share(1, w + 1)
+        row_work(step - first_work)
+
+    done_more = 2 * (per - pieces)
+
+    @pl.loop(done_more, max(share_items, done_more))
+    def _(w):
+        make_share(1, w)
+
+    line.prime(1)
+    active_spill.start()
+    down_load.start()
+
+    @pl.loop(per, line.steps)
+    def _(step):
+        line.step(step)
+        w = step - first_work
+        row_work(w)
+
+        @pl.when(w == rows.items)
+        def _():
+            more_spill.start()
             down_load.wait()
+
+        layer_item = w - rows.items
 
         @pl.when((layer_item >= 0) & (layer_item < layer_items))
         def _():
@@ -1152,52 +1248,60 @@
             layer_spill.start()
 
     rows.receive()
+    first_line.drain()
     line.drain()
     rows.drain()
-    active_spill.wait()
-    layer_spill.wait()
-
-    def piece_sent(i, size):
-        for c in piece_copies(i, size):
-            c.wait_send()
-
-    each(piece_sent)
-
-
-def back_feed(call, n, groups, gains, x_own, base, left, d_active, feed_gate, feed_up, feed_down):
-    count, width = left.shape
+    for c in (active_spill, layer_spill, hidden_spill, more_spill):
+        c.wait()
+    for b in range(2):
+        def sent(i, size, b=b):
+            for c in piece_copies(b, i, size):
+                c.wait_send()
+
+        each(sent)
+
+
+def back_feed(call, n, groups, gains, share, tokens, cotangent, feed_gate, feed_up, feed_down):
+    count, width = share.shape
     half = count // 2
     wide = feed_gate.shape[1]
     pieces = (wide + 255) // 256
     cut = (wide // 2 + LANES - 1) // LANES * LANES
     tiles = [(0, cut), (cut, wide - cut), (wide, cut), (wide + cut, wide - cut)]
+    team, per = groups // 2, width // groups
     vmem = pl.BlockSpec(memory_space=pltpu.VMEM)
     far = pl.BlockSpec(memory_space=pl.ANY)
+    shape = jax.ShapeDtypeStruct
     return pl.pallas_call(
         functools.partial(back_feed_kernel, n, groups, tiles),
-        in_specs=[vmem] + [far] * 7,
-        out_specs=[vmem] * 3 + [far] * 3,
+        in_specs=[vmem] * 2 + [far] * 5,
+        out_specs=[vmem] * 3 + [far] * 5,
         out_shape=[
-            jax.ShapeDtypeStruct((count, width), bf16),
-            jax.ShapeDtypeStruct((half, width), f32),
-            jax.ShapeDtypeStruct((8, width), f32),
-            jax.ShapeDtypeStruct((groups // 2, width // groups, 2 * wide), bf16),
-            jax.ShapeDtypeStruct((count, wide), bf16),
-            jax.ShapeDtypeStruct((count, width), bf16),
+            shape((count, width), bf16),
+            shape((half, width), f32),
+            shape((8, width), f32),
+            shape((team, per, wide + cut), bf16),
+            shape((team, per, wide - cut), bf16),
+            shape((count, wide), bf16),
+            shape((count, width), bf16),
+            shape((half, width), f32),
         ],
         scratch_shapes=[pltpu.VMEM((count, wide), bf16), pltpu.VMEM((count, width), bf16)]
         + Line.scratch(half, width)
+        + Line.scratch(half, width)
         + [
-            pltpu.VMEM((half, width), x_own.dtype),
-            pltpu.VMEM((half, width), base.dtype),
+            pltpu.VMEM((half, width), f32),
+            pltpu.VMEM((half, width), bf16),
+            pltpu.VMEM((count, width), bf16),
             pltpu.VMEM((count, width), bf16),
             pltpu.VMEM((width, 2 * wide), bf16),
             pltpu.VMEM((count, wide), bf16),
-            pltpu.SemaphoreType.DMA((6,)),
+            pltpu.SemaphoreType.DMA((8,)),
             pltpu.SemaphoreType.DMA((2, pieces)),
             Line.semaphores(half),
+            Line.semaphores(half),
         ]
-        + RowGrads.scratch(groups, count, width, 2 * wide, 2 * pieces, len(tiles)),
+        + RowGrads.scratch(groups, count, width, 2 * wide, 4 * pieces, len(tiles)),
         compiler_params=pltpu.CompilerParams(
             collective_id=call, has_side_effects=True, vmem_limit_bytes=61 << 20
         ),
@@ -1205,7 +1309,7 @@
             flops=30_000_000_000, bytes_accessed=200_000_000, transcendentals=0
         ),
         name="back_feed",
-    )(gains, x_own, base, left, d_active, feed_gate, feed_up, feed_down)
+    )(gains, share, tokens, cotangent, feed_gate, feed_up, feed_down)
 
 
 class SmallSum:
@@ -1328,9 +1432,10 @@
     take = splitter(refs)
     gains_ref, near_ref, down_rows_ref, x_far, base_far, left_far = take(6)
     parts = take(2)
-    col_left, col_right = take(2)
+    col_left, col_right, more_far = take(3)
     weights = take(len(widths))
-    out_ref, wide_out, near_out, recv, col_recv = take(5)
+    out_ref, wide_out, near_out, recv, col_recv, more_recv = take(6)
+    more_ref, more_sems, more_load_sems = take(3)
     up_in, down_in, x_ref, base_ref, share_ref, wide_ref, gain_grad_ref = take(7)
     weight_ref, latent_ref, load_sems, sems = take(4)
     rows = RowGrads(groups, left_far, tiles, recv, take(10))
@@ -1341,12 +1446,25 @@
     part_copies = [rows.piece_copy(i, parts[i], part_spans[i]) for i in range(2)]
     cols = ColGrad(groups, col_left, col_right, 0, col_recv, take(8))
     small = SmallSum(n, groups, wide_ref, near_ref, near_all, wide_out, near_out, take(6))
-    finish = norm_back(x_ref, base_ref, lambda: gains_ref[0:1, :], out_ref, None, gain_grad_ref)
+    finish = norm_back(
+        x_ref, lambda own, place: base_ref[own, :], lambda: gains_ref[0:1, :], out_ref, None,
+        gain_grad_ref,
+    )
     line = Line(n, share_ref, up_in, down_in, out_ref, sems, finish)
-    loads = [
-        pltpu.make_async_copy(x_far.at[line.own_half(), :], x_ref, load_sems.at[0]),
-        pltpu.make_async_copy(base_far, base_ref, load_sems.at[1]),
-    ]
+    loads = line.own_copies(x_far, x_ref, [load_sems.at[0], more_load_sems.at[0]])
+    loads.append(pltpu.make_async_copy(base_far, base_ref, load_sems.at[1]))
+    more_load = pltpu.make_async_copy(more_far, more_ref, more_load_sems.at[1])
+
+    def more_copy(to, source):
+        return to_dp(
+            more_ref.at[to], more_recv.at[source], more_sems.at[0, to], more_sems.at[1, source],
+            2 * to + rows.parity,
+        )
+
+    more_keep = pltpu.make_async_copy(
+        more_ref.at[rows.mine], more_recv.at[rows.mine], more_load_sems.at[2]
+    )
+    more_load.start()
     weight_loads = []
     offset = 0
     for i, wide in enumerate(widths):
@@ -1373,6 +1491,13 @@
     cols.start()
     for c in loads:
         c.start()
+    more_load.wait()
+    more_keep.start()
+
+    @pl.loop(1, rows.team)
+    def _(k):
+        more_copy(lax.rem(rows.mine + k, rows.team), rows.mine).start()
+
     for c in part_loads + weight_loads:
         c.wait()
 
@@ -1380,15 +1505,18 @@
     tile_rows, tile_columns = count // 2, 512
     across = width // tile_columns
 
-    @pl.loop(0, 2 * across)
-    def _(i):
-        at = pl.ds(pl.multiple_of((i // across) * tile_rows, tile_rows), tile_rows)
-        to = pl.ds(pl.multiple_of(lax.rem(i, across) * tile_columns, tile_columns), tile_columns)
-        share_ref[at, to] = dot_t(rows.all[at, :], weight_ref[to, :]).astype(bf16)
-
-    line.prime()
     for c in loads:
         c.wait()
+    for b in range(2):
+        at = pl.ds(b * tile_rows, tile_rows)
+
+        @pl.loop(0, across)
+        def _(i):
+            to = pl.ds(pl.multiple_of(i * tile_columns, tile_columns), tile_columns)
+            share_ref[at, to] = dot_t(rows.all[at, :], weight_ref[to, :]).astype(bf16)
+
+        line.prime(b)
+
     third = LANES // 4
     first_cols = rows.items
     last_item = first_cols + cols.items
@@ -1419,7 +1547,7 @@
             product = rows_dot(rows.all[:, pl.ds(latent_at, LANES)], rows.left[...])
             wide_ref[:16, :] = product[:16, :] + product[third : third + 16, :]
 
-        @pl.when(step == line.second + 4)
+        @pl.when(step == line.count + SKEW * (n - 2) + 2)
         def _():
             wide_ref[16:, :] = gain_grad_ref[...]
             small.send()
@@ -1427,6 +1555,13 @@
         @pl.when(step == line.second + 14)
         def _():
             small.forward()
+
+    more_keep.wait()
+
+    @pl.loop(1, rows.team)
+    def _(k):
+        more_copy(0, lax.rem(rows.mine + k, rows.team)).wait_recv()
+        more_copy(lax.rem(rows.mine + k, rows.team), rows.mine).wait_send()
 
     rows.receive()
     cols.receive()
@@ -1454,16 +1589,22 @@
     wide_shape = (24, width)
     return pl.pallas_call(
         functools.partial(back_mixer_kernel, n, groups, widths, near_all, tiles),
-        in_specs=[vmem] * 3 + [far] * (7 + len(weights)),
-        out_specs=[vmem] * 3 + [far] * 2,
+        in_specs=[vmem] * 3 + [far] * (8 + len(weights)),
+        out_specs=[vmem] * 3 + [far] * 3,
         out_shape=[
             jax.ShapeDtypeStruct((count, width), bf16),
             jax.ShapeDtypeStruct((24, width // groups), f32),
             jax.ShapeDtypeStruct(near.shape[1:], f32),
             jax.ShapeDtypeStruct((groups // 2, width // groups, total), bf16),
             jax.ShapeDtypeStruct((groups, col_rows // groups, width // 2), bf16),
+            jax.ShapeDtypeStruct(pair[2].shape, bf16),
         ],
-        scratch_shapes=Line.scratch(half, width)
+        scratch_shapes=[
+            pltpu.VMEM(pair[2].shape, bf16),
+            pltpu.SemaphoreType.DMA((2, groups // 2)),
+            pltpu.SemaphoreType.DMA((3,)),
+        ]
+        + Line.scratch(half, width)
         + [
             pltpu.VMEM((half, width), x.dtype),
             pltpu.VMEM((half, width), base_own.dtype),
@@ -1490,7 +1631,7 @@
 
 def outputs_kernel(dk, dv, rank, near_all, *refs):
     take = splitter(refs)
-    feed_ref, rows_ref, down_ref, out_ref = take(4)
+    feed_ref, feed_more_ref, rows_ref, down_ref, out_ref = take(5)
     wide_ref, near_ref, token_ref, layer_ref = take(4)
     token_out, layer_out, query_out, key_out, value_out, gate_out = take(6)
     feed_gate_out, feed_up_out, feed_down_out, out_out, decay_out, vector_out = take(6)
@@ -1505,7 +1646,9 @@
 
     wide = feed_gate_out.shape[1]
     feed_gate_out[...] = total(feed_ref, 0, wide)
-    feed_up_out[...] = total(feed_ref, wide, wide)
+    there = feed_ref.shape[2] - wide
+    feed_up_out[:, :there] = total(feed_ref, wide, there)
+    feed_up_out[:, there:] = total(feed_more_ref, 0, wide - there)
     query_out[...] = total(rows_ref, 0, dk)
     key_out[...] = total(rows_ref, dk, dk)
     value_out[...] = total(rows_ref, 2 * dk, dv)
@@ -1513,7 +1656,7 @@
     token_out[...] = token_ref[...]
     layer_out[...] = layer_ref[...]
 
-    @pl.when(lax.rem(step, 4) == 0)
+    @pl.when(lax.rem(step, pl.num_programs(0) // 2) == 0)
     def _():
         half = out_out.shape[2] // 2
         for ref, out in ((down_ref, feed_down_out), (out_ref, out_out)):
@@ -1530,11 +1673,12 @@
 
 
 def outputs(
-    groups, dk, dv, rank, near_all, feed, rows, down, out, wide_sum, near_sum, token, layer
+    groups, dk, dv, rank, near_all, feed, feed_more, rows, down, out, wide_sum, near_sum, token,
+    layer,
 ):
-    steps = 8
+    steps = 4
     count, width = token.shape
-    wide = feed.shape[2] // 2
+    wide = (feed.shape[2] + feed_more.shape[2]) // 2
     per = width // groups
     block = per // steps
     shape = jax.ShapeDtypeStruct
@@ -1550,18 +1694,18 @@
 
     def recv_half(array):
         return pl.BlockSpec(
-            (array.shape[0], array.shape[1] // 2, array.shape[2]), lambda i: (0, i // 4, 0)
+            (array.shape[0], array.shape[1] // 2, array.shape[2]), lambda i: (0, i // (steps // 2), 0)
         )
 
     def out_half(array):
-        return pl.BlockSpec((1, array.shape[1] // 2, width), lambda i: (0, i // 4, 0))
+        return pl.BlockSpec((1, array.shape[1] // 2, width), lambda i: (0, i // (steps // 2), 0))
 
     tokens_block = pl.BlockSpec((count // steps, width), lambda i: (i, 0))
     return pl.pallas_call(
         functools.partial(outputs_kernel, dk, dv, rank, near_all),
         grid=(steps,),
         in_specs=[
-            recv(feed), recv(rows), recv_half(down), recv_half(out), fixed(wide_sum),
+            recv(feed), recv(feed_more), recv(rows), recv_half(down), recv_half(out), fixed(wide_sum),
             fixed(near_sum), tokens_block, tokens_block,
         ],
         out_specs=[
@@ -1586,7 +1730,7 @@
         ],
         compiler_params=pltpu.CompilerParams(vmem_limit_bytes=60 << 20),
         name="outputs",
-    )(feed, rows, down, out, wide_sum, near_sum, token, layer)
+    )(feed, feed_more, rows, down, out, wide_sum, near_sum, token, layer)
 
 
 def recur_back_kernel(n, groups, dk, dv, beside, *refs):
@@ -1661,29 +1805,30 @@
         line.step(2 * i)
         line.step(2 * i + 1)
 
-    go.send(0, send_row_ref, 0, d_attended)
+    go.send(0, send_row_ref, 0, d_attended, lambda h: line.step(4 + h))
     d_state[...] = jnp.zeros_like(d_state)
     grad_up_ref[...] = jnp.zeros_like(grad_up_ref)
     grad_bias_ref[...] = jnp.zeros_like(grad_bias_ref)
-    done = 12
+    done = 14
     if beside:
         cols.ready()
 
         @pl.loop(0, cols.items)
         def _(i):
             cols.item(i)
-            line.step(4 + 2 * i)
-            line.step(5 + 2 * i)
-
-        done = 4 + 2 * cols.items
+            line.step(6 + 2 * i)
+            line.step(7 + 2 * i)
+
+        done = 6 + 2 * cols.items
         cols.send_all()
     else:
-        line.run(4, done)
+        line.run(6, done)
     for c in loads[1:]:
         c.wait()
 
     go.receive(0)
-    place_rows(slot_row_ref, go.came, d_placed, go.spans[0])
+    place_rows(slot_row_ref, go.came, d_placed, go.spans[0], lambda h: line.step(done + h))
+    spanned = done + 2
     spans = held_ref.shape[0] // SPAN
 
     @pl.loop(0, spans)
@@ -1694,16 +1839,19 @@
             dk, dv, step, ends, d_out, held_ref, states_ref[step], up_ref, bias_ref, down_ref,
             d_state, result, grad_up_ref, grad_bias_ref,
         )
-        line.step(done + 2 * i)
-        line.step(done + 1 + 2 * i)
-
+        line.step(spanned + 2 * i)
+        line.step(spanned + 1 + 2 * i)
+
+    sent = spanned + 2 * spans
     for p in range(2):
-        back.send(p, slot_column_ref, 1, result)
-    line.run(done + 2 * spans, line.steps)
-    if beside:
-        cols.receive()
-
+        back.send(
+            p, slot_column_ref, 1, result, lambda h, p=p: line.step(sent + 2 * p + h)
+        )
+    last_steps = (sent + 4, sent + 4 + (line.steps - sent - 4) * 2 // 3, line.steps)
     for p in range(2):
+        line.run(last_steps[p], last_steps[p + 1])
+        if beside and p:
+            cols.receive()
         back.receive(p)
         span = back.spans[p]
 
@@ -1917,24 +2065,32 @@
     last = jnp.pad(jnp.concatenate([head_gain, decay_bias]), (0, width - dv - dk))
     gains = jnp.stack([mixer_gain, feed_gain, last]).astype(f32)
     (
-        normed, gate_pre, attended, gated, held, states, feed_normed, hidden_own, d_active, send_row,
-        send_column, slot_row, slot_column,
+        normed, gate_pre, attended, gated, held, states, mixer_share, send_row, send_column, slot_row,
+        slot_column,
     ) = front(
-        1, lines, groups, lengths, token_slots.reshape(groups, count), tokens, gains, up_rows,
-        down_rows, [query_weight, key_weight, value_weight], gate_weight, out_weight, cotangent,
-        feed_down,
+        1, groups, lengths, token_slots.reshape(-1, LANES), tokens, gains, up_rows,
+        down_rows, [query_weight, key_weight, value_weight], gate_weight, out_weight,
     )
 
     if fused:
-        d_mixed, d_hidden_own, feed_gain_part, feed_recv, active, layer_share = back_feed(
-            2, lines, groups, gains, hidden_own, cotangent, feed_normed,
-            d_active, feed_gate, feed_up, feed_down,
+        (
+            d_mixed, d_hidden_own, feed_gain_part, feed_recv, feed_more, active, layer_share,
+            hidden_own,
+        ) = back_feed(
+            2, lines, groups, gains, mixer_share, tokens, cotangent, feed_gate, feed_up, feed_down
         )
     else:
-        half = count // 2
-        own_at = jnp.where(place == 0, half, 0)
-        tokens_own = lax.dynamic_slice_in_dim(tokens, own_at, half)
-        cotangent_own = lax.dynamic_slice_in_dim(cotangent, own_at, half)
+        quarter = count // 4
+
+        def own_rows(rows):
+            blocks = rows.reshape(2, 2, quarter, width)
+            return jnp.where(place == 0, blocks[:, 1], blocks[:, 0]).reshape(2 * quarter, width)
+
+        tokens_own, cotangent_own = own_rows(tokens), own_rows(cotangent)
+        feed_normed, hidden_own, _ = line_sum(
+            "norm", 5, lines, mixer_share, tokens_own, tokens_own, gains[1:2]
+        )
+        d_active = dot_t(cotangent, feed_down).astype(bf16)
         gate_hidden = dot(feed_normed, feed_gate)
         up_hidden = dot(feed_normed, feed_up)
         d_active = d_active.astype(f32)
@@ -1947,7 +2103,7 @@
         d_up_hidden = (d_active * swish_gate).astype(bf16)
         feed_share = (dot_t(d_gate_hidden, feed_gate) + dot_t(d_up_hidden, feed_up)).astype(bf16)
         d_mixed, d_hidden_own, feed_gain_part = line_sum(
-            2, lines, feed_share, hidden_own, cotangent_own, gains[1:2]
+            "back", 2, lines, feed_share, hidden_own, cotangent_own, gains[1:2]
         )
         layer_share = dot(active, feed_down).astype(bf16)
 
@@ -1976,16 +2132,16 @@
         near_all = (per + head_per + LANES - 1) // LANES
         near = jnp.concatenate(near, axis=1)
         near = jnp.pad(near, ((0, 0), (0, -near.shape[1] % (8 * LANES))))
-        token_grad, wide_sum, near_sum, rows_recv, out_recv = back_mixer(
+        token_grad, wide_sum, near_sum, rows_recv, out_recv, feed_more = back_mixer(
             3, lines, groups, gains, near.reshape(groups, -1, LANES), near_all, down_rows, tokens,
-            d_hidden_own, normed, [d_rows, d_gate_low], (gated, d_mixed),
+            d_hidden_own, normed, [d_rows, d_gate_low], (gated, d_mixed, feed_more),
             [query_weight, key_weight, value_weight, gate_weight],
         )
         (
             token_grad, layer_out, grad_query, grad_key, grad_value, grad_gate, grad_feed_gate,
             grad_feed_up, grad_feed_down, grad_out, down_sum, mixer_sum,
         ) = outputs(
-            groups, dk, dv, rank, near_all, feed_recv, rows_recv, down_recv, out_recv,
+            groups, dk, dv, rank, near_all, feed_recv, feed_more, rows_recv, down_recv, out_recv,
             wide_sum, near_sum, token_grad, layer_out,
         )
         near_sum = near_sum.reshape(-1)
@@ -2011,7 +2167,7 @@
             + dot_t(d_latent_low, down_both)
         ).astype(bf16)
         token_grad, _, mixer_gain_part = line_sum(
-            3, lines, normed_share, tokens_own, d_hidden_own, gains[0:1],
+            "back", 3, lines, normed_share, tokens_own, d_hidden_own, gains[0:1],
         )
         down_part = rows_dot(normed, d_latent_low)
         down_part = down_part[:, :rank] + down_part[:, third : third + rank]

time: 450 us -> 430 us (0.956); the launches traced: 450 us -> 422 us
  Pallas kernels: 439 us -> 411 us
    pallas_call x1, Pallas kernels: 139 us -> 66.4 us  [front(): pl.pallas_call(functools.partial(front_kernel, groups, dk, dv), in_specs=...]
    pallas_call x1, Pallas kernels: 102 us -> 153 us  [back_feed(): pl.pallas_call(functools.partial(back_feed_kernel, n, groups, tiles), in_...]
    pallas_call x1, Pallas kernels: 95.8 us -> 90.6 us  [recur_back(): pl.pallas_call(functools.partial(recur_back_kernel, n, groups, dk, dv, be...]
where the time goes in v8:
time: 430 us; the launch traced here: 422 us
  Pallas kernels  411 us (96%)
  local copies, waits for them, and re-layouts  5.35 us (1%)
    pallas_call x1, Pallas kernels, back_feed(): pl.pallas_call(functools.partial(back_feed_kernel, n, groups, tiles), in_...  153 us
    pallas_call x1, Pallas kernels, recur_back(): pl.pallas_call(functools.partial(recur_back_kernel, n, groups, dk, dv, be...  90.6 us
    pallas_call x1, Pallas kernels, back_mixer(): pl.pallas_call(functools.partial(back_mixer_kernel, n, groups, widths, ne...  89.6 us
    pallas_call x1, Pallas kernels, front(): pl.pallas_call(functools.partial(front_kernel, groups, dk, dv), in_specs=...  66.4 us
    pallas_call x1, Pallas kernels, outputs(): pl.pallas_call(functools.partial(outputs_kernel, dk, dv, rank, near_all),...  11.9 us

profile of v8, /device:TPU:0, one launch (start us, length us, event | category | flops | bytes accessed | tf_op | source)
XLA Modules:
  0.0 422.0 jit_solution(13993452709623189669)
XLA Ops:
  0.6 0.7 fusion.5
  1.4 0.7 stack.12
  2.1 0.7 stack.13
  2.7 0.6 maximum_convert_fusion.refs_3_.refs_0_.refs_9_
  3.4 66.4 %front.1 = (bf16[640,2048]{1,0:T(8,128)(2,1)}, f32[640,512]{1,0:T(8,128)}, bf16[640,512]{1,0:T(8,128)(2,1)}, bf16[640,512]{1,0:T(8,128)(2,1)}, bf16[1024,1152]{1...) custom-call(s32[1,3]{1,0:T(1,128)} %refs_0_.3, ...), custom_call_target="tpu_custom_call" | custom-call | flops 12000000000 | bytes 200000000 | tf_op jit(solution)/shard_map/front/pallas_call | solution.py:977
  69.8 152.8 %back_feed.1 = (bf16[640,2048]{1,0:T(8,128)(2,1)}, f32[320,2048]{1,0:T(8,128)}, f32[8,2048]{1,0:T(8,128)}, bf16[4,256,2176]{2,1,0:T(8,128)(2,1)}, bf16[4,256,640...) custom-call(f32[3,2048]{1,0:T(4,128)} %maximum_convert_fusion.refs_3_.refs_0_.refs_, ...), custom_call_target="tpu_custom_call" | custom-call | flops 30000001024 | bytes 200000000 | tf_op jit(solution)/shard_map/back_feed/pallas_call | solution.py:1275
  222.6 0.9 reduce_sum.18
  223.4 90.6 %recur_back.1 = (bf16[640,1152]{1,0:T(8,128)(2,1)}, bf16[640,512]{1,0:T(8,128)(2,1)}, f32[8,512]{1,0:T(8,128)}, f32[256,128]{1,0:T(8,128)}, f32[8,256]{1,0:T(8,1...) custom-call(s32[1,3]{1,0:T(1,128)} %refs_0_.3, s32[1,640]{1,0:T(1,128)} %get-tuple-element.63.refs_1_, ...), custom_call_target="tpu_custom_call" | custom-call | flops 12000000000 | bytes 200000000 | tf_op jit(solution)/shard_map/recur_back/pallas_call | solution.py:1883
  314.0 0.7 reduce_sum.19
  314.8 0.7 slice_reduce_fusion
  315.5 0.1 reshape.65
  315.6 0.1 reshape_squeeze.3
  315.6 1.2 slice_add_fusion
  316.8 0.1 reshape.66
  317.0 0.6 copy.38
  317.6 89.6 %back_mixer.1 = (bf16[640,2048]{1,0:T(8,128)(2,1)}, f32[24,256]{1,0:T(8,128)}, f32[8,128]{1,0:T(8,128)}, bf16[4,256,1664]{2,1,0:T(8,128)(2,1)}, bf16[8,64,1024]{...) custom-call(f32[3,2048]{1,0:T(4,128)} %maximum_convert_fusion.refs_3_.refs_0_.refs_9_, f32[8,8,128]{2,1,0:T(8,128)} %bitcast.13, ...), custom_call_target="tpu_custom_call" | custom-call | flops 12000000000 | bytes 200000000 | tf_op jit(solution)/shard_map/back_mixer/pallas_call | solution.py:1590
  407.2 0.0 copy-start
  407.2 11.9 %outputs.1 = (bf16[640,2048]{1,0:T(8,128)(2,1)}, bf16[640,2048]{1,0:T(8,128)(2,1)}, f32[256,256]{1,0:T(8,128)}, f32[256,256]{1,0:T(8,128)}, f32[256,512]{1,0:T(8...) custom-call(bf16[4,256,2176]{2,1,0:T(8,128)(2,1)} %get-tuple-element, ...), custom_call_target="tpu_custom_call" | custom-call | tf_op jit(solution)/shard_map/outputs/pallas_call | solution.py:1704
  419.2 0.0 copy-done
  419.2 0.5 slice.38
  419.7 0.5 slice.37
  420.2 0.6 slice_bitcast_fusion
  420.8 0.1 reshape.69
  420.9 0.7 copy.35
  (4 shorter events, 0.0 us)
Async XLA Ops:
  407.2 12.0 %copy-start = (f32[8,128]{1,0:T(8,128)S(1)}, f32[8,128]{1,0:T(8,128)}, u32[]{:S(2)}) copy-start(f32[8,128]{1,0:T(8,128)} %get-tuple-element.89.refs_6_) | copy-start | bytes 12292

commit v9 on v8

--- a/solution.py
+++ b/solution.py
@@ -1189,47 +1189,38 @@
 
     layer_items = width // 512
     first_work = 8
-
-    def row_work(w):
-        @pl.when(w == 0)
-        def _():
-            @pl.loop(0, rows.team)
-            def _(q):
-                rows.left_copy(q).wait_recv()
-
-            for b in range(2):
-                def arrive(i, size, b=b):
-                    for c in piece_copies(b, i, size):
-                        c.wait_recv()
-
-                each(arrive)
-
-        rows.item(w)
-
-    @pl.loop(0, per)
+    if 2 * (per - pieces) < share_items:
+        raise ValueError("shares late")
+
+    @pl.loop(0, line.steps)
     def _(step):
+        @pl.when(step == per)
+        def _():
+            line.prime(1)
+            active_spill.start()
+            down_load.start()
+
         line.step(step)
         at_item(step, lambda i, size: hidden_units(1, i, size))
         w = 2 * (step - pieces)
         make_share(1, w)
         make_share(1, w + 1)
-        row_work(step - first_work)
-
-    done_more = 2 * (per - pieces)
-
-    @pl.loop(done_more, max(share_items, done_more))
-    def _(w):
-        make_share(1, w)
-
-    line.prime(1)
-    active_spill.start()
-    down_load.start()
-
-    @pl.loop(per, line.steps)
-    def _(step):
-        line.step(step)
         w = step - first_work
-        row_work(w)
+
+        @pl.when(w == 0)
+        def _():
+            @pl.loop(0, rows.team)
+            def _(q):
+                rows.left_copy(q).wait_recv()
+
+            for b in range(2):
+                def arrive(i, size, b=b):
+                    for c in piece_copies(b, i, size):
+                        c.wait_recv()
+
+                each(arrive)
+
+        rows.item(w)
 
         @pl.when(w == rows.items)
         def _():

time: 430 us -> 422 us (0.981); the launches traced: 422 us -> 422 us
  no operation moved by 1% of the time
where the time goes in v9:
time: 422 us
  Pallas kernels  412 us (98%)
  local copies, waits for them, and re-layouts  5.35 us (1%)
    pallas_call x1, Pallas kernels, back_feed(): pl.pallas_call(functools.partial(back_feed_kernel, n, groups, tiles), in_...  153 us
    pallas_call x1, Pallas kernels, recur_back(): pl.pallas_call(functools.partial(recur_back_kernel, n, groups, dk, dv, be...  90.7 us
    pallas_call x1, Pallas kernels, back_mixer(): pl.pallas_call(functools.partial(back_mixer_kernel, n, groups, widths, ne...  89.6 us
    pallas_call x1, Pallas kernels, front(): pl.pallas_call(functools.partial(front_kernel, groups, dk, dv), in_specs=...  66.4 us
    pallas_call x1, Pallas kernels, outputs(): pl.pallas_call(functools.partial(outputs_kernel, dk, dv, rank, near_all),...  11.9 us

profile of v9, /device:TPU:0, one launch (start us, length us, event | category | flops | bytes accessed | tf_op | source)
XLA Modules:
  0.0 421.8 jit_solution(4122439630741143933)
XLA Ops:
  0.6 0.7 fusion.5
  1.4 0.7 stack.12
  2.1 0.7 stack.13
  2.7 0.6 maximum_convert_fusion.refs_3_.refs_0_.refs_9_
  3.4 66.4 %front.1 = (bf16[640,2048]{1,0:T(8,128)(2,1)}, f32[640,512]{1,0:T(8,128)}, bf16[640,512]{1,0:T(8,128)(2,1)}, bf16[640,512]{1,0:T(8,128)(2,1)}, bf16[1024,1152]{1...) custom-call(s32[1,3]{1,0:T(1,128)} %refs_0_.3, ...), custom_call_target="tpu_custom_call" | custom-call | flops 12000000000 | bytes 200000000 | tf_op jit(solution)/shard_map/front/pallas_call | solution.py:977
  69.8 152.9 %back_feed.1 = (bf16[640,2048]{1,0:T(8,128)(2,1)}, f32[320,2048]{1,0:T(8,128)}, f32[8,2048]{1,0:T(8,128)}, bf16[4,256,2176]{2,1,0:T(8,128)(2,1)}, bf16[4,256,640...) custom-call(f32[3,2048]{1,0:T(4,128)} %maximum_convert_fusion.refs_3_.refs_0_.refs_, ...), custom_call_target="tpu_custom_call" | custom-call | flops 30000001024 | bytes 200000000 | tf_op jit(solution)/shard_map/back_feed/pallas_call | solution.py:1266
  222.7 0.9 reduce_sum.18
  223.6 90.7 %recur_back.1 = (bf16[640,1152]{1,0:T(8,128)(2,1)}, bf16[640,512]{1,0:T(8,128)(2,1)}, f32[8,512]{1,0:T(8,128)}, f32[256,128]{1,0:T(8,128)}, f32[8,256]{1,0:T(8,1...) custom-call(s32[1,3]{1,0:T(1,128)} %refs_0_.3, s32[1,640]{1,0:T(1,128)} %get-tuple-element.63.refs_1_, ...), custom_call_target="tpu_custom_call" | custom-call | flops 12000000000 | bytes 200000000 | tf_op jit(solution)/shard_map/recur_back/pallas_call | solution.py:1874
  314.3 0.7 reduce_sum.19
  315.1 0.7 slice_reduce_fusion
  315.8 0.1 reshape.65
  315.9 0.1 reshape_squeeze.3
  315.9 1.2 slice_add_fusion
  317.1 0.1 reshape.66
  317.2 0.6 copy.38
  317.9 89.6 %back_mixer.1 = (bf16[640,2048]{1,0:T(8,128)(2,1)}, f32[24,256]{1,0:T(8,128)}, f32[8,128]{1,0:T(8,128)}, bf16[4,256,1664]{2,1,0:T(8,128)(2,1)}, bf16[8,64,1024]{...) custom-call(f32[3,2048]{1,0:T(4,128)} %maximum_convert_fusion.refs_3_.refs_0_.refs_9_, f32[8,8,128]{2,1,0:T(8,128)} %bitcast.13, ...), custom_call_target="tpu_custom_call" | custom-call | flops 12000000000 | bytes 200000000 | tf_op jit(solution)/shard_map/back_mixer/pallas_call | solution.py:1581
  407.5 0.0 copy-start
  407.5 11.9 %outputs.1 = (bf16[640,2048]{1,0:T(8,128)(2,1)}, bf16[640,2048]{1,0:T(8,128)(2,1)}, f32[256,256]{1,0:T(8,128)}, f32[256,256]{1,0:T(8,128)}, f32[256,512]{1,0:T(8...) custom-call(bf16[4,256,2176]{2,1,0:T(8,128)(2,1)} %get-tuple-element, ...), custom_call_target="tpu_custom_call" | custom-call | tf_op jit(solution)/shard_map/outputs/pallas_call | solution.py:1695
  419.4 0.0 copy-done
  419.4 0.5 slice.38
  419.9 0.5 slice.37
  420.5 0.6 slice_bitcast_fusion
  421.0 0.1 reshape.69
  421.1 0.7 copy.35
  (4 shorter events, 0.0 us)
Async XLA Ops:
  407.5 12.0 %copy-start = (f32[8,128]{1,0:T(8,128)S(1)}, f32[8,128]{1,0:T(8,128)}, u32[]{:S(2)}) copy-start(f32[8,128]{1,0:T(8,128)} %get-tuple-element.89.refs_6_) | copy-start | bytes 12292

commit v10 on v9

--- a/solution.py
+++ b/solution.py
@@ -454,9 +454,8 @@
 
 
 class ColGrad:
-    TILE = 256
-
-    def __init__(self, groups, left, right, first, recv, refs):
+    def __init__(self, groups, left, right, first, tile, recv, refs):
+        self.tile = tile
         (
             self.left, self.right, self.left_in, self.right_in, self.send,
             self.load_sems, self.pair_sems, self.sems,
@@ -467,7 +466,7 @@
         self.half = right.shape[1] // 2
         self.first, self.wide = first, self.right_in.shape[1]
         self.size = self.send.shape[0] // groups
-        self.items = self.wide // self.TILE
+        self.items = self.wide // self.tile
 
     @staticmethod
     def scratch(groups, count, rows, wide):
@@ -483,7 +482,7 @@
         ]
 
     def halves(self, parity):
-        start = pl.multiple_of(parity * self.half + self.first, self.TILE)
+        start = pl.multiple_of(parity * self.half + self.first, self.tile)
         return self.right_far.at[:, pl.ds(start, self.wide)]
 
     def loads(self):
@@ -513,7 +512,7 @@
             c.wait_recv()
 
     def item(self, t):
-        span = pl.ds(pl.multiple_of(t * self.TILE, self.TILE), self.TILE)
+        span = pl.ds(pl.multiple_of(t * self.tile, self.tile), self.tile)
         product = rows_dot(self.left[...], self.right[:, span]) + rows_dot(
             self.left_in[...], self.right_in[:, span]
         )
@@ -1152,7 +1151,7 @@
 
     per = first_line.block // FINE
     arrived = first_line.second + SKEW * (n - 2) + per
-    d_first = 3
+    d_first = 10
 
     @pl.loop(0, first_line.steps)
     def _(step):
@@ -1435,7 +1434,7 @@
     ]
     part_loads = [rows.piece_load(i, parts[i], part_spans[i]) for i in range(2)]
     part_copies = [rows.piece_copy(i, parts[i], part_spans[i]) for i in range(2)]
-    cols = ColGrad(groups, col_left, col_right, 0, col_recv, take(8))
+    cols = ColGrad(groups, col_left, col_right, 0, 256, col_recv, take(8))
     small = SmallSum(n, groups, wide_ref, near_ref, near_all, wide_out, near_out, take(6))
     finish = norm_back(
         x_ref, lambda own, place: base_ref[own, :], lambda: gains_ref[0:1, :], out_ref, None,
@@ -1727,17 +1726,18 @@
 def recur_back_kernel(n, groups, dk, dv, beside, *refs):
     (
         lengths_ref, send_row_ref, send_column_ref, slot_row_ref, slot_column_ref,
-        d_mixed_ref, out_weight_ref, attended_ref, gate_ref, gains_ref, up_rows_ref,
+        d_mixed_far, out_weight_far, attended_ref, gate_ref, gains_ref, up_rows_ref,
         share_ref, held_far, states_far, hidden_far, active_far, cotangent_far,
         d_rows_ref, d_gate_ref, head_gain_ref, grad_up_ref, grad_bias_ref, layer_ref, grad_down_ref,
         up_in, down_in, d_attended, d_placed, d_state, result,
         held_ref, states_ref, hidden_ref, up_ref, down_ref, bias_ref, load_sems, sems,
-    ) = refs[:38]
-    go = Exchange(groups, (), *refs[38:41])
-    back = Exchange(groups, (2 * dk,), *refs[41:44])
+        d_mixed_ref, out_weight_ref,
+    ) = refs[:40]
+    go = Exchange(groups, (), *refs[40:43])
+    back = Exchange(groups, (2 * dk,), *refs[43:46])
     cols = None
     if beside:
-        cols = ColGrad(groups, active_far, cotangent_far, 0, grad_down_ref, refs[44:])
+        cols = ColGrad(groups, active_far, cotangent_far, 0, 512, grad_down_ref, refs[46:])
     count = d_mixed_ref.shape[0]
     slots = slot_row_ref.shape[1]
     end0 = lengths_ref[0, 0]
@@ -1753,6 +1753,12 @@
         pltpu.make_async_copy(held_far, held_ref, load_sems.at[1]),
         pltpu.make_async_copy(states_far, states_ref, load_sems.at[2]),
     )
+    head_loads = (
+        pltpu.make_async_copy(d_mixed_far, d_mixed_ref, load_sems.at[3]),
+        pltpu.make_async_copy(out_weight_far, out_weight_ref, load_sems.at[4]),
+    )
+    for c in head_loads:
+        c.start()
     barrier = pltpu.get_barrier_semaphore()
     greet_dp(barrier, groups)
     line.greet(barrier, groups - 1)
@@ -1769,6 +1775,8 @@
 
     head_gain_ref[...] = jnp.zeros_like(head_gain_ref)
     tile = count // 2
+    for c in head_loads:
+        c.wait()
 
     @pl.loop(0, 2)
     def _(i):
@@ -1873,7 +1881,11 @@
     far = pl.BlockSpec(memory_space=pl.ANY)
     return pl.pallas_call(
         functools.partial(recur_back_kernel, n, groups, dk, dv, beside),
-        in_specs=[pl.BlockSpec(memory_space=pltpu.SMEM)] + [vmem] * (len(operands) - 6) + [far] * 5,
+        in_specs=[pl.BlockSpec(memory_space=pltpu.SMEM)]
+        + [vmem] * 4
+        + [far] * 2
+        + [vmem] * (len(operands) - 12)
+        + [far] * 5,
         out_specs=[vmem] * 6 + [far],
         out_shape=[
             jax.ShapeDtypeStruct((count, wide), bf16),
@@ -1898,8 +1910,10 @@
             pltpu.VMEM((LANES, dk), bf16),
             pltpu.VMEM((LANES, dk), bf16),
             pltpu.VMEM((1, dk), f32),
-            pltpu.SemaphoreType.DMA((3,)),
+            pltpu.SemaphoreType.DMA((5,)),
             Line.semaphores(half),
+            pltpu.VMEM(d_mixed.shape, bf16),
+            pltpu.VMEM(out_weight.shape, bf16),
         ]
         + Exchange.scratch(groups, slots, dv, 1)
         + Exchange.scratch(groups, slots, wide, 2)

time: 422 us -> 420 us (level)
  no operation moved by 1% of the time
where the time goes in v10:
time: 420 us; the launch traced here: 419 us
  Pallas kernels  409 us (97%)
  local copies, waits for them, and re-layouts  5.35 us (1%)
    pallas_call x1, Pallas kernels, back_feed(): pl.pallas_call(functools.partial(back_feed_kernel, n, groups, tiles), in_...  153 us
    pallas_call x1, Pallas kernels, recur_back(): pl.pallas_call(functools.partial(recur_back_kernel, n, groups, dk, dv, be...  90.7 us
    pallas_call x1, Pallas kernels, back_mixer(): pl.pallas_call(functools.partial(back_mixer_kernel, n, groups, widths, ne...  87 us
    pallas_call x1, Pallas kernels, front(): pl.pallas_call(functools.partial(front_kernel, groups, dk, dv), in_specs=...  66.4 us
    pallas_call x1, Pallas kernels, outputs(): pl.pallas_call(functools.partial(outputs_kernel, dk, dv, rank, near_all),...  11.9 us

profile of v10, /device:TPU:0, one launch (start us, length us, event | category | flops | bytes accessed | tf_op | source)
XLA Modules:
  0.0 419.2 jit_solution(8397155944174800189)
XLA Ops:
  0.6 0.7 fusion.5
  1.4 0.7 stack.12
  2.1 0.7 stack.13
  2.7 0.6 maximum_convert_fusion.refs_3_.refs_0_.refs_9_
  3.4 66.4 %front.1 = (bf16[640,2048]{1,0:T(8,128)(2,1)}, f32[640,512]{1,0:T(8,128)}, bf16[640,512]{1,0:T(8,128)(2,1)}, bf16[640,512]{1,0:T(8,128)(2,1)}, bf16[1024,1152]{1...) custom-call(s32[1,3]{1,0:T(1,128)} %refs_0_.3, ...), custom_call_target="tpu_custom_call" | custom-call | flops 12000000000 | bytes 200000000 | tf_op jit(solution)/shard_map/front/pallas_call | solution.py:976
  69.8 152.9 %back_feed.1 = (bf16[640,2048]{1,0:T(8,128)(2,1)}, f32[320,2048]{1,0:T(8,128)}, f32[8,2048]{1,0:T(8,128)}, bf16[4,256,2176]{2,1,0:T(8,128)(2,1)}, bf16[4,256,640...) custom-call(f32[3,2048]{1,0:T(4,128)} %maximum_convert_fusion.refs_3_.refs_0_.refs_, ...), custom_call_target="tpu_custom_call" | custom-call | flops 30000001024 | bytes 200000000 | tf_op jit(solution)/shard_map/back_feed/pallas_call | solution.py:1265
  222.7 0.9 reduce_sum.18
  223.6 90.7 %recur_back.1 = (bf16[640,1152]{1,0:T(8,128)(2,1)}, bf16[640,512]{1,0:T(8,128)(2,1)}, f32[8,512]{1,0:T(8,128)}, f32[256,128]{1,0:T(8,128)}, f32[8,256]{1,0:T(8,1...) custom-call(s32[1,3]{1,0:T(1,128)} %refs_0_.3, s32[1,640]{1,0:T(1,128)} %get-tuple-element.63.refs_1_, ...), custom_call_target="tpu_custom_call" | custom-call | flops 12000000000 | bytes 200000000 | tf_op jit(solution)/shard_map/recur_back/pallas_call | solution.py:1882
  314.3 0.7 reduce_sum.19
  315.0 0.7 slice_reduce_fusion
  315.8 0.1 reshape.65
  315.8 0.1 reshape_squeeze.3
  315.9 1.2 slice_add_fusion
  317.1 0.1 reshape.66
  317.2 0.6 copy.38
  317.9 87.0 %back_mixer.1 = (bf16[640,2048]{1,0:T(8,128)(2,1)}, f32[24,256]{1,0:T(8,128)}, f32[8,128]{1,0:T(8,128)}, bf16[4,256,1664]{2,1,0:T(8,128)(2,1)}, bf16[8,64,1024]{...) custom-call(f32[3,2048]{1,0:T(4,128)} %maximum_convert_fusion.refs_3_.refs_0_.refs_9_, f32[8,8,128]{2,1,0:T(8,128)} %bitcast.13, ...), custom_call_target="tpu_custom_call" | custom-call | flops 12000000000 | bytes 200000000 | tf_op jit(solution)/shard_map/back_mixer/pallas_call | solution.py:1580
  404.8 0.0 copy-start
  404.9 11.9 %outputs.1 = (bf16[640,2048]{1,0:T(8,128)(2,1)}, bf16[640,2048]{1,0:T(8,128)(2,1)}, f32[256,256]{1,0:T(8,128)}, f32[256,256]{1,0:T(8,128)}, f32[256,512]{1,0:T(8...) custom-call(bf16[4,256,2176]{2,1,0:T(8,128)(2,1)} %get-tuple-element, ...), custom_call_target="tpu_custom_call" | custom-call | tf_op jit(solution)/shard_map/outputs/pallas_call | solution.py:1694
  416.8 0.0 copy-done
  416.8 0.5 slice.38
  417.3 0.5 slice.37
  417.9 0.6 slice_bitcast_fusion
  418.4 0.1 reshape.69
  418.5 0.7 copy.35
  (4 shorter events, 0.0 us)
Async XLA Ops:
  404.8 12.0 %copy-start = (f32[8,128]{1,0:T(8,128)S(1)}, f32[8,128]{1,0:T(8,128)}, u32[]{:S(2)}) copy-start(f32[8,128]{1,0:T(8,128)} %get-tuple-element.89.refs_6_) | copy-start | bytes 12292

commit v11 on v10

--- a/solution.py
+++ b/solution.py
@@ -919,7 +919,7 @@
         go.receive(p)
         place_rows(slot_row_ref, go.came, held_ref, go.spans[p])
 
-    @pl.loop(0, held_ref.shape[0] // SPAN)
+    @pl.loop(0, held_ref.shape[0] // SPAN, unroll=2)
     def _(step):
         span_forward(dk, dv, step, ends, held_ref, up_ref, bias_ref, state, states_ref, result)
 

time: 420 us -> 419 us (level)
  no operation moved by 1% of the time
where the time goes in v11:
time: 419 us
  Pallas kernels  408 us (97%)
  local copies, waits for them, and re-layouts  5.35 us (1%)
    pallas_call x1, Pallas kernels, back_feed(): pl.pallas_call(functools.partial(back_feed_kernel, n, groups, tiles), in_...  153 us
    pallas_call x1, Pallas kernels, recur_back(): pl.pallas_call(functools.partial(recur_back_kernel, n, groups, dk, dv, be...  90.7 us
    pallas_call x1, Pallas kernels, back_mixer(): pl.pallas_call(functools.partial(back_mixer_kernel, n, groups, widths, ne...  86.9 us
    pallas_call x1, Pallas kernels, front(): pl.pallas_call(functools.partial(front_kernel, groups, dk, dv), in_specs=...  65.8 us
    pallas_call x1, Pallas kernels, outputs(): pl.pallas_call(functools.partial(outputs_kernel, dk, dv, rank, near_all),...  11.9 us

profile of v11, /device:TPU:0, one launch (start us, length us, event | category | flops | bytes accessed | tf_op | source)
XLA Modules:
  0.0 418.5 jit_solution(18150572484833034744)
XLA Ops:
  0.6 0.7 fusion.5
  1.4 0.7 stack.12
  2.1 0.7 stack.13
  2.7 0.6 maximum_convert_fusion.refs_3_.refs_0_.refs_9_
  3.4 65.8 %front.1 = (bf16[640,2048]{1,0:T(8,128)(2,1)}, f32[640,512]{1,0:T(8,128)}, bf16[640,512]{1,0:T(8,128)(2,1)}, bf16[640,512]{1,0:T(8,128)(2,1)}, bf16[1024,1152]{1...) custom-call(s32[1,3]{1,0:T(1,128)} %refs_0_.3, ...), custom_call_target="tpu_custom_call" | custom-call | flops 12000000000 | bytes 200000000 | tf_op jit(solution)/shard_map/front/pallas_call | solution.py:976
  69.2 152.9 %back_feed.1 = (bf16[640,2048]{1,0:T(8,128)(2,1)}, f32[320,2048]{1,0:T(8,128)}, f32[8,2048]{1,0:T(8,128)}, bf16[4,256,2176]{2,1,0:T(8,128)(2,1)}, bf16[4,256,640...) custom-call(f32[3,2048]{1,0:T(4,128)} %maximum_convert_fusion.refs_3_.refs_0_.refs_, ...), custom_call_target="tpu_custom_call" | custom-call | flops 30000001024 | bytes 200000000 | tf_op jit(solution)/shard_map/back_feed/pallas_call | solution.py:1265
  222.1 0.9 reduce_sum.18
  223.0 90.7 %recur_back.1 = (bf16[640,1152]{1,0:T(8,128)(2,1)}, bf16[640,512]{1,0:T(8,128)(2,1)}, f32[8,512]{1,0:T(8,128)}, f32[256,128]{1,0:T(8,128)}, f32[8,256]{1,0:T(8,1...) custom-call(s32[1,3]{1,0:T(1,128)} %refs_0_.3, s32[1,640]{1,0:T(1,128)} %get-tuple-element.63.refs_1_, ...), custom_call_target="tpu_custom_call" | custom-call | flops 12000000000 | bytes 200000000 | tf_op jit(solution)/shard_map/recur_back/pallas_call | solution.py:1882
  313.7 0.7 reduce_sum.19
  314.5 0.7 slice_reduce_fusion
  315.2 0.1 reshape.65
  315.3 0.1 reshape_squeeze.3
  315.3 1.2 slice_add_fusion
  316.5 0.1 reshape.66
  316.6 0.6 copy.38
  317.3 86.9 %back_mixer.1 = (bf16[640,2048]{1,0:T(8,128)(2,1)}, f32[24,256]{1,0:T(8,128)}, f32[8,128]{1,0:T(8,128)}, bf16[4,256,1664]{2,1,0:T(8,128)(2,1)}, bf16[8,64,1024]{...) custom-call(f32[3,2048]{1,0:T(4,128)} %maximum_convert_fusion.refs_3_.refs_0_.refs_9_, f32[8,8,128]{2,1,0:T(8,128)} %bitcast.13, ...), custom_call_target="tpu_custom_call" | custom-call | flops 12000000000 | bytes 200000000 | tf_op jit(solution)/shard_map/back_mixer/pallas_call | solution.py:1580
  404.2 0.0 copy-start
  404.2 11.9 %outputs.1 = (bf16[640,2048]{1,0:T(8,128)(2,1)}, bf16[640,2048]{1,0:T(8,128)(2,1)}, f32[256,256]{1,0:T(8,128)}, f32[256,256]{1,0:T(8,128)}, f32[256,512]{1,0:T(8...) custom-call(bf16[4,256,2176]{2,1,0:T(8,128)(2,1)} %get-tuple-element, ...), custom_call_target="tpu_custom_call" | custom-call | tf_op jit(solution)/shard_map/outputs/pallas_call | solution.py:1694
  416.1 0.0 copy-done
  416.2 0.5 slice.38
  416.7 0.5 slice.37
  417.2 0.6 slice_bitcast_fusion
  417.8 0.1 reshape.69
  417.8 0.7 copy.35
  (4 shorter events, 0.0 us)
Async XLA Ops:
  404.2 12.0 %copy-start = (f32[8,128]{1,0:T(8,128)S(1)}, f32[8,128]{1,0:T(8,128)}, u32[]{:S(2)}) copy-start(f32[8,128]{1,0:T(8,128)} %get-tuple-element.89.refs_6_) | copy-start | bytes 12292
